TPU v7x, 512 devices: a whole 4x4x16 slice. The times are simulated.
512 devices in a mesh: dp: 8 (over y, x_lo), ctx: 64 (over z, x_hi, core).
Axes of the slice: x: 4 (x_hi: 2, x_lo: 2; x = x_hi * 2 + x_lo), y: 4, z: 16, core: 2. Of those that a mesh axis runs over, the one named last changes fastest.
Arguments:
- events: bfloat16 [8, 16384, 1024], P('dp', 'ctx'), may hold values from -6 to 6
- w_query: bfloat16 [1024, 512], replicated, may hold values from -0.1875 to 0.1875
- w_key: bfloat16 [1024, 512], replicated, may hold values from -0.1875 to 0.1875
- values: bfloat16 [8, 16384, 512], P('dp', 'ctx'), may hold values from -6 to 6
- grad_out: bfloat16 [8, 16384, 512], P('dp', 'ctx'), may hold values from -6 to 6
- lengths: int32 [8, 32], P('dp'), may hold values from 1 to 768, 16384 in all within a row
- stream_shift: int32 [8], P('dp'), may hold values from 0 to 16383
- block_keep: int32 [8, 128], P('dp'), may hold values 0 or 1
Outputs:
- attended: bfloat16 [8, 16384, 512], P('dp', 'ctx')
- grad_values: bfloat16 [8, 16384, 512], P('dp', 'ctx')
- grad_wq: bfloat16 [1024, 512], P('ctx')
- grad_wk: bfloat16 [1024, 512], P('ctx')
Inputs may be any that keep to these rules, and one draw needn't show every extreme that they name: The lengths of a stream sum to 16384; the longest is exactly 768.
All inputs are finite; a program needn't handle non-finite values. No bound on the sum of `block_keep` on one device may be relied on, other than what follows from the above.
Results may differ from a plain program's by a relative error of at most 0.011.
Values may be sent and summed in bfloat16 or wider, within the bound.
A program may use at most 64 MiB of HBM per device.

v0:
```python
import jax
import jax.numpy as jnp
from jax import lax
from jax.sharding import PartitionSpec as P

HD = 128
SPAN = 3
BLOCK = 128
MAXLEN = 768


def from_behind(value, axis, steps):
    count = lax.axis_size(axis)
    pairs = [(source, (source + steps) % count) for source in range(count)]
    return lax.ppermute(value, axis, pairs)


def tile_terms(query, grad, key, value, valid, scale, alpha):
    z = jnp.einsum("qhd,khd->hqk", query, key, preferred_element_type=jnp.float32) * alpha
    sig = jax.nn.sigmoid(z)
    weight = valid[None, :, :].astype(jnp.float32) * scale
    att = (z * sig * weight).astype(jnp.bfloat16)
    out = jnp.einsum("hqk,khd->qhd", att, value, preferred_element_type=jnp.float32)
    dprod = jnp.einsum("qhd,khd->hqk", grad, value, preferred_element_type=jnp.float32)
    dsc = (dprod * sig * (1.0 + z * (1.0 - sig)) * weight * alpha).astype(jnp.bfloat16)
    dquery = jnp.einsum("hqk,khd->qhd", dsc, key, preferred_element_type=jnp.float32)
    dkey = jnp.einsum("hqk,qhd->khd", dsc, query, preferred_element_type=jnp.float32)
    dvalue = jnp.einsum("hqk,qhd->khd", att, grad, preferred_element_type=jnp.float32)
    return (out, dquery, dkey, dvalue)


def body(events, w_query, w_key, values, grad_out, lengths, stream_shift, block_keep):
    rows = events.shape[1]
    features = w_query.shape[1]
    nheads = features // HD
    alpha = 1.0 / HD**0.5
    scale = 1.0 / MAXLEN**0.5
    local = events[0]
    queries = jnp.dot(local, w_query, preferred_element_type=jnp.float32).astype(jnp.bfloat16)
    keys = jnp.dot(local, w_key, preferred_element_type=jnp.float32).astype(jnp.bfloat16)
    queries = queries.reshape(rows, nheads, HD)
    keys = keys.reshape(rows, nheads, HD)
    vals = values[0].reshape(rows, nheads, HD)
    cotan = grad_out[0].reshape(rows, nheads, HD)
    cycle_size = lax.axis_size("ctx")
    myself = lax.axis_index("ctx")
    total = rows * cycle_size
    ends = jnp.cumsum(lengths[0])
    offset = stream_shift[0]
    keep = block_keep[0]
    blocks_all = jnp.arange(keep.shape[0], dtype=jnp.int32)
    within = jnp.arange(rows, dtype=jnp.int32)

    def describe(anchor):
        anchor = jnp.remainder(anchor, cycle_size)
        position = jnp.remainder(anchor * rows + within - offset, total)
        owner = jnp.sum((position[:, None] >= ends[None, :]).astype(jnp.int32), axis=1)
        which = position // BLOCK
        kept = (
            jnp.sum(jnp.where(which[:, None] == blocks_all[None, :], keep[None, :], 0), axis=1) > 0
        )
        return (position, owner, kept)

    zeros = jnp.zeros((rows, nheads, HD), jnp.float32)
    qinfo = describe(myself)
    moving = (keys, vals)
    carried = (zeros, zeros)
    out_acc = zeros
    dq_acc = zeros
    for step in range(SPAN + 1):
        if step > 0:
            moving = from_behind((moving[0], moving[1]), "ctx", 1)
            carried = (
                from_behind(carried[0].astype(jnp.bfloat16), "ctx", 1).astype(jnp.float32),
                from_behind(carried[1].astype(jnp.bfloat16), "ctx", 1).astype(jnp.float32),
            )
        kinfo = describe(myself - step)
        o, a, b, c = tile_terms(
            queries,
            cotan,
            moving[0],
            moving[1],
            (qinfo[1][:, None] == kinfo[1][None, :])
            & (kinfo[0][None, :] <= qinfo[0][:, None])
            & kinfo[2][None, :],
            scale,
            alpha,
        )
        out_acc = out_acc + o
        dq_acc = dq_acc + a
        carried = (carried[0] + b, carried[1] + c)
    carried = (
        from_behind(carried[0].astype(jnp.bfloat16), "ctx", -SPAN).astype(jnp.float32),
        from_behind(carried[1].astype(jnp.bfloat16), "ctx", -SPAN).astype(jnp.float32),
    )
    dk_acc, dv_acc = carried
    attended = out_acc.reshape(1, rows, features).astype(jnp.bfloat16)
    grad_values = dv_acc.reshape(1, rows, features).astype(jnp.bfloat16)
    dq_b = dq_acc.reshape(rows, features).astype(jnp.bfloat16)
    dk_b = dk_acc.reshape(rows, features).astype(jnp.bfloat16)
    joined = jnp.concatenate([dq_b, dk_b], axis=1)
    width_rows = local.shape[1]
    share = width_rows // cycle_size
    terms = jnp.einsum("rd,rf->df", local, joined, preferred_element_type=jnp.float32)
    summed = lax.psum(terms, ("dp", "ctx"))
    mine = lax.dynamic_slice_in_dim(summed, myself * share, share, 0)
    grad_wq = mine[:, :features].astype(jnp.bfloat16)
    grad_wk = mine[:, features:].astype(jnp.bfloat16)
    return (attended, grad_values, grad_wq, grad_wk)


def solution(mesh):
    placed = (
        P("dp", "ctx", None),
        P(),
        P(),
        P("dp", "ctx", None),
        P("dp", "ctx", None),
        P("dp", None),
        P("dp"),
        P("dp", None),
    )
    return jax.shard_map(
        body,
        mesh=mesh,
        in_specs=placed,
        out_specs=(P("dp", "ctx", None), P("dp", "ctx", None), P("ctx", None), P("ctx", None)),
        check_vma=False,
    )
```

profile of v0, /device:TPU:6, one launch (start us, length us, event | category | flops | bytes accessed | tf_op | source)
XLA Modules:
  0.0 290.1 jit_solution(15227647348382941098)
XLA Ops:
  1.8 1.9 collective-permute-start.1
  3.8 1.5 fusion.20
  6.0 4.8 %collective-permute-start = (bf16[256,4,128]{2,0,1:T(8,128)(2,1)}, bf16[256,4,128]{2,0,1:T(8,128)(2,1)}, u32[]{:S(2)}, u32[]{:S(2)}) collective-permute-start(bf16[256,4,128]{2,0,1:T(8,128)(2,1)} %bitcast.88), channel_id=1, source_target_pairs={{0,1},{1,2},{2,3},{3,4},{4,5},{5,6},{6,7},{7,8},{8,9},{9,10},{10,1... | collective-permute-start | bytes 786440 | tf_op jit(solution)/shard_map/ppermute | solution.py:15
  14.6 1.8 convolution_convert_fusion.3
  19.9 1.9 collective-permute-start.10
  22.9 4.1 %collective-permute-start.6 = (bf16[256,4,128]{2,0,1:T(8,128)(2,1)}, bf16[256,4,128]{2,0,1:T(8,128)(2,1)}, u32[]{:S(2)}, u32[]{:S(2)}) collective-permute-start(bf16[256,4,128]{2,0,1:T(8,128)(2,1)} %fusion.18), channel_id=1, source_target_pairs={{0,1},{1,2},{2,3},{3,4},{4,5},{5,6},{6,7},{7,8},{8,9},{9,10},{10,1... | collective-permute-start | bytes 786440 | tf_op jit(solution)/shard_map/ppermute | solution.py:15
  27.6 1.6 multiply_convert_fusion.2
  31.0 1.9 collective-permute-start.11
  33.0 1.3 add_convert_fusion.5
  34.3 4.8 %collective-permute-start.7 = (bf16[256,4,128]{2,0,1:T(8,128)(2,1)S(1)}, bf16[256,4,128]{2,0,1:T(8,128)(2,1)S(1)}, u32[]{:S(2)}, u32[]{:S(2)}) collective-permute-start(bf16[256,4,128]{2,0,1:T(8,128)(2,1)S(1)} %add_convert_fusion.5), channel_id=1, source_target_pairs={{0,1},{1,2},{2,3},{3,4},{4,5},{5,6},{6,7},{7,8},{8,9},{9,10},{10,1... | collective-permute-start | bytes 786440 | tf_op jit(solution)/shard_map/ppermute | solution.py:15
  39.1 1.9 collective-permute-start.3
  41.0 4.1 %collective-permute-start.2 = (bf16[256,4,128]{2,0,1:T(8,128)(2,1)}, bf16[256,4,128]{2,0,1:T(8,128)(2,1)S(1)}, u32[]{:S(2)}, u32[]{:S(2)}) collective-permute-start(bf16[256,4,128]{2,0,1:T(8,128)(2,1)} %collective-permute-done), channel_id=1, source_target_pairs={{0,1},{1,2},{2,3},{3,4},{4,5},{5,6},{6,7},{7,8},{8,9},{9,10},{10,1... | collective-permute-start | bytes 786440 | tf_op jit(solution)/shard_map/ppermute | solution.py:15
  46.7 4.3 %collective-permute-done.2 = bf16[256,4,128]{2,0,1:T(8,128)(2,1)S(1)} collective-permute-done((bf16[256,4,128]{2,0,1:T(8,128)(2,1)}, bf16[256,4,128]{2,0,1:T(8,128)(2,1)S(1)}, u32[]{:S(2)}, u32[]{:S(2)}) %collective-permute-start.2) | collective-permute-done | bytes 262176 | tf_op jit(solution)/shard_map/ppermute | solution.py:15
  52.5 1.9 collective-permute-start.12
  55.5 5.0 %collective-permute-start.8 = (bf16[256,4,128]{2,0,1:T(8,128)(2,1)}, bf16[256,4,128]{2,0,1:T(8,128)(2,1)}, u32[]{:S(2)}, u32[]{:S(2)}) collective-permute-start(bf16[256,4,128]{2,0,1:T(8,128)(2,1)} %add_convert_fusion.4), channel_id=1, source_target_pairs={{0,1},{1,2},{2,3},{3,4},{4,5},{5,6},{6,7},{7,8},{8,9},{9,10},{10,1... | collective-permute-start | bytes 786440 | tf_op jit(solution)/shard_map/ppermute | solution.py:15
  60.6 1.9 collective-permute-start.5
  62.5 3.9 %collective-permute-start.4 = (bf16[256,4,128]{2,0,1:T(8,128)(2,1)S(1)}, bf16[256,4,128]{2,0,1:T(8,128)(2,1)S(1)}, u32[]{:S(2)}, u32[]{:S(2)}) collective-permute-start(bf16[256,4,128]{2,0,1:T(8,128)(2,1)S(1)} %collective-permute-done.2), channel_id=1, source_target_pairs={{0,1},{1,2},{2,3},{3,4},{4,5},{5,6},{6,7},{7,8},{8,9},{9,10},{10,1... | collective-permute-start | bytes 786440 | tf_op jit(solution)/shard_map/ppermute | solution.py:15
  67.0 5.6 %collective-permute-done.4 = bf16[256,4,128]{2,0,1:T(8,128)(2,1)S(1)} collective-permute-done((bf16[256,4,128]{2,0,1:T(8,128)(2,1)S(1)}, bf16[256,4,128]{2,0,1:T(8,128)(2,1)S(1)}, u32[]{:S(2)}, u32[]{:S(2)}) %collective-permute-start.4) | collective-permute-done | bytes 262176 | tf_op jit(solution)/shard_map/ppermute | solution.py:15
  75.8 1.8 copy.117
  77.6 3.8 %collective-permute-start.13 = (bf16[256,4,128]{0,2,1:T(8,128)(2,1)}, bf16[256,4,128]{0,2,1:T(8,128)(2,1)}, u32[]{:S(2)}, u32[]{:S(2)}) collective-permute-start(bf16[256,4,128]{0,2,1:T(8,128)(2,1)} %add_convert_fusion), channel_id=1, source_target_pairs={{0,61},{1,62},{2,63},{3,0},{4,1},{5,2},{6,3},{7,4},{8,5},{9,6},{10... | collective-permute-start | bytes 786440 | tf_op jit(solution)/shard_map/ppermute | solution.py:15
  82.8 8.4 %collective-permute-start.9 = (bf16[256,4,128]{2,0,1:T(8,128)(2,1)S(1)}, bf16[256,4,128]{2,0,1:T(8,128)(2,1)S(1)}, u32[]{:S(2)}, u32[]{:S(2)}) collective-permute-start(bf16[256,4,128]{2,0,1:T(8,128)(2,1)S(1)} %add_convert_fusion.3), channel_id=1, source_target_pairs={{0,61},{1,62},{2,63},{3,0},{4,1},{5,2},{6,3},{7,4},{8,5},{9,6},{10... | collective-permute-start | bytes 786440 | tf_op jit(solution)/shard_map/ppermute | solution.py:15
  92.5 2.4 collective-permute-done.9
  95.9 3.6 %convolution_bitcast_fusion = f32[1024,1024]{0,1:T(8,128)} fusion(bf16[256,512]{0,1:T(8,128)(2,1)} %bitcast.18, bf16[256,512]{0,1:T(8,128)(2,1)S(1)} %bitcast.104, bf16[1,256,1024]{2,1,0:T(8,128)(2,1)S(1)} %copy-done.1), kind=kOutput, calls=%fused_computation | convolution fusion | flops 537919488 | bytes 5242880 | tf_op jit(solution)/shard_map/rd,rf->df/dot_general | solution.py:104
  99.5 189.0 %all-reduce.1 = bf16[1024,1024]{0,1:T(8,128)(2,1)S(1)} all-reduce(f32[1024,1024]{0,1:T(8,128)} %convolution_bitcast_fusion), channel_id=1, replica_groups=mesh['dp'=8,'ctx'=64] {'dp','ctx'}, use_global_device_ids=true, to_apply=%region_9.10 | all-reduce | flops 1048576 | bytes 6291456 | tf_op jit(solution)/shard_map/psum | solution.py:105
  (73 shorter events, 25.0 us)
Async XLA Ops:
  0.6 3.1 %copy-start = (bf16[1024,512]{1,0:T(8,128)(2,1)S(1)}, bf16[1024,512]{1,0:T(8,128)(2,1)}, u32[]{:S(2)}) copy-start(bf16[1024,512]{1,0:T(8,128)(2,1)} %param.10) | copy-start | bytes 3145732
  1.8 27.4 %collective-permute-start.1 = (bf16[256,4,128]{0,2,1:T(8,128)(2,1)S(1)}, bf16[256,4,128]{0,2,1:T(8,128)(2,1)S(1)}, u32[]{:S(2)}, u32[]{:S(2)}) collective-permute-start(bf16[256,4,128]{0,2,1:T(8,128)(2,1)S(1)} %bitcast.101), channel_id=1, source_target_pairs={{0,1},{1,2},{2,3},{3,4},{4,5},{5,6},{6,7},{7,8},{8,9},{9,10},{10,1... | collective-permute-start | bytes 786440 | tf_op jit(solution)/shard_map/ppermute | solution.py:15
  6.0 21.6 %collective-permute-start = (bf16[256,4,128]{2,0,1:T(8,128)(2,1)}, bf16[256,4,128]{2,0,1:T(8,128)(2,1)}, u32[]{:S(2)}, u32[]{:S(2)}) collective-permute-start(bf16[256,4,128]{2,0,1:T(8,128)(2,1)} %bitcast.88), channel_id=1, source_target_pairs={{0,1},{1,2},{2,3},{3,4},{4,5},{5,6},{6,7},{7,8},{8,9},{9,10},{10,1... | collective-permute-start | bytes 786440 | tf_op jit(solution)/shard_map/ppermute | solution.py:15
  19.9 9.9 %collective-permute-start.10 = (bf16[256,4,128]{0,2,1:T(8,128)(2,1)}, bf16[256,4,128]{0,2,1:T(8,128)(2,1)}, u32[]{:S(2)}, u32[]{:S(2)}) collective-permute-start(bf16[256,4,128]{0,2,1:T(8,128)(2,1)} %fusion.19), channel_id=1, source_target_pairs={{0,1},{1,2},{2,3},{3,4},{4,5},{5,6},{6,7},{7,8},{8,9},{9,10},{10,1... | collective-permute-start | bytes 786440 | tf_op jit(solution)/shard_map/ppermute | solution.py:15
  22.9 10.1 %collective-permute-start.6 = (bf16[256,4,128]{2,0,1:T(8,128)(2,1)}, bf16[256,4,128]{2,0,1:T(8,128)(2,1)}, u32[]{:S(2)}, u32[]{:S(2)}) collective-permute-start(bf16[256,4,128]{2,0,1:T(8,128)(2,1)} %fusion.18), channel_id=1, source_target_pairs={{0,1},{1,2},{2,3},{3,4},{4,5},{5,6},{6,7},{7,8},{8,9},{9,10},{10,1... | collective-permute-start | bytes 786440 | tf_op jit(solution)/shard_map/ppermute | solution.py:15
  27.3 1.9 copy-start.4
  29.8 21.3 %copy-start.3 = (f32[256,256]{1,0:T(8,128)S(1)}, f32[256,256]{1,0:T(8,128)}, u32[]{:S(2)}) copy-start(f32[256,256]{1,0:T(8,128)} %get-tuple-element.27) | copy-start | bytes 786436
  31.0 21.4 %collective-permute-start.11 = (bf16[256,4,128]{0,2,1:T(8,128)(2,1)S(1)}, bf16[256,4,128]{0,2,1:T(8,128)(2,1)S(1)}, u32[]{:S(2)}, u32[]{:S(2)}) collective-permute-start(bf16[256,4,128]{0,2,1:T(8,128)(2,1)S(1)} %add_convert_fusion.2), channel_id=1, source_target_pairs={{0,1},{1,2},{2,3},{3,4},{4,5},{5,6},{6,7},{7,8},{8,9},{9,10},{10,1... | collective-permute-start | bytes 786440 | tf_op jit(solution)/shard_map/ppermute | solution.py:15
  34.3 20.5 %collective-permute-start.7 = (bf16[256,4,128]{2,0,1:T(8,128)(2,1)S(1)}, bf16[256,4,128]{2,0,1:T(8,128)(2,1)S(1)}, u32[]{:S(2)}, u32[]{:S(2)}) collective-permute-start(bf16[256,4,128]{2,0,1:T(8,128)(2,1)S(1)} %add_convert_fusion.5), channel_id=1, source_target_pairs={{0,1},{1,2},{2,3},{3,4},{4,5},{5,6},{6,7},{7,8},{8,9},{9,10},{10,1... | collective-permute-start | bytes 786440 | tf_op jit(solution)/shard_map/ppermute | solution.py:15
  39.1 12.6 %collective-permute-start.3 = (bf16[256,4,128]{0,2,1:T(8,128)(2,1)S(1)}, bf16[256,4,128]{0,2,1:T(8,128)(2,1)S(1)}, u32[]{:S(2)}, u32[]{:S(2)}) collective-permute-start(bf16[256,4,128]{0,2,1:T(8,128)(2,1)S(1)} %collective-permute-done.1), channel_id=1, source_target_pairs={{0,1},{1,2},{2,3},{3,4},{4,5},{5,6},{6,7},{7,8},{8,9},{9,10},{10,1... | collective-permute-start | bytes 786440 | tf_op jit(solution)/shard_map/ppermute | solution.py:15
  41.0 10.1 %collective-permute-start.2 = (bf16[256,4,128]{2,0,1:T(8,128)(2,1)}, bf16[256,4,128]{2,0,1:T(8,128)(2,1)S(1)}, u32[]{:S(2)}, u32[]{:S(2)}) collective-permute-start(bf16[256,4,128]{2,0,1:T(8,128)(2,1)} %collective-permute-done), channel_id=1, source_target_pairs={{0,1},{1,2},{2,3},{3,4},{4,5},{5,6},{6,7},{7,8},{8,9},{9,10},{10,1... | collective-permute-start | bytes 786440 | tf_op jit(solution)/shard_map/ppermute | solution.py:15
  52.2 20.4 %copy-start.2 = (f32[256,256]{1,0:T(8,128)S(1)}, f32[256,256]{1,0:T(8,128)}, u32[]{:S(2)}) copy-start(f32[256,256]{1,0:T(8,128)} %get-tuple-element.26) | copy-start | bytes 786436
  52.5 22.6 %collective-permute-start.12 = (bf16[256,4,128]{0,2,1:T(8,128)(2,1)S(1)}, bf16[256,4,128]{0,2,1:T(8,128)(2,1)S(1)}, u32[]{:S(2)}, u32[]{:S(2)}) collective-permute-start(bf16[256,4,128]{0,2,1:T(8,128)(2,1)S(1)} %add_convert_fusion.1), channel_id=1, source_target_pairs={{0,1},{1,2},{2,3},{3,4},{4,5},{5,6},{6,7},{7,8},{8,9},{9,10},{10,1... | collective-permute-start | bytes 786440 | tf_op jit(solution)/shard_map/ppermute | solution.py:15
  55.5 26.2 %collective-permute-start.8 = (bf16[256,4,128]{2,0,1:T(8,128)(2,1)}, bf16[256,4,128]{2,0,1:T(8,128)(2,1)}, u32[]{:S(2)}, u32[]{:S(2)}) collective-permute-start(bf16[256,4,128]{2,0,1:T(8,128)(2,1)} %add_convert_fusion.4), channel_id=1, source_target_pairs={{0,1},{1,2},{2,3},{3,4},{4,5},{5,6},{6,7},{7,8},{8,9},{9,10},{10,1... | collective-permute-start | bytes 786440 | tf_op jit(solution)/shard_map/ppermute | solution.py:15
  60.6 12.6 %collective-permute-start.5 = (bf16[256,4,128]{0,2,1:T(8,128)(2,1)S(1)}, bf16[256,4,128]{0,2,1:T(8,128)(2,1)S(1)}, u32[]{:S(2)}, u32[]{:S(2)}) collective-permute-start(bf16[256,4,128]{0,2,1:T(8,128)(2,1)S(1)} %collective-permute-done.3), channel_id=1, source_target_pairs={{0,1},{1,2},{2,3},{3,4},{4,5},{5,6},{6,7},{7,8},{8,9},{9,10},{10,1... | collective-permute-start | bytes 786440 | tf_op jit(solution)/shard_map/ppermute | solution.py:15
  62.5 10.1 %collective-permute-start.4 = (bf16[256,4,128]{2,0,1:T(8,128)(2,1)S(1)}, bf16[256,4,128]{2,0,1:T(8,128)(2,1)S(1)}, u32[]{:S(2)}, u32[]{:S(2)}) collective-permute-start(bf16[256,4,128]{2,0,1:T(8,128)(2,1)S(1)} %collective-permute-done.2), channel_id=1, source_target_pairs={{0,1},{1,2},{2,3},{3,4},{4,5},{5,6},{6,7},{7,8},{8,9},{9,10},{10,1... | collective-permute-start | bytes 786440 | tf_op jit(solution)/shard_map/ppermute | solution.py:15
  72.6 0.7 copy-start.5
  74.0 21.9 %copy-start.1 = (bf16[1,256,1024]{2,1,0:T(8,128)(2,1)S(1)}, bf16[1,256,1024]{2,1,0:T(8,128)(2,1)}, u32[]{:S(2)}) copy-start(bf16[1,256,1024]{2,1,0:T(8,128)(2,1)} %param.8) | copy-start | bytes 1572868
  77.6 18.3 %collective-permute-start.13 = (bf16[256,4,128]{0,2,1:T(8,128)(2,1)}, bf16[256,4,128]{0,2,1:T(8,128)(2,1)}, u32[]{:S(2)}, u32[]{:S(2)}) collective-permute-start(bf16[256,4,128]{0,2,1:T(8,128)(2,1)} %add_convert_fusion), channel_id=1, source_target_pairs={{0,61},{1,62},{2,63},{3,0},{4,1},{5,2},{6,3},{7,4},{8,5},{9,6},{10... | collective-permute-start | bytes 786440 | tf_op jit(solution)/shard_map/ppermute | solution.py:15
  82.8 12.1 %collective-permute-start.9 = (bf16[256,4,128]{2,0,1:T(8,128)(2,1)S(1)}, bf16[256,4,128]{2,0,1:T(8,128)(2,1)S(1)}, u32[]{:S(2)}, u32[]{:S(2)}) collective-permute-start(bf16[256,4,128]{2,0,1:T(8,128)(2,1)S(1)} %add_convert_fusion.3), channel_id=1, source_target_pairs={{0,61},{1,62},{2,63},{3,0},{4,1},{5,2},{6,3},{7,4},{8,5},{9,6},{10... | collective-permute-start | bytes 786440 | tf_op jit(solution)/shard_map/ppermute | solution.py:15
where the time goes:
time: 292 us; the launch traced here: 290 us
  blocking collectives  189 us (65%)
  starting transfers between devices  50.4 us (17%)
  matrix products  23 us (8%)
  waiting for transfers between devices  12.4 us (4%)
  local copies, waits for them, and re-layouts  8.31 us (3%)
  other arithmetic  5.18 us (2%)
    psum x1, blocking collectives, body(): summed = lax.psum(terms, ('dp', 'ctx'))  189 us
    ppermute x14, starting transfers between devices, from_behind(): return lax.ppermute(value, axis, pairs)  50.4 us
    ppermute x14, waiting for transfers between devices, from_behind(): return lax.ppermute(value, axis, pairs)  12.4 us
  transfers between devices with their start and end apart: 14, of which 3 were waited for; matrix products, arithmetic and copies ran while one was open for 10% of the time, Pallas kernels for 0%

commit v1 on v0

v1 whole, which is shorter than its diff:
```python
import jax
import jax.numpy as jnp
from jax import lax
from jax.sharding import PartitionSpec as P

HD = 128
SPAN = 3
BLOCK = 128
MAXLEN = 768


def shifted(value, axis, steps):
    count = lax.axis_size(axis)
    pairs = [(source, (source + steps) % count) for source in range(count)]
    return lax.ppermute(value, axis, pairs)


def scores(query, key, valid, scale, alpha):
    z = jnp.einsum("qhd,khd->hqk", query, key, preferred_element_type=jnp.float32) * alpha
    sig = jax.nn.sigmoid(z)
    weight = valid[None, :, :].astype(jnp.float32) * scale
    return z, sig, weight


def forward_terms(query, grad, key, value, valid, scale, alpha):
    z, sig, weight = scores(query, key, valid, scale, alpha)
    att = (z * sig * weight).astype(jnp.bfloat16)
    out = jnp.einsum("hqk,khd->qhd", att, value, preferred_element_type=jnp.float32)
    dprod = jnp.einsum("qhd,khd->hqk", grad, value, preferred_element_type=jnp.float32)
    dsc = (dprod * sig * (1.0 + z * (1.0 - sig)) * weight * alpha).astype(jnp.bfloat16)
    dquery = jnp.einsum("hqk,khd->qhd", dsc, key, preferred_element_type=jnp.float32)
    return out, dquery, att, dsc


def backward_terms(query, grad, key, value, valid, scale, alpha):
    z, sig, weight = scores(query, key, valid, scale, alpha)
    att = (z * sig * weight).astype(jnp.bfloat16)
    dprod = jnp.einsum("qhd,khd->hqk", grad, value, preferred_element_type=jnp.float32)
    dsc = (dprod * sig * (1.0 + z * (1.0 - sig)) * weight * alpha).astype(jnp.bfloat16)
    dkey = jnp.einsum("hqk,qhd->khd", dsc, query, preferred_element_type=jnp.float32)
    dvalue = jnp.einsum("hqk,qhd->khd", att, grad, preferred_element_type=jnp.float32)
    return dkey, dvalue


def body(events, w_query, w_key, values, grad_out, lengths, stream_shift, block_keep):
    rows = events.shape[1]
    features = w_query.shape[1]
    nheads = features // HD
    alpha = 1.0 / HD**0.5
    scale = 1.0 / MAXLEN**0.5
    local = events[0]
    queries = jnp.dot(local, w_query, preferred_element_type=jnp.float32).astype(jnp.bfloat16)
    keys = jnp.dot(local, w_key, preferred_element_type=jnp.float32).astype(jnp.bfloat16)
    cycle_size = lax.axis_size("ctx")
    myself = lax.axis_index("ctx")
    total = rows * cycle_size
    ends = jnp.cumsum(lengths[0])
    offset = stream_shift[0]
    keep = block_keep[0]
    blocks_all = jnp.arange(keep.shape[0], dtype=jnp.int32)
    within = jnp.arange(rows, dtype=jnp.int32)

    def describe(anchor):
        anchor = jnp.remainder(anchor, cycle_size)
        position = jnp.remainder(anchor * rows + within - offset, total)
        owner = jnp.sum((position[:, None] >= ends[None, :]).astype(jnp.int32), axis=1)
        which = position // BLOCK
        kept = (
            jnp.sum(jnp.where(which[:, None] == blocks_all[None, :], keep[None, :], 0), axis=1) > 0
        )
        return (position, owner, kept)

    def mask(qinfo, kinfo):
        return (
            (qinfo[1][:, None] == kinfo[1][None, :])
            & (kinfo[0][None, :] <= qinfo[0][:, None])
            & kinfo[2][None, :]
        )

    def split(packed):
        return (
            packed[:, :features].reshape(rows, nheads, HD),
            packed[:, features:].reshape(rows, nheads, HD),
        )

    kv = jnp.concatenate([keys, values[0]], axis=1)
    qg = jnp.concatenate([queries, grad_out[0]], axis=1)
    kv_from = [None] + [shifted(kv, "ctx", step) for step in range(1, SPAN + 1)]
    qg_from = [None] + [shifted(qg, "ctx", -step) for step in range(1, SPAN + 1)]

    q_me, g_me = split(qg)
    k_me, v_me = split(kv)
    info_me = describe(myself)
    out_acc, dq_acc, att0, dsc0 = forward_terms(
        q_me, g_me, k_me, v_me, mask(info_me, info_me), scale, alpha
    )
    dk_acc = jnp.einsum("hqk,qhd->khd", dsc0, q_me, preferred_element_type=jnp.float32)
    dv_acc = jnp.einsum("hqk,qhd->khd", att0, g_me, preferred_element_type=jnp.float32)
    for step in range(1, SPAN + 1):
        k_s, v_s = split(kv_from[step])
        o, a, _, _ = forward_terms(
            q_me, g_me, k_s, v_s, mask(info_me, describe(myself - step)), scale, alpha
        )
        out_acc = out_acc + o
        dq_acc = dq_acc + a
        q_s, g_s = split(qg_from[step])
        b, c = backward_terms(
            q_s, g_s, k_me, v_me, mask(describe(myself + step), info_me), scale, alpha
        )
        dk_acc = dk_acc + b
        dv_acc = dv_acc + c
    attended = out_acc.reshape(1, rows, features).astype(jnp.bfloat16)
    grad_values = dv_acc.reshape(1, rows, features).astype(jnp.bfloat16)
    dq_b = dq_acc.reshape(rows, features).astype(jnp.bfloat16)
    dk_b = dk_acc.reshape(rows, features).astype(jnp.bfloat16)
    joined = jnp.concatenate([dq_b, dk_b], axis=1)
    terms = jnp.einsum("rd,rf->df", local, joined, preferred_element_type=jnp.float32)
    mine = lax.psum_scatter(terms, "ctx", scatter_dimension=0, tiled=True)
    mine = lax.psum(mine, "dp")
    grad_wq = mine[:, :features].astype(jnp.bfloat16)
    grad_wk = mine[:, features:].astype(jnp.bfloat16)
    return (attended, grad_values, grad_wq, grad_wk)


def solution(mesh):
    placed = (
        P("dp", "ctx", None),
        P(),
        P(),
        P("dp", "ctx", None),
        P("dp", "ctx", None),
        P("dp", None),
        P("dp"),
        P("dp", None),
    )
    return jax.shard_map(
        body,
        mesh=mesh,
        in_specs=placed,
        out_specs=(P("dp", "ctx", None), P("dp", "ctx", None), P("ctx", None), P("ctx", None)),
        check_vma=False,
    )
```

time: 292 us -> 392 us (1.34)
  waiting for transfers between devices: 12.4 us -> 224 us
  blocking collectives: 189 us -> 40 us
  matrix products: 23 us -> 46.2 us
  starting transfers between devices: 50.4 us -> 28 us
  local copies, waits for them, and re-layouts: 8.31 us -> 30.3 us
  between operations: 1.85 us -> 15.3 us
    unnamed x0 -> x2, waiting for transfers between devices: none -> 216 us
    psum x1, blocking collectives: 189 us -> 40 us  [body(): mine = lax.psum(mine, 'dp')]
    dot_general x24, matrix products: 16.1 us -> 39.2 us  [the longest x7 11.5 us: scores(): jnp.einsum('qhd,khd->hqk', query, key, preferred_element_type=jnp.float32)]
    ppermute x14 -> x6, starting transfers between devices: 50.4 us -> 28 us  [shifted(): return lax.ppermute(value, axis, pairs)]
    unnamed x17 -> x62, local copies, waits for them, and re-layouts: 5.36 us -> 22.1 us
    reshape x2 -> x8, local copies, waits for them, and re-layouts: 0.88 us -> 7.94 us  [split(): packed[:, :features].reshape(rows, nheads, HD)]
    ppermute x14 -> x6, waiting for transfers between devices: 12.4 us -> 7.63 us  [shifted(): return lax.ppermute(value, axis, pairs)]
  transfers between devices with their start and end apart: 14 -> 7, of which waited for: 3 -> 2; matrix products, arithmetic and copies ran while one was open for 10% -> 8% of each run, Pallas kernels for 0% -> 0%
where the time goes in v1:
time: 392 us; the launch traced here: 388 us
  waiting for transfers between devices  224 us (57%)
  matrix products  46.2 us (12%)
  blocking collectives  40 us (10%)
  local copies, waits for them, and re-layouts  30.3 us (8%)
  starting transfers between devices  28 us (7%)
  between operations  15.3 us (4%)
  other arithmetic  4.22 us (1%)
    unnamed x2, waiting for transfers between devices  216 us
    psum x1, blocking collectives, body(): mine = lax.psum(mine, 'dp')  40 us
    ppermute x6, starting transfers between devices, shifted(): return lax.ppermute(value, axis, pairs)  28 us
    unnamed x62, local copies, waits for them, and re-layouts  22.1 us
    dot_general x7, matrix products, scores(): jnp.einsum('qhd,khd->hqk', query, key, preferred_element_type=jnp.float32)  11.5 us
    dot_general x4, matrix products, forward_terms(): jnp.einsum('hqk,khd->qhd', dsc, key, preferred_element_type=jnp.float32)  10.1 us
    dot_general x3, matrix products, backward_terms(): jnp.einsum('hqk,qhd->khd', dsc, query, preferred_element_type=jnp.float32)  8.87 us
    reshape x8, local copies, waits for them, and re-layouts, split(): packed[:, :features].reshape(rows, nheads, HD)  7.94 us
  transfers between devices with their start and end apart: 7, of which 2 were waited for; matrix products, arithmetic and copies ran while one was open for 8% of the time, Pallas kernels for 0%

profile of v1, /device:TPU:6, one launch (start us, length us, event | category | flops | bytes accessed | tf_op | source)
XLA Modules:
  0.0 388.0 jit_solution(711006471729276778)
XLA Ops:
  11.0 10.8 %collective-permute-start.5 = (bf16[256,1024]{1,0:T(8,128)(2,1)S(1)}, bf16[256,1024]{1,0:T(8,128)(2,1)}, u32[]{:S(2)}, u32[]{:S(2)}) collective-permute-start(bf16[256,1024]{1,0:T(8,128)(2,1)S(1)} %pad_maximum_fusion.1), channel_id=1, source_target_pairs={{0,61},{1,62},{2,63},{3,0},{4,1},{5,2},{6,3},{7,4},{8,5},{9,6},{10... | collective-permute-start | bytes 1572872 | tf_op jit(solution)/shard_map/ppermute | solution.py:15
  21.8 3.3 collective-permute-start.4
  25.1 4.9 %collective-permute-start.3 = (bf16[256,1024]{1,0:T(8,128)(2,1)S(1)}, bf16[256,1024]{1,0:T(8,128)(2,1)}, u32[]{:S(2)}, u32[]{:S(2)}) collective-permute-start(bf16[256,1024]{1,0:T(8,128)(2,1)S(1)} %pad_maximum_fusion.1), channel_id=1, source_target_pairs={{0,63},{1,0},{2,1},{3,2},{4,3},{5,4},{6,5},{7,6},{8,7},{9,8},{10,9... | collective-permute-start | bytes 1572872 | tf_op jit(solution)/shard_map/ppermute | solution.py:15
  32.7 2.1 collective-permute-start.2
  34.8 4.8 %collective-permute-start.1 = (bf16[256,1024]{1,0:T(8,128)(2,1)}, bf16[256,1024]{1,0:T(8,128)(2,1)}, u32[]{:S(2)}, u32[]{:S(2)}) collective-permute-start(bf16[256,1024]{1,0:T(8,128)(2,1)} %pad_maximum_fusion), channel_id=1, source_target_pairs={{0,2},{1,3},{2,4},{3,5},{4,6},{5,7},{6,8},{7,9},{8,10},{9,11},{10,... | collective-permute-start | bytes 1572872 | tf_op jit(solution)/shard_map/ppermute | solution.py:15
  46.6 2.1 collective-permute-start
  50.4 1.8 slice_bitcast_fusion.1
  56.5 1.8 slice_bitcast_fusion.3
  60.1 7.6 %collective-permute-done.1 = bf16[256,1024]{1,0:T(8,128)(2,1)} collective-permute-done((bf16[256,1024]{1,0:T(8,128)(2,1)}, bf16[256,1024]{1,0:T(8,128)(2,1)}, u32[]{:S(2)}, u32[]{:S(2)}) %collective-permute-start.1) | collective-permute-done | bytes 524320 | tf_op jit(solution)/shard_map/ppermute | solution.py:15
  71.4 1.8 slice_bitcast_fusion.5
  75.0 2.3 convolution_multiply_fusion.9
  77.3 2.3 convolution_multiply_fusion.8
  79.6 2.3 convolution_multiply_fusion.7
  85.9 2.9 fusion.36
  88.8 2.8 fusion.35
  91.6 2.9 fusion.37
  94.6 2.9 fusion.42
  97.5 3.2 fusion.49
  100.7 3.2 fusion.52
  103.8 3.7 convolution_bitcast_fusion
  107.6 5.3 %copy.193 = f32[1024,1024]{1,0:T(8,128)} copy(f32[1024,1024]{0,1:T(8,128)} %convolution_bitcast_fusion) | data formatting | bytes 8388608
  117.6 1.9 convolution_bitcast_fusion.5
  122.4 216.4 %reduce-scatter.4.cloned.1.call-done = f32[16,1024]{1,0:T(8,128)} async-done(((f32[1024,1024]{1,0:T(8,128)}), f32[16,1024]{1,0:T(8,128)}) %reduce-scatter.4.cloned.1.call-update) | async-done | bytes 65552
  339.8 40.0 %psum.7 = bf16[16,1024]{0,1:T(8,128)(2,1)S(1)} all-reduce(f32[16,1024]{0,1:T(8,128)S(1)} %copy.194), channel_id=1, replica_groups=mesh['dp'=8,'ctx'=64] {'dp'}, use_global_device_ids=true, to_apply=%region_13.14 | all-reduce | flops 16384 | bytes 98304 | tf_op jit(solution)/shard_map/psum | solution.py:119
  (110 shorter events, 39.5 us)
Async XLA Ops:
  7.2 32.6 %copy-start.7 = (bf16[1,256,512]{2,1,0:T(8,128)(2,1)S(1)}, bf16[1,256,512]{2,1,0:T(8,128)(2,1)}, u32[]{:S(2)}) copy-start(bf16[1,256,512]{2,1,0:T(8,128)(2,1)} %param.12) | copy-start | bytes 786436
  7.2 24.7 %copy-start.6 = (bf16[1,256,512]{2,1,0:T(8,128)(2,1)S(1)}, bf16[1,256,512]{2,1,0:T(8,128)(2,1)}, u32[]{:S(2)}) copy-start(bf16[1,256,512]{2,1,0:T(8,128)(2,1)} %param.11) | copy-start | bytes 786436
  7.2 33.7 %copy-start.23 = (s32[1,128]{1,0:T(1,128)S(1)}, s32[1,128]{1,0:T(1,128)}, u32[]{:S(2)}) copy-start(s32[1,128]{1,0:T(1,128)} %param.15) | copy-start | bytes 1540
  7.2 34.2 %copy-start.24 = (s32[1,32]{1,0:T(1,128)S(1)}, s32[1,32]{1,0:T(1,128)}, u32[]{:S(2)}) copy-start(s32[1,32]{1,0:T(1,128)} %param.13) | copy-start | bytes 388
  7.2 331.5 %reduce-scatter.4.cloned.1.call-start = ((), (), s32[]{:S(2)}) async-start(), calls=%async_computation.1 | async-start | bytes 4259840
  11.0 35.6 %collective-permute-start.5 = (bf16[256,1024]{1,0:T(8,128)(2,1)S(1)}, bf16[256,1024]{1,0:T(8,128)(2,1)}, u32[]{:S(2)}, u32[]{:S(2)}) collective-permute-start(bf16[256,1024]{1,0:T(8,128)(2,1)S(1)} %pad_maximum_fusion.1), channel_id=1, source_target_pairs={{0,61},{1,62},{2,63},{3,0},{4,1},{5,2},{6,3},{7,4},{8,5},{9,6},{10... | collective-permute-start | bytes 1572872 | tf_op jit(solution)/shard_map/ppermute | solution.py:15
  21.8 28.6 %collective-permute-start.4 = (bf16[256,1024]{1,0:T(8,128)(2,1)S(1)}, bf16[256,1024]{1,0:T(8,128)(2,1)}, u32[]{:S(2)}, u32[]{:S(2)}) collective-permute-start(bf16[256,1024]{1,0:T(8,128)(2,1)S(1)} %pad_maximum_fusion.1), channel_id=1, source_target_pairs={{0,62},{1,63},{2,0},{3,1},{4,2},{5,3},{6,4},{7,5},{8,6},{9,7},{10,... | collective-permute-start | bytes 1572872 | tf_op jit(solution)/shard_map/ppermute | solution.py:15
  25.1 27.2 %collective-permute-start.3 = (bf16[256,1024]{1,0:T(8,128)(2,1)S(1)}, bf16[256,1024]{1,0:T(8,128)(2,1)}, u32[]{:S(2)}, u32[]{:S(2)}) collective-permute-start(bf16[256,1024]{1,0:T(8,128)(2,1)S(1)} %pad_maximum_fusion.1), channel_id=1, source_target_pairs={{0,63},{1,0},{2,1},{3,2},{4,3},{5,4},{6,5},{7,6},{8,7},{9,8},{10,9... | collective-permute-start | bytes 1572872 | tf_op jit(solution)/shard_map/ppermute | solution.py:15
  32.7 23.7 %collective-permute-start.2 = (bf16[256,1024]{1,0:T(8,128)(2,1)}, bf16[256,1024]{1,0:T(8,128)(2,1)}, u32[]{:S(2)}, u32[]{:S(2)}) collective-permute-start(bf16[256,1024]{1,0:T(8,128)(2,1)} %pad_maximum_fusion), channel_id=1, source_target_pairs={{0,3},{1,4},{2,5},{3,6},{4,7},{5,8},{6,9},{7,10},{8,11},{9,12},{10... | collective-permute-start | bytes 1572872 | tf_op jit(solution)/shard_map/ppermute | solution.py:15
  34.8 32.9 %collective-permute-start.1 = (bf16[256,1024]{1,0:T(8,128)(2,1)}, bf16[256,1024]{1,0:T(8,128)(2,1)}, u32[]{:S(2)}, u32[]{:S(2)}) collective-permute-start(bf16[256,1024]{1,0:T(8,128)(2,1)} %pad_maximum_fusion), channel_id=1, source_target_pairs={{0,2},{1,3},{2,4},{3,5},{4,6},{5,7},{6,8},{7,9},{8,10},{9,11},{10,... | collective-permute-start | bytes 1572872 | tf_op jit(solution)/shard_map/ppermute | solution.py:15
  46.6 24.8 %collective-permute-start = (bf16[256,1024]{1,0:T(8,128)(2,1)}, bf16[256,1024]{1,0:T(8,128)(2,1)}, u32[]{:S(2)}, u32[]{:S(2)}) collective-permute-start(bf16[256,1024]{1,0:T(8,128)(2,1)} %pad_maximum_fusion), channel_id=1, source_target_pairs={{0,1},{1,2},{2,3},{3,4},{4,5},{5,6},{6,7},{7,8},{8,9},{9,10},{10,1... | collective-permute-start | bytes 1572872 | tf_op jit(solution)/shard_map/ppermute | solution.py:15
  84.6 4.2 %copy-start.14 = (f32[256,256]{1,0:T(8,128)S(1)}, f32[256,256]{1,0:T(8,128)}, u32[]{:S(2)}) copy-start(f32[256,256]{1,0:T(8,128)} %get-tuple-element.47) | copy-start | bytes 786436
  88.8 2.9 copy-start.8
  91.6 2.9 copy-start.10
  91.6 2.9 copy-start.12
  94.6 2.9 copy-start.9
  97.5 3.2 copy-start.11
  100.7 3.2 copy-start.1
  112.9 2.8 copy-start.5
  116.7 2.8 copy-start.3
  116.7 2.8 copy-start.15
  117.6 3.4 copy-start.2
  117.6 3.4 copy-start.13
  117.6 3.4 copy-start.19
  (8 other events, 15.8 us)
Sparse Core Ops, SparseCore 0:
  113.1 225.6 reduce-scatter.3

commit v2 on v1

--- a/solution.py
+++ b/solution.py
@@ -13,6 +13,43 @@
     count = lax.axis_size(axis)
     pairs = [(source, (source + steps) % count) for source in range(count)]
     return lax.ppermute(value, axis, pairs)
+
+
+def exchange(value, axis, mask):
+    count = lax.axis_size(axis)
+    return lax.ppermute(value, axis, [(source, source ^ mask) for source in range(count)])
+
+
+def pick(value, bit, axis):
+    return (
+        lax.dynamic_index_in_dim(value, bit, axis, keepdims=False),
+        lax.dynamic_index_in_dim(value, 1 - bit, axis, keepdims=False),
+    )
+
+
+def reduce_rows(local, partner_events, joined, myself, cycle_size):
+    width = local.shape[1]
+    share = width // cycle_size
+    core = myself % 2
+    partner_joined = exchange(joined, "ctx", 1)
+    both_events = jnp.concatenate([local, partner_events], axis=0)
+    both_joined = jnp.concatenate([joined, partner_joined], axis=0)
+    halves = both_events.reshape(both_events.shape[0], width // (2 * share), 2, share)
+    kept = lax.dynamic_index_in_dim(halves, core, 2, keepdims=False).reshape(both_events.shape[0], width // 2)
+    acc = jnp.dot(kept.T, both_joined, preferred_element_type=jnp.float32)
+    acc = acc.reshape(width // (2 * share), share, joined.shape[1])
+    mask = 2
+    while mask < cycle_size:
+        acc = acc.reshape(acc.shape[0] // 2, 2, share, joined.shape[1])
+        keep_part, send_part = pick(acc, (myself // mask) % 2, 1)
+        acc = keep_part + exchange(send_part, "ctx", mask)
+        mask *= 2
+    acc = acc.reshape(share, joined.shape[1])
+    mask = 1
+    while mask < lax.axis_size("dp"):
+        acc = acc + exchange(acc, "dp", mask)
+        mask *= 2
+    return acc
 
 
 def scores(query, key, valid, scale, alpha):
@@ -83,6 +120,7 @@
             packed[:, features:].reshape(rows, nheads, HD),
         )
 
+    partner_events = exchange(local, "ctx", 1)
     kv = jnp.concatenate([keys, values[0]], axis=1)
     qg = jnp.concatenate([queries, grad_out[0]], axis=1)
     kv_from = [None] + [shifted(kv, "ctx", step) for step in range(1, SPAN + 1)]
@@ -114,9 +152,7 @@
     dq_b = dq_acc.reshape(rows, features).astype(jnp.bfloat16)
     dk_b = dk_acc.reshape(rows, features).astype(jnp.bfloat16)
     joined = jnp.concatenate([dq_b, dk_b], axis=1)
-    terms = jnp.einsum("rd,rf->df", local, joined, preferred_element_type=jnp.float32)
-    mine = lax.psum_scatter(terms, "ctx", scatter_dimension=0, tiled=True)
-    mine = lax.psum(mine, "dp")
+    mine = reduce_rows(local, partner_events, joined, myself, cycle_size)
     grad_wq = mine[:, :features].astype(jnp.bfloat16)
     grad_wk = mine[:, features:].astype(jnp.bfloat16)
     return (attended, grad_values, grad_wq, grad_wk)

time: 392 us -> 234 us (0.60)
  waiting for transfers between devices: 224 us -> 89.6 us
  blocking collectives: 40 us -> 0 us
  starting transfers between devices: 28 us -> 67.7 us
  between operations: 15.3 us -> 2.51 us
  matrix products: 46.2 us -> 37.2 us
  local copies, waits for them, and re-layouts: 30.3 us -> 25.5 us
  other arithmetic: 4.22 us -> 8.98 us
    unnamed x2 -> x0, waiting for transfers between devices: 216 us -> none
    ppermute x0 -> x10, waiting for transfers between devices: none -> 76.7 us  [exchange(): lax.ppermute(value, axis, [(source, source ^ mask) for source in range(co...]
    psum x1 -> x0, blocking collectives: 40 us -> none  [body(): mine = lax.psum(mine, 'dp')]
    ppermute x0 -> x10, starting transfers between devices: none -> 39.9 us  [exchange(): lax.ppermute(value, axis, [(source, source ^ mask) for source in range(co...]
    unnamed x62 -> x81, local copies, waits for them, and re-layouts: 22.1 us -> 15.5 us
    ppermute x6, waiting for transfers between devices: 7.63 us -> 12.9 us  [shifted(): return lax.ppermute(value, axis, pairs)]
  transfers between devices with their start and end apart: 7 -> 16, of which waited for: 2 -> 10; matrix products, arithmetic and copies ran while one was open for 8% -> 26% of each run, Pallas kernels for 0% -> 0%
where the time goes in v2:
time: 234 us; the launch traced here: 231 us
  waiting for transfers between devices  89.6 us (38%)
  starting transfers between devices  67.7 us (29%)
  matrix products  37.2 us (16%)
  local copies, waits for them, and re-layouts  25.5 us (11%)
  other arithmetic  8.98 us (4%)
  between operations  2.51 us (1%)
    ppermute x10, waiting for transfers between devices, exchange(): lax.ppermute(value, axis, [(source, source ^ mask) for source in range(co...  76.7 us
    ppermute x10, starting transfers between devices, exchange(): lax.ppermute(value, axis, [(source, source ^ mask) for source in range(co...  39.9 us
    ppermute x6, starting transfers between devices, shifted(): return lax.ppermute(value, axis, pairs)  27.8 us
    unnamed x81, local copies, waits for them, and re-layouts  15.5 us
    ppermute x6, waiting for transfers between devices, shifted(): return lax.ppermute(value, axis, pairs)  12.9 us
    dot_general x7, matrix products, scores(): jnp.einsum('qhd,khd->hqk', query, key, preferred_element_type=jnp.float32)  10.6 us
    dot_general x4, matrix products, forward_terms(): jnp.einsum('hqk,khd->qhd', dsc, key, preferred_element_type=jnp.float32)  9.56 us
    dot_general x3, matrix products, backward_terms(): jnp.einsum('hqk,qhd->khd', dsc, query, preferred_element_type=jnp.float32)  8.42 us
  transfers between devices with their start and end apart: 16, of which 10 were waited for; matrix products, arithmetic and copies ran while one was open for 26% of the time, Pallas kernels for 0%

profile of v2, /device:TPU:6, one launch (start us, length us, event | category | flops | bytes accessed | tf_op | source)
XLA Modules:
  0.0 231.5 jit_solution(8890701394166038406)
XLA Ops:
  5.2 10.8 %collective-permute-start.5 = (bf16[256,1024]{1,0:T(8,128)(2,1)}, bf16[256,1024]{1,0:T(8,128)(2,1)}, u32[]{:S(2)}, u32[]{:S(2)}) collective-permute-start(bf16[256,1024]{1,0:T(8,128)(2,1)} %pad_maximum_fusion.1), channel_id=1, source_target_pairs={{0,61},{1,62},{2,63},{3,0},{4,1},{5,2},{6,3},{7,4},{8,5},{9,6},{10... | collective-permute-start | bytes 1572872 | tf_op jit(solution)/shard_map/ppermute | solution.py:15
  16.1 3.3 %collective-permute-start.4 = (bf16[256,1024]{1,0:T(8,128)(2,1)}, bf16[256,1024]{1,0:T(8,128)(2,1)}, u32[]{:S(2)}, u32[]{:S(2)}) collective-permute-start(bf16[256,1024]{1,0:T(8,128)(2,1)} %pad_maximum_fusion.1), channel_id=1, source_target_pairs={{0,62},{1,63},{2,0},{3,1},{4,2},{5,3},{6,4},{7,5},{8,6},{9,7},{10,... | collective-permute-start | bytes 1572872 | tf_op jit(solution)/shard_map/ppermute | solution.py:15
  19.4 4.9 %collective-permute-start.3 = (bf16[256,1024]{1,0:T(8,128)(2,1)}, bf16[256,1024]{1,0:T(8,128)(2,1)}, u32[]{:S(2)}, u32[]{:S(2)}) collective-permute-start(bf16[256,1024]{1,0:T(8,128)(2,1)} %pad_maximum_fusion.1), channel_id=1, source_target_pairs={{0,63},{1,0},{2,1},{3,2},{4,3},{5,4},{6,5},{7,6},{8,7},{9,8},{10,9... | collective-permute-start | bytes 1572872 | tf_op jit(solution)/shard_map/ppermute | solution.py:15
  27.7 4.8 %collective-permute-start.1 = (bf16[256,1024]{1,0:T(8,128)(2,1)}, bf16[256,1024]{1,0:T(8,128)(2,1)}, u32[]{:S(2)}, u32[]{:S(2)}) collective-permute-start(bf16[256,1024]{1,0:T(8,128)(2,1)} %pad_maximum_fusion), channel_id=1, source_target_pairs={{0,2},{1,3},{2,4},{3,5},{4,6},{5,7},{6,8},{7,9},{8,10},{9,11},{10,... | collective-permute-start | bytes 1572872 | tf_op jit(solution)/shard_map/ppermute | solution.py:15
  47.2 12.9 %collective-permute-done.3 = bf16[256,1024]{1,0:T(8,128)(2,1)} collective-permute-done((bf16[256,1024]{1,0:T(8,128)(2,1)}, bf16[256,1024]{1,0:T(8,128)(2,1)}, u32[]{:S(2)}, u32[]{:S(2)}) %collective-permute-start.3) | collective-permute-done | bytes 524320 | tf_op jit(solution)/shard_map/ppermute | solution.py:15
  75.1 2.3 %convolution_multiply_fusion.9 = f32[4,256,256]{2,1,0:T(8,128)} fusion(bf16[256,4,128]{0,2,1:T(8,128)(2,1)S(1)} %bitcast.233, bf16[256,4,128]{0,2,1:T(8,128)(2,1)} %bitcast.254), kind=kOutput, calls=%fused_computation.22 | convolution fusion | flops 67371008 | bytes 1572864 | tf_op jit(solution)/shard_map/qhd,khd->hqk/dot_general | solution.py:56
  85.2 2.9 %fusion.36 = f32[4,128,256]{2,1,0:T(8,128)} fusion(bf16[256,4,128]{0,2,1:T(8,128)(2,1)S(1)} %bitcast.249, f32[4,256,256]{2,1,0:T(8,128)} %convolution_multiply_fusion.4, f32[256,256]{1,0:T(8,128)} %get-tuple-element.50, bf16[32,4,8,128]{3,2,1,0:T(8,128)(2,1)} %get-tuple-element.39, bf16[256,4,128]{2,1,0:T(4,128)(2,1)S(1)} %reshape_squeeze.6), kind=kOutput, calls=%fused_computation.58 | convolution fusion | flops 137101312 | bytes 2621440 | tf_op jit(solution)/shard_map/hqk,qhd->khd/dot_general | solution.py:77
  88.1 3.0 %fusion.35 = f32[4,128,256]{2,1,0:T(8,128)} fusion(bf16[256,4,128]{0,2,1:T(8,128)(2,1)S(1)} %bitcast.247, f32[4,256,256]{2,1,0:T(8,128)} %convolution_multiply_fusion.5, f32[256,256]{1,0:T(8,128)} %get-tuple-element.51, bf16[32,4,8,128]{3,2,1,0:T(8,128)(2,1)} %get-tuple-element.37, bf16[256,4,128]{2,1,0:T(4,128)(2,1)S(1)} %reshape_squeeze.6), kind=kOutput, calls=%fused_computation.57 | convolution fusion | flops 137101312 | bytes 2621440 | tf_op jit(solution)/shard_map/hqk,qhd->khd/dot_general | solution.py:77
  91.1 2.9 %fusion.37 = f32[4,128,256]{2,1,0:T(8,128)} fusion(bf16[256,4,128]{0,2,1:T(8,128)(2,1)S(1)} %bitcast.251, f32[4,256,256]{2,1,0:T(8,128)} %convolution_multiply_fusion.7, f32[256,256]{1,0:T(8,128)} %get-tuple-element.53, bf16[32,4,8,128]{3,2,1,0:T(8,128)(2,1)} %get-tuple-element.45, bf16[256,4,128]{2,1,0:T(4,128)(2,1)S(1)} %copy-done.5), kind=kOutput, calls=%fused_computation.59 | convolution fusion | flops 137101312 | bytes 2621440 | tf_op jit(solution)/shard_map/hqk,khd->qhd/dot_general | solution.py:68
  93.9 3.2 %fusion.42 = f32[4,128,256]{2,1,0:T(8,128)} fusion(f32[4,128,256]{2,1,0:T(8,128)} %fusion.180, bf16[256,4,128]{0,2,1:T(8,128)(2,1)} %bitcast.255, f32[4,256,256]{2,1,0:T(8,128)} %convolution_multiply_fusion.9, f32[256,256]{1,0:T(8,128)} %get-tuple-element.55, bf16[32,4,8,128]{3,2,1,0:T(8,128)(2,1)} %get-tuple-element.41, bf16[256,4,128]{2,1,0:T(4,128)(2,1)S(1)} %copy-done.5), kind=kOutput, calls=%fused_computation.64 | convolution fusion | flops 137232384 | bytes 3145728 | tf_op jit(solution)/shard_map/hqk,khd->qhd/dot_general | solution.py:68
  97.1 2.4 %fusion.49 = bf16[4,128,256]{2,1,0:T(8,128)(2,1)S(1)} fusion(f32[4,128,256]{2,1,0:T(8,128)} %fusion.37, f32[4,128,256]{2,1,0:T(8,128)} %fusion.42, bf16[256,4,128]{0,2,1:T(8,128)(2,1)S(1)} %bitcast.253, f32[4,256,256]{2,1,0:T(8,128)} %convolution_multiply_fusion.8, f32[256,256]{1,0:T(8,128)} %get-tuple-element.54, ...), kind=kOutput, calls=%fused_computation.71 | convolution fusion | flops 137494528 | bytes 3407872 | tf_op jit(solution)/shard_map/hqk,khd->qhd/dot_general | solution.py:68
  99.5 2.5 %fusion.52 = bf16[4,128,256]{2,1,0:T(8,128)(2,1)S(1)} fusion(f32[4,128,256]{2,1,0:T(8,128)} %fusion.36, f32[4,128,256]{2,1,0:T(8,128)} %fusion.35, f32[4,128,256]{2,1,0:T(8,128)} %fusion.181, bf16[256,4,128]{0,2,1:T(8,128)(2,1)S(1)} %bitcast.245, f32[4,256,256]{2,1,0:T(8,128)} %convolution_multiply_fusion.6, f32[256,256]{1,0:T(8,128)} %get-tuple-element.49, ...), kind=kOutput, calls=%fused_computation.74 | convolution fusion | flops 137625600 | bytes 3932160 | tf_op jit(solution)/shard_map/hqk,qhd->khd/dot_general | solution.py:77
  109.6 5.5 %collective-permute-start.8 = (f32[16,16,1024]{2,1,0:T(8,128)S(1)}, f32[16,16,1024]{2,1,0:T(8,128)}, u32[]{:S(2)}, u32[]{:S(2)}) collective-permute-start(f32[16,16,1024]{2,1,0:T(8,128)S(1)} %dynamic-slice_bitcast_fusion), channel_id=1, source_target_pairs={{0,2},{1,3},{2,0},{3,1},{4,6},{5,7},{6,4},{7,5},{8,10},{9,11},{10,... | collective-permute-start | bytes 3145736 | tf_op jit(solution)/shard_map/ppermute | solution.py:20
  115.2 23.5 %collective-permute-done.8 = f32[16,16,1024]{2,1,0:T(8,128)} collective-permute-done((f32[16,16,1024]{2,1,0:T(8,128)S(1)}, f32[16,16,1024]{2,1,0:T(8,128)}, u32[]{:S(2)}, u32[]{:S(2)}) %collective-permute-start.8) | collective-permute-done | bytes 1048608 | tf_op jit(solution)/shard_map/ppermute | solution.py:20
  143.9 13.2 %collective-permute-done.9 = f32[8,16,1024]{2,1,0:T(8,128)} collective-permute-done((f32[8,16,1024]{2,1,0:T(8,128)}, f32[8,16,1024]{2,1,0:T(8,128)}, u32[]{:S(2)}, u32[]{:S(2)}) %collective-permute-start.9) | collective-permute-done | bytes 524320 | tf_op jit(solution)/shard_map/ppermute | solution.py:20
  160.8 13.1 %collective-permute-done.10 = f32[4,16,1024]{2,1,0:T(8,128)S(1)} collective-permute-done((f32[4,16,1024]{2,1,0:T(8,128)S(1)}, f32[4,16,1024]{2,1,0:T(8,128)S(1)}, u32[]{:S(2)}, u32[]{:S(2)}) %collective-permute-start.10) | collective-permute-done | bytes 262176 | tf_op jit(solution)/shard_map/ppermute | solution.py:20
  174.0 5.3 %collective-permute-start.11 = (f32[2,16,1024]{2,1,0:T(8,128)S(1)}, f32[2,16,1024]{2,1,0:T(8,128)S(1)}, u32[]{:S(2)}, u32[]{:S(2)}) collective-permute-start(f32[2,16,1024]{2,1,0:T(8,128)S(1)} %dynamic-slice_bitcast_fusion.3), channel_id=1, source_target_pairs={{0,16},{1,17},{2,18},{3,19},{4,20},{5,21},{6,22},{7,23},{8,24},{9,... | collective-permute-start | bytes 393224 | tf_op jit(solution)/shard_map/ppermute | solution.py:20
  179.8 11.7 %collective-permute-done.11 = f32[2,16,1024]{2,1,0:T(8,128)S(1)} collective-permute-done((f32[2,16,1024]{2,1,0:T(8,128)S(1)}, f32[2,16,1024]{2,1,0:T(8,128)S(1)}, u32[]{:S(2)}, u32[]{:S(2)}) %collective-permute-start.11) | collective-permute-done | bytes 131104 | tf_op jit(solution)/shard_map/ppermute | solution.py:20
  191.6 10.7 %collective-permute-start.12 = (f32[1,16,1024]{2,1,0:T(8,128)S(1)}, f32[1,16,1024]{2,1,0:T(8,128)S(1)}, u32[]{:S(2)}, u32[]{:S(2)}) collective-permute-start(f32[1,16,1024]{2,1,0:T(8,128)S(1)} %constant_dynamic-slice_fusion), channel_id=1, source_target_pairs={{0,32},{1,33},{2,34},{3,35},{4,36},{5,37},{6,38},{7,39},{8,40},{9,... | collective-permute-start | bytes 196616 | tf_op jit(solution)/shard_map/ppermute | solution.py:20
  202.9 7.3 %collective-permute-done.12 = f32[1,16,1024]{2,1,0:T(8,128)S(1)} collective-permute-done((f32[1,16,1024]{2,1,0:T(8,128)S(1)}, f32[1,16,1024]{2,1,0:T(8,128)S(1)}, u32[]{:S(2)}, u32[]{:S(2)}) %collective-permute-start.12) | collective-permute-done | bytes 65568 | tf_op jit(solution)/shard_map/ppermute | solution.py:20
  212.7 3.7 %collective-permute-done.13 = f32[16,1024]{1,0:T(8,128)S(1)} collective-permute-done((f32[16,1024]{1,0:T(8,128)S(1)}, f32[16,1024]{1,0:T(8,128)S(1)}, u32[]{:S(2)}, u32[]{:S(2)}) %collective-permute-start.13) | collective-permute-done | bytes 65568 | tf_op jit(solution)/shard_map/ppermute | solution.py:20
  216.5 3.6 %collective-permute-start.14 = (f32[16,1024]{1,0:T(8,128)S(1)}, f32[16,1024]{1,0:T(8,128)S(1)}, u32[]{:S(2)}, u32[]{:S(2)}) collective-permute-start(f32[16,1024]{1,0:T(8,128)S(1)} %add.492), channel_id=1, source_target_pairs={{0,128},{64,192},{128,0},{192,64},{256,384},{320,448},{384,256},{4... | collective-permute-start | bytes 196616 | tf_op jit(solution)/shard_map/ppermute | solution.py:20
  220.6 2.5 %collective-permute-done.14 = f32[16,1024]{1,0:T(8,128)S(1)} collective-permute-done((f32[16,1024]{1,0:T(8,128)S(1)}, f32[16,1024]{1,0:T(8,128)S(1)}, u32[]{:S(2)}, u32[]{:S(2)}) %collective-permute-start.14) | collective-permute-done | bytes 65568 | tf_op jit(solution)/shard_map/ppermute | solution.py:20
  223.2 4.8 %collective-permute-start.15 = (f32[16,1024]{1,0:T(8,128)S(1)}, f32[16,1024]{1,0:T(8,128)S(1)}, u32[]{:S(2)}, u32[]{:S(2)}) collective-permute-start(f32[16,1024]{1,0:T(8,128)S(1)} %add.493), channel_id=1, source_target_pairs={{0,256},{64,320},{128,384},{192,448},{256,0},{320,64},{384,128},{4... | collective-permute-start | bytes 196616 | tf_op jit(solution)/shard_map/ppermute | solution.py:20
  (162 shorter events, 68.0 us)
Async XLA Ops:
  0.6 23.6 %copy-start.1 = (bf16[1,256,1024]{2,1,0:T(8,128)(2,1)S(1)}, bf16[1,256,1024]{2,1,0:T(8,128)(2,1)}, u32[]{:S(2)}) copy-start(bf16[1,256,1024]{2,1,0:T(8,128)(2,1)} %param.8) | copy-start | bytes 1572868
  0.7 23.6 %copy-start.3 = (bf16[1024,512]{1,0:T(8,128)(2,1)S(1)}, bf16[1024,512]{1,0:T(8,128)(2,1)}, u32[]{:S(2)}) copy-start(bf16[1024,512]{1,0:T(8,128)(2,1)} %param.10) | copy-start | bytes 3145732
  0.7 24.1 %copy-start.13 = (bf16[1,256,512]{2,1,0:T(8,128)(2,1)S(1)}, bf16[1,256,512]{2,1,0:T(8,128)(2,1)}, u32[]{:S(2)}) copy-start(bf16[1,256,512]{2,1,0:T(8,128)(2,1)} %param.11) | copy-start | bytes 786436
  3.3 29.3 %copy-start.14 = (bf16[1,256,512]{2,1,0:T(8,128)(2,1)S(1)}, bf16[1,256,512]{2,1,0:T(8,128)(2,1)}, u32[]{:S(2)}) copy-start(bf16[1,256,512]{2,1,0:T(8,128)(2,1)} %param.12) | copy-start | bytes 786436
  5.2 34.5 %collective-permute-start.5 = (bf16[256,1024]{1,0:T(8,128)(2,1)}, bf16[256,1024]{1,0:T(8,128)(2,1)}, u32[]{:S(2)}, u32[]{:S(2)}) collective-permute-start(bf16[256,1024]{1,0:T(8,128)(2,1)} %pad_maximum_fusion.1), channel_id=1, source_target_pairs={{0,61},{1,62},{2,63},{3,0},{4,1},{5,2},{6,3},{7,4},{8,5},{9,6},{10... | collective-permute-start | bytes 1572872 | tf_op jit(solution)/shard_map/ppermute | solution.py:15
  16.1 27.3 %collective-permute-start.4 = (bf16[256,1024]{1,0:T(8,128)(2,1)}, bf16[256,1024]{1,0:T(8,128)(2,1)}, u32[]{:S(2)}, u32[]{:S(2)}) collective-permute-start(bf16[256,1024]{1,0:T(8,128)(2,1)} %pad_maximum_fusion.1), channel_id=1, source_target_pairs={{0,62},{1,63},{2,0},{3,1},{4,2},{5,3},{6,4},{7,5},{8,6},{9,7},{10,... | collective-permute-start | bytes 1572872 | tf_op jit(solution)/shard_map/ppermute | solution.py:15
  19.4 40.7 %collective-permute-start.3 = (bf16[256,1024]{1,0:T(8,128)(2,1)}, bf16[256,1024]{1,0:T(8,128)(2,1)}, u32[]{:S(2)}, u32[]{:S(2)}) collective-permute-start(bf16[256,1024]{1,0:T(8,128)(2,1)} %pad_maximum_fusion.1), channel_id=1, source_target_pairs={{0,63},{1,0},{2,1},{3,2},{4,3},{5,4},{6,5},{7,6},{8,7},{9,8},{10,9... | collective-permute-start | bytes 1572872 | tf_op jit(solution)/shard_map/ppermute | solution.py:15
  25.6 38.5 %collective-permute-start.2 = (bf16[256,1024]{1,0:T(8,128)(2,1)}, bf16[256,1024]{1,0:T(8,128)(2,1)}, u32[]{:S(2)}, u32[]{:S(2)}) collective-permute-start(bf16[256,1024]{1,0:T(8,128)(2,1)} %pad_maximum_fusion), channel_id=1, source_target_pairs={{0,3},{1,4},{2,5},{3,6},{4,7},{5,8},{6,9},{7,10},{8,11},{9,12},{10... | collective-permute-start | bytes 1572872 | tf_op jit(solution)/shard_map/ppermute | solution.py:15
  27.7 40.1 %collective-permute-start.1 = (bf16[256,1024]{1,0:T(8,128)(2,1)}, bf16[256,1024]{1,0:T(8,128)(2,1)}, u32[]{:S(2)}, u32[]{:S(2)}) collective-permute-start(bf16[256,1024]{1,0:T(8,128)(2,1)} %pad_maximum_fusion), channel_id=1, source_target_pairs={{0,2},{1,3},{2,4},{3,5},{4,6},{5,7},{6,8},{7,9},{8,10},{9,11},{10,... | collective-permute-start | bytes 1572872 | tf_op jit(solution)/shard_map/ppermute | solution.py:15
  39.7 31.7 %collective-permute-start = (bf16[256,1024]{1,0:T(8,128)(2,1)}, bf16[256,1024]{1,0:T(8,128)(2,1)}, u32[]{:S(2)}, u32[]{:S(2)}) collective-permute-start(bf16[256,1024]{1,0:T(8,128)(2,1)} %pad_maximum_fusion), channel_id=1, source_target_pairs={{0,1},{1,2},{2,3},{3,4},{4,5},{5,6},{6,7},{7,8},{8,9},{9,10},{10,1... | collective-permute-start | bytes 1572872 | tf_op jit(solution)/shard_map/ppermute | solution.py:15
  43.4 61.0 %collective-permute-start.6 = (bf16[256,1024]{0,1:T(8,128)(2,1)S(1)}, bf16[256,1024]{0,1:T(8,128)(2,1)}, u32[]{:S(2)}, u32[]{:S(2)}) collective-permute-start(bf16[256,1024]{0,1:T(8,128)(2,1)S(1)} %bitcast.238), channel_id=1, source_target_pairs={{0,1},{1,0},{2,3},{3,2},{4,5},{5,4},{6,7},{7,6},{8,9},{9,8},{10,11... | collective-permute-start | bytes 1572872 | tf_op jit(solution)/shard_map/ppermute | solution.py:20
  102.4 3.9 %collective-permute-start.7 = (bf16[256,1024]{1,0:T(8,128)(2,1)S(1)}, bf16[256,1024]{1,0:T(8,128)(2,1)}, u32[]{:S(2)}, u32[]{:S(2)}) collective-permute-start(bf16[256,1024]{1,0:T(8,128)(2,1)S(1)} %pad_maximum_fusion.2), channel_id=1, source_target_pairs={{0,1},{1,0},{2,3},{3,2},{4,5},{5,4},{6,7},{7,6},{8,9},{9,8},{10,11... | collective-permute-start | bytes 1572872 | tf_op jit(solution)/shard_map/ppermute | solution.py:20
  109.6 29.1 %collective-permute-start.8 = (f32[16,16,1024]{2,1,0:T(8,128)S(1)}, f32[16,16,1024]{2,1,0:T(8,128)}, u32[]{:S(2)}, u32[]{:S(2)}) collective-permute-start(f32[16,16,1024]{2,1,0:T(8,128)S(1)} %dynamic-slice_bitcast_fusion), channel_id=1, source_target_pairs={{0,2},{1,3},{2,0},{3,1},{4,6},{5,7},{6,4},{7,5},{8,10},{9,11},{10,... | collective-permute-start | bytes 3145736 | tf_op jit(solution)/shard_map/ppermute | solution.py:20
  115.2 28.1 %copy-start.6 = (bf16[256,4,128]{2,1,0:T(4,128)(2,1)S(1)}, bf16[256,4,128]{2,1,0:T(4,128)(2,1)}, u32[]{:S(2)}) copy-start(bf16[256,4,128]{2,1,0:T(4,128)(2,1)} %copy-done.4) | copy-start | bytes 786436
  141.2 15.8 %collective-permute-start.9 = (f32[8,16,1024]{2,1,0:T(8,128)}, f32[8,16,1024]{2,1,0:T(8,128)}, u32[]{:S(2)}, u32[]{:S(2)}) collective-permute-start(f32[8,16,1024]{2,1,0:T(8,128)} %dynamic-slice_bitcast_fusion.1), channel_id=1, source_target_pairs={{0,4},{1,5},{2,6},{3,7},{4,0},{5,1},{6,2},{7,3},{8,12},{9,13},{10,... | collective-permute-start | bytes 1572872 | tf_op jit(solution)/shard_map/ppermute | solution.py:20
  158.2 15.7 %collective-permute-start.10 = (f32[4,16,1024]{2,1,0:T(8,128)S(1)}, f32[4,16,1024]{2,1,0:T(8,128)S(1)}, u32[]{:S(2)}, u32[]{:S(2)}) collective-permute-start(f32[4,16,1024]{2,1,0:T(8,128)S(1)} %dynamic-slice_bitcast_fusion.2), channel_id=1, source_target_pairs={{0,8},{1,9},{2,10},{3,11},{4,12},{5,13},{6,14},{7,15},{8,0},{9,1},... | collective-permute-start | bytes 786440 | tf_op jit(solution)/shard_map/ppermute | solution.py:20
  174.0 28.4 %copy-start.10 = (f32[4,256,256]{2,1,0:T(8,128)S(1)}, f32[4,256,256]{2,1,0:T(8,128)}, u32[]{:S(2)}) copy-start(f32[4,256,256]{2,1,0:T(8,128)} %convolution_multiply_fusion.6) | copy-start | bytes 3145732
  174.0 28.4 %copy-start.25 = (f32[256,256]{1,0:T(8,128)S(1)}, f32[256,256]{1,0:T(8,128)}, u32[]{:S(2)}) copy-start(f32[256,256]{1,0:T(8,128)} %get-tuple-element.49) | copy-start | bytes 786436
  174.0 28.4 %copy-start.31 = (bf16[32,4,8,128]{3,2,1,0:T(8,128)(2,1)S(1)}, bf16[32,4,8,128]{3,2,1,0:T(8,128)(2,1)}, u32[]{:S(2)}) copy-start(bf16[32,4,8,128]{3,2,1,0:T(8,128)(2,1)} %get-tuple-element.35) | copy-start | bytes 786436
  174.0 17.6 %collective-permute-start.11 = (f32[2,16,1024]{2,1,0:T(8,128)S(1)}, f32[2,16,1024]{2,1,0:T(8,128)S(1)}, u32[]{:S(2)}, u32[]{:S(2)}) collective-permute-start(f32[2,16,1024]{2,1,0:T(8,128)S(1)} %dynamic-slice_bitcast_fusion.3), channel_id=1, source_target_pairs={{0,16},{1,17},{2,18},{3,19},{4,20},{5,21},{6,22},{7,23},{8,24},{9,... | collective-permute-start | bytes 393224 | tf_op jit(solution)/shard_map/ppermute | solution.py:20
  191.6 18.5 %collective-permute-start.12 = (f32[1,16,1024]{2,1,0:T(8,128)S(1)}, f32[1,16,1024]{2,1,0:T(8,128)S(1)}, u32[]{:S(2)}, u32[]{:S(2)}) collective-permute-start(f32[1,16,1024]{2,1,0:T(8,128)S(1)} %constant_dynamic-slice_fusion), channel_id=1, source_target_pairs={{0,32},{1,33},{2,34},{3,35},{4,36},{5,37},{6,38},{7,39},{8,40},{9,... | collective-permute-start | bytes 196616 | tf_op jit(solution)/shard_map/ppermute | solution.py:20
  210.2 6.3 %collective-permute-start.13 = (f32[16,1024]{1,0:T(8,128)S(1)}, f32[16,1024]{1,0:T(8,128)S(1)}, u32[]{:S(2)}, u32[]{:S(2)}) collective-permute-start(f32[16,1024]{1,0:T(8,128)S(1)} %add_bitcast_fusion), channel_id=1, source_target_pairs={{0,64},{64,0},{128,192},{192,128},{256,320},{320,256},{384,448},{4... | collective-permute-start | bytes 196616 | tf_op jit(solution)/shard_map/ppermute | solution.py:20
  216.5 6.6 %collective-permute-start.14 = (f32[16,1024]{1,0:T(8,128)S(1)}, f32[16,1024]{1,0:T(8,128)S(1)}, u32[]{:S(2)}, u32[]{:S(2)}) collective-permute-start(f32[16,1024]{1,0:T(8,128)S(1)} %add.492), channel_id=1, source_target_pairs={{0,128},{64,192},{128,0},{192,64},{256,384},{320,448},{384,256},{4... | collective-permute-start | bytes 196616 | tf_op jit(solution)/shard_map/ppermute | solution.py:20
  223.2 7.7 %collective-permute-start.15 = (f32[16,1024]{1,0:T(8,128)S(1)}, f32[16,1024]{1,0:T(8,128)S(1)}, u32[]{:S(2)}, u32[]{:S(2)}) collective-permute-start(f32[16,1024]{1,0:T(8,128)S(1)} %add.493), channel_id=1, source_target_pairs={{0,256},{64,320},{128,384},{192,448},{256,0},{320,64},{384,128},{4... | collective-permute-start | bytes 196616 | tf_op jit(solution)/shard_map/ppermute | solution.py:20
  (28 other events, 310.3 us)

commit v3 on v2

--- a/solution.py
+++ b/solution.py
@@ -42,7 +42,7 @@
     while mask < cycle_size:
         acc = acc.reshape(acc.shape[0] // 2, 2, share, joined.shape[1])
         keep_part, send_part = pick(acc, (myself // mask) % 2, 1)
-        acc = keep_part + exchange(send_part, "ctx", mask)
+        acc = keep_part + exchange(send_part.astype(jnp.bfloat16), "ctx", mask).astype(jnp.float32)
         mask *= 2
     acc = acc.reshape(share, joined.shape[1])
     mask = 1

time: 234 us -> 200 us (0.85)
  waiting for transfers between devices: 89.6 us -> 55.9 us
    ppermute x10, waiting for transfers between devices: 76.7 us -> 43.1 us  [exchange(): lax.ppermute(value, axis, [(source, source ^ mask) for source in range(co...]
    unnamed x81 -> x83, local copies, waits for them, and re-layouts: 15.5 us -> 15.6 us
  transfers between devices with their start and end apart: 16 -> 16, of which waited for: 10 -> 10; matrix products, arithmetic and copies ran while one was open for 26% -> 30% of each run, Pallas kernels for 0% -> 0%
where the time goes in v3:
time: 200 us; the launch traced here: 198 us
  starting transfers between devices  68.3 us (34%)
  waiting for transfers between devices  55.9 us (28%)
  matrix products  38 us (19%)
  local copies, waits for them, and re-layouts  25.4 us (13%)
  other arithmetic  7.82 us (4%)
  between operations  2.4 us (1%)
    ppermute x10, waiting for transfers between devices, exchange(): lax.ppermute(value, axis, [(source, source ^ mask) for source in range(co...  43.1 us
    ppermute x10, starting transfers between devices, exchange(): lax.ppermute(value, axis, [(source, source ^ mask) for source in range(co...  40.5 us
    ppermute x6, starting transfers between devices, shifted(): return lax.ppermute(value, axis, pairs)  27.8 us
    unnamed x83, local copies, waits for them, and re-layouts  15.6 us
    ppermute x6, waiting for transfers between devices, shifted(): return lax.ppermute(value, axis, pairs)  12.8 us
    dot_general x7, matrix products, scores(): jnp.einsum('qhd,khd->hqk', query, key, preferred_element_type=jnp.float32)  10.5 us
    dot_general x4, matrix products, forward_terms(): jnp.einsum('hqk,khd->qhd', dsc, key, preferred_element_type=jnp.float32)  9.6 us
    dot_general x3, matrix products, backward_terms(): jnp.einsum('hqk,qhd->khd', dsc, query, preferred_element_type=jnp.float32)  8.43 us
  transfers between devices with their start and end apart: 16, of which 10 were waited for; matrix products, arithmetic and copies ran while one was open for 30% of the time, Pallas kernels for 0%

profile of v3, /device:TPU:6, one launch (start us, length us, event | category | flops | bytes accessed | tf_op | source)
XLA Modules:
  0.0 197.9 jit_solution(15759282936874093147)
XLA Ops:
  5.2 10.8 %collective-permute-start.5 = (bf16[256,1024]{1,0:T(8,128)(2,1)}, bf16[256,1024]{1,0:T(8,128)(2,1)}, u32[]{:S(2)}, u32[]{:S(2)}) collective-permute-start(bf16[256,1024]{1,0:T(8,128)(2,1)} %pad_maximum_fusion.1), channel_id=1, source_target_pairs={{0,61},{1,62},{2,63},{3,0},{4,1},{5,2},{6,3},{7,4},{8,5},{9,6},{10... | collective-permute-start | bytes 1572872 | tf_op jit(solution)/shard_map/ppermute | solution.py:15
  16.1 3.3 %collective-permute-start.4 = (bf16[256,1024]{1,0:T(8,128)(2,1)}, bf16[256,1024]{1,0:T(8,128)(2,1)}, u32[]{:S(2)}, u32[]{:S(2)}) collective-permute-start(bf16[256,1024]{1,0:T(8,128)(2,1)} %pad_maximum_fusion.1), channel_id=1, source_target_pairs={{0,62},{1,63},{2,0},{3,1},{4,2},{5,3},{6,4},{7,5},{8,6},{9,7},{10,... | collective-permute-start | bytes 1572872 | tf_op jit(solution)/shard_map/ppermute | solution.py:15
  19.4 4.9 %collective-permute-start.3 = (bf16[256,1024]{1,0:T(8,128)(2,1)}, bf16[256,1024]{1,0:T(8,128)(2,1)}, u32[]{:S(2)}, u32[]{:S(2)}) collective-permute-start(bf16[256,1024]{1,0:T(8,128)(2,1)} %pad_maximum_fusion.1), channel_id=1, source_target_pairs={{0,63},{1,0},{2,1},{3,2},{4,3},{5,4},{6,5},{7,6},{8,7},{9,8},{10,9... | collective-permute-start | bytes 1572872 | tf_op jit(solution)/shard_map/ppermute | solution.py:15
  27.7 4.8 %collective-permute-start.1 = (bf16[256,1024]{1,0:T(8,128)(2,1)}, bf16[256,1024]{1,0:T(8,128)(2,1)}, u32[]{:S(2)}, u32[]{:S(2)}) collective-permute-start(bf16[256,1024]{1,0:T(8,128)(2,1)} %pad_maximum_fusion), channel_id=1, source_target_pairs={{0,2},{1,3},{2,4},{3,5},{4,6},{5,7},{6,8},{7,9},{8,10},{9,11},{10,... | collective-permute-start | bytes 1572872 | tf_op jit(solution)/shard_map/ppermute | solution.py:15
  47.3 12.8 %collective-permute-done.3 = bf16[256,1024]{1,0:T(8,128)(2,1)} collective-permute-done((bf16[256,1024]{1,0:T(8,128)(2,1)}, bf16[256,1024]{1,0:T(8,128)(2,1)}, u32[]{:S(2)}, u32[]{:S(2)}) %collective-permute-start.3) | collective-permute-done | bytes 524320 | tf_op jit(solution)/shard_map/ppermute | solution.py:15
  75.2 2.3 %convolution_multiply_fusion.9 = f32[4,256,256]{2,1,0:T(8,128)} fusion(bf16[256,4,128]{0,2,1:T(8,128)(2,1)S(1)} %bitcast.237, bf16[256,4,128]{0,2,1:T(8,128)(2,1)} %bitcast.258), kind=kOutput, calls=%fused_computation.22 | convolution fusion | flops 67371008 | bytes 1572864 | tf_op jit(solution)/shard_map/qhd,khd->hqk/dot_general | solution.py:56
  77.5 2.3 %convolution_multiply_fusion.8 = f32[4,256,256]{2,1,0:T(8,128)} fusion(bf16[256,4,128]{0,2,1:T(8,128)(2,1)S(1)} %bitcast.238, bf16[256,4,128]{0,2,1:T(8,128)(2,1)} %bitcast.256), kind=kOutput, calls=%fused_computation.21 | convolution fusion | flops 67371008 | bytes 1572864 | tf_op jit(solution)/shard_map/qhd,khd->hqk/dot_general | solution.py:56
  85.2 2.9 %fusion.36 = f32[4,128,256]{2,1,0:T(8,128)} fusion(bf16[256,4,128]{0,2,1:T(8,128)(2,1)S(1)} %bitcast.253, f32[4,256,256]{2,1,0:T(8,128)} %convolution_multiply_fusion.4, f32[256,256]{1,0:T(8,128)} %get-tuple-element.46, bf16[32,4,8,128]{3,2,1,0:T(8,128)(2,1)} %get-tuple-element.35, bf16[256,4,128]{2,1,0:T(4,128)(2,1)S(1)} %reshape_squeeze.6), kind=kOutput, calls=%fused_computation.58 | convolution fusion | flops 137101312 | bytes 2621440 | tf_op jit(solution)/shard_map/hqk,qhd->khd/dot_general | solution.py:77
  88.1 3.0 %fusion.35 = f32[4,128,256]{2,1,0:T(8,128)} fusion(bf16[256,4,128]{0,2,1:T(8,128)(2,1)S(1)} %bitcast.251, f32[4,256,256]{2,1,0:T(8,128)} %convolution_multiply_fusion.5, f32[256,256]{1,0:T(8,128)} %get-tuple-element.47, bf16[32,4,8,128]{3,2,1,0:T(8,128)(2,1)} %get-tuple-element.33, bf16[256,4,128]{2,1,0:T(4,128)(2,1)S(1)} %reshape_squeeze.6), kind=kOutput, calls=%fused_computation.57 | convolution fusion | flops 137101312 | bytes 2621440 | tf_op jit(solution)/shard_map/hqk,qhd->khd/dot_general | solution.py:77
  91.1 2.9 %fusion.37 = f32[4,128,256]{2,1,0:T(8,128)} fusion(bf16[256,4,128]{0,2,1:T(8,128)(2,1)S(1)} %bitcast.255, f32[4,256,256]{2,1,0:T(8,128)} %convolution_multiply_fusion.7, f32[256,256]{1,0:T(8,128)} %get-tuple-element.49, bf16[32,4,8,128]{3,2,1,0:T(8,128)(2,1)} %get-tuple-element.41, bf16[256,4,128]{2,1,0:T(4,128)(2,1)S(1)} %copy-done.5), kind=kOutput, calls=%fused_computation.59 | convolution fusion | flops 137101312 | bytes 2621440 | tf_op jit(solution)/shard_map/hqk,khd->qhd/dot_general | solution.py:68
  93.9 3.2 %fusion.42 = f32[4,128,256]{2,1,0:T(8,128)} fusion(f32[4,128,256]{2,1,0:T(8,128)} %fusion.184, bf16[256,4,128]{0,2,1:T(8,128)(2,1)} %bitcast.259, f32[4,256,256]{2,1,0:T(8,128)} %convolution_multiply_fusion.9, f32[256,256]{1,0:T(8,128)} %get-tuple-element.51, bf16[32,4,8,128]{3,2,1,0:T(8,128)(2,1)} %get-tuple-element.37, bf16[256,4,128]{2,1,0:T(4,128)(2,1)S(1)} %copy-done.5), kind=kOutput, calls=%fused_computation.64 | convolution fusion | flops 137232384 | bytes 3145728 | tf_op jit(solution)/shard_map/hqk,khd->qhd/dot_general | solution.py:68
  97.1 2.4 %fusion.49 = bf16[4,128,256]{2,1,0:T(8,128)(2,1)S(1)} fusion(f32[4,128,256]{2,1,0:T(8,128)} %fusion.37, f32[4,128,256]{2,1,0:T(8,128)} %fusion.42, bf16[256,4,128]{0,2,1:T(8,128)(2,1)S(1)} %bitcast.257, f32[4,256,256]{2,1,0:T(8,128)} %convolution_multiply_fusion.8, f32[256,256]{1,0:T(8,128)} %get-tuple-element.50, ...), kind=kOutput, calls=%fused_computation.71 | convolution fusion | flops 137494528 | bytes 3407872 | tf_op jit(solution)/shard_map/hqk,khd->qhd/dot_general | solution.py:68
  99.6 2.6 %fusion.52 = bf16[4,128,256]{2,1,0:T(8,128)(2,1)S(1)} fusion(f32[4,128,256]{2,1,0:T(8,128)} %fusion.36, f32[4,128,256]{2,1,0:T(8,128)} %fusion.35, f32[4,128,256]{2,1,0:T(8,128)} %fusion.185, bf16[256,4,128]{0,2,1:T(8,128)(2,1)S(1)} %bitcast.249, f32[4,256,256]{2,1,0:T(8,128)} %convolution_multiply_fusion.6, f32[256,256]{1,0:T(8,128)} %get-tuple-element.45, ...), kind=kOutput, calls=%fused_computation.74 | convolution fusion | flops 137625600 | bytes 3932160 | tf_op jit(solution)/shard_map/hqk,qhd->khd/dot_general | solution.py:77
  109.6 5.5 %collective-permute-start.8 = (bf16[16,16,1024]{2,1,0:T(8,128)(2,1)S(1)}, bf16[16,16,1024]{2,1,0:T(8,128)(2,1)}, u32[]{:S(2)}, u32[]{:S(2)}) collective-permute-start(bf16[16,16,1024]{2,1,0:T(8,128)(2,1)S(1)} %fusion.76), channel_id=1, source_target_pairs={{0,2},{1,3},{2,0},{3,1},{4,6},{5,7},{6,4},{7,5},{8,10},{9,11},{10,... | collective-permute-start | bytes 1572872 | tf_op jit(solution)/shard_map/ppermute | solution.py:20
  115.2 12.3 %collective-permute-done.8 = bf16[16,16,1024]{2,1,0:T(8,128)(2,1)} collective-permute-done((bf16[16,16,1024]{2,1,0:T(8,128)(2,1)S(1)}, bf16[16,16,1024]{2,1,0:T(8,128)(2,1)}, u32[]{:S(2)}, u32[]{:S(2)}) %collective-permute-start.8) | collective-permute-done | bytes 524320 | tf_op jit(solution)/shard_map/ppermute | solution.py:20
  133.1 6.8 %collective-permute-done.9 = bf16[8,16,1024]{2,1,0:T(8,128)(2,1)S(1)} collective-permute-done((bf16[8,16,1024]{2,1,0:T(8,128)(2,1)}, bf16[8,16,1024]{2,1,0:T(8,128)(2,1)S(1)}, u32[]{:S(2)}, u32[]{:S(2)}) %collective-permute-start.9) | collective-permute-done | bytes 262176 | tf_op jit(solution)/shard_map/ppermute | solution.py:20
  142.6 7.5 %collective-permute-done.10 = bf16[4,16,1024]{2,1,0:T(8,128)(2,1)S(1)} collective-permute-done((bf16[4,16,1024]{2,1,0:T(8,128)(2,1)S(1)}, bf16[4,16,1024]{2,1,0:T(8,128)(2,1)S(1)}, u32[]{:S(2)}, u32[]{:S(2)}) %collective-permute-start.10) | collective-permute-done | bytes 131104 | tf_op jit(solution)/shard_map/ppermute | solution.py:20
  150.2 5.4 %collective-permute-start.11 = (bf16[2,16,1024]{2,1,0:T(8,128)(2,1)S(1)}, bf16[2,16,1024]{2,1,0:T(8,128)(2,1)S(1)}, u32[]{:S(2)}, u32[]{:S(2)}) collective-permute-start(bf16[2,16,1024]{2,1,0:T(8,128)(2,1)S(1)} %fusion.156), channel_id=1, source_target_pairs={{0,16},{1,17},{2,18},{3,19},{4,20},{5,21},{6,22},{7,23},{8,24},{9,... | collective-permute-start | bytes 196616 | tf_op jit(solution)/shard_map/ppermute | solution.py:20
  156.1 6.1 %collective-permute-done.11 = bf16[2,16,1024]{2,1,0:T(8,128)(2,1)S(1)} collective-permute-done((bf16[2,16,1024]{2,1,0:T(8,128)(2,1)S(1)}, bf16[2,16,1024]{2,1,0:T(8,128)(2,1)S(1)}, u32[]{:S(2)}, u32[]{:S(2)}) %collective-permute-start.11) | collective-permute-done | bytes 65568 | tf_op jit(solution)/shard_map/ppermute | solution.py:20
  162.2 10.9 %collective-permute-start.12 = (bf16[1,16,1024]{2,1,0:T(8,128)(2,1)S(1)}, bf16[1,16,1024]{2,1,0:T(8,128)(2,1)S(1)}, u32[]{:S(2)}, u32[]{:S(2)}) collective-permute-start(bf16[1,16,1024]{2,1,0:T(8,128)(2,1)S(1)} %dynamic-slice_convert_fusion.3), channel_id=1, source_target_pairs={{0,32},{1,33},{2,34},{3,35},{4,36},{5,37},{6,38},{7,39},{8,40},{9,... | collective-permute-start | bytes 98312 | tf_op jit(solution)/shard_map/ppermute | solution.py:20
  173.6 3.2 %collective-permute-done.12 = bf16[1,16,1024]{2,1,0:T(8,128)(2,1)S(1)} collective-permute-done((bf16[1,16,1024]{2,1,0:T(8,128)(2,1)S(1)}, bf16[1,16,1024]{2,1,0:T(8,128)(2,1)S(1)}, u32[]{:S(2)}, u32[]{:S(2)}) %collective-permute-start.12) | collective-permute-done | bytes 32800 | tf_op jit(solution)/shard_map/ppermute | solution.py:20
  179.5 3.7 %collective-permute-done.13 = f32[16,1024]{1,0:T(8,128)S(1)} collective-permute-done((f32[16,1024]{1,0:T(8,128)S(1)}, f32[16,1024]{1,0:T(8,128)S(1)}, u32[]{:S(2)}, u32[]{:S(2)}) %collective-permute-start.13) | collective-permute-done | bytes 65568 | tf_op jit(solution)/shard_map/ppermute | solution.py:20
  183.3 3.6 %collective-permute-start.14 = (f32[16,1024]{1,0:T(8,128)S(1)}, f32[16,1024]{1,0:T(8,128)S(1)}, u32[]{:S(2)}, u32[]{:S(2)}) collective-permute-start(f32[16,1024]{1,0:T(8,128)S(1)} %add.492), channel_id=1, source_target_pairs={{0,128},{64,192},{128,0},{192,64},{256,384},{320,448},{384,256},{4... | collective-permute-start | bytes 196616 | tf_op jit(solution)/shard_map/ppermute | solution.py:20
  189.6 5.1 %collective-permute-start.15 = (f32[16,1024]{1,0:T(8,128)S(1)}, f32[16,1024]{1,0:T(8,128)S(1)}, u32[]{:S(2)}, u32[]{:S(2)}) collective-permute-start(f32[16,1024]{1,0:T(8,128)S(1)} %add.493), channel_id=1, source_target_pairs={{0,256},{64,320},{128,384},{192,448},{256,0},{320,64},{384,128},{4... | collective-permute-start | bytes 196616 | tf_op jit(solution)/shard_map/ppermute | solution.py:20
  (164 shorter events, 67.2 us)
Async XLA Ops:
  0.6 23.6 %copy-start.1 = (bf16[1,256,1024]{2,1,0:T(8,128)(2,1)S(1)}, bf16[1,256,1024]{2,1,0:T(8,128)(2,1)}, u32[]{:S(2)}) copy-start(bf16[1,256,1024]{2,1,0:T(8,128)(2,1)} %param.8) | copy-start | bytes 1572868
  0.7 23.6 %copy-start.3 = (bf16[1024,512]{1,0:T(8,128)(2,1)S(1)}, bf16[1024,512]{1,0:T(8,128)(2,1)}, u32[]{:S(2)}) copy-start(bf16[1024,512]{1,0:T(8,128)(2,1)} %param.10) | copy-start | bytes 3145732
  0.7 24.1 %copy-start.13 = (bf16[1,256,512]{2,1,0:T(8,128)(2,1)S(1)}, bf16[1,256,512]{2,1,0:T(8,128)(2,1)}, u32[]{:S(2)}) copy-start(bf16[1,256,512]{2,1,0:T(8,128)(2,1)} %param.11) | copy-start | bytes 786436
  3.3 29.3 %copy-start.14 = (bf16[1,256,512]{2,1,0:T(8,128)(2,1)S(1)}, bf16[1,256,512]{2,1,0:T(8,128)(2,1)}, u32[]{:S(2)}) copy-start(bf16[1,256,512]{2,1,0:T(8,128)(2,1)} %param.12) | copy-start | bytes 786436
  5.2 34.6 %collective-permute-start.5 = (bf16[256,1024]{1,0:T(8,128)(2,1)}, bf16[256,1024]{1,0:T(8,128)(2,1)}, u32[]{:S(2)}, u32[]{:S(2)}) collective-permute-start(bf16[256,1024]{1,0:T(8,128)(2,1)} %pad_maximum_fusion.1), channel_id=1, source_target_pairs={{0,61},{1,62},{2,63},{3,0},{4,1},{5,2},{6,3},{7,4},{8,5},{9,6},{10... | collective-permute-start | bytes 1572872 | tf_op jit(solution)/shard_map/ppermute | solution.py:15
  16.1 27.4 %collective-permute-start.4 = (bf16[256,1024]{1,0:T(8,128)(2,1)}, bf16[256,1024]{1,0:T(8,128)(2,1)}, u32[]{:S(2)}, u32[]{:S(2)}) collective-permute-start(bf16[256,1024]{1,0:T(8,128)(2,1)} %pad_maximum_fusion.1), channel_id=1, source_target_pairs={{0,62},{1,63},{2,0},{3,1},{4,2},{5,3},{6,4},{7,5},{8,6},{9,7},{10,... | collective-permute-start | bytes 1572872 | tf_op jit(solution)/shard_map/ppermute | solution.py:15
  19.4 40.7 %collective-permute-start.3 = (bf16[256,1024]{1,0:T(8,128)(2,1)}, bf16[256,1024]{1,0:T(8,128)(2,1)}, u32[]{:S(2)}, u32[]{:S(2)}) collective-permute-start(bf16[256,1024]{1,0:T(8,128)(2,1)} %pad_maximum_fusion.1), channel_id=1, source_target_pairs={{0,63},{1,0},{2,1},{3,2},{4,3},{5,4},{6,5},{7,6},{8,7},{9,8},{10,9... | collective-permute-start | bytes 1572872 | tf_op jit(solution)/shard_map/ppermute | solution.py:15
  25.6 38.5 %collective-permute-start.2 = (bf16[256,1024]{1,0:T(8,128)(2,1)}, bf16[256,1024]{1,0:T(8,128)(2,1)}, u32[]{:S(2)}, u32[]{:S(2)}) collective-permute-start(bf16[256,1024]{1,0:T(8,128)(2,1)} %pad_maximum_fusion), channel_id=1, source_target_pairs={{0,3},{1,4},{2,5},{3,6},{4,7},{5,8},{6,9},{7,10},{8,11},{9,12},{10... | collective-permute-start | bytes 1572872 | tf_op jit(solution)/shard_map/ppermute | solution.py:15
  27.7 40.1 %collective-permute-start.1 = (bf16[256,1024]{1,0:T(8,128)(2,1)}, bf16[256,1024]{1,0:T(8,128)(2,1)}, u32[]{:S(2)}, u32[]{:S(2)}) collective-permute-start(bf16[256,1024]{1,0:T(8,128)(2,1)} %pad_maximum_fusion), channel_id=1, source_target_pairs={{0,2},{1,3},{2,4},{3,5},{4,6},{5,7},{6,8},{7,9},{8,10},{9,11},{10,... | collective-permute-start | bytes 1572872 | tf_op jit(solution)/shard_map/ppermute | solution.py:15
  39.8 31.7 %collective-permute-start = (bf16[256,1024]{1,0:T(8,128)(2,1)}, bf16[256,1024]{1,0:T(8,128)(2,1)}, u32[]{:S(2)}, u32[]{:S(2)}) collective-permute-start(bf16[256,1024]{1,0:T(8,128)(2,1)} %pad_maximum_fusion), channel_id=1, source_target_pairs={{0,1},{1,2},{2,3},{3,4},{4,5},{5,6},{6,7},{7,8},{8,9},{9,10},{10,1... | collective-permute-start | bytes 1572872 | tf_op jit(solution)/shard_map/ppermute | solution.py:15
  43.5 61.0 %collective-permute-start.6 = (bf16[256,1024]{0,1:T(8,128)(2,1)S(1)}, bf16[256,1024]{0,1:T(8,128)(2,1)}, u32[]{:S(2)}, u32[]{:S(2)}) collective-permute-start(bf16[256,1024]{0,1:T(8,128)(2,1)S(1)} %bitcast.242), channel_id=1, source_target_pairs={{0,1},{1,0},{2,3},{3,2},{4,5},{5,4},{6,7},{7,6},{8,9},{9,8},{10,11... | collective-permute-start | bytes 1572872 | tf_op jit(solution)/shard_map/ppermute | solution.py:20
  102.5 3.9 %collective-permute-start.7 = (bf16[256,1024]{1,0:T(8,128)(2,1)S(1)}, bf16[256,1024]{1,0:T(8,128)(2,1)}, u32[]{:S(2)}, u32[]{:S(2)}) collective-permute-start(bf16[256,1024]{1,0:T(8,128)(2,1)S(1)} %pad_maximum_fusion.2), channel_id=1, source_target_pairs={{0,1},{1,0},{2,3},{3,2},{4,5},{5,4},{6,7},{7,6},{8,9},{9,8},{10,11... | collective-permute-start | bytes 1572872 | tf_op jit(solution)/shard_map/ppermute | solution.py:20
  109.6 17.9 %collective-permute-start.8 = (bf16[16,16,1024]{2,1,0:T(8,128)(2,1)S(1)}, bf16[16,16,1024]{2,1,0:T(8,128)(2,1)}, u32[]{:S(2)}, u32[]{:S(2)}) collective-permute-start(bf16[16,16,1024]{2,1,0:T(8,128)(2,1)S(1)} %fusion.76), channel_id=1, source_target_pairs={{0,2},{1,3},{2,0},{3,1},{4,6},{5,7},{6,4},{7,5},{8,10},{9,11},{10,... | collective-permute-start | bytes 1572872 | tf_op jit(solution)/shard_map/ppermute | solution.py:20
  129.8 10.1 %collective-permute-start.9 = (bf16[8,16,1024]{2,1,0:T(8,128)(2,1)}, bf16[8,16,1024]{2,1,0:T(8,128)(2,1)S(1)}, u32[]{:S(2)}, u32[]{:S(2)}) collective-permute-start(bf16[8,16,1024]{2,1,0:T(8,128)(2,1)} %fusion.102), channel_id=1, source_target_pairs={{0,4},{1,5},{2,6},{3,7},{4,0},{5,1},{6,2},{7,3},{8,12},{9,13},{10,... | collective-permute-start | bytes 786440 | tf_op jit(solution)/shard_map/ppermute | solution.py:20
  140.0 10.1 %collective-permute-start.10 = (bf16[4,16,1024]{2,1,0:T(8,128)(2,1)S(1)}, bf16[4,16,1024]{2,1,0:T(8,128)(2,1)S(1)}, u32[]{:S(2)}, u32[]{:S(2)}) collective-permute-start(bf16[4,16,1024]{2,1,0:T(8,128)(2,1)S(1)} %fusion.155), channel_id=1, source_target_pairs={{0,8},{1,9},{2,10},{3,11},{4,12},{5,13},{6,14},{7,15},{8,0},{9,1},... | collective-permute-start | bytes 393224 | tf_op jit(solution)/shard_map/ppermute | solution.py:20
  150.1 23.0 %copy-start.10 = (f32[4,256,256]{2,1,0:T(8,128)S(1)}, f32[4,256,256]{2,1,0:T(8,128)}, u32[]{:S(2)}) copy-start(f32[4,256,256]{2,1,0:T(8,128)} %convolution_multiply_fusion.6) | copy-start | bytes 3145732
  150.1 23.0 %copy-start.22 = (f32[256,4,128]{0,2,1:T(8,128)S(1)}, f32[256,4,128]{0,2,1:T(8,128)}, u32[]{:S(2)}) copy-start(f32[256,4,128]{0,2,1:T(8,128)} %convolution_bitcast_fusion.3) | copy-start | bytes 1572868
  150.2 23.0 %copy-start.26 = (f32[256,256]{1,0:T(8,128)S(1)}, f32[256,256]{1,0:T(8,128)}, u32[]{:S(2)}) copy-start(f32[256,256]{1,0:T(8,128)} %get-tuple-element.45) | copy-start | bytes 786436
  150.2 23.0 %copy-start.32 = (bf16[32,4,8,128]{3,2,1,0:T(8,128)(2,1)S(1)}, bf16[32,4,8,128]{3,2,1,0:T(8,128)(2,1)}, u32[]{:S(2)}) copy-start(bf16[32,4,8,128]{3,2,1,0:T(8,128)(2,1)} %get-tuple-element.31) | copy-start | bytes 786436
  150.2 12.0 %collective-permute-start.11 = (bf16[2,16,1024]{2,1,0:T(8,128)(2,1)S(1)}, bf16[2,16,1024]{2,1,0:T(8,128)(2,1)S(1)}, u32[]{:S(2)}, u32[]{:S(2)}) collective-permute-start(bf16[2,16,1024]{2,1,0:T(8,128)(2,1)S(1)} %fusion.156), channel_id=1, source_target_pairs={{0,16},{1,17},{2,18},{3,19},{4,20},{5,21},{6,22},{7,23},{8,24},{9,... | collective-permute-start | bytes 196616 | tf_op jit(solution)/shard_map/ppermute | solution.py:20
  162.2 14.7 %collective-permute-start.12 = (bf16[1,16,1024]{2,1,0:T(8,128)(2,1)S(1)}, bf16[1,16,1024]{2,1,0:T(8,128)(2,1)S(1)}, u32[]{:S(2)}, u32[]{:S(2)}) collective-permute-start(bf16[1,16,1024]{2,1,0:T(8,128)(2,1)S(1)} %dynamic-slice_convert_fusion.3), channel_id=1, source_target_pairs={{0,32},{1,33},{2,34},{3,35},{4,36},{5,37},{6,38},{7,39},{8,40},{9,... | collective-permute-start | bytes 98312 | tf_op jit(solution)/shard_map/ppermute | solution.py:20
  176.9 6.3 %collective-permute-start.13 = (f32[16,1024]{1,0:T(8,128)S(1)}, f32[16,1024]{1,0:T(8,128)S(1)}, u32[]{:S(2)}, u32[]{:S(2)}) collective-permute-start(f32[16,1024]{1,0:T(8,128)S(1)} %add_bitcast_fusion), channel_id=1, source_target_pairs={{0,64},{64,0},{128,192},{192,128},{256,320},{320,256},{384,448},{4... | collective-permute-start | bytes 196616 | tf_op jit(solution)/shard_map/ppermute | solution.py:20
  183.3 6.3 %collective-permute-start.14 = (f32[16,1024]{1,0:T(8,128)S(1)}, f32[16,1024]{1,0:T(8,128)S(1)}, u32[]{:S(2)}, u32[]{:S(2)}) collective-permute-start(f32[16,1024]{1,0:T(8,128)S(1)} %add.492), channel_id=1, source_target_pairs={{0,128},{64,192},{128,0},{192,64},{256,384},{320,448},{384,256},{4... | collective-permute-start | bytes 196616 | tf_op jit(solution)/shard_map/ppermute | solution.py:20
  189.6 7.7 %collective-permute-start.15 = (f32[16,1024]{1,0:T(8,128)S(1)}, f32[16,1024]{1,0:T(8,128)S(1)}, u32[]{:S(2)}, u32[]{:S(2)}) collective-permute-start(f32[16,1024]{1,0:T(8,128)S(1)} %add.493), channel_id=1, source_target_pairs={{0,256},{64,320},{128,384},{192,448},{256,0},{320,64},{384,128},{4... | collective-permute-start | bytes 196616 | tf_op jit(solution)/shard_map/ppermute | solution.py:20
  (29 other events, 281.0 us)

commit v4 on v3

--- a/solution.py
+++ b/solution.py
@@ -1,7 +1,10 @@
 import jax
 import jax.numpy as jnp
 from jax import lax
+from jax.experimental import pallas as pl
+from jax.experimental.pallas import tpu as pltpu
 from jax.sharding import PartitionSpec as P
+import functools
 
 HD = 128
 SPAN = 3
@@ -52,6 +55,84 @@
     return acc
 
 
+def tiles_kernel(span, alpha, scale, infoc, infor, *refs):
+    count = 2 * span + 2
+    qs = refs[0:count:2]
+    gs = refs[1:count:2]
+    ks = refs[count:2 * count:2]
+    vs = refs[count + 1:2 * count:2]
+    out_ref, dq_ref, dk_ref, dv_ref = refs[2 * count:]
+    lanes = 2 * span + 1
+
+    def valid(qa, ka):
+        qpos = infoc[:, qa:qa + 1]
+        quser = infoc[:, lanes + qa:lanes + qa + 1]
+        kpos = infor[ka:ka + 1, :]
+        kuser = infor[lanes + ka:lanes + ka + 1, :]
+        kkept = infor[2 * lanes + ka:2 * lanes + ka + 1, :]
+        return (quser == kuser) & (kpos <= qpos) & (kkept > 0)
+
+    def terms(q, g, k, v, ok):
+        z = lax.dot_general(q, k, (((1,), (1,)), ((), ())), preferred_element_type=jnp.float32) * alpha
+        sig = 1.0 / (1.0 + jnp.exp(-z))
+        weight = jnp.where(ok, scale, 0.0)
+        att = (z * sig * weight).astype(jnp.bfloat16)
+        dprod = lax.dot_general(g, v, (((1,), (1,)), ((), ())), preferred_element_type=jnp.float32)
+        dsc = (dprod * sig * (1.0 + z * (1.0 - sig)) * weight * alpha).astype(jnp.bfloat16)
+        return att, dsc
+
+    def back(att, dsc, q, g):
+        dk = lax.dot_general(dsc, q, (((0,), (0,)), ((), ())), preferred_element_type=jnp.float32)
+        dv = lax.dot_general(att, g, (((0,), (0,)), ((), ())), preferred_element_type=jnp.float32)
+        return dk, dv
+
+    q0, g0, k0, v0 = qs[0][...], gs[0][...], ks[0][...], vs[0][...]
+    att, dsc = terms(q0, g0, k0, v0, valid(span, span))
+    out = jnp.dot(att, v0, preferred_element_type=jnp.float32)
+    dq = jnp.dot(dsc, k0, preferred_element_type=jnp.float32)
+    dk, dv = back(att, dsc, q0, g0)
+    for step in range(1, span + 1):
+        k, v = ks[step][...], vs[step][...]
+        att, dsc = terms(q0, g0, k, v, valid(span, span - step))
+        out = out + jnp.dot(att, v, preferred_element_type=jnp.float32)
+        dq = dq + jnp.dot(dsc, k, preferred_element_type=jnp.float32)
+        q, g = qs[step][...], gs[step][...]
+        att, dsc = terms(q, g, k0, v0, valid(span + step, span))
+        b, c = back(att, dsc, q, g)
+        dk = dk + b
+        dv = dv + c
+    out_ref[...] = out.astype(out_ref.dtype)
+    dq_ref[...] = dq.astype(dq_ref.dtype)
+    dk_ref[...] = dk.astype(dk_ref.dtype)
+    dv_ref[...] = dv.astype(dv_ref.dtype)
+
+
+def attention_tiles(qg_list, kv_list, infoc, infor, nheads, alpha, scale):
+    rows = qg_list[0].shape[0]
+    span = len(qg_list) - 1
+    blk = lambda offset: pl.BlockSpec((rows, HD), lambda h: (0, h + offset))
+    full = lambda arr: pl.BlockSpec(arr.shape, lambda h: (0, 0))
+    operands, specs = [infoc, infor], [full(infoc), full(infor)]
+    for group in (qg_list, kv_list):
+        for packed in group:
+            operands += [packed, packed]
+            specs += [blk(0), blk(nheads)]
+    shape = jax.ShapeDtypeStruct((rows, nheads * HD), jnp.bfloat16)
+    tile = rows * rows * HD * 2
+    return pl.pallas_call(
+        functools.partial(tiles_kernel, span, alpha, scale),
+        grid=(nheads,),
+        in_specs=specs,
+        out_specs=[blk(0)] * 4,
+        out_shape=[shape] * 4,
+        cost_estimate=pl.CostEstimate(
+            flops=nheads * (2 * span + 1) * 5 * tile,
+            transcendentals=nheads * (2 * span + 1) * rows * rows,
+            bytes_accessed=(2 * span + 2) * 2 * rows * nheads * HD * 2 * 2 + 4 * rows * nheads * HD * 2,
+        ),
+    )(*operands)
+
+
 def scores(query, key, valid, scale, alpha):
     z = jnp.einsum("qhd,khd->hqk", query, key, preferred_element_type=jnp.float32) * alpha
     sig = jax.nn.sigmoid(z)
@@ -126,31 +207,17 @@
     kv_from = [None] + [shifted(kv, "ctx", step) for step in range(1, SPAN + 1)]
     qg_from = [None] + [shifted(qg, "ctx", -step) for step in range(1, SPAN + 1)]
 
-    q_me, g_me = split(qg)
-    k_me, v_me = split(kv)
-    info_me = describe(myself)
-    out_acc, dq_acc, att0, dsc0 = forward_terms(
-        q_me, g_me, k_me, v_me, mask(info_me, info_me), scale, alpha
-    )
-    dk_acc = jnp.einsum("hqk,qhd->khd", dsc0, q_me, preferred_element_type=jnp.float32)
-    dv_acc = jnp.einsum("hqk,qhd->khd", att0, g_me, preferred_element_type=jnp.float32)
-    for step in range(1, SPAN + 1):
-        k_s, v_s = split(kv_from[step])
-        o, a, _, _ = forward_terms(
-            q_me, g_me, k_s, v_s, mask(info_me, describe(myself - step)), scale, alpha
-        )
-        out_acc = out_acc + o
-        dq_acc = dq_acc + a
-        q_s, g_s = split(qg_from[step])
-        b, c = backward_terms(
-            q_s, g_s, k_me, v_me, mask(describe(myself + step), info_me), scale, alpha
-        )
-        dk_acc = dk_acc + b
-        dv_acc = dv_acc + c
-    attended = out_acc.reshape(1, rows, features).astype(jnp.bfloat16)
-    grad_values = dv_acc.reshape(1, rows, features).astype(jnp.bfloat16)
-    dq_b = dq_acc.reshape(rows, features).astype(jnp.bfloat16)
-    dk_b = dk_acc.reshape(rows, features).astype(jnp.bfloat16)
+    offsets = range(-SPAN, SPAN + 1)
+    described = [describe(myself + offset) for offset in offsets]
+    infor = jnp.stack(
+        [d[0] for d in described] + [d[1] for d in described] + [d[2].astype(jnp.int32) for d in described]
+    ).astype(jnp.int32)
+    infoc = infor.T
+    out_b, dq_b, dk_b, dv_b = attention_tiles(
+        [qg] + qg_from[1:], [kv] + kv_from[1:], infoc, infor, nheads, alpha, scale
+    )
+    attended = out_b.reshape(1, rows, features)
+    grad_values = dv_b.reshape(1, rows, features)
     joined = jnp.concatenate([dq_b, dk_b], axis=1)
     mine = reduce_rows(local, partner_events, joined, myself, cycle_size)
     grad_wq = mine[:, :features].astype(jnp.bfloat16)

time: 200 us -> 172 us (0.86)
  matrix products: 38 us -> 3.81 us
  local copies, waits for them, and re-layouts: 25.4 us -> 7.66 us
  Pallas kernels: 0 us -> 12.8 us
  starting transfers between devices: 68.3 us -> 75.9 us
  waiting for transfers between devices: 55.9 us -> 62.2 us
  other arithmetic: 7.82 us -> 5.58 us
    dot_general x24 -> x0, matrix products: 34.4 us -> none  [the longest x7 10.5 us: scores(): jnp.einsum('qhd,khd->hqk', query, key, preferred_element_type=jnp.float32)]
    pallas_call x0 -> x1, Pallas kernels: none -> 12.8 us  [attention_tiles(): pl.pallas_call(functools.partial(tiles_kernel, span, alpha, scale), grid=...]
    unnamed x83 -> x26, local copies, waits for them, and re-layouts: 15.6 us -> 4.19 us
    reshape x8 -> x0, local copies, waits for them, and re-layouts: 7.83 us -> none  [split(): packed[:, :features].reshape(rows, nheads, HD)]
    ppermute x10, starting transfers between devices: 40.5 us -> 47.9 us  [exchange(): lax.ppermute(value, axis, [(source, source ^ mask) for source in range(co...]
    ppermute x6, waiting for transfers between devices: 12.8 us -> 19.7 us  [shifted(): return lax.ppermute(value, axis, pairs)]
  transfers between devices with their start and end apart: 16 -> 16, of which waited for: 10 -> 11; matrix products, arithmetic and copies ran while one was open for 30% -> 3% of each run, Pallas kernels for 0% -> 8%
where the time goes in v4:
time: 172 us; the launch traced here: 170 us
  starting transfers between devices  75.9 us (44%)
  waiting for transfers between devices  62.2 us (36%)
  Pallas kernels  12.8 us (7%)
  local copies, waits for them, and re-layouts  7.66 us (4%)
  other arithmetic  5.58 us (3%)
  matrix products  3.81 us (2%)
  between operations  2.17 us (1%)
    ppermute x10, starting transfers between devices, exchange(): lax.ppermute(value, axis, [(source, source ^ mask) for source in range(co...  47.9 us
    ppermute x10, waiting for transfers between devices, exchange(): lax.ppermute(value, axis, [(source, source ^ mask) for source in range(co...  42.4 us
    ppermute x6, starting transfers between devices, shifted(): return lax.ppermute(value, axis, pairs)  28 us
    ppermute x6, waiting for transfers between devices, shifted(): return lax.ppermute(value, axis, pairs)  19.7 us
    pallas_call x1, Pallas kernels, attention_tiles(): pl.pallas_call(functools.partial(tiles_kernel, span, alpha, scale), grid=...  12.8 us
    unnamed x26, local copies, waits for them, and re-layouts  4.19 us
  transfers between devices with their start and end apart: 16, of which 11 were waited for; matrix products, arithmetic and copies ran while one was open for 3% of the time, Pallas kernels for 8%

profile of v4, /device:TPU:6, one launch (start us, length us, event | category | flops | bytes accessed | tf_op | source)
XLA Modules:
  0.0 170.1 jit_solution(17493103570859340278)
XLA Ops:
  4.4 2.9 %collective-permute-start = (bf16[256,1024]{1,0:T(8,128)(2,1)S(1)}, bf16[256,1024]{1,0:T(8,128)(2,1)}, u32[]{:S(2)}, u32[]{:S(2)}) collective-permute-start(bf16[256,1024]{1,0:T(8,128)(2,1)S(1)} %pad_maximum_fusion.refs_0_.refs_1_), channel_id=1, source_target_pairs={{0,63},{1,0},{2,1},{3,2},{4,3},{5,4},{6,5},{7,6},{8,7},{9,8},{10,9... | collective-permute-start | bytes 1572872 | tf_op jit(solution)/shard_map/ppermute | solution.py:18
  7.3 13.0 %collective-permute-start.1 = (bf16[256,1024]{1,0:T(8,128)(2,1)S(1)}, bf16[256,1024]{1,0:T(8,128)(2,1)}, u32[]{:S(2)}, u32[]{:S(2)}) collective-permute-start(bf16[256,1024]{1,0:T(8,128)(2,1)S(1)} %pad_maximum_fusion.refs_0_.refs_1_), channel_id=1, source_target_pairs={{0,62},{1,63},{2,0},{3,1},{4,2},{5,3},{6,4},{7,5},{8,6},{9,7},{10,... | collective-permute-start | bytes 1572872 | tf_op jit(solution)/shard_map/ppermute | solution.py:18
  20.3 1.9 %collective-permute-start.2 = (bf16[256,1024]{1,0:T(8,128)(2,1)S(1)}, bf16[256,1024]{1,0:T(8,128)(2,1)}, u32[]{:S(2)}, u32[]{:S(2)}) collective-permute-start(bf16[256,1024]{1,0:T(8,128)(2,1)S(1)} %pad_maximum_fusion.refs_0_.refs_1_), channel_id=1, source_target_pairs={{0,61},{1,62},{2,63},{3,0},{4,1},{5,2},{6,3},{7,4},{8,5},{9,6},{10... | collective-permute-start | bytes 1572872 | tf_op jit(solution)/shard_map/ppermute | solution.py:18
  22.7 3.4 %collective-permute-start.3 = (bf16[256,1024]{1,0:T(8,128)(2,1)S(1)}, bf16[256,1024]{1,0:T(8,128)(2,1)}, u32[]{:S(2)}, u32[]{:S(2)}) collective-permute-start(bf16[256,1024]{1,0:T(8,128)(2,1)S(1)} %pad_maximum_fusion.1.refs_8_.refs_9_), channel_id=1, source_target_pairs={{0,1},{1,2},{2,3},{3,4},{4,5},{5,6},{6,7},{7,8},{8,9},{9,10},{10,1... | collective-permute-start | bytes 1572872 | tf_op jit(solution)/shard_map/ppermute | solution.py:18
  26.2 4.9 %collective-permute-start.4 = (bf16[256,1024]{1,0:T(8,128)(2,1)S(1)}, bf16[256,1024]{1,0:T(8,128)(2,1)}, u32[]{:S(2)}, u32[]{:S(2)}) collective-permute-start(bf16[256,1024]{1,0:T(8,128)(2,1)S(1)} %pad_maximum_fusion.1.refs_8_.refs_9_), channel_id=1, source_target_pairs={{0,2},{1,3},{2,4},{3,5},{4,6},{5,7},{6,8},{7,9},{8,10},{9,11},{10,... | collective-permute-start | bytes 1572872 | tf_op jit(solution)/shard_map/ppermute | solution.py:18
  36.2 11.3 %collective-permute-done.1.refs_4_.refs_5_ = bf16[256,1024]{1,0:T(8,128)(2,1)} collective-permute-done((bf16[256,1024]{1,0:T(8,128)(2,1)S(1)}, bf16[256,1024]{1,0:T(8,128)(2,1)}, u32[]{:S(2)}, u32[]{:S(2)}) %collective-permute-start.1) | collective-permute-done | bytes 524320 | tf_op jit(solution)/shard_map/ppermute | solution.py:18
  49.5 8.4 %collective-permute-done.5.refs_14_.refs_15_ = bf16[256,1024]{1,0:T(8,128)(2,1)} collective-permute-done((bf16[256,1024]{1,0:T(8,128)(2,1)S(1)}, bf16[256,1024]{1,0:T(8,128)(2,1)}, u32[]{:S(2)}, u32[]{:S(2)}) %collective-permute-start.5) | collective-permute-done | bytes 524320 | tf_op jit(solution)/shard_map/ppermute | solution.py:18
  57.9 12.8 %shard_map.111 = (bf16[256,512]{1,0:T(8,128)(2,1)}, bf16[256,512]{1,0:T(8,128)(2,1)}, bf16[256,512]{1,0:T(8,128)(2,1)}, bf16[256,512]{1,0:T(8,128)(2,1)}) custom-call(s32[256,21]{1,0:T(8,128)} %copy.26.infoc, s32[21,256]{1,0:T(8,128)} %copy-done.9, bf16[256,1024]{1,0:T(8,128)(2,1)} %copy-done.6, bf16[256,1024]{1,0:T(8,128)(2,1)} %copy-done.6, ...), custom_call_target="tpu_custom_call" | custom-call | flops 2348810240 | bytes 9437184 | tf_op jit(solution)/shard_map/pallas_call | solution.py:122
  80.1 3.9 %collective-permute-start.8 = (bf16[16,16,1024]{2,1,0:T(8,128)(2,1)}, bf16[16,16,1024]{2,1,0:T(8,128)(2,1)}, u32[]{:S(2)}, u32[]{:S(2)}) collective-permute-start(bf16[16,16,1024]{2,1,0:T(8,128)(2,1)} %fusion.3), channel_id=1, source_target_pairs={{0,2},{1,3},{2,0},{3,1},{4,6},{5,7},{6,4},{7,5},{8,10},{9,11},{10,... | collective-permute-start | bytes 1572872 | tf_op jit(solution)/shard_map/ppermute | solution.py:23
  84.0 13.8 %collective-permute-done.8 = bf16[16,16,1024]{2,1,0:T(8,128)(2,1)} collective-permute-done((bf16[16,16,1024]{2,1,0:T(8,128)(2,1)}, bf16[16,16,1024]{2,1,0:T(8,128)(2,1)}, u32[]{:S(2)}, u32[]{:S(2)}) %collective-permute-start.8) | collective-permute-done | bytes 524320 | tf_op jit(solution)/shard_map/ppermute | solution.py:23
  100.0 2.4 %collective-permute-start.9 = (bf16[8,16,1024]{2,1,0:T(8,128)(2,1)S(1)}, bf16[8,16,1024]{2,1,0:T(8,128)(2,1)S(1)}, u32[]{:S(2)}, u32[]{:S(2)}) collective-permute-start(bf16[8,16,1024]{2,1,0:T(8,128)(2,1)S(1)} %fusion.7), channel_id=1, source_target_pairs={{0,4},{1,5},{2,6},{3,7},{4,0},{5,1},{6,2},{7,3},{8,12},{9,13},{10,... | collective-permute-start | bytes 786440 | tf_op jit(solution)/shard_map/ppermute | solution.py:23
  102.5 6.9 %collective-permute-done.9 = bf16[8,16,1024]{2,1,0:T(8,128)(2,1)S(1)} collective-permute-done((bf16[8,16,1024]{2,1,0:T(8,128)(2,1)S(1)}, bf16[8,16,1024]{2,1,0:T(8,128)(2,1)S(1)}, u32[]{:S(2)}, u32[]{:S(2)}) %collective-permute-start.9) | collective-permute-done | bytes 262176 | tf_op jit(solution)/shard_map/ppermute | solution.py:23
  110.6 5.5 %collective-permute-start.10 = (bf16[4,16,1024]{2,1,0:T(8,128)(2,1)S(1)}, bf16[4,16,1024]{2,1,0:T(8,128)(2,1)S(1)}, u32[]{:S(2)}, u32[]{:S(2)}) collective-permute-start(bf16[4,16,1024]{2,1,0:T(8,128)(2,1)S(1)} %fusion.8), channel_id=1, source_target_pairs={{0,8},{1,9},{2,10},{3,11},{4,12},{5,13},{6,14},{7,15},{8,0},{9,1},... | collective-permute-start | bytes 393224 | tf_op jit(solution)/shard_map/ppermute | solution.py:23
  116.1 5.4 %collective-permute-done.10 = bf16[4,16,1024]{2,1,0:T(8,128)(2,1)S(1)} collective-permute-done((bf16[4,16,1024]{2,1,0:T(8,128)(2,1)S(1)}, bf16[4,16,1024]{2,1,0:T(8,128)(2,1)S(1)}, u32[]{:S(2)}, u32[]{:S(2)}) %collective-permute-start.10) | collective-permute-done | bytes 131104 | tf_op jit(solution)/shard_map/ppermute | solution.py:23
  121.5 9.1 %collective-permute-start.11 = (bf16[2,16,1024]{2,1,0:T(8,128)(2,1)S(1)}, bf16[2,16,1024]{2,1,0:T(8,128)(2,1)S(1)}, u32[]{:S(2)}, u32[]{:S(2)}) collective-permute-start(bf16[2,16,1024]{2,1,0:T(8,128)(2,1)S(1)} %fusion.9), channel_id=1, source_target_pairs={{0,16},{1,17},{2,18},{3,19},{4,20},{5,21},{6,22},{7,23},{8,24},{9,... | collective-permute-start | bytes 196616 | tf_op jit(solution)/shard_map/ppermute | solution.py:23
  130.7 4.3 %collective-permute-done.11 = bf16[2,16,1024]{2,1,0:T(8,128)(2,1)S(1)} collective-permute-done((bf16[2,16,1024]{2,1,0:T(8,128)(2,1)S(1)}, bf16[2,16,1024]{2,1,0:T(8,128)(2,1)S(1)}, u32[]{:S(2)}, u32[]{:S(2)}) %collective-permute-start.11) | collective-permute-done | bytes 65568 | tf_op jit(solution)/shard_map/ppermute | solution.py:23
  135.0 11.7 %collective-permute-start.12 = (bf16[1,16,1024]{2,1,0:T(8,128)(2,1)S(1)}, bf16[1,16,1024]{2,1,0:T(8,128)(2,1)S(1)}, u32[]{:S(2)}, u32[]{:S(2)}) collective-permute-start(bf16[1,16,1024]{2,1,0:T(8,128)(2,1)S(1)} %dynamic-slice_convert_fusion.3), channel_id=1, source_target_pairs={{0,32},{1,33},{2,34},{3,35},{4,36},{5,37},{6,38},{7,39},{8,40},{9,... | collective-permute-start | bytes 98312 | tf_op jit(solution)/shard_map/ppermute | solution.py:23
  146.7 2.8 %collective-permute-done.12 = bf16[1,16,1024]{2,1,0:T(8,128)(2,1)S(1)} collective-permute-done((bf16[1,16,1024]{2,1,0:T(8,128)(2,1)S(1)}, bf16[1,16,1024]{2,1,0:T(8,128)(2,1)S(1)}, u32[]{:S(2)}, u32[]{:S(2)}) %collective-permute-start.12) | collective-permute-done | bytes 32800 | tf_op jit(solution)/shard_map/ppermute | solution.py:23
  149.5 2.7 %collective-permute-start.13 = (f32[16,1024]{1,0:T(8,128)S(1)}, f32[16,1024]{1,0:T(8,128)S(1)}, u32[]{:S(2)}, u32[]{:S(2)}) collective-permute-start(f32[16,1024]{1,0:T(8,128)S(1)} %add_bitcast_fusion), channel_id=1, source_target_pairs={{0,64},{64,0},{128,192},{192,128},{256,320},{320,256},{384,448},{4... | collective-permute-start | bytes 196616 | tf_op jit(solution)/shard_map/ppermute | solution.py:23
  152.2 3.4 %collective-permute-done.13 = f32[16,1024]{1,0:T(8,128)S(1)} collective-permute-done((f32[16,1024]{1,0:T(8,128)S(1)}, f32[16,1024]{1,0:T(8,128)S(1)}, u32[]{:S(2)}, u32[]{:S(2)}) %collective-permute-start.13) | collective-permute-done | bytes 65568 | tf_op jit(solution)/shard_map/ppermute | solution.py:23
  155.7 3.5 %collective-permute-start.14 = (f32[16,1024]{1,0:T(8,128)S(1)}, f32[16,1024]{1,0:T(8,128)S(1)}, u32[]{:S(2)}, u32[]{:S(2)}) collective-permute-start(f32[16,1024]{1,0:T(8,128)S(1)} %add.553), channel_id=1, source_target_pairs={{0,128},{64,192},{128,0},{192,64},{256,384},{320,448},{384,256},{4... | collective-permute-start | bytes 196616 | tf_op jit(solution)/shard_map/ppermute | solution.py:23
  159.2 2.7 %collective-permute-done.14 = f32[16,1024]{1,0:T(8,128)S(1)} collective-permute-done((f32[16,1024]{1,0:T(8,128)S(1)}, f32[16,1024]{1,0:T(8,128)S(1)}, u32[]{:S(2)}, u32[]{:S(2)}) %collective-permute-start.14) | collective-permute-done | bytes 65568 | tf_op jit(solution)/shard_map/ppermute | solution.py:23
  161.8 5.3 %collective-permute-start.15 = (f32[16,1024]{1,0:T(8,128)S(1)}, f32[16,1024]{1,0:T(8,128)S(1)}, u32[]{:S(2)}, u32[]{:S(2)}) collective-permute-start(f32[16,1024]{1,0:T(8,128)S(1)} %add.554), channel_id=1, source_target_pairs={{0,256},{64,320},{128,384},{192,448},{256,0},{320,64},{384,128},{4... | collective-permute-start | bytes 196616 | tf_op jit(solution)/shard_map/ppermute | solution.py:23
  167.1 2.4 %collective-permute-done.15 = f32[16,1024]{1,0:T(8,128)S(1)} collective-permute-done((f32[16,1024]{1,0:T(8,128)S(1)}, f32[16,1024]{1,0:T(8,128)S(1)}, u32[]{:S(2)}, u32[]{:S(2)}) %collective-permute-start.15) | collective-permute-done | bytes 65568 | tf_op jit(solution)/shard_map/ppermute | solution.py:23
  (82 shorter events, 23.6 us)
Async XLA Ops:
  0.6 21.5 %copy-start.1 = (bf16[1,256,1024]{2,1,0:T(8,128)(2,1)S(1)}, bf16[1,256,1024]{2,1,0:T(8,128)(2,1)}, u32[]{:S(2)}) copy-start(bf16[1,256,1024]{2,1,0:T(8,128)(2,1)} %param.8) | copy-start | bytes 1572868
  0.7 21.5 %copy-start.4 = (bf16[1024,512]{1,0:T(8,128)(2,1)S(1)}, bf16[1024,512]{1,0:T(8,128)(2,1)}, u32[]{:S(2)}) copy-start(bf16[1024,512]{1,0:T(8,128)(2,1)} %param.10) | copy-start | bytes 3145732
  0.7 22.0 %copy-start.8 = (bf16[1,256,512]{2,1,0:T(8,128)(2,1)S(1)}, bf16[1,256,512]{2,1,0:T(8,128)(2,1)}, u32[]{:S(2)}) copy-start(bf16[1,256,512]{2,1,0:T(8,128)(2,1)} %param.11) | copy-start | bytes 786436
  4.4 28.1 %copy-start.6 = (bf16[256,1024]{1,0:T(8,128)(2,1)}, bf16[256,1024]{1,0:T(8,128)(2,1)S(1)}, u32[]{:S(2)}) copy-start(bf16[256,1024]{1,0:T(8,128)(2,1)S(1)} %pad_maximum_fusion.refs_0_.refs_1_) | copy-start | bytes 1572868
  4.4 28.0 %copy-start.10 = (s32[1,32]{1,0:T(1,128)S(1)}, s32[1,32]{1,0:T(1,128)}, u32[]{:S(2)}) copy-start(s32[1,32]{1,0:T(1,128)} %param.13) | copy-start | bytes 388
  4.4 28.3 %copy-start.11 = (s32[1,128]{1,0:T(1,128)S(1)}, s32[1,128]{1,0:T(1,128)}, u32[]{:S(2)}) copy-start(s32[1,128]{1,0:T(1,128)} %param.15) | copy-start | bytes 1540
  4.4 29.0 %collective-permute-start = (bf16[256,1024]{1,0:T(8,128)(2,1)S(1)}, bf16[256,1024]{1,0:T(8,128)(2,1)}, u32[]{:S(2)}, u32[]{:S(2)}) collective-permute-start(bf16[256,1024]{1,0:T(8,128)(2,1)S(1)} %pad_maximum_fusion.refs_0_.refs_1_), channel_id=1, source_target_pairs={{0,63},{1,0},{2,1},{3,2},{4,3},{5,4},{6,5},{7,6},{8,7},{9,8},{10,9... | collective-permute-start | bytes 1572872 | tf_op jit(solution)/shard_map/ppermute | solution.py:18
  7.3 40.3 %collective-permute-start.1 = (bf16[256,1024]{1,0:T(8,128)(2,1)S(1)}, bf16[256,1024]{1,0:T(8,128)(2,1)}, u32[]{:S(2)}, u32[]{:S(2)}) collective-permute-start(bf16[256,1024]{1,0:T(8,128)(2,1)S(1)} %pad_maximum_fusion.refs_0_.refs_1_), channel_id=1, source_target_pairs={{0,62},{1,63},{2,0},{3,1},{4,2},{5,3},{6,4},{7,5},{8,6},{9,7},{10,... | collective-permute-start | bytes 1572872 | tf_op jit(solution)/shard_map/ppermute | solution.py:18
  20.3 29.2 %collective-permute-start.2 = (bf16[256,1024]{1,0:T(8,128)(2,1)S(1)}, bf16[256,1024]{1,0:T(8,128)(2,1)}, u32[]{:S(2)}, u32[]{:S(2)}) collective-permute-start(bf16[256,1024]{1,0:T(8,128)(2,1)S(1)} %pad_maximum_fusion.refs_0_.refs_1_), channel_id=1, source_target_pairs={{0,61},{1,62},{2,63},{3,0},{4,1},{5,2},{6,3},{7,4},{8,5},{9,6},{10... | collective-permute-start | bytes 1572872 | tf_op jit(solution)/shard_map/ppermute | solution.py:18
  22.7 35.2 %copy-start.7 = (bf16[256,1024]{1,0:T(8,128)(2,1)}, bf16[256,1024]{1,0:T(8,128)(2,1)S(1)}, u32[]{:S(2)}) copy-start(bf16[256,1024]{1,0:T(8,128)(2,1)S(1)} %pad_maximum_fusion.1.refs_8_.refs_9_) | copy-start | bytes 1572868
  22.7 26.8 %collective-permute-start.3 = (bf16[256,1024]{1,0:T(8,128)(2,1)S(1)}, bf16[256,1024]{1,0:T(8,128)(2,1)}, u32[]{:S(2)}, u32[]{:S(2)}) collective-permute-start(bf16[256,1024]{1,0:T(8,128)(2,1)S(1)} %pad_maximum_fusion.1.refs_8_.refs_9_), channel_id=1, source_target_pairs={{0,1},{1,2},{2,3},{3,4},{4,5},{5,6},{6,7},{7,8},{8,9},{9,10},{10,1... | collective-permute-start | bytes 1572872 | tf_op jit(solution)/shard_map/ppermute | solution.py:18
  26.2 23.4 %collective-permute-start.4 = (bf16[256,1024]{1,0:T(8,128)(2,1)S(1)}, bf16[256,1024]{1,0:T(8,128)(2,1)}, u32[]{:S(2)}, u32[]{:S(2)}) collective-permute-start(bf16[256,1024]{1,0:T(8,128)(2,1)S(1)} %pad_maximum_fusion.1.refs_8_.refs_9_), channel_id=1, source_target_pairs={{0,2},{1,3},{2,4},{3,5},{4,6},{5,7},{6,8},{7,9},{8,10},{9,11},{10,... | collective-permute-start | bytes 1572872 | tf_op jit(solution)/shard_map/ppermute | solution.py:18
  33.4 24.5 %collective-permute-start.5 = (bf16[256,1024]{1,0:T(8,128)(2,1)S(1)}, bf16[256,1024]{1,0:T(8,128)(2,1)}, u32[]{:S(2)}, u32[]{:S(2)}) collective-permute-start(bf16[256,1024]{1,0:T(8,128)(2,1)S(1)} %pad_maximum_fusion.1.refs_8_.refs_9_), channel_id=1, source_target_pairs={{0,3},{1,4},{2,5},{3,6},{4,7},{5,8},{6,9},{7,10},{8,11},{9,12},{10... | collective-permute-start | bytes 1572872 | tf_op jit(solution)/shard_map/ppermute | solution.py:18
  35.5 22.4 %copy-start.9 = (s32[21,256]{1,0:T(8,128)}, s32[21,256]{1,0:T(8,128)S(1)}, u32[]{:S(2)}) copy-start(s32[21,256]{1,0:T(8,128)S(1)} %stack.45.infor) | copy-start | bytes 64516
  47.6 27.1 %collective-permute-start.6 = (bf16[256,1024]{0,1:T(8,128)(2,1)S(1)}, bf16[256,1024]{0,1:T(8,128)(2,1)}, u32[]{:S(2)}, u32[]{:S(2)}) collective-permute-start(bf16[256,1024]{0,1:T(8,128)(2,1)S(1)} %bitcast.87), channel_id=1, source_target_pairs={{0,1},{1,0},{2,3},{3,2},{4,5},{5,4},{6,7},{7,6},{8,9},{9,8},{10,11... | collective-permute-start | bytes 1572872 | tf_op jit(solution)/shard_map/ppermute | solution.py:23
  72.7 3.8 %collective-permute-start.7 = (bf16[256,1024]{1,0:T(8,128)(2,1)S(1)}, bf16[256,1024]{1,0:T(8,128)(2,1)S(1)}, u32[]{:S(2)}, u32[]{:S(2)}) collective-permute-start(bf16[256,1024]{1,0:T(8,128)(2,1)S(1)} %constant_dynamic-update-slice_fusion), channel_id=1, source_target_pairs={{0,1},{1,0},{2,3},{3,2},{4,5},{5,4},{6,7},{7,6},{8,9},{9,8},{10,11... | collective-permute-start | bytes 1572872 | tf_op jit(solution)/shard_map/ppermute | solution.py:23
  80.1 17.7 %collective-permute-start.8 = (bf16[16,16,1024]{2,1,0:T(8,128)(2,1)}, bf16[16,16,1024]{2,1,0:T(8,128)(2,1)}, u32[]{:S(2)}, u32[]{:S(2)}) collective-permute-start(bf16[16,16,1024]{2,1,0:T(8,128)(2,1)} %fusion.3), channel_id=1, source_target_pairs={{0,2},{1,3},{2,0},{3,1},{4,6},{5,7},{6,4},{7,5},{8,10},{9,11},{10,... | collective-permute-start | bytes 1572872 | tf_op jit(solution)/shard_map/ppermute | solution.py:23
  100.0 9.4 %collective-permute-start.9 = (bf16[8,16,1024]{2,1,0:T(8,128)(2,1)S(1)}, bf16[8,16,1024]{2,1,0:T(8,128)(2,1)S(1)}, u32[]{:S(2)}, u32[]{:S(2)}) collective-permute-start(bf16[8,16,1024]{2,1,0:T(8,128)(2,1)S(1)} %fusion.7), channel_id=1, source_target_pairs={{0,4},{1,5},{2,6},{3,7},{4,0},{5,1},{6,2},{7,3},{8,12},{9,13},{10,... | collective-permute-start | bytes 786440 | tf_op jit(solution)/shard_map/ppermute | solution.py:23
  110.6 10.9 %collective-permute-start.10 = (bf16[4,16,1024]{2,1,0:T(8,128)(2,1)S(1)}, bf16[4,16,1024]{2,1,0:T(8,128)(2,1)S(1)}, u32[]{:S(2)}, u32[]{:S(2)}) collective-permute-start(bf16[4,16,1024]{2,1,0:T(8,128)(2,1)S(1)} %fusion.8), channel_id=1, source_target_pairs={{0,8},{1,9},{2,10},{3,11},{4,12},{5,13},{6,14},{7,15},{8,0},{9,1},... | collective-permute-start | bytes 393224 | tf_op jit(solution)/shard_map/ppermute | solution.py:23
  121.5 13.4 %collective-permute-start.11 = (bf16[2,16,1024]{2,1,0:T(8,128)(2,1)S(1)}, bf16[2,16,1024]{2,1,0:T(8,128)(2,1)S(1)}, u32[]{:S(2)}, u32[]{:S(2)}) collective-permute-start(bf16[2,16,1024]{2,1,0:T(8,128)(2,1)S(1)} %fusion.9), channel_id=1, source_target_pairs={{0,16},{1,17},{2,18},{3,19},{4,20},{5,21},{6,22},{7,23},{8,24},{9,... | collective-permute-start | bytes 196616 | tf_op jit(solution)/shard_map/ppermute | solution.py:23
  135.0 14.5 %collective-permute-start.12 = (bf16[1,16,1024]{2,1,0:T(8,128)(2,1)S(1)}, bf16[1,16,1024]{2,1,0:T(8,128)(2,1)S(1)}, u32[]{:S(2)}, u32[]{:S(2)}) collective-permute-start(bf16[1,16,1024]{2,1,0:T(8,128)(2,1)S(1)} %dynamic-slice_convert_fusion.3), channel_id=1, source_target_pairs={{0,32},{1,33},{2,34},{3,35},{4,36},{5,37},{6,38},{7,39},{8,40},{9,... | collective-permute-start | bytes 98312 | tf_op jit(solution)/shard_map/ppermute | solution.py:23
  149.5 6.2 %collective-permute-start.13 = (f32[16,1024]{1,0:T(8,128)S(1)}, f32[16,1024]{1,0:T(8,128)S(1)}, u32[]{:S(2)}, u32[]{:S(2)}) collective-permute-start(f32[16,1024]{1,0:T(8,128)S(1)} %add_bitcast_fusion), channel_id=1, source_target_pairs={{0,64},{64,0},{128,192},{192,128},{256,320},{320,256},{384,448},{4... | collective-permute-start | bytes 196616 | tf_op jit(solution)/shard_map/ppermute | solution.py:23
  155.7 6.2 %collective-permute-start.14 = (f32[16,1024]{1,0:T(8,128)S(1)}, f32[16,1024]{1,0:T(8,128)S(1)}, u32[]{:S(2)}, u32[]{:S(2)}) collective-permute-start(f32[16,1024]{1,0:T(8,128)S(1)} %add.553), channel_id=1, source_target_pairs={{0,128},{64,192},{128,0},{192,64},{256,384},{320,448},{384,256},{4... | collective-permute-start | bytes 196616 | tf_op jit(solution)/shard_map/ppermute | solution.py:23
  161.8 7.7 %collective-permute-start.15 = (f32[16,1024]{1,0:T(8,128)S(1)}, f32[16,1024]{1,0:T(8,128)S(1)}, u32[]{:S(2)}, u32[]{:S(2)}) collective-permute-start(f32[16,1024]{1,0:T(8,128)S(1)} %add.554), channel_id=1, source_target_pairs={{0,256},{64,320},{128,384},{192,448},{256,0},{320,64},{384,128},{4... | collective-permute-start | bytes 196616 | tf_op jit(solution)/shard_map/ppermute | solution.py:23
  (4 other events, 6.8 us)

commit v5 on v4

--- a/solution.py
+++ b/solution.py
@@ -133,31 +133,70 @@
     )(*operands)
 
 
-def scores(query, key, valid, scale, alpha):
-    z = jnp.einsum("qhd,khd->hqk", query, key, preferred_element_type=jnp.float32) * alpha
-    sig = jax.nn.sigmoid(z)
-    weight = valid[None, :, :].astype(jnp.float32) * scale
-    return z, sig, weight
-
-
-def forward_terms(query, grad, key, value, valid, scale, alpha):
-    z, sig, weight = scores(query, key, valid, scale, alpha)
-    att = (z * sig * weight).astype(jnp.bfloat16)
-    out = jnp.einsum("hqk,khd->qhd", att, value, preferred_element_type=jnp.float32)
-    dprod = jnp.einsum("qhd,khd->hqk", grad, value, preferred_element_type=jnp.float32)
-    dsc = (dprod * sig * (1.0 + z * (1.0 - sig)) * weight * alpha).astype(jnp.bfloat16)
-    dquery = jnp.einsum("hqk,khd->qhd", dsc, key, preferred_element_type=jnp.float32)
-    return out, dquery, att, dsc
-
-
-def backward_terms(query, grad, key, value, valid, scale, alpha):
-    z, sig, weight = scores(query, key, valid, scale, alpha)
-    att = (z * sig * weight).astype(jnp.bfloat16)
-    dprod = jnp.einsum("qhd,khd->hqk", grad, value, preferred_element_type=jnp.float32)
-    dsc = (dprod * sig * (1.0 + z * (1.0 - sig)) * weight * alpha).astype(jnp.bfloat16)
-    dkey = jnp.einsum("hqk,qhd->khd", dsc, query, preferred_element_type=jnp.float32)
-    dvalue = jnp.einsum("hqk,qhd->khd", att, grad, preferred_element_type=jnp.float32)
-    return dkey, dvalue
+def exchange_kernel(span, kv_ref, qg_ref, ev_ref, out_ref, ev_out, landed, ev_land, send_sem, recv_sem):
+    count = lax.axis_size("ctx")
+    me = lax.axis_index("ctx")
+    group = lax.axis_index("dp")
+    barrier = pltpu.get_barrier_semaphore()
+    for step in range(1, span + 1):
+        for peer in ((me + step) % count, (me + count - step) % count):
+            pl.semaphore_signal(barrier, inc=1, device_id=(group, peer), device_id_type=pl.DeviceIdType.MESH)
+    pl.semaphore_wait(barrier, 2 * span)
+    copies = []
+    for step in range(1, span + 1):
+        forward = pltpu.make_async_remote_copy(
+            src_ref=kv_ref,
+            dst_ref=landed.at[step - 1],
+            send_sem=send_sem.at[step - 1],
+            recv_sem=recv_sem.at[step - 1],
+            device_id=(group, (me + step) % count),
+            device_id_type=pl.DeviceIdType.MESH,
+        )
+        backward = pltpu.make_async_remote_copy(
+            src_ref=qg_ref,
+            dst_ref=landed.at[span + step - 1],
+            send_sem=send_sem.at[span + step - 1],
+            recv_sem=recv_sem.at[span + step - 1],
+            device_id=(group, (me + count - step) % count),
+            device_id_type=pl.DeviceIdType.MESH,
+        )
+        copies += [forward, backward]
+    partner = pltpu.make_async_remote_copy(
+        src_ref=ev_ref,
+        dst_ref=ev_land,
+        send_sem=send_sem.at[2 * span],
+        recv_sem=recv_sem.at[2 * span],
+        device_id=(group, me + 1 - 2 * (me % 2)),
+        device_id_type=pl.DeviceIdType.MESH,
+    )
+    copies.append(partner)
+    for copy in copies:
+        copy.start()
+    for copy in copies:
+        copy.wait()
+    out_ref[...] = landed[...]
+    ev_out[...] = ev_land[...]
+
+
+def exchange_blocks(kv, qg, events, span):
+    rows, width = kv.shape
+    vmem = pl.BlockSpec(memory_space=pltpu.VMEM)
+    return pl.pallas_call(
+        functools.partial(exchange_kernel, span),
+        in_specs=[vmem] * 3,
+        out_specs=[vmem, vmem],
+        out_shape=[
+            jax.ShapeDtypeStruct((2 * span, rows, width), kv.dtype),
+            jax.ShapeDtypeStruct(events.shape, events.dtype),
+        ],
+        scratch_shapes=[
+            pltpu.VMEM((2 * span, rows, width), kv.dtype),
+            pltpu.VMEM(events.shape, events.dtype),
+            pltpu.SemaphoreType.DMA((2 * span + 1,)),
+            pltpu.SemaphoreType.DMA((2 * span + 1,)),
+        ],
+        compiler_params=pltpu.CompilerParams(collective_id=0, has_side_effects=True),
+    )(kv, qg, events)
 
 
 def body(events, w_query, w_key, values, grad_out, lengths, stream_shift, block_keep):
@@ -188,24 +227,11 @@
         )
         return (position, owner, kept)
 
-    def mask(qinfo, kinfo):
-        return (
-            (qinfo[1][:, None] == kinfo[1][None, :])
-            & (kinfo[0][None, :] <= qinfo[0][:, None])
-            & kinfo[2][None, :]
-        )
-
-    def split(packed):
-        return (
-            packed[:, :features].reshape(rows, nheads, HD),
-            packed[:, features:].reshape(rows, nheads, HD),
-        )
-
-    partner_events = exchange(local, "ctx", 1)
     kv = jnp.concatenate([keys, values[0]], axis=1)
     qg = jnp.concatenate([queries, grad_out[0]], axis=1)
-    kv_from = [None] + [shifted(kv, "ctx", step) for step in range(1, SPAN + 1)]
-    qg_from = [None] + [shifted(qg, "ctx", -step) for step in range(1, SPAN + 1)]
+    landed, partner_events = exchange_blocks(kv, qg, local, SPAN)
+    kv_from = [None] + [landed[step - 1] for step in range(1, SPAN + 1)]
+    qg_from = [None] + [landed[SPAN + step - 1] for step in range(1, SPAN + 1)]
 
     offsets = range(-SPAN, SPAN + 1)
     described = [describe(myself + offset) for offset in offsets]

time: 172 us -> 180 us (1.047)
  Pallas kernels: 12.8 us -> 65.2 us
  starting transfers between devices: 75.9 us -> 48.6 us
  waiting for transfers between devices: 62.2 us -> 41.5 us
  local copies, waits for them, and re-layouts: 7.66 us -> 11.9 us
    pallas_call x0 -> x1, Pallas kernels: none -> 52.4 us  [exchange_blocks(): pl.pallas_call(functools.partial(exchange_kernel, span), in_specs=[vmem]...]
    ppermute x6 -> x0, starting transfers between devices: 28 us -> none  [shifted(): return lax.ppermute(value, axis, pairs)]
    ppermute x6 -> x0, waiting for transfers between devices: 19.7 us -> none  [shifted(): return lax.ppermute(value, axis, pairs)]
    squeeze x0 -> x1, local copies, waits for them, and re-layouts: none -> 3.51 us  [body(): kv_from = [None] + [landed[step - 1] for step in range(1, SPAN + 1)]]
    unnamed x26 -> x22, local copies, waits for them, and re-layouts: 4.19 us -> 3.01 us
    ppermute x10 -> x9, waiting for transfers between devices: 42.4 us -> 41.5 us  [exchange(): lax.ppermute(value, axis, [(source, source ^ mask) for source in range(co...]
    ppermute x10 -> x9, starting transfers between devices: 47.9 us -> 48.6 us  [exchange(): lax.ppermute(value, axis, [(source, source ^ mask) for source in range(co...]
  transfers between devices with their start and end apart: 16 -> 9, of which waited for: 11 -> 8; matrix products, arithmetic and copies ran while one was open for 3% -> 1% of each run, Pallas kernels for 8% -> 0%
where the time goes in v5:
time: 180 us; the launch traced here: 179 us
  Pallas kernels  65.2 us (36%)
  starting transfers between devices  48.6 us (27%)
  waiting for transfers between devices  41.5 us (23%)
  local copies, waits for them, and re-layouts  11.9 us (7%)
  other arithmetic  5.34 us (3%)
  matrix products  3.81 us (2%)
  between operations  2.18 us (1%)
    pallas_call x1, Pallas kernels, exchange_blocks(): pl.pallas_call(functools.partial(exchange_kernel, span), in_specs=[vmem]...  52.4 us
    ppermute x9, starting transfers between devices, exchange(): lax.ppermute(value, axis, [(source, source ^ mask) for source in range(co...  48.6 us
    ppermute x9, waiting for transfers between devices, exchange(): lax.ppermute(value, axis, [(source, source ^ mask) for source in range(co...  41.5 us
    pallas_call x1, Pallas kernels, attention_tiles(): pl.pallas_call(functools.partial(tiles_kernel, span, alpha, scale), grid=...  12.8 us
  transfers between devices with their start and end apart: 9, of which 8 were waited for; matrix products, arithmetic and copies ran while one was open for 1% of the time, Pallas kernels for 0%

profile of v5, /device:TPU:6, one launch (start us, length us, event | category | flops | bytes accessed | tf_op | source)
XLA Modules:
  0.0 178.5 jit_solution(4090147842226774410)
XLA Ops:
  1.7 1.2 select_reduce_fusion
  5.0 1.5 convolution_convert_fusion
  8.1 52.4 %shard_map.111 = (bf16[6,256,1024]{2,1,0:T(8,128)(2,1)}, bf16[256,1024]{1,0:T(8,128)(2,1)}) custom-call(bf16[256,1024]{1,0:T(8,128)(2,1)} %get-tuple-element.57.kv_ref.refs_8_.refs_9_, bf16[256,1024]{1,0:T(8,128)(2,1)} %get-tuple-element.56.qg_ref.refs_0_.refs_1_, bf16[256,1024]{1,0:T(8,128)(2,1)} %bitcast.94), custom_call_target="tpu_custom_call" | custom-call | tf_op jit(solution)/shard_map/pallas_call | solution.py:184
  60.5 3.5 %slice_bitcast_fusion = (bf16[256,1024]{1,0:T(8,128)(2,1)}, bf16[256,1024]{1,0:T(8,128)(2,1)}, bf16[256,1024]{1,0:T(8,128)(2,1)}, bf16[256,1024]{1,0:T(8,128)(2,...) fusion(bf16[6,256,1024]{2,1,0:T(8,128)(2,1)} %get-tuple-element.10), kind=kLoop, calls=%fused_computation.16 | loop fusion | bytes 6291456 | tf_op jit(solution)/shard_map/squeeze | solution.py:233
  64.0 12.8 %shard_map.112 = (bf16[256,512]{1,0:T(8,128)(2,1)}, bf16[256,512]{1,0:T(8,128)(2,1)}, bf16[256,512]{1,0:T(8,128)(2,1)}, bf16[256,512]{1,0:T(8,128)(2,1)}) custom-call(s32[256,21]{1,0:T(8,128)} %copy.24.infoc, s32[21,256]{1,0:T(8,128)} %copy-done.9, bf16[256,1024]{1,0:T(8,128)(2,1)} %get-tuple-element.56.qg_ref.refs_0_.refs_1_, ...), custom_call_target="tpu_custom_call" | custom-call | flops 2348810240 | bytes 9437184 | tf_op jit(solution)/shard_map/pallas_call | solution.py:122
  78.8 4.3 %collective-permute-start = (bf16[256,1024]{1,0:T(8,128)(2,1)S(1)}, bf16[256,1024]{1,0:T(8,128)(2,1)S(1)}, u32[]{:S(2)}, u32[]{:S(2)}) collective-permute-start(bf16[256,1024]{1,0:T(8,128)(2,1)S(1)} %constant_dynamic-update-slice_fusion), channel_id=1, source_target_pairs={{0,1},{1,0},{2,3},{3,2},{4,5},{5,4},{6,7},{7,6},{8,9},{9,8},{10,11... | collective-permute-start | bytes 1572872 | tf_op jit(solution)/shard_map/ppermute | solution.py:23
  83.4 1.2 copy.26
  85.5 1.9 %fusion = f32[16,2,16,1024]{3,2,1,0:T(8,128)S(1)} fusion(bf16[16,2,16,512]{3,2,1,0:T(8,128)(2,1)S(1)} %bitcast.97, bf16[256,1024]{1,0:T(8,128)(2,1)} %copy-done.6, bf16[256,1024]{1,0:T(8,128)(2,1)} %copy-done.4), kind=kOutput, calls=%fused_computation.5 | convolution fusion | flops 538968064 | bytes 3670016 | tf_op jit(solution)/shard_map/dot_general | solution.py:42
  88.3 3.8 %collective-permute-start.1 = (bf16[16,16,1024]{2,1,0:T(8,128)(2,1)}, bf16[16,16,1024]{2,1,0:T(8,128)(2,1)}, u32[]{:S(2)}, u32[]{:S(2)}) collective-permute-start(bf16[16,16,1024]{2,1,0:T(8,128)(2,1)} %fusion.3), channel_id=1, source_target_pairs={{0,2},{1,3},{2,0},{3,1},{4,6},{5,7},{6,4},{7,5},{8,10},{9,11},{10,... | collective-permute-start | bytes 1572872 | tf_op jit(solution)/shard_map/ppermute | solution.py:23
  92.1 14.0 %collective-permute-done.1 = bf16[16,16,1024]{2,1,0:T(8,128)(2,1)} collective-permute-done((bf16[16,16,1024]{2,1,0:T(8,128)(2,1)}, bf16[16,16,1024]{2,1,0:T(8,128)(2,1)}, u32[]{:S(2)}, u32[]{:S(2)}) %collective-permute-start.1) | collective-permute-done | bytes 524320 | tf_op jit(solution)/shard_map/ppermute | solution.py:23
  108.4 2.5 %collective-permute-start.2 = (bf16[8,16,1024]{2,1,0:T(8,128)(2,1)S(1)}, bf16[8,16,1024]{2,1,0:T(8,128)(2,1)S(1)}, u32[]{:S(2)}, u32[]{:S(2)}) collective-permute-start(bf16[8,16,1024]{2,1,0:T(8,128)(2,1)S(1)} %fusion.5), channel_id=1, source_target_pairs={{0,4},{1,5},{2,6},{3,7},{4,0},{5,1},{6,2},{7,3},{8,12},{9,13},{10,... | collective-permute-start | bytes 786440 | tf_op jit(solution)/shard_map/ppermute | solution.py:23
  111.0 7.0 %collective-permute-done.2 = bf16[8,16,1024]{2,1,0:T(8,128)(2,1)S(1)} collective-permute-done((bf16[8,16,1024]{2,1,0:T(8,128)(2,1)S(1)}, bf16[8,16,1024]{2,1,0:T(8,128)(2,1)S(1)}, u32[]{:S(2)}, u32[]{:S(2)}) %collective-permute-start.2) | collective-permute-done | bytes 262176 | tf_op jit(solution)/shard_map/ppermute | solution.py:23
  119.1 4.6 %collective-permute-start.3 = (bf16[4,16,1024]{2,1,0:T(8,128)(2,1)S(1)}, bf16[4,16,1024]{2,1,0:T(8,128)(2,1)S(1)}, u32[]{:S(2)}, u32[]{:S(2)}) collective-permute-start(bf16[4,16,1024]{2,1,0:T(8,128)(2,1)S(1)} %fusion.6), channel_id=1, source_target_pairs={{0,8},{1,9},{2,10},{3,11},{4,12},{5,13},{6,14},{7,15},{8,0},{9,1},... | collective-permute-start | bytes 393224 | tf_op jit(solution)/shard_map/ppermute | solution.py:23
  123.8 5.3 %collective-permute-done.3 = bf16[4,16,1024]{2,1,0:T(8,128)(2,1)S(1)} collective-permute-done((bf16[4,16,1024]{2,1,0:T(8,128)(2,1)S(1)}, bf16[4,16,1024]{2,1,0:T(8,128)(2,1)S(1)}, u32[]{:S(2)}, u32[]{:S(2)}) %collective-permute-start.3) | collective-permute-done | bytes 131104 | tf_op jit(solution)/shard_map/ppermute | solution.py:23
  129.2 9.1 %collective-permute-start.4 = (bf16[2,16,1024]{2,1,0:T(8,128)(2,1)S(1)}, bf16[2,16,1024]{2,1,0:T(8,128)(2,1)S(1)}, u32[]{:S(2)}, u32[]{:S(2)}) collective-permute-start(bf16[2,16,1024]{2,1,0:T(8,128)(2,1)S(1)} %fusion.7), channel_id=1, source_target_pairs={{0,16},{1,17},{2,18},{3,19},{4,20},{5,21},{6,22},{7,23},{8,24},{9,... | collective-permute-start | bytes 196616 | tf_op jit(solution)/shard_map/ppermute | solution.py:23
  138.3 4.3 %collective-permute-done.4 = bf16[2,16,1024]{2,1,0:T(8,128)(2,1)S(1)} collective-permute-done((bf16[2,16,1024]{2,1,0:T(8,128)(2,1)S(1)}, bf16[2,16,1024]{2,1,0:T(8,128)(2,1)S(1)}, u32[]{:S(2)}, u32[]{:S(2)}) %collective-permute-start.4) | collective-permute-done | bytes 65568 | tf_op jit(solution)/shard_map/ppermute | solution.py:23
  142.6 12.7 %collective-permute-start.5 = (bf16[1,16,1024]{2,1,0:T(8,128)(2,1)S(1)}, bf16[1,16,1024]{2,1,0:T(8,128)(2,1)S(1)}, u32[]{:S(2)}, u32[]{:S(2)}) collective-permute-start(bf16[1,16,1024]{2,1,0:T(8,128)(2,1)S(1)} %dynamic-slice_convert_fusion.3), channel_id=1, source_target_pairs={{0,32},{1,33},{2,34},{3,35},{4,36},{5,37},{6,38},{7,39},{8,40},{9,... | collective-permute-start | bytes 98312 | tf_op jit(solution)/shard_map/ppermute | solution.py:23
  155.3 2.2 %collective-permute-done.5 = bf16[1,16,1024]{2,1,0:T(8,128)(2,1)S(1)} collective-permute-done((bf16[1,16,1024]{2,1,0:T(8,128)(2,1)S(1)}, bf16[1,16,1024]{2,1,0:T(8,128)(2,1)S(1)}, u32[]{:S(2)}, u32[]{:S(2)}) %collective-permute-start.5) | collective-permute-done | bytes 32800 | tf_op jit(solution)/shard_map/ppermute | solution.py:23
  157.6 3.3 %collective-permute-start.6 = (f32[16,1024]{1,0:T(8,128)S(1)}, f32[16,1024]{1,0:T(8,128)S(1)}, u32[]{:S(2)}, u32[]{:S(2)}) collective-permute-start(f32[16,1024]{1,0:T(8,128)S(1)} %add_bitcast_fusion), channel_id=1, source_target_pairs={{0,64},{64,0},{128,192},{192,128},{256,320},{320,256},{384,448},{4... | collective-permute-start | bytes 196616 | tf_op jit(solution)/shard_map/ppermute | solution.py:23
  160.9 2.8 %collective-permute-done.6 = f32[16,1024]{1,0:T(8,128)S(1)} collective-permute-done((f32[16,1024]{1,0:T(8,128)S(1)}, f32[16,1024]{1,0:T(8,128)S(1)}, u32[]{:S(2)}, u32[]{:S(2)}) %collective-permute-start.6) | collective-permute-done | bytes 65568 | tf_op jit(solution)/shard_map/ppermute | solution.py:23
  163.7 3.5 %collective-permute-start.7 = (f32[16,1024]{1,0:T(8,128)S(1)}, f32[16,1024]{1,0:T(8,128)S(1)}, u32[]{:S(2)}, u32[]{:S(2)}) collective-permute-start(f32[16,1024]{1,0:T(8,128)S(1)} %add.553), channel_id=1, source_target_pairs={{0,128},{64,192},{128,0},{192,64},{256,384},{320,448},{384,256},{4... | collective-permute-start | bytes 196616 | tf_op jit(solution)/shard_map/ppermute | solution.py:23
  167.2 3.0 %collective-permute-done.7 = f32[16,1024]{1,0:T(8,128)S(1)} collective-permute-done((f32[16,1024]{1,0:T(8,128)S(1)}, f32[16,1024]{1,0:T(8,128)S(1)}, u32[]{:S(2)}, u32[]{:S(2)}) %collective-permute-start.7) | collective-permute-done | bytes 65568 | tf_op jit(solution)/shard_map/ppermute | solution.py:23
  170.2 4.8 %collective-permute-start.8 = (f32[16,1024]{1,0:T(8,128)S(1)}, f32[16,1024]{1,0:T(8,128)S(1)}, u32[]{:S(2)}, u32[]{:S(2)}) collective-permute-start(f32[16,1024]{1,0:T(8,128)S(1)} %add.554), channel_id=1, source_target_pairs={{0,256},{64,320},{128,384},{192,448},{256,0},{320,64},{384,128},{4... | collective-permute-start | bytes 196616 | tf_op jit(solution)/shard_map/ppermute | solution.py:23
  175.1 2.9 %collective-permute-done.8 = f32[16,1024]{1,0:T(8,128)S(1)} collective-permute-done((f32[16,1024]{1,0:T(8,128)S(1)}, f32[16,1024]{1,0:T(8,128)S(1)}, u32[]{:S(2)}, u32[]{:S(2)}) %collective-permute-start.8) | collective-permute-done | bytes 65568 | tf_op jit(solution)/shard_map/ppermute | solution.py:23
  (66 shorter events, 11.7 us)
Async XLA Ops:
  0.6 4.4 %copy-start = (bf16[1024,512]{1,0:T(8,128)(2,1)S(1)}, bf16[1024,512]{1,0:T(8,128)(2,1)}, u32[]{:S(2)}) copy-start(bf16[1024,512]{1,0:T(8,128)(2,1)} %param.10) | copy-start | bytes 3145732
  0.6 5.9 %copy-start.1 = (bf16[1,256,1024]{2,1,0:T(8,128)(2,1)S(1)}, bf16[1,256,1024]{2,1,0:T(8,128)(2,1)}, u32[]{:S(2)}) copy-start(bf16[1,256,1024]{2,1,0:T(8,128)(2,1)} %param.8) | copy-start | bytes 1572868
  0.7 5.9 %copy-start.5 = (bf16[1024,512]{1,0:T(8,128)(2,1)S(1)}, bf16[1024,512]{1,0:T(8,128)(2,1)}, u32[]{:S(2)}) copy-start(bf16[1024,512]{1,0:T(8,128)(2,1)} %param.9) | copy-start | bytes 3145732
  0.7 6.3 %copy-start.7 = (bf16[1,256,512]{2,1,0:T(8,128)(2,1)S(1)}, bf16[1,256,512]{2,1,0:T(8,128)(2,1)}, u32[]{:S(2)}) copy-start(bf16[1,256,512]{2,1,0:T(8,128)(2,1)} %param.12) | copy-start | bytes 786436
  0.7 6.3 %copy-start.8 = (bf16[1,256,512]{2,1,0:T(8,128)(2,1)S(1)}, bf16[1,256,512]{2,1,0:T(8,128)(2,1)}, u32[]{:S(2)}) copy-start(bf16[1,256,512]{2,1,0:T(8,128)(2,1)} %param.11) | copy-start | bytes 786436
  4.3 3.8 %copy-start.9 = (s32[21,256]{1,0:T(8,128)}, s32[21,256]{1,0:T(8,128)S(1)}, u32[]{:S(2)}) copy-start(s32[21,256]{1,0:T(8,128)S(1)} %stack.45.infor) | copy-start | bytes 64516
  64.0 19.1 %copy-start.2 = (bf16[1,256,1024]{2,1,0:T(8,128)(2,1)S(1)}, bf16[1,256,1024]{2,1,0:T(8,128)(2,1)}, u32[]{:S(2)}) copy-start(bf16[1,256,1024]{2,1,0:T(8,128)(2,1)} %param.8) | copy-start | bytes 1572868
  78.8 5.9 %copy-start.4 = (bf16[256,1024]{1,0:T(8,128)(2,1)}, bf16[256,1024]{1,0:T(8,128)(2,1)S(1)}, u32[]{:S(2)}) copy-start(bf16[256,1024]{1,0:T(8,128)(2,1)S(1)} %constant_dynamic-update-slice_fusion) | copy-start | bytes 1572868
  78.8 5.8 %collective-permute-start = (bf16[256,1024]{1,0:T(8,128)(2,1)S(1)}, bf16[256,1024]{1,0:T(8,128)(2,1)S(1)}, u32[]{:S(2)}, u32[]{:S(2)}) collective-permute-start(bf16[256,1024]{1,0:T(8,128)(2,1)S(1)} %constant_dynamic-update-slice_fusion), channel_id=1, source_target_pairs={{0,1},{1,0},{2,3},{3,2},{4,5},{5,4},{6,7},{7,6},{8,9},{9,8},{10,11... | collective-permute-start | bytes 1572872 | tf_op jit(solution)/shard_map/ppermute | solution.py:23
  84.7 0.8 copy-start.6
  88.3 17.8 %collective-permute-start.1 = (bf16[16,16,1024]{2,1,0:T(8,128)(2,1)}, bf16[16,16,1024]{2,1,0:T(8,128)(2,1)}, u32[]{:S(2)}, u32[]{:S(2)}) collective-permute-start(bf16[16,16,1024]{2,1,0:T(8,128)(2,1)} %fusion.3), channel_id=1, source_target_pairs={{0,2},{1,3},{2,0},{3,1},{4,6},{5,7},{6,4},{7,5},{8,10},{9,11},{10,... | collective-permute-start | bytes 1572872 | tf_op jit(solution)/shard_map/ppermute | solution.py:23
  107.4 1.0 copy-start.3
  108.4 9.6 %collective-permute-start.2 = (bf16[8,16,1024]{2,1,0:T(8,128)(2,1)S(1)}, bf16[8,16,1024]{2,1,0:T(8,128)(2,1)S(1)}, u32[]{:S(2)}, u32[]{:S(2)}) collective-permute-start(bf16[8,16,1024]{2,1,0:T(8,128)(2,1)S(1)} %fusion.5), channel_id=1, source_target_pairs={{0,4},{1,5},{2,6},{3,7},{4,0},{5,1},{6,2},{7,3},{8,12},{9,13},{10,... | collective-permute-start | bytes 786440 | tf_op jit(solution)/shard_map/ppermute | solution.py:23
  119.1 10.0 %collective-permute-start.3 = (bf16[4,16,1024]{2,1,0:T(8,128)(2,1)S(1)}, bf16[4,16,1024]{2,1,0:T(8,128)(2,1)S(1)}, u32[]{:S(2)}, u32[]{:S(2)}) collective-permute-start(bf16[4,16,1024]{2,1,0:T(8,128)(2,1)S(1)} %fusion.6), channel_id=1, source_target_pairs={{0,8},{1,9},{2,10},{3,11},{4,12},{5,13},{6,14},{7,15},{8,0},{9,1},... | collective-permute-start | bytes 393224 | tf_op jit(solution)/shard_map/ppermute | solution.py:23
  129.2 13.4 %collective-permute-start.4 = (bf16[2,16,1024]{2,1,0:T(8,128)(2,1)S(1)}, bf16[2,16,1024]{2,1,0:T(8,128)(2,1)S(1)}, u32[]{:S(2)}, u32[]{:S(2)}) collective-permute-start(bf16[2,16,1024]{2,1,0:T(8,128)(2,1)S(1)} %fusion.7), channel_id=1, source_target_pairs={{0,16},{1,17},{2,18},{3,19},{4,20},{5,21},{6,22},{7,23},{8,24},{9,... | collective-permute-start | bytes 196616 | tf_op jit(solution)/shard_map/ppermute | solution.py:23
  142.6 14.9 %collective-permute-start.5 = (bf16[1,16,1024]{2,1,0:T(8,128)(2,1)S(1)}, bf16[1,16,1024]{2,1,0:T(8,128)(2,1)S(1)}, u32[]{:S(2)}, u32[]{:S(2)}) collective-permute-start(bf16[1,16,1024]{2,1,0:T(8,128)(2,1)S(1)} %dynamic-slice_convert_fusion.3), channel_id=1, source_target_pairs={{0,32},{1,33},{2,34},{3,35},{4,36},{5,37},{6,38},{7,39},{8,40},{9,... | collective-permute-start | bytes 98312 | tf_op jit(solution)/shard_map/ppermute | solution.py:23
  157.6 6.2 %collective-permute-start.6 = (f32[16,1024]{1,0:T(8,128)S(1)}, f32[16,1024]{1,0:T(8,128)S(1)}, u32[]{:S(2)}, u32[]{:S(2)}) collective-permute-start(f32[16,1024]{1,0:T(8,128)S(1)} %add_bitcast_fusion), channel_id=1, source_target_pairs={{0,64},{64,0},{128,192},{192,128},{256,320},{320,256},{384,448},{4... | collective-permute-start | bytes 196616 | tf_op jit(solution)/shard_map/ppermute | solution.py:23
  163.7 6.5 %collective-permute-start.7 = (f32[16,1024]{1,0:T(8,128)S(1)}, f32[16,1024]{1,0:T(8,128)S(1)}, u32[]{:S(2)}, u32[]{:S(2)}) collective-permute-start(f32[16,1024]{1,0:T(8,128)S(1)} %add.553), channel_id=1, source_target_pairs={{0,128},{64,192},{128,0},{192,64},{256,384},{320,448},{384,256},{4... | collective-permute-start | bytes 196616 | tf_op jit(solution)/shard_map/ppermute | solution.py:23
  170.2 7.7 %collective-permute-start.8 = (f32[16,1024]{1,0:T(8,128)S(1)}, f32[16,1024]{1,0:T(8,128)S(1)}, u32[]{:S(2)}, u32[]{:S(2)}) collective-permute-start(f32[16,1024]{1,0:T(8,128)S(1)} %add.554), channel_id=1, source_target_pairs={{0,256},{64,320},{128,384},{192,448},{256,0},{320,64},{384,128},{4... | collective-permute-start | bytes 196616 | tf_op jit(solution)/shard_map/ppermute | solution.py:23

commit v6 on v4

--- a/solution.py
+++ b/solution.py
@@ -28,6 +28,82 @@
         lax.dynamic_index_in_dim(value, bit, axis, keepdims=False),
         lax.dynamic_index_in_dim(value, 1 - bit, axis, keepdims=False),
     )
+
+
+def reduce_kernel(groups, spread, part_ref, out_ref, sent, landed, dp_landed, send_a, recv_a, send_b, recv_b):
+    count = lax.axis_size("ctx")
+    me = lax.axis_index("ctx")
+    group = lax.axis_index("dp")
+    core = me % 2
+    slot = me // 2
+    barrier = pltpu.get_barrier_semaphore()
+    for step in range(1, groups):
+        peer = 2 * ((slot + step) % groups) + core
+        pl.semaphore_signal(barrier, inc=1, device_id=(group, peer), device_id_type=pl.DeviceIdType.MESH)
+    for step in range(1, spread):
+        pl.semaphore_signal(
+            barrier, inc=1, device_id=((group + step) % spread, me), device_id_type=pl.DeviceIdType.MESH
+        )
+    pl.semaphore_wait(barrier, groups - 1 + spread - 1)
+    sent[...] = part_ref[...].astype(sent.dtype)
+    copies = []
+    for step in range(1, groups):
+        target = (slot + step) % groups
+        copy = pltpu.make_async_remote_copy(
+            src_ref=sent.at[target],
+            dst_ref=landed.at[slot],
+            send_sem=send_a.at[step - 1],
+            recv_sem=recv_a.at[step - 1],
+            device_id=(group, 2 * target + core),
+            device_id_type=pl.DeviceIdType.MESH,
+        )
+        copy.start()
+        copies.append(copy)
+    for copy in copies:
+        copy.wait()
+    total = part_ref[slot]
+    for step in range(1, groups):
+        total = total + landed[(slot + groups - step) % groups].astype(jnp.float32)
+    dp_landed[group] = total
+    copies = []
+    for step in range(1, spread):
+        copy = pltpu.make_async_remote_copy(
+            src_ref=dp_landed.at[group],
+            dst_ref=dp_landed.at[group],
+            send_sem=send_b.at[step - 1],
+            recv_sem=recv_b.at[step - 1],
+            device_id=((group + step) % spread, me),
+            device_id_type=pl.DeviceIdType.MESH,
+        )
+        copy.start()
+        copies.append(copy)
+    for copy in copies:
+        copy.wait()
+    result = dp_landed[0]
+    for index in range(1, spread):
+        result = result + dp_landed[index]
+    out_ref[...] = result
+
+
+def reduce_blocks(part, spread):
+    groups, share, width = part.shape
+    vmem = pl.BlockSpec(memory_space=pltpu.VMEM)
+    return pl.pallas_call(
+        functools.partial(reduce_kernel, groups, spread),
+        in_specs=[vmem],
+        out_specs=vmem,
+        out_shape=jax.ShapeDtypeStruct((share, width), jnp.float32),
+        scratch_shapes=[
+            pltpu.VMEM((groups, share, width), jnp.bfloat16),
+            pltpu.VMEM((groups, share, width), jnp.bfloat16),
+            pltpu.VMEM((spread, share, width), jnp.float32),
+            pltpu.SemaphoreType.DMA((groups - 1,)),
+            pltpu.SemaphoreType.DMA((groups - 1,)),
+            pltpu.SemaphoreType.DMA((spread - 1,)),
+            pltpu.SemaphoreType.DMA((spread - 1,)),
+        ],
+        compiler_params=pltpu.CompilerParams(collective_id=1, has_side_effects=True),
+    )(part)
 
 
 def reduce_rows(local, partner_events, joined, myself, cycle_size):
@@ -41,17 +117,7 @@
     kept = lax.dynamic_index_in_dim(halves, core, 2, keepdims=False).reshape(both_events.shape[0], width // 2)
     acc = jnp.dot(kept.T, both_joined, preferred_element_type=jnp.float32)
     acc = acc.reshape(width // (2 * share), share, joined.shape[1])
-    mask = 2
-    while mask < cycle_size:
-        acc = acc.reshape(acc.shape[0] // 2, 2, share, joined.shape[1])
-        keep_part, send_part = pick(acc, (myself // mask) % 2, 1)
-        acc = keep_part + exchange(send_part.astype(jnp.bfloat16), "ctx", mask).astype(jnp.float32)
-        mask *= 2
-    acc = acc.reshape(share, joined.shape[1])
-    mask = 1
-    while mask < lax.axis_size("dp"):
-        acc = acc + exchange(acc, "dp", mask)
-        mask *= 2
+    acc = reduce_blocks(acc, lax.axis_size("dp"))
     return acc
 
 

time: 172 us -> 156 us (0.907)
  Pallas kernels: 12.8 us -> 88 us
  starting transfers between devices: 75.9 us -> 31.9 us
  waiting for transfers between devices: 62.2 us -> 21.6 us
  local copies, waits for them, and re-layouts: 7.66 us -> 4.94 us
  other arithmetic: 5.58 us -> 2.99 us
    pallas_call x0 -> x1, Pallas kernels: none -> 75.2 us  [reduce_blocks(): pl.pallas_call(functools.partial(reduce_kernel, groups, spread), in_specs...]
    ppermute x10 -> x2, starting transfers between devices: 47.9 us -> 3.83 us  [exchange(): lax.ppermute(value, axis, [(source, source ^ mask) for source in range(co...]
    ppermute x10 -> x2, waiting for transfers between devices: 42.4 us -> 1.85 us  [exchange(): lax.ppermute(value, axis, [(source, source ^ mask) for source in range(co...]
    add x6 -> x0, other arithmetic: 2.37 us -> none  [the longest x4 2.35 us: reduce_rows(): keep_part + exchange(send_part.astype(jnp.bfloat16), 'ctx', mask).astype(...]
    unnamed x26 -> x20, local copies, waits for them, and re-layouts: 4.19 us -> 2.41 us
  transfers between devices with their start and end apart: 16 -> 8, of which waited for: 11 -> 3; matrix products, arithmetic and copies ran while one was open for 3% -> 3% of each run, Pallas kernels for 8% -> 8%
where the time goes in v6:
time: 156 us; the launch traced here: 155 us
  Pallas kernels  88 us (56%)
  starting transfers between devices  31.9 us (20%)
  waiting for transfers between devices  21.6 us (14%)
  local copies, waits for them, and re-layouts  4.94 us (3%)
  matrix products  3.97 us (3%)
  other arithmetic  2.99 us (2%)
  between operations  1.83 us (1%)
    pallas_call x1, Pallas kernels, reduce_blocks(): pl.pallas_call(functools.partial(reduce_kernel, groups, spread), in_specs...  75.2 us
    ppermute x6, starting transfers between devices, shifted(): return lax.ppermute(value, axis, pairs)  28 us
    ppermute x6, waiting for transfers between devices, shifted(): return lax.ppermute(value, axis, pairs)  19.8 us
    pallas_call x1, Pallas kernels, attention_tiles(): pl.pallas_call(functools.partial(tiles_kernel, span, alpha, scale), grid=...  12.8 us
    ppermute x2, starting transfers between devices, exchange(): lax.ppermute(value, axis, [(source, source ^ mask) for source in range(co...  3.83 us
  transfers between devices with their start and end apart: 8, of which 3 were waited for; matrix products, arithmetic and copies ran while one was open for 3% of the time, Pallas kernels for 8%

profile of v6, /device:TPU:6, one launch (start us, length us, event | category | flops | bytes accessed | tf_op | source)
XLA Modules:
  0.0 155.2 jit_solution(10631550916689805887)
XLA Ops:
  0.7 1.2 copy-done
  1.9 1.5 convolution_convert_fusion.1
  3.3 1.0 pad_maximum_fusion.refs_0_.refs_1_
  4.4 2.9 %collective-permute-start = (bf16[256,1024]{1,0:T(8,128)(2,1)S(1)}, bf16[256,1024]{1,0:T(8,128)(2,1)}, u32[]{:S(2)}, u32[]{:S(2)}) collective-permute-start(bf16[256,1024]{1,0:T(8,128)(2,1)S(1)} %pad_maximum_fusion.refs_0_.refs_1_), channel_id=1, source_target_pairs={{0,63},{1,0},{2,1},{3,2},{4,3},{5,4},{6,5},{7,6},{8,7},{9,8},{10,9... | collective-permute-start | bytes 1572872 | tf_op jit(solution)/shard_map/ppermute | solution.py:18
  7.3 13.0 %collective-permute-start.1 = (bf16[256,1024]{1,0:T(8,128)(2,1)S(1)}, bf16[256,1024]{1,0:T(8,128)(2,1)}, u32[]{:S(2)}, u32[]{:S(2)}) collective-permute-start(bf16[256,1024]{1,0:T(8,128)(2,1)S(1)} %pad_maximum_fusion.refs_0_.refs_1_), channel_id=1, source_target_pairs={{0,62},{1,63},{2,0},{3,1},{4,2},{5,3},{6,4},{7,5},{8,6},{9,7},{10,... | collective-permute-start | bytes 1572872 | tf_op jit(solution)/shard_map/ppermute | solution.py:18
  20.3 1.9 %collective-permute-start.2 = (bf16[256,1024]{1,0:T(8,128)(2,1)S(1)}, bf16[256,1024]{1,0:T(8,128)(2,1)}, u32[]{:S(2)}, u32[]{:S(2)}) collective-permute-start(bf16[256,1024]{1,0:T(8,128)(2,1)S(1)} %pad_maximum_fusion.refs_0_.refs_1_), channel_id=1, source_target_pairs={{0,61},{1,62},{2,63},{3,0},{4,1},{5,2},{6,3},{7,4},{8,5},{9,6},{10... | collective-permute-start | bytes 1572872 | tf_op jit(solution)/shard_map/ppermute | solution.py:18
  22.2 0.4 convolution_convert_fusion
  22.7 3.4 %collective-permute-start.3 = (bf16[256,1024]{1,0:T(8,128)(2,1)S(1)}, bf16[256,1024]{1,0:T(8,128)(2,1)}, u32[]{:S(2)}, u32[]{:S(2)}) collective-permute-start(bf16[256,1024]{1,0:T(8,128)(2,1)S(1)} %pad_maximum_fusion.1.refs_8_.refs_9_), channel_id=1, source_target_pairs={{0,1},{1,2},{2,3},{3,4},{4,5},{5,6},{6,7},{7,8},{8,9},{9,10},{10,1... | collective-permute-start | bytes 1572872 | tf_op jit(solution)/shard_map/ppermute | solution.py:18
  26.2 4.9 %collective-permute-start.4 = (bf16[256,1024]{1,0:T(8,128)(2,1)S(1)}, bf16[256,1024]{1,0:T(8,128)(2,1)}, u32[]{:S(2)}, u32[]{:S(2)}) collective-permute-start(bf16[256,1024]{1,0:T(8,128)(2,1)S(1)} %pad_maximum_fusion.1.refs_8_.refs_9_), channel_id=1, source_target_pairs={{0,2},{1,3},{2,4},{3,5},{4,6},{5,7},{6,8},{7,9},{8,10},{9,11},{10,... | collective-permute-start | bytes 1572872 | tf_op jit(solution)/shard_map/ppermute | solution.py:18
  32.2 0.6 select_reduce_fusion
  33.4 1.9 %collective-permute-start.5 = (bf16[256,1024]{1,0:T(8,128)(2,1)S(1)}, bf16[256,1024]{1,0:T(8,128)(2,1)}, u32[]{:S(2)}, u32[]{:S(2)}) collective-permute-start(bf16[256,1024]{1,0:T(8,128)(2,1)S(1)} %pad_maximum_fusion.1.refs_8_.refs_9_), channel_id=1, source_target_pairs={{0,3},{1,4},{2,5},{3,6},{4,7},{5,8},{6,9},{7,10},{8,11},{9,12},{10... | collective-permute-start | bytes 1572872 | tf_op jit(solution)/shard_map/ppermute | solution.py:18
  35.4 0.8 copy.21.infoc
  36.2 11.4 %collective-permute-done.1.refs_4_.refs_5_ = bf16[256,1024]{1,0:T(8,128)(2,1)} collective-permute-done((bf16[256,1024]{1,0:T(8,128)(2,1)S(1)}, bf16[256,1024]{1,0:T(8,128)(2,1)}, u32[]{:S(2)}, u32[]{:S(2)}) %collective-permute-start.1) | collective-permute-done | bytes 524320 | tf_op jit(solution)/shard_map/ppermute | solution.py:18
  47.6 1.9 %collective-permute-start.6 = (bf16[256,1024]{0,1:T(8,128)(2,1)S(1)}, bf16[256,1024]{0,1:T(8,128)(2,1)S(1)}, u32[]{:S(2)}, u32[]{:S(2)}) collective-permute-start(bf16[256,1024]{0,1:T(8,128)(2,1)S(1)} %bitcast.54), channel_id=1, source_target_pairs={{0,1},{1,0},{2,3},{3,2},{4,5},{5,4},{6,7},{7,6},{8,9},{9,8},{10,11... | collective-permute-start | bytes 1572872 | tf_op jit(solution)/shard_map/ppermute | solution.py:23
  49.5 8.4 %collective-permute-done.5.refs_14_.refs_15_ = bf16[256,1024]{1,0:T(8,128)(2,1)} collective-permute-done((bf16[256,1024]{1,0:T(8,128)(2,1)S(1)}, bf16[256,1024]{1,0:T(8,128)(2,1)}, u32[]{:S(2)}, u32[]{:S(2)}) %collective-permute-start.5) | collective-permute-done | bytes 524320 | tf_op jit(solution)/shard_map/ppermute | solution.py:18
  57.9 12.8 %shard_map.111 = (bf16[256,512]{1,0:T(8,128)(2,1)}, bf16[256,512]{1,0:T(8,128)(2,1)}, bf16[256,512]{1,0:T(8,128)(2,1)}, bf16[256,512]{1,0:T(8,128)(2,1)}) custom-call(s32[256,21]{1,0:T(8,128)} %copy.21.infoc, s32[21,256]{1,0:T(8,128)} %copy-done.6, bf16[256,1024]{1,0:T(8,128)(2,1)} %copy-done.3, bf16[256,1024]{1,0:T(8,128)(2,1)} %copy-done.3, ...), custom_call_target="tpu_custom_call" | custom-call | flops 2348810240 | bytes 9437184 | tf_op jit(solution)/shard_map/pallas_call | solution.py:188
  70.7 1.0 constant_dynamic-update-slice_fusion.1
  71.7 1.0 constant_dynamic-update-slice_fusion
  72.7 1.9 %collective-permute-start.7 = (bf16[256,1024]{1,0:T(8,128)(2,1)S(1)}, bf16[256,1024]{1,0:T(8,128)(2,1)S(1)}, u32[]{:S(2)}, u32[]{:S(2)}) collective-permute-start(bf16[256,1024]{1,0:T(8,128)(2,1)S(1)} %constant_dynamic-update-slice_fusion), channel_id=1, source_target_pairs={{0,1},{1,0},{2,3},{3,2},{4,5},{5,4},{6,7},{7,6},{8,9},{9,8},{10,11... | collective-permute-start | bytes 1572872 | tf_op jit(solution)/shard_map/ppermute | solution.py:23
  74.6 1.9 %collective-permute-done.7 = bf16[256,1024]{1,0:T(8,128)(2,1)S(1)} collective-permute-done((bf16[256,1024]{1,0:T(8,128)(2,1)S(1)}, bf16[256,1024]{1,0:T(8,128)(2,1)S(1)}, u32[]{:S(2)}, u32[]{:S(2)}) %collective-permute-start.7) | collective-permute-done | bytes 524320 | tf_op jit(solution)/shard_map/ppermute | solution.py:23
  76.5 2.1 %fusion.part_ref = f32[32,16,1024]{2,1,0:T(8,128)} fusion(bf16[256,1024]{1,0:T(8,128)(2,1)S(1)} %collective-permute-done.7, bf16[256,1024]{1,0:T(8,128)(2,1)S(1)} %constant_dynamic-update-slice_fusion, s32[]{:T(128)S(6)} %select_n.290, bf16[256,32,2,16]{0,3,2,1:T(8,128)(2,1)S(1)} %bitcast.55, bf16[256,32,2,16]{0,3,2,1:T(8,128)(2,1)S(1)} %bitcast.75), kind=kOutput, calls=%fused_computation.5 | convolution fusion | flops 540016640 | bytes 4194308 | tf_op jit(solution)/shard_map/dot_general | solution.py:118
  78.6 75.2 %shard_map.112 = f32[16,1024]{1,0:T(8,128)} custom-call(f32[32,16,1024]{2,1,0:T(8,128)} %fusion.part_ref), custom_call_target="tpu_custom_call" | custom-call | tf_op jit(solution)/shard_map/pallas_call | solution.py:91
  153.8 0.8 convert.11
  154.6 0.6 fusion.24
  (47 shorter events, 1.0 us)
Async XLA Ops:
  0.6 1.2 copy-start
  0.6 21.5 %copy-start.1 = (bf16[1,256,1024]{2,1,0:T(8,128)(2,1)S(1)}, bf16[1,256,1024]{2,1,0:T(8,128)(2,1)}, u32[]{:S(2)}) copy-start(bf16[1,256,1024]{2,1,0:T(8,128)(2,1)} %param.8) | copy-start | bytes 1572868
  0.7 21.5 %copy-start.2 = (bf16[1024,512]{1,0:T(8,128)(2,1)S(1)}, bf16[1024,512]{1,0:T(8,128)(2,1)}, u32[]{:S(2)}) copy-start(bf16[1024,512]{1,0:T(8,128)(2,1)} %param.10) | copy-start | bytes 3145732
  0.7 22.0 %copy-start.5 = (bf16[1,256,512]{2,1,0:T(8,128)(2,1)S(1)}, bf16[1,256,512]{2,1,0:T(8,128)(2,1)}, u32[]{:S(2)}) copy-start(bf16[1,256,512]{2,1,0:T(8,128)(2,1)} %param.11) | copy-start | bytes 786436
  4.4 28.5 %copy-start.3 = (bf16[256,1024]{1,0:T(8,128)(2,1)}, bf16[256,1024]{1,0:T(8,128)(2,1)S(1)}, u32[]{:S(2)}) copy-start(bf16[256,1024]{1,0:T(8,128)(2,1)S(1)} %pad_maximum_fusion.refs_0_.refs_1_) | copy-start | bytes 1572868
  4.4 27.8 %copy-start.8 = (s32[1,128]{1,0:T(1,128)S(1)}, s32[1,128]{1,0:T(1,128)}, u32[]{:S(2)}) copy-start(s32[1,128]{1,0:T(1,128)} %param.15) | copy-start | bytes 1540
  4.4 28.5 %copy-start.7 = (s32[1,32]{1,0:T(1,128)S(1)}, s32[1,32]{1,0:T(1,128)}, u32[]{:S(2)}) copy-start(s32[1,32]{1,0:T(1,128)} %param.13) | copy-start | bytes 388
  4.4 29.0 %collective-permute-start = (bf16[256,1024]{1,0:T(8,128)(2,1)S(1)}, bf16[256,1024]{1,0:T(8,128)(2,1)}, u32[]{:S(2)}, u32[]{:S(2)}) collective-permute-start(bf16[256,1024]{1,0:T(8,128)(2,1)S(1)} %pad_maximum_fusion.refs_0_.refs_1_), channel_id=1, source_target_pairs={{0,63},{1,0},{2,1},{3,2},{4,3},{5,4},{6,5},{7,6},{8,7},{9,8},{10,9... | collective-permute-start | bytes 1572872 | tf_op jit(solution)/shard_map/ppermute | solution.py:18
  7.3 40.3 %collective-permute-start.1 = (bf16[256,1024]{1,0:T(8,128)(2,1)S(1)}, bf16[256,1024]{1,0:T(8,128)(2,1)}, u32[]{:S(2)}, u32[]{:S(2)}) collective-permute-start(bf16[256,1024]{1,0:T(8,128)(2,1)S(1)} %pad_maximum_fusion.refs_0_.refs_1_), channel_id=1, source_target_pairs={{0,62},{1,63},{2,0},{3,1},{4,2},{5,3},{6,4},{7,5},{8,6},{9,7},{10,... | collective-permute-start | bytes 1572872 | tf_op jit(solution)/shard_map/ppermute | solution.py:18
  20.3 29.2 %collective-permute-start.2 = (bf16[256,1024]{1,0:T(8,128)(2,1)S(1)}, bf16[256,1024]{1,0:T(8,128)(2,1)}, u32[]{:S(2)}, u32[]{:S(2)}) collective-permute-start(bf16[256,1024]{1,0:T(8,128)(2,1)S(1)} %pad_maximum_fusion.refs_0_.refs_1_), channel_id=1, source_target_pairs={{0,61},{1,62},{2,63},{3,0},{4,1},{5,2},{6,3},{7,4},{8,5},{9,6},{10... | collective-permute-start | bytes 1572872 | tf_op jit(solution)/shard_map/ppermute | solution.py:18
  22.7 35.2 %copy-start.4 = (bf16[256,1024]{1,0:T(8,128)(2,1)}, bf16[256,1024]{1,0:T(8,128)(2,1)S(1)}, u32[]{:S(2)}) copy-start(bf16[256,1024]{1,0:T(8,128)(2,1)S(1)} %pad_maximum_fusion.1.refs_8_.refs_9_) | copy-start | bytes 1572868
  22.7 26.8 %collective-permute-start.3 = (bf16[256,1024]{1,0:T(8,128)(2,1)S(1)}, bf16[256,1024]{1,0:T(8,128)(2,1)}, u32[]{:S(2)}, u32[]{:S(2)}) collective-permute-start(bf16[256,1024]{1,0:T(8,128)(2,1)S(1)} %pad_maximum_fusion.1.refs_8_.refs_9_), channel_id=1, source_target_pairs={{0,1},{1,2},{2,3},{3,4},{4,5},{5,6},{6,7},{7,8},{8,9},{9,10},{10,1... | collective-permute-start | bytes 1572872 | tf_op jit(solution)/shard_map/ppermute | solution.py:18
  26.2 23.3 %collective-permute-start.4 = (bf16[256,1024]{1,0:T(8,128)(2,1)S(1)}, bf16[256,1024]{1,0:T(8,128)(2,1)}, u32[]{:S(2)}, u32[]{:S(2)}) collective-permute-start(bf16[256,1024]{1,0:T(8,128)(2,1)S(1)} %pad_maximum_fusion.1.refs_8_.refs_9_), channel_id=1, source_target_pairs={{0,2},{1,3},{2,4},{3,5},{4,6},{5,7},{6,8},{7,9},{8,10},{9,11},{10,... | collective-permute-start | bytes 1572872 | tf_op jit(solution)/shard_map/ppermute | solution.py:18
  33.4 24.5 %collective-permute-start.5 = (bf16[256,1024]{1,0:T(8,128)(2,1)S(1)}, bf16[256,1024]{1,0:T(8,128)(2,1)}, u32[]{:S(2)}, u32[]{:S(2)}) collective-permute-start(bf16[256,1024]{1,0:T(8,128)(2,1)S(1)} %pad_maximum_fusion.1.refs_8_.refs_9_), channel_id=1, source_target_pairs={{0,3},{1,4},{2,5},{3,6},{4,7},{5,8},{6,9},{7,10},{8,11},{9,12},{10... | collective-permute-start | bytes 1572872 | tf_op jit(solution)/shard_map/ppermute | solution.py:18
  35.4 22.5 %copy-start.6 = (s32[21,256]{1,0:T(8,128)}, s32[21,256]{1,0:T(8,128)S(1)}, u32[]{:S(2)}) copy-start(s32[21,256]{1,0:T(8,128)S(1)} %stack.45.infor) | copy-start | bytes 64516
  47.6 27.1 %collective-permute-start.6 = (bf16[256,1024]{0,1:T(8,128)(2,1)S(1)}, bf16[256,1024]{0,1:T(8,128)(2,1)S(1)}, u32[]{:S(2)}, u32[]{:S(2)}) collective-permute-start(bf16[256,1024]{0,1:T(8,128)(2,1)S(1)} %bitcast.54), channel_id=1, source_target_pairs={{0,1},{1,0},{2,3},{3,2},{4,5},{5,4},{6,7},{7,6},{8,9},{9,8},{10,11... | collective-permute-start | bytes 1572872 | tf_op jit(solution)/shard_map/ppermute | solution.py:23
  72.7 3.8 %collective-permute-start.7 = (bf16[256,1024]{1,0:T(8,128)(2,1)S(1)}, bf16[256,1024]{1,0:T(8,128)(2,1)S(1)}, u32[]{:S(2)}, u32[]{:S(2)}) collective-permute-start(bf16[256,1024]{1,0:T(8,128)(2,1)S(1)} %constant_dynamic-update-slice_fusion), channel_id=1, source_target_pairs={{0,1},{1,0},{2,3},{3,2},{4,5},{5,4},{6,7},{7,6},{8,9},{9,8},{10,11... | collective-permute-start | bytes 1572872 | tf_op jit(solution)/shard_map/ppermute | solution.py:23

commit v7 on v6

--- a/solution.py
+++ b/solution.py
@@ -30,80 +30,99 @@
     )
 
 
-def reduce_kernel(groups, spread, part_ref, out_ref, sent, landed, dp_landed, send_a, recv_a, send_b, recv_b):
-    count = lax.axis_size("ctx")
+def reduce_kernel(groups, spread, part_ref, out_ref, sent, landed, sums, mixed, finals, sems):
     me = lax.axis_index("ctx")
     group = lax.axis_index("dp")
     core = me % 2
     slot = me // 2
+    mesh_id = pl.DeviceIdType.MESH
     barrier = pltpu.get_barrier_semaphore()
     for step in range(1, groups):
         peer = 2 * ((slot + step) % groups) + core
-        pl.semaphore_signal(barrier, inc=1, device_id=(group, peer), device_id_type=pl.DeviceIdType.MESH)
-    for step in range(1, spread):
-        pl.semaphore_signal(
-            barrier, inc=1, device_id=((group + step) % spread, me), device_id_type=pl.DeviceIdType.MESH
-        )
+        pl.semaphore_signal(barrier, inc=1, device_id=(group, peer), device_id_type=mesh_id)
+    for step in range(1, spread):
+        pl.semaphore_signal(barrier, inc=1, device_id=((group + step) % spread, me), device_id_type=mesh_id)
     pl.semaphore_wait(barrier, groups - 1 + spread - 1)
     sent[...] = part_ref[...].astype(sent.dtype)
+    copies = []
+    for step in range(1, spread):
+        target = (group + step) % spread
+        copy = pltpu.make_async_remote_copy(
+            src_ref=sent.at[target],
+            dst_ref=landed.at[group],
+            send_sem=sems.at[0, step - 1],
+            recv_sem=sems.at[1, step - 1],
+            device_id=(target, me),
+            device_id_type=mesh_id,
+        )
+        copy.start()
+        copies.append(copy)
+    for copy in copies:
+        copy.wait()
+    total = part_ref[group]
+    for step in range(1, spread):
+        total = total + landed[(group + spread - step) % spread].astype(jnp.float32)
+    sums[...] = total.astype(sums.dtype)
     copies = []
     for step in range(1, groups):
         target = (slot + step) % groups
         copy = pltpu.make_async_remote_copy(
-            src_ref=sent.at[target],
-            dst_ref=landed.at[slot],
-            send_sem=send_a.at[step - 1],
-            recv_sem=recv_a.at[step - 1],
+            src_ref=sums.at[target],
+            dst_ref=mixed.at[slot],
+            send_sem=sems.at[2, step - 1],
+            recv_sem=sems.at[3, step - 1],
             device_id=(group, 2 * target + core),
-            device_id_type=pl.DeviceIdType.MESH,
+            device_id_type=mesh_id,
         )
         copy.start()
         copies.append(copy)
     for copy in copies:
         copy.wait()
-    total = part_ref[slot]
+    result = part_ref[group, slot]
+    for step in range(1, spread):
+        result = result + landed[(group + spread - step) % spread, slot].astype(jnp.float32)
     for step in range(1, groups):
-        total = total + landed[(slot + groups - step) % groups].astype(jnp.float32)
-    dp_landed[group] = total
+        result = result + mixed[(slot + groups - step) % groups].astype(jnp.float32)
+    finals[group] = result
     copies = []
     for step in range(1, spread):
+        target = (group + step) % spread
         copy = pltpu.make_async_remote_copy(
-            src_ref=dp_landed.at[group],
-            dst_ref=dp_landed.at[group],
-            send_sem=send_b.at[step - 1],
-            recv_sem=recv_b.at[step - 1],
-            device_id=((group + step) % spread, me),
-            device_id_type=pl.DeviceIdType.MESH,
+            src_ref=finals.at[group],
+            dst_ref=finals.at[group],
+            send_sem=sems.at[4, step - 1],
+            recv_sem=sems.at[5, step - 1],
+            device_id=(target, me),
+            device_id_type=mesh_id,
         )
         copy.start()
         copies.append(copy)
     for copy in copies:
         copy.wait()
-    result = dp_landed[0]
-    for index in range(1, spread):
-        result = result + dp_landed[index]
-    out_ref[...] = result
+    out_ref[...] = finals[...]
 
 
 def reduce_blocks(part, spread):
     groups, share, width = part.shape
+    lanes = width // spread
+    part = part.reshape(groups, share, spread, lanes).transpose(2, 0, 1, 3)
     vmem = pl.BlockSpec(memory_space=pltpu.VMEM)
-    return pl.pallas_call(
+    finals = pl.pallas_call(
         functools.partial(reduce_kernel, groups, spread),
         in_specs=[vmem],
         out_specs=vmem,
-        out_shape=jax.ShapeDtypeStruct((share, width), jnp.float32),
+        out_shape=jax.ShapeDtypeStruct((spread, share, lanes), jnp.float32),
         scratch_shapes=[
-            pltpu.VMEM((groups, share, width), jnp.bfloat16),
-            pltpu.VMEM((groups, share, width), jnp.bfloat16),
-            pltpu.VMEM((spread, share, width), jnp.float32),
-            pltpu.SemaphoreType.DMA((groups - 1,)),
-            pltpu.SemaphoreType.DMA((groups - 1,)),
-            pltpu.SemaphoreType.DMA((spread - 1,)),
-            pltpu.SemaphoreType.DMA((spread - 1,)),
+            pltpu.VMEM((spread, groups, share, lanes), jnp.bfloat16),
+            pltpu.VMEM((spread, groups, share, lanes), jnp.bfloat16),
+            pltpu.VMEM((groups, share, lanes), jnp.bfloat16),
+            pltpu.VMEM((groups, share, lanes), jnp.bfloat16),
+            pltpu.VMEM((spread, share, lanes), jnp.float32),
+            pltpu.SemaphoreType.DMA((6, max(groups, spread))),
         ],
         compiler_params=pltpu.CompilerParams(collective_id=1, has_side_effects=True),
     )(part)
+    return finals.transpose(1, 0, 2).reshape(share, width)
 
 
 def reduce_rows(local, partner_events, joined, myself, cycle_size):

time: 156 us -> 133 us (0.85)
  Pallas kernels: 88 us -> 60.3 us
    pallas_call x1, Pallas kernels: 75.2 us -> 47.5 us  [reduce_blocks(): pl.pallas_call(functools.partial(reduce_kernel, groups, spread), in_specs...]
    ppermute x6, waiting for transfers between devices: 19.8 us -> 22 us  [shifted(): return lax.ppermute(value, axis, pairs)]
    ppermute x2, waiting for transfers between devices: 1.85 us -> 0.17 us  [exchange(): lax.ppermute(value, axis, [(source, source ^ mask) for source in range(co...]
    unnamed x20 -> x22, local copies, waits for them, and re-layouts: 2.41 us -> 3.21 us
  transfers between devices with their start and end apart: 8 -> 8, of which waited for: 3 -> 3; matrix products, arithmetic and copies ran while one was open for 3% -> 4% of each run, Pallas kernels for 8% -> 0%
where the time goes in v7:
time: 133 us; the launch traced here: 132 us
  Pallas kernels  60.3 us (45%)
  starting transfers between devices  32.2 us (24%)
  waiting for transfers between devices  22.1 us (17%)
  local copies, waits for them, and re-layouts  6.29 us (5%)
  matrix products  5.03 us (4%)
  other arithmetic  4.11 us (3%)
  between operations  1.77 us (1%)
    pallas_call x1, Pallas kernels, reduce_blocks(): pl.pallas_call(functools.partial(reduce_kernel, groups, spread), in_specs...  47.5 us
    ppermute x6, starting transfers between devices, shifted(): return lax.ppermute(value, axis, pairs)  27.9 us
    ppermute x6, waiting for transfers between devices, shifted(): return lax.ppermute(value, axis, pairs)  22 us
    pallas_call x1, Pallas kernels, attention_tiles(): pl.pallas_call(functools.partial(tiles_kernel, span, alpha, scale), grid=...  12.8 us
    ppermute x2, starting transfers between devices, exchange(): lax.ppermute(value, axis, [(source, source ^ mask) for source in range(co...  4.32 us
    unnamed x22, local copies, waits for them, and re-layouts  3.21 us
    dot_general x1, matrix products, reduce_rows(): acc = jnp.dot(kept.T, both_joined, preferred_element_type=jnp.float32)  3.13 us
  transfers between devices with their start and end apart: 8, of which 3 were waited for; matrix products, arithmetic and copies ran while one was open for 4% of the time, Pallas kernels for 0%

profile of v7, /device:TPU:6, one launch (start us, length us, event | category | flops | bytes accessed | tf_op | source)
XLA Modules:
  0.0 131.9 jit_solution(2741532671409482122)
XLA Ops:
  0.7 1.2 copy-done
  1.9 1.5 %convolution_convert_fusion.1 = bf16[256,512]{1,0:T(8,128)(2,1)S(1)} fusion(bf16[1024,512]{1,0:T(8,128)(2,1)S(1)} %copy-done, bf16[1,256,1024]{2,1,0:T(8,128)(2,1)} %param.8), kind=kOutput, calls=%fused_computation.2 | convolution fusion | flops 268566528 | bytes 1835008 | tf_op jit(solution)/shard_map/dot_general | solution.py:255
  3.4 1.0 pad_maximum_fusion.refs_0_.refs_1_
  4.4 2.8 %collective-permute-start = (bf16[256,1024]{1,0:T(8,128)(2,1)S(1)}, bf16[256,1024]{1,0:T(8,128)(2,1)S(1)}, u32[]{:S(2)}, u32[]{:S(2)}) collective-permute-start(bf16[256,1024]{1,0:T(8,128)(2,1)S(1)} %pad_maximum_fusion.refs_0_.refs_1_), channel_id=1, source_target_pairs={{0,63},{1,0},{2,1},{3,2},{4,3},{5,4},{6,5},{7,6},{8,7},{9,8},{10,9... | collective-permute-start | bytes 1572872 | tf_op jit(solution)/shard_map/ppermute | solution.py:18
  7.2 13.0 %collective-permute-start.1 = (bf16[256,1024]{1,0:T(8,128)(2,1)S(1)}, bf16[256,1024]{1,0:T(8,128)(2,1)}, u32[]{:S(2)}, u32[]{:S(2)}) collective-permute-start(bf16[256,1024]{1,0:T(8,128)(2,1)S(1)} %pad_maximum_fusion.refs_0_.refs_1_), channel_id=1, source_target_pairs={{0,62},{1,63},{2,0},{3,1},{4,2},{5,3},{6,4},{7,5},{8,6},{9,7},{10,... | collective-permute-start | bytes 1572872 | tf_op jit(solution)/shard_map/ppermute | solution.py:18
  20.1 1.9 %collective-permute-start.2 = (bf16[256,1024]{1,0:T(8,128)(2,1)S(1)}, bf16[256,1024]{1,0:T(8,128)(2,1)}, u32[]{:S(2)}, u32[]{:S(2)}) collective-permute-start(bf16[256,1024]{1,0:T(8,128)(2,1)S(1)} %pad_maximum_fusion.refs_0_.refs_1_), channel_id=1, source_target_pairs={{0,61},{1,62},{2,63},{3,0},{4,1},{5,2},{6,3},{7,4},{8,5},{9,6},{10... | collective-permute-start | bytes 1572872 | tf_op jit(solution)/shard_map/ppermute | solution.py:18
  22.6 3.4 %collective-permute-start.3 = (bf16[256,1024]{1,0:T(8,128)(2,1)S(1)}, bf16[256,1024]{1,0:T(8,128)(2,1)}, u32[]{:S(2)}, u32[]{:S(2)}) collective-permute-start(bf16[256,1024]{1,0:T(8,128)(2,1)S(1)} %pad_maximum_fusion.1.refs_8_.refs_9_), channel_id=1, source_target_pairs={{0,1},{1,2},{2,3},{3,4},{4,5},{5,6},{6,7},{7,8},{8,9},{9,10},{10,1... | collective-permute-start | bytes 1572872 | tf_op jit(solution)/shard_map/ppermute | solution.py:18
  26.0 4.9 %collective-permute-start.4 = (bf16[256,1024]{1,0:T(8,128)(2,1)S(1)}, bf16[256,1024]{1,0:T(8,128)(2,1)}, u32[]{:S(2)}, u32[]{:S(2)}) collective-permute-start(bf16[256,1024]{1,0:T(8,128)(2,1)S(1)} %pad_maximum_fusion.1.refs_8_.refs_9_), channel_id=1, source_target_pairs={{0,2},{1,3},{2,4},{3,5},{4,6},{5,7},{6,8},{7,9},{8,10},{9,11},{10,... | collective-permute-start | bytes 1572872 | tf_op jit(solution)/shard_map/ppermute | solution.py:18
  31.8 0.6 select_reduce_fusion
  33.0 1.9 %collective-permute-start.5 = (bf16[256,1024]{1,0:T(8,128)(2,1)S(1)}, bf16[256,1024]{1,0:T(8,128)(2,1)}, u32[]{:S(2)}, u32[]{:S(2)}) collective-permute-start(bf16[256,1024]{1,0:T(8,128)(2,1)S(1)} %pad_maximum_fusion.1.refs_8_.refs_9_), channel_id=1, source_target_pairs={{0,3},{1,4},{2,5},{3,6},{4,7},{5,8},{6,9},{7,10},{8,11},{9,12},{10... | collective-permute-start | bytes 1572872 | tf_op jit(solution)/shard_map/ppermute | solution.py:18
  35.0 0.8 copy.26.infoc
  35.8 11.6 %collective-permute-done.1.refs_4_.refs_5_ = bf16[256,1024]{1,0:T(8,128)(2,1)} collective-permute-done((bf16[256,1024]{1,0:T(8,128)(2,1)S(1)}, bf16[256,1024]{1,0:T(8,128)(2,1)}, u32[]{:S(2)}, u32[]{:S(2)}) %collective-permute-start.1) | collective-permute-done | bytes 524320 | tf_op jit(solution)/shard_map/ppermute | solution.py:18
  47.4 10.3 %collective-permute-done.5.refs_14_.refs_15_ = bf16[256,1024]{1,0:T(8,128)(2,1)} collective-permute-done((bf16[256,1024]{1,0:T(8,128)(2,1)S(1)}, bf16[256,1024]{1,0:T(8,128)(2,1)}, u32[]{:S(2)}, u32[]{:S(2)}) %collective-permute-start.5) | collective-permute-done | bytes 524320 | tf_op jit(solution)/shard_map/ppermute | solution.py:18
  57.8 12.8 %shard_map.111 = (bf16[256,512]{1,0:T(8,128)(2,1)}, bf16[256,512]{1,0:T(8,128)(2,1)}, bf16[256,512]{1,0:T(8,128)(2,1)}, bf16[256,512]{1,0:T(8,128)(2,1)}) custom-call(s32[256,21]{1,0:T(8,128)} %copy.26.infoc, s32[21,256]{1,0:T(8,128)} %copy-done.6, bf16[256,1024]{1,0:T(8,128)(2,1)} %copy-done.3, bf16[256,1024]{1,0:T(8,128)(2,1)} %copy-done.3, ...), custom_call_target="tpu_custom_call" | custom-call | flops 2348810240 | bytes 9437184 | tf_op jit(solution)/shard_map/pallas_call | solution.py:207
  70.6 1.0 constant_dynamic-update-slice_fusion.1
  71.6 1.0 constant_dynamic-update-slice_fusion
  72.6 1.9 %collective-permute-start.7 = (bf16[256,1024]{1,0:T(8,128)(2,1)S(1)}, bf16[256,1024]{1,0:T(8,128)(2,1)}, u32[]{:S(2)}, u32[]{:S(2)}) collective-permute-start(bf16[256,1024]{1,0:T(8,128)(2,1)S(1)} %constant_dynamic-update-slice_fusion), channel_id=1, source_target_pairs={{0,1},{1,0},{2,3},{3,2},{4,5},{5,4},{6,7},{7,6},{8,9},{9,8},{10,11... | collective-permute-start | bytes 1572872 | tf_op jit(solution)/shard_map/ppermute | solution.py:23
  74.5 1.0 copy.25
  75.5 2.4 %collective-permute-start.6 = (bf16[256,1024]{0,1:T(8,128)(2,1)}, bf16[256,1024]{0,1:T(8,128)(2,1)}, u32[]{:S(2)}, u32[]{:S(2)}) collective-permute-start(bf16[256,1024]{0,1:T(8,128)(2,1)} %bitcast.18), channel_id=1, source_target_pairs={{0,1},{1,0},{2,3},{3,2},{4,5},{5,4},{6,7},{7,6},{8,9},{9,8},{10,11... | collective-permute-start | bytes 1572872 | tf_op jit(solution)/shard_map/ppermute | solution.py:23
  78.0 1.1 maximum_bitcast_fusion
  79.8 3.1 %convolution_bitcast_fusion.part_ref = f32[8,32,16,128]{3,2,1,0:T(8,128)} fusion(bf16[8,128,512,1]{2,1,3,0:T(8,128)(2,1)S(1)} %bitcast.69, s32[]{:T(128)S(6)} %select_n.290, bf16[256,32,2,16]{0,3,2,1:T(8,128)(2,1)} %bitcast.23, bf16[256,32,2,16]{0,3,2,1:T(8,128)(2,1)} %bitcast.24), kind=kOutput, calls=%fused_computation | convolution fusion | flops 537919488 | bytes 4194308 | tf_op jit(solution)/shard_map/dot_general | solution.py:137
  82.9 47.5 %shard_map.112 = f32[8,16,128]{2,1,0:T(8,128)} custom-call(f32[8,32,16,128]{3,2,1,0:T(8,128)} %convolution_bitcast_fusion.part_ref), custom_call_target="tpu_custom_call" | custom-call | tf_op jit(solution)/shard_map/pallas_call | solution.py:110
  130.4 0.8 copy_bitcast_fusion
  131.3 0.6 fusion.21
  (51 shorter events, 1.9 us)
Async XLA Ops:
  0.6 1.2 copy-start
  0.6 21.4 %copy-start.1 = (bf16[1,256,1024]{2,1,0:T(8,128)(2,1)S(1)}, bf16[1,256,1024]{2,1,0:T(8,128)(2,1)}, u32[]{:S(2)}) copy-start(bf16[1,256,1024]{2,1,0:T(8,128)(2,1)} %param.8) | copy-start | bytes 1572868
  0.7 21.4 %copy-start.2 = (bf16[1024,512]{1,0:T(8,128)(2,1)S(1)}, bf16[1024,512]{1,0:T(8,128)(2,1)}, u32[]{:S(2)}) copy-start(bf16[1024,512]{1,0:T(8,128)(2,1)} %param.10) | copy-start | bytes 3145732
  0.7 21.9 %copy-start.5 = (bf16[1,256,512]{2,1,0:T(8,128)(2,1)S(1)}, bf16[1,256,512]{2,1,0:T(8,128)(2,1)}, u32[]{:S(2)}) copy-start(bf16[1,256,512]{2,1,0:T(8,128)(2,1)} %param.11) | copy-start | bytes 786436
  3.3 28.5 %copy-start.8 = (s32[1,128]{1,0:T(1,128)S(1)}, s32[1,128]{1,0:T(1,128)}, u32[]{:S(2)}) copy-start(s32[1,128]{1,0:T(1,128)} %param.15) | copy-start | bytes 1540
  3.4 29.1 %copy-start.7 = (s32[1,32]{1,0:T(1,128)S(1)}, s32[1,32]{1,0:T(1,128)}, u32[]{:S(2)}) copy-start(s32[1,32]{1,0:T(1,128)} %param.13) | copy-start | bytes 388
  4.4 53.4 %copy-start.3 = (bf16[256,1024]{1,0:T(8,128)(2,1)}, bf16[256,1024]{1,0:T(8,128)(2,1)S(1)}, u32[]{:S(2)}) copy-start(bf16[256,1024]{1,0:T(8,128)(2,1)S(1)} %pad_maximum_fusion.refs_0_.refs_1_) | copy-start | bytes 1572868
  4.4 28.6 %collective-permute-start = (bf16[256,1024]{1,0:T(8,128)(2,1)S(1)}, bf16[256,1024]{1,0:T(8,128)(2,1)S(1)}, u32[]{:S(2)}, u32[]{:S(2)}) collective-permute-start(bf16[256,1024]{1,0:T(8,128)(2,1)S(1)} %pad_maximum_fusion.refs_0_.refs_1_), channel_id=1, source_target_pairs={{0,63},{1,0},{2,1},{3,2},{4,3},{5,4},{6,5},{7,6},{8,7},{9,8},{10,9... | collective-permute-start | bytes 1572872 | tf_op jit(solution)/shard_map/ppermute | solution.py:18
  7.2 40.3 %collective-permute-start.1 = (bf16[256,1024]{1,0:T(8,128)(2,1)S(1)}, bf16[256,1024]{1,0:T(8,128)(2,1)}, u32[]{:S(2)}, u32[]{:S(2)}) collective-permute-start(bf16[256,1024]{1,0:T(8,128)(2,1)S(1)} %pad_maximum_fusion.refs_0_.refs_1_), channel_id=1, source_target_pairs={{0,62},{1,63},{2,0},{3,1},{4,2},{5,3},{6,4},{7,5},{8,6},{9,7},{10,... | collective-permute-start | bytes 1572872 | tf_op jit(solution)/shard_map/ppermute | solution.py:18
  20.1 27.3 %collective-permute-start.2 = (bf16[256,1024]{1,0:T(8,128)(2,1)S(1)}, bf16[256,1024]{1,0:T(8,128)(2,1)}, u32[]{:S(2)}, u32[]{:S(2)}) collective-permute-start(bf16[256,1024]{1,0:T(8,128)(2,1)S(1)} %pad_maximum_fusion.refs_0_.refs_1_), channel_id=1, source_target_pairs={{0,61},{1,62},{2,63},{3,0},{4,1},{5,2},{6,3},{7,4},{8,5},{9,6},{10... | collective-permute-start | bytes 1572872 | tf_op jit(solution)/shard_map/ppermute | solution.py:18
  22.6 35.2 %copy-start.4 = (bf16[256,1024]{1,0:T(8,128)(2,1)}, bf16[256,1024]{1,0:T(8,128)(2,1)S(1)}, u32[]{:S(2)}) copy-start(bf16[256,1024]{1,0:T(8,128)(2,1)S(1)} %pad_maximum_fusion.1.refs_8_.refs_9_) | copy-start | bytes 1572868
  22.6 24.8 %collective-permute-start.3 = (bf16[256,1024]{1,0:T(8,128)(2,1)S(1)}, bf16[256,1024]{1,0:T(8,128)(2,1)}, u32[]{:S(2)}, u32[]{:S(2)}) collective-permute-start(bf16[256,1024]{1,0:T(8,128)(2,1)S(1)} %pad_maximum_fusion.1.refs_8_.refs_9_), channel_id=1, source_target_pairs={{0,1},{1,2},{2,3},{3,4},{4,5},{5,6},{6,7},{7,8},{8,9},{9,10},{10,1... | collective-permute-start | bytes 1572872 | tf_op jit(solution)/shard_map/ppermute | solution.py:18
  26.0 21.4 %collective-permute-start.4 = (bf16[256,1024]{1,0:T(8,128)(2,1)S(1)}, bf16[256,1024]{1,0:T(8,128)(2,1)}, u32[]{:S(2)}, u32[]{:S(2)}) collective-permute-start(bf16[256,1024]{1,0:T(8,128)(2,1)S(1)} %pad_maximum_fusion.1.refs_8_.refs_9_), channel_id=1, source_target_pairs={{0,2},{1,3},{2,4},{3,5},{4,6},{5,7},{6,8},{7,9},{8,10},{9,11},{10,... | collective-permute-start | bytes 1572872 | tf_op jit(solution)/shard_map/ppermute | solution.py:18
  33.0 24.8 %copy-start.9 = (bf16[256,1024]{1,0:T(8,128)(2,1)}, bf16[256,1024]{1,0:T(8,128)(2,1)S(1)}, u32[]{:S(2)}) copy-start(bf16[256,1024]{1,0:T(8,128)(2,1)S(1)} %collective-permute-done.refs_2_.refs_3_) | copy-start | bytes 1572868
  33.0 24.8 %collective-permute-start.5 = (bf16[256,1024]{1,0:T(8,128)(2,1)S(1)}, bf16[256,1024]{1,0:T(8,128)(2,1)}, u32[]{:S(2)}, u32[]{:S(2)}) collective-permute-start(bf16[256,1024]{1,0:T(8,128)(2,1)S(1)} %pad_maximum_fusion.1.refs_8_.refs_9_), channel_id=1, source_target_pairs={{0,3},{1,4},{2,5},{3,6},{4,7},{5,8},{6,9},{7,10},{8,11},{9,12},{10... | collective-permute-start | bytes 1572872 | tf_op jit(solution)/shard_map/ppermute | solution.py:18
  35.0 22.8 %copy-start.6 = (s32[21,256]{1,0:T(8,128)}, s32[21,256]{1,0:T(8,128)S(1)}, u32[]{:S(2)}) copy-start(s32[21,256]{1,0:T(8,128)S(1)} %stack.45.infor) | copy-start | bytes 64516
  72.6 5.4 %collective-permute-start.7 = (bf16[256,1024]{1,0:T(8,128)(2,1)S(1)}, bf16[256,1024]{1,0:T(8,128)(2,1)}, u32[]{:S(2)}, u32[]{:S(2)}) collective-permute-start(bf16[256,1024]{1,0:T(8,128)(2,1)S(1)} %constant_dynamic-update-slice_fusion), channel_id=1, source_target_pairs={{0,1},{1,0},{2,3},{3,2},{4,5},{5,4},{6,7},{7,6},{8,9},{9,8},{10,11... | collective-permute-start | bytes 1572872 | tf_op jit(solution)/shard_map/ppermute | solution.py:23
  75.5 4.3 %collective-permute-start.6 = (bf16[256,1024]{0,1:T(8,128)(2,1)}, bf16[256,1024]{0,1:T(8,128)(2,1)}, u32[]{:S(2)}, u32[]{:S(2)}) collective-permute-start(bf16[256,1024]{0,1:T(8,128)(2,1)} %bitcast.18), channel_id=1, source_target_pairs={{0,1},{1,0},{2,3},{3,2},{4,5},{5,4},{6,7},{7,6},{8,9},{9,8},{10,11... | collective-permute-start | bytes 1572872 | tf_op jit(solution)/shard_map/ppermute | solution.py:23

commit v8 on v7

--- a/solution.py
+++ b/solution.py
@@ -21,6 +21,22 @@
 def exchange(value, axis, mask):
     count = lax.axis_size(axis)
     return lax.ppermute(value, axis, [(source, source ^ mask) for source in range(count)])
+
+
+def relayed(value, myself, sign):
+    count = lax.axis_size("ctx")
+    odd = myself % 2
+    pairs = []
+    for source in range(count):
+        step = 3 if (source % 2 == 1) == (sign > 0) else 1
+        pairs.append((source, (source + sign * step) % count))
+    far = shifted(value, "ctx", 2 * sign)
+    mixed = lax.ppermute(value, "ctx", pairs)
+    swapped = exchange(far, "ctx", 1)
+    lead = odd if sign > 0 else 1 - odd
+    mixed_anchor = myself - sign * (3 - 2 * lead)
+    swapped_anchor = myself - sign * (1 + 2 * lead)
+    return [None, far, mixed, swapped], [myself - 2 * sign, mixed_anchor, swapped_anchor]
 
 
 def pick(value, bit, axis):
@@ -172,17 +188,17 @@
         return dk, dv
 
     q0, g0, k0, v0 = qs[0][...], gs[0][...], ks[0][...], vs[0][...]
-    att, dsc = terms(q0, g0, k0, v0, valid(span, span))
+    att, dsc = terms(q0, g0, k0, v0, valid(0, 0))
     out = jnp.dot(att, v0, preferred_element_type=jnp.float32)
     dq = jnp.dot(dsc, k0, preferred_element_type=jnp.float32)
     dk, dv = back(att, dsc, q0, g0)
     for step in range(1, span + 1):
         k, v = ks[step][...], vs[step][...]
-        att, dsc = terms(q0, g0, k, v, valid(span, span - step))
+        att, dsc = terms(q0, g0, k, v, valid(0, step))
         out = out + jnp.dot(att, v, preferred_element_type=jnp.float32)
         dq = dq + jnp.dot(dsc, k, preferred_element_type=jnp.float32)
         q, g = qs[step][...], gs[step][...]
-        att, dsc = terms(q, g, k0, v0, valid(span + step, span))
+        att, dsc = terms(q, g, k0, v0, valid(span + step, 0))
         b, c = back(att, dsc, q, g)
         dk = dk + b
         dv = dv + c
@@ -289,11 +305,10 @@
     partner_events = exchange(local, "ctx", 1)
     kv = jnp.concatenate([keys, values[0]], axis=1)
     qg = jnp.concatenate([queries, grad_out[0]], axis=1)
-    kv_from = [None] + [shifted(kv, "ctx", step) for step in range(1, SPAN + 1)]
-    qg_from = [None] + [shifted(qg, "ctx", -step) for step in range(1, SPAN + 1)]
-
-    offsets = range(-SPAN, SPAN + 1)
-    described = [describe(myself + offset) for offset in offsets]
+    kv_from, kv_anchor = relayed(kv, myself, 1)
+    qg_from, qg_anchor = relayed(qg, myself, -1)
+
+    described = [describe(anchor) for anchor in [myself] + kv_anchor + qg_anchor]
     infor = jnp.stack(
         [d[0] for d in described] + [d[1] for d in described] + [d[2].astype(jnp.int32) for d in described]
     ).astype(jnp.int32)

time: 133 us -> 115 us (0.86)
  waiting for transfers between devices: 22.1 us -> 13.4 us
  starting transfers between devices: 32.2 us -> 25.1 us
  Pallas kernels: 60.3 us -> 58.1 us
    ppermute x6 -> x2, starting transfers between devices: 27.9 us -> 8.25 us  [shifted(): return lax.ppermute(value, axis, pairs)]
    ppermute x6 -> x2, waiting for transfers between devices: 22 us -> 8.08 us  [shifted(): return lax.ppermute(value, axis, pairs)]
    ppermute x0 -> x2, starting transfers between devices: none -> 8.69 us  [relayed(): mixed = lax.ppermute(value, 'ctx', pairs)]
    ppermute x0 -> x2, waiting for transfers between devices: none -> 5.18 us  [relayed(): mixed = lax.ppermute(value, 'ctx', pairs)]
    ppermute x2 -> x4, starting transfers between devices: 4.32 us -> 8.15 us  [exchange(): lax.ppermute(value, axis, [(source, source ^ mask) for source in range(co...]
    pallas_call x1, Pallas kernels: 47.5 us -> 45.2 us  [reduce_blocks(): pl.pallas_call(functools.partial(reduce_kernel, groups, spread), in_specs...]
  transfers between devices with their start and end apart: 8 -> 8, of which waited for: 3 -> 3; matrix products, arithmetic and copies ran while one was open for 4% -> 5% of each run, Pallas kernels for 0% -> 0%
where the time goes in v8:
time: 115 us; the launch traced here: 114 us
  Pallas kernels  58.1 us (51%)
  starting transfers between devices  25.1 us (22%)
  waiting for transfers between devices  13.4 us (12%)
  local copies, waits for them, and re-layouts  6.29 us (5%)
  matrix products  5.03 us (4%)
  other arithmetic  4.11 us (4%)
  between operations  1.78 us (2%)
    pallas_call x1, Pallas kernels, reduce_blocks(): pl.pallas_call(functools.partial(reduce_kernel, groups, spread), in_specs...  45.2 us
    pallas_call x1, Pallas kernels, attention_tiles(): pl.pallas_call(functools.partial(tiles_kernel, span, alpha, scale), grid=...  12.8 us
    ppermute x2, starting transfers between devices, relayed(): mixed = lax.ppermute(value, 'ctx', pairs)  8.69 us
    ppermute x2, starting transfers between devices, shifted(): return lax.ppermute(value, axis, pairs)  8.25 us
    ppermute x4, starting transfers between devices, exchange(): lax.ppermute(value, axis, [(source, source ^ mask) for source in range(co...  8.15 us
    ppermute x2, waiting for transfers between devices, shifted(): return lax.ppermute(value, axis, pairs)  8.08 us
    ppermute x2, waiting for transfers between devices, relayed(): mixed = lax.ppermute(value, 'ctx', pairs)  5.18 us
    unnamed x22, local copies, waits for them, and re-layouts  3.21 us
  transfers between devices with their start and end apart: 8, of which 3 were waited for; matrix products, arithmetic and copies ran while one was open for 5% of the time, Pallas kernels for 0%

profile of v8, /device:TPU:6, one launch (start us, length us, event | category | flops | bytes accessed | tf_op | source)
XLA Modules:
  0.0 113.8 jit_solution(819306901479671989)
XLA Ops:
  0.7 1.2 %copy-done = bf16[1024,512]{1,0:T(8,128)(2,1)S(1)} copy-done((bf16[1024,512]{1,0:T(8,128)(2,1)S(1)}, bf16[1024,512]{1,0:T(8,128)(2,1)}, u32[]{:S(2)}) %copy-start) | copy-done | bytes 1048600
  1.9 1.5 %convolution_convert_fusion.1 = bf16[256,512]{1,0:T(8,128)(2,1)S(1)} fusion(bf16[1024,512]{1,0:T(8,128)(2,1)S(1)} %copy-done, bf16[1,256,1024]{2,1,0:T(8,128)(2,1)} %param.8), kind=kOutput, calls=%fused_computation.2 | convolution fusion | flops 268566528 | bytes 1835008 | tf_op jit(solution)/shard_map/dot_general | solution.py:271
  3.4 1.0 pad_maximum_fusion.refs_0_.refs_1_
  4.4 3.3 %collective-permute-start = (bf16[256,1024]{1,0:T(8,128)(2,1)S(1)}, bf16[256,1024]{1,0:T(8,128)(2,1)S(1)}, u32[]{:S(2)}, u32[]{:S(2)}) collective-permute-start(bf16[256,1024]{1,0:T(8,128)(2,1)S(1)} %pad_maximum_fusion.refs_0_.refs_1_), channel_id=1, source_target_pairs={{0,62},{1,63},{2,0},{3,1},{4,2},{5,3},{6,4},{7,5},{8,6},{9,7},{10,... | collective-permute-start | bytes 1572872 | tf_op jit(solution)/shard_map/ppermute | solution.py:18
  7.7 8.7 %collective-permute-start.1 = (bf16[256,1024]{1,0:T(8,128)(2,1)S(1)}, bf16[256,1024]{1,0:T(8,128)(2,1)}, u32[]{:S(2)}, u32[]{:S(2)}) collective-permute-start(bf16[256,1024]{1,0:T(8,128)(2,1)S(1)} %pad_maximum_fusion.refs_0_.refs_1_), channel_id=1, source_target_pairs={{0,61},{1,0},{2,63},{3,2},{4,1},{5,4},{6,3},{7,6},{8,5},{9,8},{10,... | collective-permute-start | bytes 1572872 | tf_op jit(solution)/shard_map/ppermute | solution.py:34
  16.9 4.9 %collective-permute-start.3 = (bf16[256,1024]{1,0:T(8,128)(2,1)S(1)}, bf16[256,1024]{1,0:T(8,128)(2,1)}, u32[]{:S(2)}, u32[]{:S(2)}) collective-permute-start(bf16[256,1024]{1,0:T(8,128)(2,1)S(1)} %pad_maximum_fusion.1.refs_8_.refs_9_), channel_id=1, source_target_pairs={{0,2},{1,3},{2,4},{3,5},{4,6},{5,7},{6,8},{7,9},{8,10},{9,11},{10,... | collective-permute-start | bytes 1572872 | tf_op jit(solution)/shard_map/ppermute | solution.py:18
  22.7 0.6 select_reduce_fusion
  23.9 1.9 %collective-permute-start.2 = (bf16[256,1024]{1,0:T(8,128)(2,1)S(1)}, bf16[256,1024]{1,0:T(8,128)(2,1)}, u32[]{:S(2)}, u32[]{:S(2)}) collective-permute-start(bf16[256,1024]{1,0:T(8,128)(2,1)S(1)} %collective-permute-done.refs_2_.refs_3_), channel_id=1, source_target_pairs={{0,1},{1,0},{2,3},{3,2},{4,5},{5,4},{6,7},{7,6},{8,9},{9,8},{10,11... | collective-permute-start | bytes 1572872 | tf_op jit(solution)/shard_map/ppermute | solution.py:23
  25.8 8.1 %collective-permute-done.3.refs_10_.refs_11_ = bf16[256,1024]{1,0:T(8,128)(2,1)} collective-permute-done((bf16[256,1024]{1,0:T(8,128)(2,1)S(1)}, bf16[256,1024]{1,0:T(8,128)(2,1)}, u32[]{:S(2)}, u32[]{:S(2)}) %collective-permute-start.3) | collective-permute-done | bytes 524320 | tf_op jit(solution)/shard_map/ppermute | solution.py:18
  33.9 1.9 %collective-permute-start.5 = (bf16[256,1024]{1,0:T(8,128)(2,1)}, bf16[256,1024]{1,0:T(8,128)(2,1)}, u32[]{:S(2)}, u32[]{:S(2)}) collective-permute-start(bf16[256,1024]{1,0:T(8,128)(2,1)} %collective-permute-done.3.refs_10_.refs_11_), channel_id=1, source_target_pairs={{0,1},{1,0},{2,3},{3,2},{4,5},{5,4},{6,7},{7,6},{8,9},{9,8},{10,11... | collective-permute-start | bytes 1572872 | tf_op jit(solution)/shard_map/ppermute | solution.py:23
  36.0 0.8 copy.26.infoc
  36.7 5.2 %collective-permute-done.4.refs_12_.refs_13_ = bf16[256,1024]{1,0:T(8,128)(2,1)} collective-permute-done((bf16[256,1024]{1,0:T(8,128)(2,1)S(1)}, bf16[256,1024]{1,0:T(8,128)(2,1)}, u32[]{:S(2)}, u32[]{:S(2)}) %collective-permute-start.4) | collective-permute-done | bytes 524320 | tf_op jit(solution)/shard_map/ppermute | solution.py:34
  42.0 12.8 %shard_map.111 = (bf16[256,512]{1,0:T(8,128)(2,1)}, bf16[256,512]{1,0:T(8,128)(2,1)}, bf16[256,512]{1,0:T(8,128)(2,1)}, bf16[256,512]{1,0:T(8,128)(2,1)}) custom-call(s32[256,21]{1,0:T(8,128)} %copy.26.infoc, s32[21,256]{1,0:T(8,128)} %copy-done.6, bf16[256,1024]{1,0:T(8,128)(2,1)} %copy-done.3, bf16[256,1024]{1,0:T(8,128)(2,1)} %copy-done.3, ...), custom_call_target="tpu_custom_call" | custom-call | flops 2348810240 | bytes 9437184 | tf_op jit(solution)/shard_map/pallas_call | solution.py:223
  54.8 1.0 constant_dynamic-update-slice_fusion.1
  55.8 1.0 constant_dynamic-update-slice_fusion
  56.7 1.9 %collective-permute-start.7 = (bf16[256,1024]{1,0:T(8,128)(2,1)S(1)}, bf16[256,1024]{1,0:T(8,128)(2,1)}, u32[]{:S(2)}, u32[]{:S(2)}) collective-permute-start(bf16[256,1024]{1,0:T(8,128)(2,1)S(1)} %constant_dynamic-update-slice_fusion), channel_id=1, source_target_pairs={{0,1},{1,0},{2,3},{3,2},{4,5},{5,4},{6,7},{7,6},{8,9},{9,8},{10,11... | collective-permute-start | bytes 1572872 | tf_op jit(solution)/shard_map/ppermute | solution.py:23
  58.7 1.0 copy.25
  59.7 2.4 %collective-permute-start.6 = (bf16[256,1024]{0,1:T(8,128)(2,1)}, bf16[256,1024]{0,1:T(8,128)(2,1)}, u32[]{:S(2)}, u32[]{:S(2)}) collective-permute-start(bf16[256,1024]{0,1:T(8,128)(2,1)} %bitcast.18), channel_id=1, source_target_pairs={{0,1},{1,0},{2,3},{3,2},{4,5},{5,4},{6,7},{7,6},{8,9},{9,8},{10,11... | collective-permute-start | bytes 1572872 | tf_op jit(solution)/shard_map/ppermute | solution.py:23
  62.1 1.1 maximum_bitcast_fusion
  63.2 0.5 copy.31
  63.9 3.1 %convolution_bitcast_fusion.part_ref = f32[8,32,16,128]{3,2,1,0:T(8,128)} fusion(bf16[8,128,512,1]{2,1,3,0:T(8,128)(2,1)S(1)} %bitcast.69, s32[]{:T(128)S(6)} %select_n.294, bf16[256,32,2,16]{0,3,2,1:T(8,128)(2,1)} %bitcast.23, bf16[256,32,2,16]{0,3,2,1:T(8,128)(2,1)} %bitcast.24), kind=kOutput, calls=%fused_computation | convolution fusion | flops 537919488 | bytes 4194308 | tf_op jit(solution)/shard_map/dot_general | solution.py:153
  67.1 45.2 %shard_map.112 = f32[8,16,128]{2,1,0:T(8,128)} custom-call(f32[8,32,16,128]{3,2,1,0:T(8,128)} %convolution_bitcast_fusion.part_ref), custom_call_target="tpu_custom_call" | custom-call | tf_op jit(solution)/shard_map/pallas_call | solution.py:126
  112.3 0.8 copy_bitcast_fusion
  113.2 0.6 fusion.21
  (51 shorter events, 1.4 us)
Async XLA Ops:
  0.6 1.2 %copy-start = (bf16[1024,512]{1,0:T(8,128)(2,1)S(1)}, bf16[1024,512]{1,0:T(8,128)(2,1)}, u32[]{:S(2)}) copy-start(bf16[1024,512]{1,0:T(8,128)(2,1)} %param.9) | copy-start | bytes 3145732
  0.6 15.7 %copy-start.1 = (bf16[1,256,1024]{2,1,0:T(8,128)(2,1)S(1)}, bf16[1,256,1024]{2,1,0:T(8,128)(2,1)}, u32[]{:S(2)}) copy-start(bf16[1,256,1024]{2,1,0:T(8,128)(2,1)} %param.8) | copy-start | bytes 1572868
  0.7 15.7 %copy-start.2 = (bf16[1024,512]{1,0:T(8,128)(2,1)S(1)}, bf16[1024,512]{1,0:T(8,128)(2,1)}, u32[]{:S(2)}) copy-start(bf16[1024,512]{1,0:T(8,128)(2,1)} %param.10) | copy-start | bytes 3145732
  0.7 16.2 %copy-start.5 = (bf16[1,256,512]{2,1,0:T(8,128)(2,1)S(1)}, bf16[1,256,512]{2,1,0:T(8,128)(2,1)}, u32[]{:S(2)}) copy-start(bf16[1,256,512]{2,1,0:T(8,128)(2,1)} %param.11) | copy-start | bytes 786436
  3.3 19.4 %copy-start.8 = (s32[1,128]{1,0:T(1,128)S(1)}, s32[1,128]{1,0:T(1,128)}, u32[]{:S(2)}) copy-start(s32[1,128]{1,0:T(1,128)} %param.15) | copy-start | bytes 1540
  3.4 20.1 %copy-start.7 = (s32[1,32]{1,0:T(1,128)S(1)}, s32[1,32]{1,0:T(1,128)}, u32[]{:S(2)}) copy-start(s32[1,32]{1,0:T(1,128)} %param.13) | copy-start | bytes 388
  4.4 37.5 %copy-start.3 = (bf16[256,1024]{1,0:T(8,128)(2,1)}, bf16[256,1024]{1,0:T(8,128)(2,1)S(1)}, u32[]{:S(2)}) copy-start(bf16[256,1024]{1,0:T(8,128)(2,1)S(1)} %pad_maximum_fusion.refs_0_.refs_1_) | copy-start | bytes 1572868
  4.4 19.5 %collective-permute-start = (bf16[256,1024]{1,0:T(8,128)(2,1)S(1)}, bf16[256,1024]{1,0:T(8,128)(2,1)S(1)}, u32[]{:S(2)}, u32[]{:S(2)}) collective-permute-start(bf16[256,1024]{1,0:T(8,128)(2,1)S(1)} %pad_maximum_fusion.refs_0_.refs_1_), channel_id=1, source_target_pairs={{0,62},{1,63},{2,0},{3,1},{4,2},{5,3},{6,4},{7,5},{8,6},{9,7},{10,... | collective-permute-start | bytes 1572872 | tf_op jit(solution)/shard_map/ppermute | solution.py:18
  7.7 29.0 %collective-permute-start.1 = (bf16[256,1024]{1,0:T(8,128)(2,1)S(1)}, bf16[256,1024]{1,0:T(8,128)(2,1)}, u32[]{:S(2)}, u32[]{:S(2)}) collective-permute-start(bf16[256,1024]{1,0:T(8,128)(2,1)S(1)} %pad_maximum_fusion.refs_0_.refs_1_), channel_id=1, source_target_pairs={{0,61},{1,0},{2,63},{3,2},{4,1},{5,4},{6,3},{7,6},{8,5},{9,8},{10,... | collective-permute-start | bytes 1572872 | tf_op jit(solution)/shard_map/ppermute | solution.py:34
  16.9 25.0 %copy-start.4 = (bf16[256,1024]{1,0:T(8,128)(2,1)}, bf16[256,1024]{1,0:T(8,128)(2,1)S(1)}, u32[]{:S(2)}) copy-start(bf16[256,1024]{1,0:T(8,128)(2,1)S(1)} %pad_maximum_fusion.1.refs_8_.refs_9_) | copy-start | bytes 1572868
  16.9 17.0 %collective-permute-start.3 = (bf16[256,1024]{1,0:T(8,128)(2,1)S(1)}, bf16[256,1024]{1,0:T(8,128)(2,1)}, u32[]{:S(2)}, u32[]{:S(2)}) collective-permute-start(bf16[256,1024]{1,0:T(8,128)(2,1)S(1)} %pad_maximum_fusion.1.refs_8_.refs_9_), channel_id=1, source_target_pairs={{0,2},{1,3},{2,4},{3,5},{4,6},{5,7},{6,8},{7,9},{8,10},{9,11},{10,... | collective-permute-start | bytes 1572872 | tf_op jit(solution)/shard_map/ppermute | solution.py:18
  21.9 20.1 %collective-permute-start.4 = (bf16[256,1024]{1,0:T(8,128)(2,1)S(1)}, bf16[256,1024]{1,0:T(8,128)(2,1)}, u32[]{:S(2)}, u32[]{:S(2)}) collective-permute-start(bf16[256,1024]{1,0:T(8,128)(2,1)S(1)} %pad_maximum_fusion.1.refs_8_.refs_9_), channel_id=1, source_target_pairs={{0,1},{1,4},{2,3},{3,6},{4,5},{5,8},{6,7},{7,10},{8,9},{9,12},{10,... | collective-permute-start | bytes 1572872 | tf_op jit(solution)/shard_map/ppermute | solution.py:34
  23.9 18.0 %copy-start.9 = (bf16[256,1024]{1,0:T(8,128)(2,1)}, bf16[256,1024]{1,0:T(8,128)(2,1)S(1)}, u32[]{:S(2)}) copy-start(bf16[256,1024]{1,0:T(8,128)(2,1)S(1)} %collective-permute-done.refs_2_.refs_3_) | copy-start | bytes 1572868
  23.9 18.0 %collective-permute-start.2 = (bf16[256,1024]{1,0:T(8,128)(2,1)S(1)}, bf16[256,1024]{1,0:T(8,128)(2,1)}, u32[]{:S(2)}, u32[]{:S(2)}) collective-permute-start(bf16[256,1024]{1,0:T(8,128)(2,1)S(1)} %collective-permute-done.refs_2_.refs_3_), channel_id=1, source_target_pairs={{0,1},{1,0},{2,3},{3,2},{4,5},{5,4},{6,7},{7,6},{8,9},{9,8},{10,11... | collective-permute-start | bytes 1572872 | tf_op jit(solution)/shard_map/ppermute | solution.py:23
  33.9 8.0 %collective-permute-start.5 = (bf16[256,1024]{1,0:T(8,128)(2,1)}, bf16[256,1024]{1,0:T(8,128)(2,1)}, u32[]{:S(2)}, u32[]{:S(2)}) collective-permute-start(bf16[256,1024]{1,0:T(8,128)(2,1)} %collective-permute-done.3.refs_10_.refs_11_), channel_id=1, source_target_pairs={{0,1},{1,0},{2,3},{3,2},{4,5},{5,4},{6,7},{7,6},{8,9},{9,8},{10,11... | collective-permute-start | bytes 1572872 | tf_op jit(solution)/shard_map/ppermute | solution.py:23
  36.0 6.0 %copy-start.6 = (s32[21,256]{1,0:T(8,128)}, s32[21,256]{1,0:T(8,128)S(1)}, u32[]{:S(2)}) copy-start(s32[21,256]{1,0:T(8,128)S(1)} %stack.45.infor) | copy-start | bytes 64516
  56.7 5.3 %collective-permute-start.7 = (bf16[256,1024]{1,0:T(8,128)(2,1)S(1)}, bf16[256,1024]{1,0:T(8,128)(2,1)}, u32[]{:S(2)}, u32[]{:S(2)}) collective-permute-start(bf16[256,1024]{1,0:T(8,128)(2,1)S(1)} %constant_dynamic-update-slice_fusion), channel_id=1, source_target_pairs={{0,1},{1,0},{2,3},{3,2},{4,5},{5,4},{6,7},{7,6},{8,9},{9,8},{10,11... | collective-permute-start | bytes 1572872 | tf_op jit(solution)/shard_map/ppermute | solution.py:23
  59.7 4.3 %collective-permute-start.6 = (bf16[256,1024]{0,1:T(8,128)(2,1)}, bf16[256,1024]{0,1:T(8,128)(2,1)}, u32[]{:S(2)}, u32[]{:S(2)}) collective-permute-start(bf16[256,1024]{0,1:T(8,128)(2,1)} %bitcast.18), channel_id=1, source_target_pairs={{0,1},{1,0},{2,3},{3,2},{4,5},{5,4},{6,7},{7,6},{8,9},{9,8},{10,11... | collective-permute-start | bytes 1572872 | tf_op jit(solution)/shard_map/ppermute | solution.py:23

commit v9 on v8

--- a/solution.py
+++ b/solution.py
@@ -46,7 +46,7 @@
     )
 
 
-def reduce_kernel(groups, spread, part_ref, out_ref, sent, landed, sums, mixed, finals, sems):
+def reduce_kernel(groups, spread, xsel_ref, joined_ref, out_ref, joined_land, part_ref, sent, landed, sums, mixed, finals, sems):
     me = lax.axis_index("ctx")
     group = lax.axis_index("dp")
     core = me % 2
@@ -58,7 +58,26 @@
         pl.semaphore_signal(barrier, inc=1, device_id=(group, peer), device_id_type=mesh_id)
     for step in range(1, spread):
         pl.semaphore_signal(barrier, inc=1, device_id=((group + step) % spread, me), device_id_type=mesh_id)
-    pl.semaphore_wait(barrier, groups - 1 + spread - 1)
+    partner = me + 1 - 2 * core
+    pl.semaphore_signal(barrier, inc=1, device_id=(group, partner), device_id_type=mesh_id)
+    pl.semaphore_wait(barrier, groups - 1 + spread - 1 + 1)
+    pair = pltpu.make_async_remote_copy(
+        src_ref=joined_ref,
+        dst_ref=joined_land,
+        send_sem=sems.at[6, 0],
+        recv_sem=sems.at[6, 1],
+        device_id=(group, partner),
+        device_id_type=mesh_id,
+    )
+    pair.start()
+    rows = joined_ref.shape[0]
+    contract = (((0,), (0,)), ((), ()))
+    acc = lax.dot_general(xsel_ref[:rows], joined_ref[...], contract, preferred_element_type=jnp.float32)
+    pair.wait()
+    acc = acc + lax.dot_general(xsel_ref[rows:], joined_land[...], contract, preferred_element_type=jnp.float32)
+    _, _, share, lanes = part_ref.shape
+    for index in range(spread):
+        part_ref[index] = acc[:, index * lanes:(index + 1) * lanes].reshape(groups, share, lanes)
     sent[...] = part_ref[...].astype(sent.dtype)
     copies = []
     for step in range(1, spread):
@@ -118,26 +137,28 @@
     out_ref[...] = finals[...]
 
 
-def reduce_blocks(part, spread):
-    groups, share, width = part.shape
+def reduce_blocks(xsel, joined, share, spread):
+    rows, width = joined.shape
+    groups = xsel.shape[1] // share
     lanes = width // spread
-    part = part.reshape(groups, share, spread, lanes).transpose(2, 0, 1, 3)
     vmem = pl.BlockSpec(memory_space=pltpu.VMEM)
     finals = pl.pallas_call(
         functools.partial(reduce_kernel, groups, spread),
-        in_specs=[vmem],
+        in_specs=[vmem, vmem],
         out_specs=vmem,
         out_shape=jax.ShapeDtypeStruct((spread, share, lanes), jnp.float32),
         scratch_shapes=[
+            pltpu.VMEM((rows, width), jnp.bfloat16),
+            pltpu.VMEM((spread, groups, share, lanes), jnp.float32),
             pltpu.VMEM((spread, groups, share, lanes), jnp.bfloat16),
             pltpu.VMEM((spread, groups, share, lanes), jnp.bfloat16),
             pltpu.VMEM((groups, share, lanes), jnp.bfloat16),
             pltpu.VMEM((groups, share, lanes), jnp.bfloat16),
             pltpu.VMEM((spread, share, lanes), jnp.float32),
-            pltpu.SemaphoreType.DMA((6, max(groups, spread))),
+            pltpu.SemaphoreType.DMA((7, max(groups, spread))),
         ],
         compiler_params=pltpu.CompilerParams(collective_id=1, has_side_effects=True),
-    )(part)
+    )(xsel, joined)
     return finals.transpose(1, 0, 2).reshape(share, width)
 
 
@@ -145,14 +166,10 @@
     width = local.shape[1]
     share = width // cycle_size
     core = myself % 2
-    partner_joined = exchange(joined, "ctx", 1)
     both_events = jnp.concatenate([local, partner_events], axis=0)
-    both_joined = jnp.concatenate([joined, partner_joined], axis=0)
     halves = both_events.reshape(both_events.shape[0], width // (2 * share), 2, share)
     kept = lax.dynamic_index_in_dim(halves, core, 2, keepdims=False).reshape(both_events.shape[0], width // 2)
-    acc = jnp.dot(kept.T, both_joined, preferred_element_type=jnp.float32)
-    acc = acc.reshape(width // (2 * share), share, joined.shape[1])
-    acc = reduce_blocks(acc, lax.axis_size("dp"))
+    acc = reduce_blocks(kept, joined, share, lax.axis_size("dp"))
     return acc
 
 

time: 115 us -> 108 us (0.939)
  waiting for transfers between devices: 13.4 us -> 6.57 us
  Pallas kernels: 58.1 us -> 62.4 us
  matrix products: 5.03 us -> 1.9 us
  starting transfers between devices: 25.1 us -> 23.3 us
    pallas_call x1, Pallas kernels: 45.2 us -> 49.6 us  [reduce_blocks(): pl.pallas_call(functools.partial(reduce_kernel, groups, spread), in_specs...]
    ppermute x2, waiting for transfers between devices: 8.08 us -> 4.14 us  [shifted(): return lax.ppermute(value, axis, pairs)]
    dot_general x1 -> x0, matrix products: 3.13 us -> none  [reduce_rows(): acc = jnp.dot(kept.T, both_joined, preferred_element_type=jnp.float32)]
    concatenate x0 -> x2, other arithmetic: none -> 2.88 us  [the longest x1 1.89 us: body(): joined = jnp.concatenate([dq_b, dk_b], axis=1)]
    ppermute x2, waiting for transfers between devices: 5.18 us -> 2.42 us  [relayed(): mixed = lax.ppermute(value, 'ctx', pairs)]
    ppermute x4 -> x3, starting transfers between devices: 8.15 us -> 6.24 us  [exchange(): lax.ppermute(value, axis, [(source, source ^ mask) for source in range(co...]
    unnamed x22 -> x23, local copies, waits for them, and re-layouts: 3.21 us -> 3.53 us
  transfers between devices with their start and end apart: 8 -> 7, of which waited for: 3 -> 2; matrix products, arithmetic and copies ran while one was open for 5% -> 4% of each run, Pallas kernels for 0% -> 0%
where the time goes in v9:
time: 108 us; the launch traced here: 107 us
  Pallas kernels  62.4 us (58%)
  starting transfers between devices  23.3 us (22%)
  waiting for transfers between devices  6.57 us (6%)
  local copies, waits for them, and re-layouts  6.07 us (6%)
  other arithmetic  4.92 us (5%)
  matrix products  1.9 us (2%)
  between operations  1.72 us (2%)
    pallas_call x1, Pallas kernels, reduce_blocks(): pl.pallas_call(functools.partial(reduce_kernel, groups, spread), in_specs...  49.6 us
    pallas_call x1, Pallas kernels, attention_tiles(): pl.pallas_call(functools.partial(tiles_kernel, span, alpha, scale), grid=...  12.8 us
    ppermute x2, starting transfers between devices, relayed(): mixed = lax.ppermute(value, 'ctx', pairs)  8.69 us
    ppermute x2, starting transfers between devices, shifted(): return lax.ppermute(value, axis, pairs)  8.38 us
    ppermute x3, starting transfers between devices, exchange(): lax.ppermute(value, axis, [(source, source ^ mask) for source in range(co...  6.24 us
    ppermute x2, waiting for transfers between devices, shifted(): return lax.ppermute(value, axis, pairs)  4.14 us
    unnamed x23, local copies, waits for them, and re-layouts  3.53 us
    ppermute x2, waiting for transfers between devices, relayed(): mixed = lax.ppermute(value, 'ctx', pairs)  2.42 us
  transfers between devices with their start and end apart: 7, of which 2 were waited for; matrix products, arithmetic and copies ran while one was open for 4% of the time, Pallas kernels for 0%

profile of v9, /device:TPU:6, one launch (start us, length us, event | category | flops | bytes accessed | tf_op | source)
XLA Modules:
  0.0 106.9 jit_solution(2332772782656387988)
XLA Ops:
  0.7 1.2 %copy-done = bf16[1024,512]{1,0:T(8,128)(2,1)S(1)} copy-done((bf16[1024,512]{1,0:T(8,128)(2,1)S(1)}, bf16[1024,512]{1,0:T(8,128)(2,1)}, u32[]{:S(2)}) %copy-start) | copy-done | bytes 1048600
  1.9 1.5 %convolution_convert_fusion.1 = bf16[256,512]{1,0:T(8,128)(2,1)S(1)} fusion(bf16[1024,512]{1,0:T(8,128)(2,1)S(1)} %copy-done, bf16[1,256,1024]{2,1,0:T(8,128)(2,1)} %param.8), kind=kOutput, calls=%fused_computation.1 | convolution fusion | flops 268566528 | bytes 1835008 | tf_op jit(solution)/shard_map/dot_general | solution.py:288
  3.5 3.4 %collective-permute-start = (bf16[256,1024]{1,0:T(8,128)(2,1)S(1)}, bf16[256,1024]{1,0:T(8,128)(2,1)}, u32[]{:S(2)}, u32[]{:S(2)}) collective-permute-start(bf16[256,1024]{1,0:T(8,128)(2,1)S(1)} %pad_maximum_fusion.refs_0_.refs_1_), channel_id=1, source_target_pairs={{0,62},{1,63},{2,0},{3,1},{4,2},{5,3},{6,4},{7,5},{8,6},{9,7},{10,... | collective-permute-start | bytes 1572872 | tf_op jit(solution)/shard_map/ppermute | solution.py:18
  6.9 8.7 %collective-permute-start.1 = (bf16[256,1024]{1,0:T(8,128)(2,1)S(1)}, bf16[256,1024]{1,0:T(8,128)(2,1)}, u32[]{:S(2)}, u32[]{:S(2)}) collective-permute-start(bf16[256,1024]{1,0:T(8,128)(2,1)S(1)} %pad_maximum_fusion.refs_0_.refs_1_), channel_id=1, source_target_pairs={{0,61},{1,0},{2,63},{3,2},{4,1},{5,4},{6,3},{7,6},{8,5},{9,8},{10,... | collective-permute-start | bytes 1572872 | tf_op jit(solution)/shard_map/ppermute | solution.py:34
  15.6 0.4 convolution_convert_fusion
  16.1 4.9 %collective-permute-start.3 = (bf16[256,1024]{1,0:T(8,128)(2,1)S(1)}, bf16[256,1024]{1,0:T(8,128)(2,1)}, u32[]{:S(2)}, u32[]{:S(2)}) collective-permute-start(bf16[256,1024]{1,0:T(8,128)(2,1)S(1)} %pad_maximum_fusion.1.refs_8_.refs_9_), channel_id=1, source_target_pairs={{0,2},{1,3},{2,4},{3,5},{4,6},{5,7},{6,8},{7,9},{8,10},{9,11},{10,... | collective-permute-start | bytes 1572872 | tf_op jit(solution)/shard_map/ppermute | solution.py:18
  21.1 0.2 copy.23
  21.3 1.9 %collective-permute-start.6 = (bf16[256,1024]{0,1:T(8,128)(2,1)S(1)}, bf16[256,1024]{0,1:T(8,128)(2,1)S(1)}, u32[]{:S(2)}, u32[]{:S(2)}) collective-permute-start(bf16[256,1024]{0,1:T(8,128)(2,1)S(1)} %bitcast.51), channel_id=1, source_target_pairs={{0,1},{1,0},{2,3},{3,2},{4,5},{5,4},{6,7},{7,6},{8,9},{9,8},{10,11... | collective-permute-start | bytes 1572872 | tf_op jit(solution)/shard_map/ppermute | solution.py:23
  24.1 0.6 copy-done.10
  24.7 0.6 select_reduce_fusion
  25.4 0.6 copy-done.9
  26.6 2.4 %collective-permute-start.2 = (bf16[256,1024]{1,0:T(8,128)(2,1)}, bf16[256,1024]{1,0:T(8,128)(2,1)}, u32[]{:S(2)}, u32[]{:S(2)}) collective-permute-start(bf16[256,1024]{1,0:T(8,128)(2,1)} %collective-permute-done.refs_2_.refs_3_), channel_id=1, source_target_pairs={{0,1},{1,0},{2,3},{3,2},{4,5},{5,4},{6,7},{7,6},{8,9},{9,8},{10,11... | collective-permute-start | bytes 1572872 | tf_op jit(solution)/shard_map/ppermute | solution.py:23
  29.0 4.1 %collective-permute-done.3.refs_10_.refs_11_ = bf16[256,1024]{1,0:T(8,128)(2,1)} collective-permute-done((bf16[256,1024]{1,0:T(8,128)(2,1)S(1)}, bf16[256,1024]{1,0:T(8,128)(2,1)}, u32[]{:S(2)}, u32[]{:S(2)}) %collective-permute-start.3) | collective-permute-done | bytes 524320 | tf_op jit(solution)/shard_map/ppermute | solution.py:18
  33.1 1.9 %collective-permute-start.5 = (bf16[256,1024]{1,0:T(8,128)(2,1)}, bf16[256,1024]{1,0:T(8,128)(2,1)}, u32[]{:S(2)}, u32[]{:S(2)}) collective-permute-start(bf16[256,1024]{1,0:T(8,128)(2,1)} %collective-permute-done.3.refs_10_.refs_11_), channel_id=1, source_target_pairs={{0,1},{1,0},{2,3},{3,2},{4,5},{5,4},{6,7},{7,6},{8,9},{9,8},{10,11... | collective-permute-start | bytes 1572872 | tf_op jit(solution)/shard_map/ppermute | solution.py:23
  35.2 0.8 copy.24.infoc
  35.9 0.8 copy-done.5
  36.7 1.0 fusion
  37.7 1.0 copy.26.xsel_ref
  38.7 2.4 %collective-permute-done.4.refs_12_.refs_13_ = bf16[256,1024]{1,0:T(8,128)(2,1)} collective-permute-done((bf16[256,1024]{1,0:T(8,128)(2,1)S(1)}, bf16[256,1024]{1,0:T(8,128)(2,1)}, u32[]{:S(2)}, u32[]{:S(2)}) %collective-permute-start.4) | collective-permute-done | bytes 524320 | tf_op jit(solution)/shard_map/ppermute | solution.py:34
  41.1 12.8 %shard_map.111 = (bf16[256,512]{1,0:T(8,128)(2,1)}, bf16[256,512]{1,0:T(8,128)(2,1)}, bf16[256,512]{1,0:T(8,128)(2,1)}, bf16[256,512]{1,0:T(8,128)(2,1)}) custom-call(s32[256,21]{1,0:T(8,128)} %copy.24.infoc, s32[21,256]{1,0:T(8,128)} %copy-done.8, bf16[256,1024]{1,0:T(8,128)(2,1)} %copy-done.3, bf16[256,1024]{1,0:T(8,128)(2,1)} %copy-done.3, ...), custom_call_target="tpu_custom_call" | custom-call | flops 2348810240 | bytes 9437184 | tf_op jit(solution)/shard_map/pallas_call | solution.py:240
  53.9 1.9 %pad_maximum_fusion.2.joined_ref = bf16[256,1024]{1,0:T(8,128)(2,1)} fusion(bf16[256,512]{1,0:T(8,128)(2,1)} %get-tuple-element.11, bf16[256,512]{1,0:T(8,128)(2,1)} %get-tuple-element.10), kind=kLoop, calls=%fused_computation.7 | loop fusion | flops 1048576 | bytes 1048576 | tf_op jit(solution)/shard_map/concatenate | solution.py:338
  55.8 49.6 %shard_map.112 = f32[8,16,128]{2,1,0:T(8,128)} custom-call(bf16[512,512]{1,0:T(8,128)(2,1)} %copy.26.xsel_ref, bf16[256,1024]{1,0:T(8,128)(2,1)} %pad_maximum_fusion.2.joined_ref), custom_call_target="tpu_custom_call" | custom-call | tf_op jit(solution)/shard_map/pallas_call | solution.py:145
  105.4 0.8 copy_bitcast_fusion
  106.3 0.6 fusion.17
  (49 shorter events, 0.9 us)
Async XLA Ops:
  0.6 1.2 %copy-start = (bf16[1024,512]{1,0:T(8,128)(2,1)S(1)}, bf16[1024,512]{1,0:T(8,128)(2,1)}, u32[]{:S(2)}) copy-start(bf16[1024,512]{1,0:T(8,128)(2,1)} %param.9) | copy-start | bytes 3145732
  0.6 2.7 %copy-start.6 = (bf16[1,256,512]{2,1,0:T(8,128)(2,1)S(1)}, bf16[1,256,512]{2,1,0:T(8,128)(2,1)}, u32[]{:S(2)}) copy-start(bf16[1,256,512]{2,1,0:T(8,128)(2,1)} %param.12) | copy-start | bytes 786436
  0.7 14.9 %copy-start.2 = (bf16[1024,512]{1,0:T(8,128)(2,1)S(1)}, bf16[1024,512]{1,0:T(8,128)(2,1)}, u32[]{:S(2)}) copy-start(bf16[1024,512]{1,0:T(8,128)(2,1)} %param.10) | copy-start | bytes 3145732
  3.4 12.2 %copy-start.1 = (bf16[1,256,1024]{2,1,0:T(8,128)(2,1)S(1)}, bf16[1,256,1024]{2,1,0:T(8,128)(2,1)}, u32[]{:S(2)}) copy-start(bf16[1,256,1024]{2,1,0:T(8,128)(2,1)} %param.8) | copy-start | bytes 1572868
  3.4 12.6 %copy-start.3 = (bf16[256,1024]{1,0:T(8,128)(2,1)}, bf16[256,1024]{1,0:T(8,128)(2,1)S(1)}, u32[]{:S(2)}) copy-start(bf16[256,1024]{1,0:T(8,128)(2,1)S(1)} %pad_maximum_fusion.refs_0_.refs_1_) | copy-start | bytes 1572868
  3.4 12.6 %copy-start.7 = (bf16[1,256,512]{2,1,0:T(8,128)(2,1)S(1)}, bf16[1,256,512]{2,1,0:T(8,128)(2,1)}, u32[]{:S(2)}) copy-start(bf16[1,256,512]{2,1,0:T(8,128)(2,1)} %param.11) | copy-start | bytes 786436
  3.5 23.1 %collective-permute-start = (bf16[256,1024]{1,0:T(8,128)(2,1)S(1)}, bf16[256,1024]{1,0:T(8,128)(2,1)}, u32[]{:S(2)}, u32[]{:S(2)}) collective-permute-start(bf16[256,1024]{1,0:T(8,128)(2,1)S(1)} %pad_maximum_fusion.refs_0_.refs_1_), channel_id=1, source_target_pairs={{0,62},{1,63},{2,0},{3,1},{4,2},{5,3},{6,4},{7,5},{8,6},{9,7},{10,... | collective-permute-start | bytes 1572872 | tf_op jit(solution)/shard_map/ppermute | solution.py:18
  6.9 31.8 %collective-permute-start.1 = (bf16[256,1024]{1,0:T(8,128)(2,1)S(1)}, bf16[256,1024]{1,0:T(8,128)(2,1)}, u32[]{:S(2)}, u32[]{:S(2)}) collective-permute-start(bf16[256,1024]{1,0:T(8,128)(2,1)S(1)} %pad_maximum_fusion.refs_0_.refs_1_), channel_id=1, source_target_pairs={{0,61},{1,0},{2,63},{3,2},{4,1},{5,4},{6,3},{7,6},{8,5},{9,8},{10,... | collective-permute-start | bytes 1572872 | tf_op jit(solution)/shard_map/ppermute | solution.py:34
  16.1 5.2 %copy-start.4 = (bf16[256,1024]{1,0:T(8,128)(2,1)}, bf16[256,1024]{1,0:T(8,128)(2,1)S(1)}, u32[]{:S(2)}) copy-start(bf16[256,1024]{1,0:T(8,128)(2,1)S(1)} %pad_maximum_fusion.1.refs_8_.refs_9_) | copy-start | bytes 1572868
  16.1 17.0 %collective-permute-start.3 = (bf16[256,1024]{1,0:T(8,128)(2,1)S(1)}, bf16[256,1024]{1,0:T(8,128)(2,1)}, u32[]{:S(2)}, u32[]{:S(2)}) collective-permute-start(bf16[256,1024]{1,0:T(8,128)(2,1)S(1)} %pad_maximum_fusion.1.refs_8_.refs_9_), channel_id=1, source_target_pairs={{0,2},{1,3},{2,4},{3,5},{4,6},{5,7},{6,8},{7,9},{8,10},{9,11},{10,... | collective-permute-start | bytes 1572872 | tf_op jit(solution)/shard_map/ppermute | solution.py:18
  21.1 20.1 %collective-permute-start.4 = (bf16[256,1024]{1,0:T(8,128)(2,1)S(1)}, bf16[256,1024]{1,0:T(8,128)(2,1)}, u32[]{:S(2)}, u32[]{:S(2)}) collective-permute-start(bf16[256,1024]{1,0:T(8,128)(2,1)S(1)} %pad_maximum_fusion.1.refs_8_.refs_9_), channel_id=1, source_target_pairs={{0,1},{1,4},{2,3},{3,6},{4,5},{5,8},{6,7},{7,10},{8,9},{9,12},{10,... | collective-permute-start | bytes 1572872 | tf_op jit(solution)/shard_map/ppermute | solution.py:34
  21.3 14.6 %collective-permute-start.6 = (bf16[256,1024]{0,1:T(8,128)(2,1)S(1)}, bf16[256,1024]{0,1:T(8,128)(2,1)S(1)}, u32[]{:S(2)}, u32[]{:S(2)}) collective-permute-start(bf16[256,1024]{0,1:T(8,128)(2,1)S(1)} %bitcast.51), channel_id=1, source_target_pairs={{0,1},{1,0},{2,3},{3,2},{4,5},{5,4},{6,7},{7,6},{8,9},{9,8},{10,11... | collective-permute-start | bytes 1572872 | tf_op jit(solution)/shard_map/ppermute | solution.py:23
  24.1 0.7 copy-start.10
  25.4 0.7 copy-start.9
  26.6 14.6 %collective-permute-start.2 = (bf16[256,1024]{1,0:T(8,128)(2,1)}, bf16[256,1024]{1,0:T(8,128)(2,1)}, u32[]{:S(2)}, u32[]{:S(2)}) collective-permute-start(bf16[256,1024]{1,0:T(8,128)(2,1)} %collective-permute-done.refs_2_.refs_3_), channel_id=1, source_target_pairs={{0,1},{1,0},{2,3},{3,2},{4,5},{5,4},{6,7},{7,6},{8,9},{9,8},{10,11... | collective-permute-start | bytes 1572872 | tf_op jit(solution)/shard_map/ppermute | solution.py:23
  33.1 8.0 %collective-permute-start.5 = (bf16[256,1024]{1,0:T(8,128)(2,1)}, bf16[256,1024]{1,0:T(8,128)(2,1)}, u32[]{:S(2)}, u32[]{:S(2)}) collective-permute-start(bf16[256,1024]{1,0:T(8,128)(2,1)} %collective-permute-done.3.refs_10_.refs_11_), channel_id=1, source_target_pairs={{0,1},{1,0},{2,3},{3,2},{4,5},{5,4},{6,7},{7,6},{8,9},{9,8},{10,11... | collective-permute-start | bytes 1572872 | tf_op jit(solution)/shard_map/ppermute | solution.py:23
  35.1 0.8 copy-start.8
  35.9 0.8 copy-start.5

commit v10 on v9

--- a/solution.py
+++ b/solution.py
@@ -278,6 +278,196 @@
     return dkey, dvalue
 
 
+def fused_kernel(span, alpha, scale, nheads, groups, spread, infoc, infor, *refs):
+    count = span + 1
+    qgs = refs[:count]
+    kvs = refs[count:2 * count]
+    xsel_ref = refs[2 * count]
+    out_ref, dv_ref, fin_ref = refs[2 * count + 1:2 * count + 4]
+    weights, joined, joined_land, part, sent, landed, sums, mixed, finals, sems = refs[2 * count + 4:]
+    me = lax.axis_index("ctx")
+    group = lax.axis_index("dp")
+    core = me % 2
+    slot = me // 2
+    partner = me + 1 - 2 * core
+    mesh_id = pl.DeviceIdType.MESH
+    lanes = 2 * span + 1
+    rows = joined.shape[1]
+    share = part.shape[2]
+    landed[group] = jnp.zeros(landed.shape[1:], landed.dtype)
+
+    def valid(qa, ka):
+        qpos = infoc[:, qa:qa + 1]
+        quser = infoc[:, lanes + qa:lanes + qa + 1]
+        kpos = infor[ka:ka + 1, :]
+        kuser = infor[lanes + ka:lanes + ka + 1, :]
+        kkept = infor[2 * lanes + ka:2 * lanes + ka + 1, :]
+        return (quser == kuser) & (kpos <= qpos) & (kkept > 0)
+
+    pairs = [(0, 0)] + [(0, step) for step in range(1, span + 1)] + [(span + step, 0) for step in range(1, span + 1)]
+    for index, (qa, ka) in enumerate(pairs):
+        weights[index] = jnp.where(valid(qa, ka), scale, 0.0)
+
+    barrier = pltpu.get_barrier_semaphore()
+    for step in range(1, groups):
+        peer = 2 * ((slot + step) % groups) + core
+        pl.semaphore_signal(barrier, inc=1, device_id=(group, peer), device_id_type=mesh_id)
+    for step in range(1, spread):
+        pl.semaphore_signal(barrier, inc=1, device_id=((group + step) % spread, me), device_id_type=mesh_id)
+    pl.semaphore_signal(barrier, inc=1, device_id=(group, partner), device_id_type=mesh_id)
+    pl.semaphore_wait(barrier, groups - 1 + spread - 1 + 1)
+
+    def terms(q, g, k, v, w):
+        z = lax.dot_general(q, k, (((1,), (1,)), ((), ())), preferred_element_type=jnp.float32) * alpha
+        sig = 1.0 / (1.0 + jnp.exp(-z))
+        att = (z * sig * w).astype(jnp.bfloat16)
+        dprod = lax.dot_general(g, v, (((1,), (1,)), ((), ())), preferred_element_type=jnp.float32)
+        dsc = (dprod * sig * (1.0 + z * (1.0 - sig)) * w * alpha).astype(jnp.bfloat16)
+        return att, dsc
+
+    contract = (((0,), (0,)), ((), ()))
+
+    def pair_copy(block):
+        return pltpu.make_async_remote_copy(
+            src_ref=joined.at[block],
+            dst_ref=joined_land.at[block],
+            send_sem=sems.at[0, block],
+            recv_sem=sems.at[1, block],
+            device_id=(group, partner),
+            device_id_type=mesh_id,
+        )
+
+    def spread_copy(block, source):
+        return pltpu.make_async_remote_copy(
+            src_ref=sent.at[block],
+            dst_ref=landed.at[source],
+            send_sem=sems.at[2, block],
+            recv_sem=sems.at[3, source],
+            device_id=(block, me),
+            device_id_type=mesh_id,
+        )
+
+    def handle(block):
+        pair_copy(block).wait()
+        acc = lax.dot_general(xsel_ref[:rows], joined[block], contract, preferred_element_type=jnp.float32)
+        acc = acc + lax.dot_general(xsel_ref[rows:], joined_land[block], contract, preferred_element_type=jnp.float32)
+        part[block] = acc.reshape(part.shape[1:])
+        sent[block] = part[block].astype(sent.dtype)
+
+        @pl.when(group != block)
+        def _():
+            spread_copy(block, group).start()
+
+    for head in range(nheads):
+        cq = slice(head * HD, (head + 1) * HD)
+        cg = slice((nheads + head) * HD, (nheads + head + 1) * HD)
+        q0, g0 = qgs[0][:, cq], qgs[0][:, cg]
+        k0, v0 = kvs[0][:, cq], kvs[0][:, cg]
+        att, dsc = terms(q0, g0, k0, v0, weights[0])
+        out = jnp.dot(att, v0, preferred_element_type=jnp.float32)
+        dq = jnp.dot(dsc, k0, preferred_element_type=jnp.float32)
+        dk = lax.dot_general(dsc, q0, contract, preferred_element_type=jnp.float32)
+        dv = lax.dot_general(att, g0, contract, preferred_element_type=jnp.float32)
+        for step in range(1, span + 1):
+            k, v = kvs[step][:, cq], kvs[step][:, cg]
+            att, dsc = terms(q0, g0, k, v, weights[step])
+            out = out + jnp.dot(att, v, preferred_element_type=jnp.float32)
+            dq = dq + jnp.dot(dsc, k, preferred_element_type=jnp.float32)
+            q, g = qgs[step][:, cq], qgs[step][:, cg]
+            att, dsc = terms(q, g, k0, v0, weights[span + step])
+            dk = dk + lax.dot_general(dsc, q, contract, preferred_element_type=jnp.float32)
+            dv = dv + lax.dot_general(att, g, contract, preferred_element_type=jnp.float32)
+        out_ref[:, cq] = out.astype(out_ref.dtype)
+        dv_ref[:, cq] = dv.astype(dv_ref.dtype)
+        joined[head] = dq.astype(joined.dtype)
+        joined[nheads + head] = dk.astype(joined.dtype)
+        pair_copy(head).start()
+        pair_copy(nheads + head).start()
+        if head > 0:
+            handle(head - 1)
+            handle(nheads + head - 1)
+    handle(nheads - 1)
+    handle(2 * nheads - 1)
+
+    for block in range(spread):
+        @pl.when(group != block)
+        def _():
+            spread_copy(block, group).wait_send()
+            spread_copy(block, block).wait_recv()
+
+    total = part[group]
+    for source in range(spread):
+        total = total + landed[source].astype(jnp.float32)
+    sums[...] = total.astype(sums.dtype)
+    copies = []
+    for step in range(1, groups):
+        target = (slot + step) % groups
+        copy = pltpu.make_async_remote_copy(
+            src_ref=sums.at[target],
+            dst_ref=mixed.at[slot],
+            send_sem=sems.at[4, step - 1],
+            recv_sem=sems.at[5, step - 1],
+            device_id=(group, 2 * target + core),
+            device_id_type=mesh_id,
+        )
+        copy.start()
+        copies.append(copy)
+    for copy in copies:
+        copy.wait()
+    result = part[group, slot]
+    for source in range(spread):
+        result = result + landed[source, slot].astype(jnp.float32)
+    for step in range(1, groups):
+        result = result + mixed[(slot + groups - step) % groups].astype(jnp.float32)
+    finals[group] = result
+    copies = []
+    for step in range(1, spread):
+        target = (group + step) % spread
+        copy = pltpu.make_async_remote_copy(
+            src_ref=finals.at[group],
+            dst_ref=finals.at[group],
+            send_sem=sems.at[6, step - 1],
+            recv_sem=sems.at[7, step - 1],
+            device_id=(target, me),
+            device_id_type=mesh_id,
+        )
+        copy.start()
+        copies.append(copy)
+    for copy in copies:
+        copy.wait()
+    fin_ref[...] = finals[...]
+
+
+def fused_call(qg_list, kv_list, infoc, infor, xsel, nheads, alpha, scale, spread, share):
+    rows, width = qg_list[0].shape
+    span = len(qg_list) - 1
+    groups = xsel.shape[1] // share
+    lanes = HD
+    vmem = pl.BlockSpec(memory_space=pltpu.VMEM)
+    operands = [infoc, infor] + list(qg_list) + list(kv_list) + [xsel]
+    half = jax.ShapeDtypeStruct((rows, nheads * HD), jnp.bfloat16)
+    out, dv, finals = pl.pallas_call(
+        functools.partial(fused_kernel, span, alpha, scale, nheads, groups, spread),
+        in_specs=[vmem] * len(operands),
+        out_specs=[vmem] * 3,
+        out_shape=[half, half, jax.ShapeDtypeStruct((spread, share, lanes), jnp.float32)],
+        scratch_shapes=[
+            pltpu.VMEM((2 * span + 1, rows, rows), jnp.float32),
+            pltpu.VMEM((2 * nheads, rows, HD), jnp.bfloat16),
+            pltpu.VMEM((2 * nheads, rows, HD), jnp.bfloat16),
+            pltpu.VMEM((spread, groups, share, lanes), jnp.float32),
+            pltpu.VMEM((spread, groups, share, lanes), jnp.bfloat16),
+            pltpu.VMEM((spread, groups, share, lanes), jnp.bfloat16),
+            pltpu.VMEM((groups, share, lanes), jnp.bfloat16),
+            pltpu.VMEM((groups, share, lanes), jnp.bfloat16),
+            pltpu.VMEM((spread, share, lanes), jnp.float32),
+            pltpu.SemaphoreType.DMA((8, max(groups, spread, 2 * nheads))),
+        ],
+        compiler_params=pltpu.CompilerParams(collective_id=1, has_side_effects=True),
+    )(*operands)
+    return out, dv, finals.transpose(1, 0, 2).reshape(share, spread * lanes)
+
+
 def body(events, w_query, w_key, values, grad_out, lengths, stream_shift, block_keep):
     rows = events.shape[1]
     features = w_query.shape[1]
@@ -330,13 +520,15 @@
         [d[0] for d in described] + [d[1] for d in described] + [d[2].astype(jnp.int32) for d in described]
     ).astype(jnp.int32)
     infoc = infor.T
-    out_b, dq_b, dk_b, dv_b = attention_tiles(
-        [qg] + qg_from[1:], [kv] + kv_from[1:], infoc, infor, nheads, alpha, scale
+    share = local.shape[1] // cycle_size
+    both_events = jnp.concatenate([local, partner_events], axis=0)
+    halves = both_events.reshape(both_events.shape[0], local.shape[1] // (2 * share), 2, share)
+    xsel = lax.dynamic_index_in_dim(halves, myself % 2, 2, keepdims=False).reshape(both_events.shape[0], local.shape[1] // 2)
+    out_b, dv_b, mine = fused_call(
+        [qg] + qg_from[1:], [kv] + kv_from[1:], infoc, infor, xsel, nheads, alpha, scale, lax.axis_size("dp"), share
     )
     attended = out_b.reshape(1, rows, features)
     grad_values = dv_b.reshape(1, rows, features)
-    joined = jnp.concatenate([dq_b, dk_b], axis=1)
-    mine = reduce_rows(local, partner_events, joined, myself, cycle_size)
     grad_wq = mine[:, :features].astype(jnp.bfloat16)
     grad_wk = mine[:, features:].astype(jnp.bfloat16)
     return (attended, grad_values, grad_wq, grad_wk)

time: 108 us -> 109 us (level)
  local copies, waits for them, and re-layouts: 6.07 us -> 8.51 us
  other arithmetic: 4.92 us -> 3.03 us
    ppermute x2, waiting for transfers between devices: 4.14 us -> 7.43 us  [shifted(): return lax.ppermute(value, axis, pairs)]
    ppermute x2, starting transfers between devices: 8.69 us -> 6.22 us  [relayed(): mixed = lax.ppermute(value, 'ctx', pairs)]
    unnamed x23 -> x27, local copies, waits for them, and re-layouts: 3.53 us -> 5.95 us
    ppermute x2, waiting for transfers between devices: 2.42 us -> 0.01 us  [relayed(): mixed = lax.ppermute(value, 'ctx', pairs)]
    concatenate x2 -> x1, other arithmetic: 2.88 us -> 0.99 us  [body(): both_events = jnp.concatenate([local, partner_events], axis=0)]
    ppermute x2, starting transfers between devices: 8.38 us -> 9.94 us  [shifted(): return lax.ppermute(value, axis, pairs)]
    pallas_call x2 -> x1, Pallas kernels: 62.4 us -> 61.7 us  [fused_call(): pl.pallas_call(functools.partial(fused_kernel, span, alpha, scale, nheads...]
where the time goes in v10:
time: 109 us; the launch traced here: 107 us
  Pallas kernels  61.7 us (57%)
  starting transfers between devices  22.8 us (21%)
  local copies, waits for them, and re-layouts  8.51 us (8%)
  waiting for transfers between devices  7.44 us (7%)
  other arithmetic  3.03 us (3%)
  matrix products  1.9 us (2%)
  between operations  1.75 us (2%)
    pallas_call x1, Pallas kernels, fused_call(): pl.pallas_call(functools.partial(fused_kernel, span, alpha, scale, nheads...  61.7 us
    ppermute x2, starting transfers between devices, shifted(): return lax.ppermute(value, axis, pairs)  9.94 us
    ppermute x2, waiting for transfers between devices, shifted(): return lax.ppermute(value, axis, pairs)  7.43 us
    ppermute x3, starting transfers between devices, exchange(): lax.ppermute(value, axis, [(source, source ^ mask) for source in range(co...  6.62 us
    ppermute x2, starting transfers between devices, relayed(): mixed = lax.ppermute(value, 'ctx', pairs)  6.22 us
    unnamed x27, local copies, waits for them, and re-layouts  5.95 us
  transfers between devices with their start and end apart: 7, of which 2 were waited for; matrix products, arithmetic and copies ran while one was open for 4% of the time, Pallas kernels for 0%

profile of v10, /device:TPU:6, one launch (start us, length us, event | category | flops | bytes accessed | tf_op | source)
XLA Modules:
  0.0 107.1 jit_solution(1970541134578681572)
XLA Ops:
  0.7 1.2 %copy-done = bf16[1024,512]{1,0:T(8,128)(2,1)S(1)} copy-done((bf16[1024,512]{1,0:T(8,128)(2,1)S(1)}, bf16[1024,512]{1,0:T(8,128)(2,1)}, u32[]{:S(2)}) %copy-start) | copy-done | bytes 1048600
  1.9 1.5 %convolution_convert_fusion = bf16[256,512]{1,0:T(8,128)(2,1)S(1)} fusion(bf16[1024,512]{1,0:T(8,128)(2,1)S(1)} %copy-done, bf16[1,256,1024]{2,1,0:T(8,128)(2,1)} %param.8), kind=kOutput, calls=%fused_computation | convolution fusion | flops 268566528 | bytes 1835008 | tf_op jit(solution)/shard_map/dot_general | solution.py:479
  3.5 4.8 %collective-permute-start.3 = (bf16[256,1024]{1,0:T(8,128)(2,1)S(1)}, bf16[256,1024]{1,0:T(8,128)(2,1)}, u32[]{:S(2)}, u32[]{:S(2)}) collective-permute-start(bf16[256,1024]{1,0:T(8,128)(2,1)S(1)} %pad_maximum_fusion.1.refs_4_), channel_id=1, source_target_pairs={{0,2},{1,3},{2,4},{3,5},{4,6},{5,7},{6,8},{7,9},{8,10},{9,11},{10,... | collective-permute-start | bytes 1572872 | tf_op jit(solution)/shard_map/ppermute | solution.py:18
  8.3 0.4 convolution_convert_fusion.1
  8.8 6.2 %collective-permute-start.1 = (bf16[256,1024]{1,0:T(8,128)(2,1)S(1)}, bf16[256,1024]{1,0:T(8,128)(2,1)}, u32[]{:S(2)}, u32[]{:S(2)}) collective-permute-start(bf16[256,1024]{1,0:T(8,128)(2,1)S(1)} %pad_maximum_fusion.refs_0_), channel_id=1, source_target_pairs={{0,61},{1,0},{2,63},{3,2},{4,1},{5,4},{6,3},{7,6},{8,5},{9,8},{10,... | collective-permute-start | bytes 1572872 | tf_op jit(solution)/shard_map/ppermute | solution.py:34
  15.0 5.1 %collective-permute-start = (bf16[256,1024]{1,0:T(8,128)(2,1)S(1)}, bf16[256,1024]{1,0:T(8,128)(2,1)}, u32[]{:S(2)}, u32[]{:S(2)}) collective-permute-start(bf16[256,1024]{1,0:T(8,128)(2,1)S(1)} %pad_maximum_fusion.refs_0_), channel_id=1, source_target_pairs={{0,62},{1,63},{2,0},{3,1},{4,2},{5,3},{6,4},{7,5},{8,6},{9,7},{10,... | collective-permute-start | bytes 1572872 | tf_op jit(solution)/shard_map/ppermute | solution.py:18
  20.2 0.2 copy.23
  20.4 1.9 %collective-permute-start.6 = (bf16[256,1024]{0,1:T(8,128)(2,1)S(1)}, bf16[256,1024]{0,1:T(8,128)(2,1)S(1)}, u32[]{:S(2)}, u32[]{:S(2)}) collective-permute-start(bf16[256,1024]{0,1:T(8,128)(2,1)S(1)} %bitcast.51), channel_id=1, source_target_pairs={{0,1},{1,0},{2,3},{3,2},{4,5},{5,4},{6,7},{7,6},{8,9},{9,8},{10,11... | collective-permute-start | bytes 1572872 | tf_op jit(solution)/shard_map/ppermute | solution.py:23
  23.3 0.6 copy-done.11
  24.0 0.6 select_reduce_fusion
  24.6 0.6 copy-done.10
  25.7 6.6 %collective-permute-done.3.refs_5_ = bf16[256,1024]{1,0:T(8,128)(2,1)} collective-permute-done((bf16[256,1024]{1,0:T(8,128)(2,1)S(1)}, bf16[256,1024]{1,0:T(8,128)(2,1)}, u32[]{:S(2)}, u32[]{:S(2)}) %collective-permute-start.3) | collective-permute-done | bytes 524320 | tf_op jit(solution)/shard_map/ppermute | solution.py:18
  32.3 2.6 %collective-permute-start.5 = (bf16[256,1024]{1,0:T(8,128)(2,1)}, bf16[256,1024]{1,0:T(8,128)(2,1)}, u32[]{:S(2)}, u32[]{:S(2)}) collective-permute-start(bf16[256,1024]{1,0:T(8,128)(2,1)} %collective-permute-done.3.refs_5_), channel_id=1, source_target_pairs={{0,1},{1,0},{2,3},{3,2},{4,5},{5,4},{6,7},{7,6},{8,9},{9,8},{10,11... | collective-permute-start | bytes 1572872 | tf_op jit(solution)/shard_map/ppermute | solution.py:23
  34.9 0.8 collective-permute-done.refs_1_
  35.7 2.1 %collective-permute-start.2 = (bf16[256,1024]{1,0:T(8,128)(2,1)}, bf16[256,1024]{1,0:T(8,128)(2,1)}, u32[]{:S(2)}, u32[]{:S(2)}) collective-permute-start(bf16[256,1024]{1,0:T(8,128)(2,1)} %collective-permute-done.refs_1_), channel_id=1, source_target_pairs={{0,1},{1,0},{2,3},{3,2},{4,5},{5,4},{6,7},{7,6},{8,9},{9,8},{10,11... | collective-permute-start | bytes 1572872 | tf_op jit(solution)/shard_map/ppermute | solution.py:23
  37.9 0.8 copy.25.infoc
  38.7 0.8 copy-done.5
  39.5 1.0 fusion
  40.5 1.0 copy.26.refs_8_
  41.5 61.7 %shard_map.111 = (bf16[256,512]{1,0:T(8,128)(2,1)}, bf16[256,512]{1,0:T(8,128)(2,1)}, f32[8,16,128]{2,1,0:T(8,128)}) custom-call(s32[256,21]{1,0:T(8,128)} %copy.25.infoc, s32[21,256]{1,0:T(8,128)} %copy-done.9, bf16[256,1024]{1,0:T(8,128)(2,1)} %copy-done.3, bf16[256,1024]{1,0:T(8,128)(2,1)} %collective-permute-done.refs_1_, ...), custom_call_target="tpu_custom_call" | custom-call | tf_op jit(solution)/shard_map/pallas_call | solution.py:449
  103.2 0.8 copy_bitcast_fusion
  104.1 0.6 fusion.17
  104.7 1.7 %copy.33 = bf16[1,256,512]{2,1,0:T(8,128)(2,1)} copy(bf16[1,256,512]{2,1,0:T(8,128)(2,1)} %bitcast.56) | data formatting | bytes 524288
  106.4 0.7 copy.34
  (51 shorter events, 0.9 us)
Async XLA Ops:
  0.6 1.2 %copy-start = (bf16[1024,512]{1,0:T(8,128)(2,1)S(1)}, bf16[1024,512]{1,0:T(8,128)(2,1)}, u32[]{:S(2)}) copy-start(bf16[1024,512]{1,0:T(8,128)(2,1)} %param.10) | copy-start | bytes 3145732
  0.6 2.7 %copy-start.7 = (bf16[1,256,512]{2,1,0:T(8,128)(2,1)S(1)}, bf16[1,256,512]{2,1,0:T(8,128)(2,1)}, u32[]{:S(2)}) copy-start(bf16[1,256,512]{2,1,0:T(8,128)(2,1)} %param.11) | copy-start | bytes 786436
  0.7 7.6 %copy-start.4 = (bf16[1024,512]{1,0:T(8,128)(2,1)S(1)}, bf16[1024,512]{1,0:T(8,128)(2,1)}, u32[]{:S(2)}) copy-start(bf16[1024,512]{1,0:T(8,128)(2,1)} %param.9) | copy-start | bytes 3145732
  3.4 4.9 %copy-start.1 = (bf16[1,256,1024]{2,1,0:T(8,128)(2,1)S(1)}, bf16[1,256,1024]{2,1,0:T(8,128)(2,1)}, u32[]{:S(2)}) copy-start(bf16[1,256,1024]{2,1,0:T(8,128)(2,1)} %param.8) | copy-start | bytes 1572868
  3.4 5.3 %copy-start.2 = (bf16[256,1024]{1,0:T(8,128)(2,1)}, bf16[256,1024]{1,0:T(8,128)(2,1)S(1)}, u32[]{:S(2)}) copy-start(bf16[256,1024]{1,0:T(8,128)(2,1)S(1)} %pad_maximum_fusion.1.refs_4_) | copy-start | bytes 1572868
  3.4 5.3 %copy-start.8 = (bf16[1,256,512]{2,1,0:T(8,128)(2,1)S(1)}, bf16[1,256,512]{2,1,0:T(8,128)(2,1)}, u32[]{:S(2)}) copy-start(bf16[1,256,512]{2,1,0:T(8,128)(2,1)} %param.12) | copy-start | bytes 786436
  3.5 38.0 %collective-permute-start.4 = (bf16[256,1024]{1,0:T(8,128)(2,1)S(1)}, bf16[256,1024]{1,0:T(8,128)(2,1)}, u32[]{:S(2)}, u32[]{:S(2)}) collective-permute-start(bf16[256,1024]{1,0:T(8,128)(2,1)S(1)} %pad_maximum_fusion.1.refs_4_), channel_id=1, source_target_pairs={{0,1},{1,4},{2,3},{3,6},{4,5},{5,8},{6,7},{7,10},{8,9},{9,12},{10,... | collective-permute-start | bytes 1572872 | tf_op jit(solution)/shard_map/ppermute | solution.py:34
  3.5 28.8 %collective-permute-start.3 = (bf16[256,1024]{1,0:T(8,128)(2,1)S(1)}, bf16[256,1024]{1,0:T(8,128)(2,1)}, u32[]{:S(2)}, u32[]{:S(2)}) collective-permute-start(bf16[256,1024]{1,0:T(8,128)(2,1)S(1)} %pad_maximum_fusion.1.refs_4_), channel_id=1, source_target_pairs={{0,2},{1,3},{2,4},{3,5},{4,6},{5,7},{6,8},{7,9},{8,10},{9,11},{10,... | collective-permute-start | bytes 1572872 | tf_op jit(solution)/shard_map/ppermute | solution.py:18
  8.8 11.6 %copy-start.3 = (bf16[256,1024]{1,0:T(8,128)(2,1)}, bf16[256,1024]{1,0:T(8,128)(2,1)S(1)}, u32[]{:S(2)}) copy-start(bf16[256,1024]{1,0:T(8,128)(2,1)S(1)} %pad_maximum_fusion.refs_0_) | copy-start | bytes 1572868
  8.8 32.7 %collective-permute-start.1 = (bf16[256,1024]{1,0:T(8,128)(2,1)S(1)}, bf16[256,1024]{1,0:T(8,128)(2,1)}, u32[]{:S(2)}, u32[]{:S(2)}) collective-permute-start(bf16[256,1024]{1,0:T(8,128)(2,1)S(1)} %pad_maximum_fusion.refs_0_), channel_id=1, source_target_pairs={{0,61},{1,0},{2,63},{3,2},{4,1},{5,4},{6,3},{7,6},{8,5},{9,8},{10,... | collective-permute-start | bytes 1572872 | tf_op jit(solution)/shard_map/ppermute | solution.py:34
  15.0 20.7 %collective-permute-start = (bf16[256,1024]{1,0:T(8,128)(2,1)S(1)}, bf16[256,1024]{1,0:T(8,128)(2,1)}, u32[]{:S(2)}, u32[]{:S(2)}) collective-permute-start(bf16[256,1024]{1,0:T(8,128)(2,1)S(1)} %pad_maximum_fusion.refs_0_), channel_id=1, source_target_pairs={{0,62},{1,63},{2,0},{3,1},{4,2},{5,3},{6,4},{7,5},{8,6},{9,7},{10,... | collective-permute-start | bytes 1572872 | tf_op jit(solution)/shard_map/ppermute | solution.py:18
  20.4 18.3 %collective-permute-start.6 = (bf16[256,1024]{0,1:T(8,128)(2,1)S(1)}, bf16[256,1024]{0,1:T(8,128)(2,1)S(1)}, u32[]{:S(2)}, u32[]{:S(2)}) collective-permute-start(bf16[256,1024]{0,1:T(8,128)(2,1)S(1)} %bitcast.51), channel_id=1, source_target_pairs={{0,1},{1,0},{2,3},{3,2},{4,5},{5,4},{6,7},{7,6},{8,9},{9,8},{10,11... | collective-permute-start | bytes 1572872 | tf_op jit(solution)/shard_map/ppermute | solution.py:23
  23.3 0.7 copy-start.11
  24.6 0.7 copy-start.10
  32.3 9.3 %collective-permute-start.5 = (bf16[256,1024]{1,0:T(8,128)(2,1)}, bf16[256,1024]{1,0:T(8,128)(2,1)}, u32[]{:S(2)}, u32[]{:S(2)}) collective-permute-start(bf16[256,1024]{1,0:T(8,128)(2,1)} %collective-permute-done.3.refs_5_), channel_id=1, source_target_pairs={{0,1},{1,0},{2,3},{3,2},{4,5},{5,4},{6,7},{7,6},{8,9},{9,8},{10,11... | collective-permute-start | bytes 1572872 | tf_op jit(solution)/shard_map/ppermute | solution.py:23
  35.7 5.8 %collective-permute-start.2 = (bf16[256,1024]{1,0:T(8,128)(2,1)}, bf16[256,1024]{1,0:T(8,128)(2,1)}, u32[]{:S(2)}, u32[]{:S(2)}) collective-permute-start(bf16[256,1024]{1,0:T(8,128)(2,1)} %collective-permute-done.refs_1_), channel_id=1, source_target_pairs={{0,1},{1,0},{2,3},{3,2},{4,5},{5,4},{6,7},{7,6},{8,9},{9,8},{10,11... | collective-permute-start | bytes 1572872 | tf_op jit(solution)/shard_map/ppermute | solution.py:23
  37.9 0.8 copy-start.9
  38.7 0.8 copy-start.5
  104.7 1.7 %copy-start.6 = (bf16[256,512]{1,0:T(8,128)(2,1)S(1)}, bf16[256,512]{1,0:T(8,128)(2,1)}, u32[]{:S(2)}) copy-start(bf16[256,512]{1,0:T(8,128)(2,1)} %get-tuple-element.8) | copy-start | bytes 786436

commit v11 on v9

--- a/solution.py
+++ b/solution.py
@@ -192,7 +192,7 @@
 
     def terms(q, g, k, v, ok):
         z = lax.dot_general(q, k, (((1,), (1,)), ((), ())), preferred_element_type=jnp.float32) * alpha
-        sig = 1.0 / (1.0 + jnp.exp(-z))
+        sig = 0.5 + 0.5 * jnp.tanh(0.5 * z)
         weight = jnp.where(ok, scale, 0.0)
         att = (z * sig * weight).astype(jnp.bfloat16)
         dprod = lax.dot_general(g, v, (((1,), (1,)), ((), ())), preferred_element_type=jnp.float32)

time: 108 us -> 108 us (level)
  no operation moved by 1% of the time
where the time goes in v11:
time: 108 us; the launch traced here: 106 us
  Pallas kernels  62 us (57%)
  starting transfers between devices  23.3 us (22%)
  waiting for transfers between devices  6.57 us (6%)
  local copies, waits for them, and re-layouts  6.07 us (6%)
  other arithmetic  4.92 us (5%)
  matrix products  1.9 us (2%)
  between operations  1.72 us (2%)
    pallas_call x1, Pallas kernels, reduce_blocks(): pl.pallas_call(functools.partial(reduce_kernel, groups, spread), in_specs...  49.5 us
    pallas_call x1, Pallas kernels, attention_tiles(): pl.pallas_call(functools.partial(tiles_kernel, span, alpha, scale), grid=...  12.5 us
    ppermute x2, starting transfers between devices, relayed(): mixed = lax.ppermute(value, 'ctx', pairs)  8.69 us
    ppermute x2, starting transfers between devices, shifted(): return lax.ppermute(value, axis, pairs)  8.38 us
    ppermute x3, starting transfers between devices, exchange(): lax.ppermute(value, axis, [(source, source ^ mask) for source in range(co...  6.24 us
    ppermute x2, waiting for transfers between devices, shifted(): return lax.ppermute(value, axis, pairs)  4.14 us
    unnamed x23, local copies, waits for them, and re-layouts  3.53 us
    ppermute x2, waiting for transfers between devices, relayed(): mixed = lax.ppermute(value, 'ctx', pairs)  2.42 us
  transfers between devices with their start and end apart: 7, of which 2 were waited for; matrix products, arithmetic and copies ran while one was open for 4% of the time, Pallas kernels for 0%

profile of v11, /device:TPU:6, one launch (start us, length us, event | category | flops | bytes accessed | tf_op | source)
XLA Modules:
  0.0 106.5 jit_solution(1703019120242842481)
XLA Ops:
  0.7 1.2 %copy-done = bf16[1024,512]{1,0:T(8,128)(2,1)S(1)} copy-done((bf16[1024,512]{1,0:T(8,128)(2,1)S(1)}, bf16[1024,512]{1,0:T(8,128)(2,1)}, u32[]{:S(2)}) %copy-start) | copy-done | bytes 1048600
  1.9 1.5 %convolution_convert_fusion.1 = bf16[256,512]{1,0:T(8,128)(2,1)S(1)} fusion(bf16[1024,512]{1,0:T(8,128)(2,1)S(1)} %copy-done, bf16[1,256,1024]{2,1,0:T(8,128)(2,1)} %param.8), kind=kOutput, calls=%fused_computation.1 | convolution fusion | flops 268566528 | bytes 1835008 | tf_op jit(solution)/shard_map/dot_general | solution.py:288
  3.5 3.4 %collective-permute-start = (bf16[256,1024]{1,0:T(8,128)(2,1)S(1)}, bf16[256,1024]{1,0:T(8,128)(2,1)}, u32[]{:S(2)}, u32[]{:S(2)}) collective-permute-start(bf16[256,1024]{1,0:T(8,128)(2,1)S(1)} %pad_maximum_fusion.refs_0_.refs_1_), channel_id=1, source_target_pairs={{0,62},{1,63},{2,0},{3,1},{4,2},{5,3},{6,4},{7,5},{8,6},{9,7},{10,... | collective-permute-start | bytes 1572872 | tf_op jit(solution)/shard_map/ppermute | solution.py:18
  6.9 8.7 %collective-permute-start.1 = (bf16[256,1024]{1,0:T(8,128)(2,1)S(1)}, bf16[256,1024]{1,0:T(8,128)(2,1)}, u32[]{:S(2)}, u32[]{:S(2)}) collective-permute-start(bf16[256,1024]{1,0:T(8,128)(2,1)S(1)} %pad_maximum_fusion.refs_0_.refs_1_), channel_id=1, source_target_pairs={{0,61},{1,0},{2,63},{3,2},{4,1},{5,4},{6,3},{7,6},{8,5},{9,8},{10,... | collective-permute-start | bytes 1572872 | tf_op jit(solution)/shard_map/ppermute | solution.py:34
  15.6 0.4 convolution_convert_fusion
  16.1 4.9 %collective-permute-start.3 = (bf16[256,1024]{1,0:T(8,128)(2,1)S(1)}, bf16[256,1024]{1,0:T(8,128)(2,1)}, u32[]{:S(2)}, u32[]{:S(2)}) collective-permute-start(bf16[256,1024]{1,0:T(8,128)(2,1)S(1)} %pad_maximum_fusion.1.refs_8_.refs_9_), channel_id=1, source_target_pairs={{0,2},{1,3},{2,4},{3,5},{4,6},{5,7},{6,8},{7,9},{8,10},{9,11},{10,... | collective-permute-start | bytes 1572872 | tf_op jit(solution)/shard_map/ppermute | solution.py:18
  21.1 0.2 copy.23
  21.3 1.9 %collective-permute-start.6 = (bf16[256,1024]{0,1:T(8,128)(2,1)S(1)}, bf16[256,1024]{0,1:T(8,128)(2,1)S(1)}, u32[]{:S(2)}, u32[]{:S(2)}) collective-permute-start(bf16[256,1024]{0,1:T(8,128)(2,1)S(1)} %bitcast.51), channel_id=1, source_target_pairs={{0,1},{1,0},{2,3},{3,2},{4,5},{5,4},{6,7},{7,6},{8,9},{9,8},{10,11... | collective-permute-start | bytes 1572872 | tf_op jit(solution)/shard_map/ppermute | solution.py:23
  24.1 0.6 copy-done.10
  24.7 0.6 select_reduce_fusion
  25.4 0.6 copy-done.9
  26.6 2.4 %collective-permute-start.2 = (bf16[256,1024]{1,0:T(8,128)(2,1)}, bf16[256,1024]{1,0:T(8,128)(2,1)}, u32[]{:S(2)}, u32[]{:S(2)}) collective-permute-start(bf16[256,1024]{1,0:T(8,128)(2,1)} %collective-permute-done.refs_2_.refs_3_), channel_id=1, source_target_pairs={{0,1},{1,0},{2,3},{3,2},{4,5},{5,4},{6,7},{7,6},{8,9},{9,8},{10,11... | collective-permute-start | bytes 1572872 | tf_op jit(solution)/shard_map/ppermute | solution.py:23
  29.0 4.1 %collective-permute-done.3.refs_10_.refs_11_ = bf16[256,1024]{1,0:T(8,128)(2,1)} collective-permute-done((bf16[256,1024]{1,0:T(8,128)(2,1)S(1)}, bf16[256,1024]{1,0:T(8,128)(2,1)}, u32[]{:S(2)}, u32[]{:S(2)}) %collective-permute-start.3) | collective-permute-done | bytes 524320 | tf_op jit(solution)/shard_map/ppermute | solution.py:18
  33.1 1.9 %collective-permute-start.5 = (bf16[256,1024]{1,0:T(8,128)(2,1)}, bf16[256,1024]{1,0:T(8,128)(2,1)}, u32[]{:S(2)}, u32[]{:S(2)}) collective-permute-start(bf16[256,1024]{1,0:T(8,128)(2,1)} %collective-permute-done.3.refs_10_.refs_11_), channel_id=1, source_target_pairs={{0,1},{1,0},{2,3},{3,2},{4,5},{5,4},{6,7},{7,6},{8,9},{9,8},{10,11... | collective-permute-start | bytes 1572872 | tf_op jit(solution)/shard_map/ppermute | solution.py:23
  35.2 0.8 copy.24.infoc
  35.9 0.8 copy-done.5
  36.7 1.0 fusion
  37.7 1.0 copy.26.xsel_ref
  38.7 2.4 %collective-permute-done.4.refs_12_.refs_13_ = bf16[256,1024]{1,0:T(8,128)(2,1)} collective-permute-done((bf16[256,1024]{1,0:T(8,128)(2,1)S(1)}, bf16[256,1024]{1,0:T(8,128)(2,1)}, u32[]{:S(2)}, u32[]{:S(2)}) %collective-permute-start.4) | collective-permute-done | bytes 524320 | tf_op jit(solution)/shard_map/ppermute | solution.py:34
  41.1 12.5 %shard_map.111 = (bf16[256,512]{1,0:T(8,128)(2,1)}, bf16[256,512]{1,0:T(8,128)(2,1)}, bf16[256,512]{1,0:T(8,128)(2,1)}, bf16[256,512]{1,0:T(8,128)(2,1)}) custom-call(s32[256,21]{1,0:T(8,128)} %copy.24.infoc, s32[21,256]{1,0:T(8,128)} %copy-done.8, bf16[256,1024]{1,0:T(8,128)(2,1)} %copy-done.3, bf16[256,1024]{1,0:T(8,128)(2,1)} %copy-done.3, ...), custom_call_target="tpu_custom_call" | custom-call | flops 2348810240 | bytes 9437184 | tf_op jit(solution)/shard_map/pallas_call | solution.py:240
  53.6 1.9 %pad_maximum_fusion.2.joined_ref = bf16[256,1024]{1,0:T(8,128)(2,1)} fusion(bf16[256,512]{1,0:T(8,128)(2,1)} %get-tuple-element.11, bf16[256,512]{1,0:T(8,128)(2,1)} %get-tuple-element.10), kind=kLoop, calls=%fused_computation.7 | loop fusion | flops 1048576 | bytes 1048576 | tf_op jit(solution)/shard_map/concatenate | solution.py:338
  55.5 49.5 %shard_map.112 = f32[8,16,128]{2,1,0:T(8,128)} custom-call(bf16[512,512]{1,0:T(8,128)(2,1)} %copy.26.xsel_ref, bf16[256,1024]{1,0:T(8,128)(2,1)} %pad_maximum_fusion.2.joined_ref), custom_call_target="tpu_custom_call" | custom-call | tf_op jit(solution)/shard_map/pallas_call | solution.py:145
  105.0 0.8 copy_bitcast_fusion
  105.9 0.6 fusion.17
  (49 shorter events, 0.9 us)
Async XLA Ops:
  0.6 1.2 %copy-start = (bf16[1024,512]{1,0:T(8,128)(2,1)S(1)}, bf16[1024,512]{1,0:T(8,128)(2,1)}, u32[]{:S(2)}) copy-start(bf16[1024,512]{1,0:T(8,128)(2,1)} %param.9) | copy-start | bytes 3145732
  0.6 2.7 %copy-start.6 = (bf16[1,256,512]{2,1,0:T(8,128)(2,1)S(1)}, bf16[1,256,512]{2,1,0:T(8,128)(2,1)}, u32[]{:S(2)}) copy-start(bf16[1,256,512]{2,1,0:T(8,128)(2,1)} %param.12) | copy-start | bytes 786436
  0.7 14.9 %copy-start.2 = (bf16[1024,512]{1,0:T(8,128)(2,1)S(1)}, bf16[1024,512]{1,0:T(8,128)(2,1)}, u32[]{:S(2)}) copy-start(bf16[1024,512]{1,0:T(8,128)(2,1)} %param.10) | copy-start | bytes 3145732
  3.4 12.2 %copy-start.1 = (bf16[1,256,1024]{2,1,0:T(8,128)(2,1)S(1)}, bf16[1,256,1024]{2,1,0:T(8,128)(2,1)}, u32[]{:S(2)}) copy-start(bf16[1,256,1024]{2,1,0:T(8,128)(2,1)} %param.8) | copy-start | bytes 1572868
  3.4 12.6 %copy-start.3 = (bf16[256,1024]{1,0:T(8,128)(2,1)}, bf16[256,1024]{1,0:T(8,128)(2,1)S(1)}, u32[]{:S(2)}) copy-start(bf16[256,1024]{1,0:T(8,128)(2,1)S(1)} %pad_maximum_fusion.refs_0_.refs_1_) | copy-start | bytes 1572868
  3.4 12.6 %copy-start.7 = (bf16[1,256,512]{2,1,0:T(8,128)(2,1)S(1)}, bf16[1,256,512]{2,1,0:T(8,128)(2,1)}, u32[]{:S(2)}) copy-start(bf16[1,256,512]{2,1,0:T(8,128)(2,1)} %param.11) | copy-start | bytes 786436
  3.5 23.1 %collective-permute-start = (bf16[256,1024]{1,0:T(8,128)(2,1)S(1)}, bf16[256,1024]{1,0:T(8,128)(2,1)}, u32[]{:S(2)}, u32[]{:S(2)}) collective-permute-start(bf16[256,1024]{1,0:T(8,128)(2,1)S(1)} %pad_maximum_fusion.refs_0_.refs_1_), channel_id=1, source_target_pairs={{0,62},{1,63},{2,0},{3,1},{4,2},{5,3},{6,4},{7,5},{8,6},{9,7},{10,... | collective-permute-start | bytes 1572872 | tf_op jit(solution)/shard_map/ppermute | solution.py:18
  6.9 31.8 %collective-permute-start.1 = (bf16[256,1024]{1,0:T(8,128)(2,1)S(1)}, bf16[256,1024]{1,0:T(8,128)(2,1)}, u32[]{:S(2)}, u32[]{:S(2)}) collective-permute-start(bf16[256,1024]{1,0:T(8,128)(2,1)S(1)} %pad_maximum_fusion.refs_0_.refs_1_), channel_id=1, source_target_pairs={{0,61},{1,0},{2,63},{3,2},{4,1},{5,4},{6,3},{7,6},{8,5},{9,8},{10,... | collective-permute-start | bytes 1572872 | tf_op jit(solution)/shard_map/ppermute | solution.py:34
  16.1 5.2 %copy-start.4 = (bf16[256,1024]{1,0:T(8,128)(2,1)}, bf16[256,1024]{1,0:T(8,128)(2,1)S(1)}, u32[]{:S(2)}) copy-start(bf16[256,1024]{1,0:T(8,128)(2,1)S(1)} %pad_maximum_fusion.1.refs_8_.refs_9_) | copy-start | bytes 1572868
  16.1 17.0 %collective-permute-start.3 = (bf16[256,1024]{1,0:T(8,128)(2,1)S(1)}, bf16[256,1024]{1,0:T(8,128)(2,1)}, u32[]{:S(2)}, u32[]{:S(2)}) collective-permute-start(bf16[256,1024]{1,0:T(8,128)(2,1)S(1)} %pad_maximum_fusion.1.refs_8_.refs_9_), channel_id=1, source_target_pairs={{0,2},{1,3},{2,4},{3,5},{4,6},{5,7},{6,8},{7,9},{8,10},{9,11},{10,... | collective-permute-start | bytes 1572872 | tf_op jit(solution)/shard_map/ppermute | solution.py:18
  21.1 20.1 %collective-permute-start.4 = (bf16[256,1024]{1,0:T(8,128)(2,1)S(1)}, bf16[256,1024]{1,0:T(8,128)(2,1)}, u32[]{:S(2)}, u32[]{:S(2)}) collective-permute-start(bf16[256,1024]{1,0:T(8,128)(2,1)S(1)} %pad_maximum_fusion.1.refs_8_.refs_9_), channel_id=1, source_target_pairs={{0,1},{1,4},{2,3},{3,6},{4,5},{5,8},{6,7},{7,10},{8,9},{9,12},{10,... | collective-permute-start | bytes 1572872 | tf_op jit(solution)/shard_map/ppermute | solution.py:34
  21.3 14.6 %collective-permute-start.6 = (bf16[256,1024]{0,1:T(8,128)(2,1)S(1)}, bf16[256,1024]{0,1:T(8,128)(2,1)S(1)}, u32[]{:S(2)}, u32[]{:S(2)}) collective-permute-start(bf16[256,1024]{0,1:T(8,128)(2,1)S(1)} %bitcast.51), channel_id=1, source_target_pairs={{0,1},{1,0},{2,3},{3,2},{4,5},{5,4},{6,7},{7,6},{8,9},{9,8},{10,11... | collective-permute-start | bytes 1572872 | tf_op jit(solution)/shard_map/ppermute | solution.py:23
  24.1 0.7 copy-start.10
  25.4 0.7 copy-start.9
  26.6 14.6 %collective-permute-start.2 = (bf16[256,1024]{1,0:T(8,128)(2,1)}, bf16[256,1024]{1,0:T(8,128)(2,1)}, u32[]{:S(2)}, u32[]{:S(2)}) collective-permute-start(bf16[256,1024]{1,0:T(8,128)(2,1)} %collective-permute-done.refs_2_.refs_3_), channel_id=1, source_target_pairs={{0,1},{1,0},{2,3},{3,2},{4,5},{5,4},{6,7},{7,6},{8,9},{9,8},{10,11... | collective-permute-start | bytes 1572872 | tf_op jit(solution)/shard_map/ppermute | solution.py:23
  33.1 8.0 %collective-permute-start.5 = (bf16[256,1024]{1,0:T(8,128)(2,1)}, bf16[256,1024]{1,0:T(8,128)(2,1)}, u32[]{:S(2)}, u32[]{:S(2)}) collective-permute-start(bf16[256,1024]{1,0:T(8,128)(2,1)} %collective-permute-done.3.refs_10_.refs_11_), channel_id=1, source_target_pairs={{0,1},{1,0},{2,3},{3,2},{4,5},{5,4},{6,7},{7,6},{8,9},{9,8},{10,11... | collective-permute-start | bytes 1572872 | tf_op jit(solution)/shard_map/ppermute | solution.py:23
  35.1 0.8 copy-start.8
  35.9 0.8 copy-start.5

commit v12 on v9

--- a/solution.py
+++ b/solution.py
@@ -173,13 +173,15 @@
     return acc
 
 
-def tiles_kernel(span, alpha, scale, infoc, infor, *refs):
-    count = 2 * span + 2
+def tiles_kernel(span, steps, diag, alpha, scale, infoc, infor, *refs):
+    count = 2 * (len(steps) + 1)
     qs = refs[0:count:2]
     gs = refs[1:count:2]
     ks = refs[count:2 * count:2]
     vs = refs[count + 1:2 * count:2]
-    out_ref, dq_ref, dk_ref, dv_ref = refs[2 * count:]
+    rest = refs[2 * count:]
+    partials = None if diag else rest[:4]
+    out_ref, dq_ref, dk_ref, dv_ref = rest if diag else rest[4:]
     lanes = 2 * span + 1
 
     def valid(qa, ka):
@@ -205,16 +207,19 @@
         return dk, dv
 
     q0, g0, k0, v0 = qs[0][...], gs[0][...], ks[0][...], vs[0][...]
-    att, dsc = terms(q0, g0, k0, v0, valid(0, 0))
-    out = jnp.dot(att, v0, preferred_element_type=jnp.float32)
-    dq = jnp.dot(dsc, k0, preferred_element_type=jnp.float32)
-    dk, dv = back(att, dsc, q0, g0)
-    for step in range(1, span + 1):
-        k, v = ks[step][...], vs[step][...]
+    if diag:
+        att, dsc = terms(q0, g0, k0, v0, valid(0, 0))
+        out = jnp.dot(att, v0, preferred_element_type=jnp.float32)
+        dq = jnp.dot(dsc, k0, preferred_element_type=jnp.float32)
+        dk, dv = back(att, dsc, q0, g0)
+    else:
+        out, dq, dk, dv = (ref[...] for ref in partials)
+    for index, step in enumerate(steps, 1):
+        k, v = ks[index][...], vs[index][...]
         att, dsc = terms(q0, g0, k, v, valid(0, step))
         out = out + jnp.dot(att, v, preferred_element_type=jnp.float32)
         dq = dq + jnp.dot(dsc, k, preferred_element_type=jnp.float32)
-        q, g = qs[step][...], gs[step][...]
+        q, g = qs[index][...], gs[index][...]
         att, dsc = terms(q, g, k0, v0, valid(span + step, 0))
         b, c = back(att, dsc, q, g)
         dk = dk + b
@@ -225,28 +230,33 @@
     dv_ref[...] = dv.astype(dv_ref.dtype)
 
 
-def attention_tiles(qg_list, kv_list, infoc, infor, nheads, alpha, scale):
+def attention_tiles(qg_list, kv_list, infoc, infor, nheads, alpha, scale, steps, partials, out_dtype):
     rows = qg_list[0].shape[0]
     span = len(qg_list) - 1
+    diag = partials is None
     blk = lambda offset: pl.BlockSpec((rows, HD), lambda h: (0, h + offset))
     full = lambda arr: pl.BlockSpec(arr.shape, lambda h: (0, 0))
     operands, specs = [infoc, infor], [full(infoc), full(infor)]
     for group in (qg_list, kv_list):
-        for packed in group:
+        for packed in [group[0]] + [group[step] for step in steps]:
             operands += [packed, packed]
             specs += [blk(0), blk(nheads)]
-    shape = jax.ShapeDtypeStruct((rows, nheads * HD), jnp.bfloat16)
+    if not diag:
+        operands += list(partials)
+        specs += [blk(0)] * 4
+    shape = jax.ShapeDtypeStruct((rows, nheads * HD), out_dtype)
     tile = rows * rows * HD * 2
+    tiles = 2 * len(steps) + (1 if diag else 0)
     return pl.pallas_call(
-        functools.partial(tiles_kernel, span, alpha, scale),
+        functools.partial(tiles_kernel, span, tuple(steps), diag, alpha, scale),
         grid=(nheads,),
         in_specs=specs,
         out_specs=[blk(0)] * 4,
         out_shape=[shape] * 4,
         cost_estimate=pl.CostEstimate(
-            flops=nheads * (2 * span + 1) * 5 * tile,
-            transcendentals=nheads * (2 * span + 1) * rows * rows,
-            bytes_accessed=(2 * span + 2) * 2 * rows * nheads * HD * 2 * 2 + 4 * rows * nheads * HD * 2,
+            flops=nheads * tiles * 5 * tile,
+            transcendentals=nheads * tiles * rows * rows,
+            bytes_accessed=(len(steps) + 1) * 2 * rows * nheads * HD * 2 * 2 + 8 * rows * nheads * HD * 4,
         ),
     )(*operands)
 
@@ -330,8 +340,12 @@
         [d[0] for d in described] + [d[1] for d in described] + [d[2].astype(jnp.int32) for d in described]
     ).astype(jnp.int32)
     infoc = infor.T
+    qg_list, kv_list = [qg] + qg_from[1:], [kv] + kv_from[1:]
+    partials = attention_tiles(
+        qg_list, kv_list, infoc, infor, nheads, alpha, scale, (1, 2), None, jnp.float32
+    )
     out_b, dq_b, dk_b, dv_b = attention_tiles(
-        [qg] + qg_from[1:], [kv] + kv_from[1:], infoc, infor, nheads, alpha, scale
+        qg_list, kv_list, infoc, infor, nheads, alpha, scale, (3,), partials, jnp.bfloat16
     )
     attended = out_b.reshape(1, rows, features)
     grad_values = dv_b.reshape(1, rows, features)

time: 108 us -> 114 us (1.056)
  Pallas kernels: 62.4 us -> 67.1 us
  waiting for transfers between devices: 6.57 us -> 4.6 us
  local copies, waits for them, and re-layouts: 6.07 us -> 7.96 us
    pallas_call x1 -> x2, Pallas kernels: 12.8 us -> 16.4 us  [attention_tiles(): pl.pallas_call(functools.partial(tiles_kernel, span, tuple(steps), diag,...]
    ppermute x2, waiting for transfers between devices: 2.42 us -> 1.24 us  [relayed(): mixed = lax.ppermute(value, 'ctx', pairs)]
    unnamed x23 -> x25, local copies, waits for them, and re-layouts: 3.53 us -> 4.35 us
  transfers between devices with their start and end apart: 7 -> 7, of which waited for: 2 -> 2; matrix products, arithmetic and copies ran while one was open for 4% -> 7% of each run, Pallas kernels for 0% -> 9%
where the time goes in v12:
time: 114 us; the launch traced here: 112 us
  Pallas kernels  67.1 us (59%)
  starting transfers between devices  23.3 us (20%)
  local copies, waits for them, and re-layouts  7.96 us (7%)
  other arithmetic  5.79 us (5%)
  waiting for transfers between devices  4.6 us (4%)
  matrix products  1.9 us (2%)
  between operations  1.75 us (2%)
    pallas_call x1, Pallas kernels, reduce_blocks(): pl.pallas_call(functools.partial(reduce_kernel, groups, spread), in_specs...  50.7 us
    pallas_call x2, Pallas kernels, attention_tiles(): pl.pallas_call(functools.partial(tiles_kernel, span, tuple(steps), diag,...  16.4 us
    ppermute x2, starting transfers between devices, relayed(): mixed = lax.ppermute(value, 'ctx', pairs)  8.69 us
    ppermute x2, starting transfers between devices, shifted(): return lax.ppermute(value, axis, pairs)  8.38 us
    ppermute x3, starting transfers between devices, exchange(): lax.ppermute(value, axis, [(source, source ^ mask) for source in range(co...  6.23 us
    unnamed x25, local copies, waits for them, and re-layouts  4.35 us
    ppermute x2, waiting for transfers between devices, shifted(): return lax.ppermute(value, axis, pairs)  3.35 us
  transfers between devices with their start and end apart: 7, of which 2 were waited for; matrix products, arithmetic and copies ran while one was open for 7% of the time, Pallas kernels for 9%

profile of v12, /device:TPU:6, one launch (start us, length us, event | category | flops | bytes accessed | tf_op | source)
XLA Modules:
  0.0 112.4 jit_solution(7621209856775304271)
XLA Ops:
  0.7 1.2 %copy-done = bf16[1024,512]{1,0:T(8,128)(2,1)S(1)} copy-done((bf16[1024,512]{1,0:T(8,128)(2,1)S(1)}, bf16[1024,512]{1,0:T(8,128)(2,1)}, u32[]{:S(2)}) %copy-start) | copy-done | bytes 1048600
  1.9 1.5 %convolution_convert_fusion.1 = bf16[256,512]{1,0:T(8,128)(2,1)S(1)} fusion(bf16[1024,512]{1,0:T(8,128)(2,1)S(1)} %copy-done, bf16[1,256,1024]{2,1,0:T(8,128)(2,1)} %param.8), kind=kOutput, calls=%fused_computation.1 | convolution fusion | flops 268566528 | bytes 1835008 | tf_op jit(solution)/shard_map/dot_general | solution.py:298
  3.5 3.4 %collective-permute-start = (bf16[256,1024]{1,0:T(8,128)(2,1)S(1)}, bf16[256,1024]{1,0:T(8,128)(2,1)S(1)}, u32[]{:S(2)}, u32[]{:S(2)}) collective-permute-start(bf16[256,1024]{1,0:T(8,128)(2,1)S(1)} %pad_maximum_fusion.refs_0_.refs_1_), channel_id=1, source_target_pairs={{0,62},{1,63},{2,0},{3,1},{4,2},{5,3},{6,4},{7,5},{8,6},{9,7},{10,... | collective-permute-start | bytes 1572872 | tf_op jit(solution)/shard_map/ppermute | solution.py:18
  6.9 8.7 %collective-permute-start.4 = (bf16[256,1024]{1,0:T(8,128)(2,1)S(1)}, bf16[256,1024]{1,0:T(8,128)(2,1)}, u32[]{:S(2)}, u32[]{:S(2)}) collective-permute-start(bf16[256,1024]{1,0:T(8,128)(2,1)S(1)} %pad_maximum_fusion.refs_0_.refs_1_), channel_id=1, source_target_pairs={{0,61},{1,0},{2,63},{3,2},{4,1},{5,4},{6,3},{7,6},{8,5},{9,8},{10,... | collective-permute-start | bytes 1572872 | tf_op jit(solution)/shard_map/ppermute | solution.py:34
  16.1 4.9 %collective-permute-start.2 = (bf16[256,1024]{1,0:T(8,128)(2,1)S(1)}, bf16[256,1024]{1,0:T(8,128)(2,1)}, u32[]{:S(2)}, u32[]{:S(2)}) collective-permute-start(bf16[256,1024]{1,0:T(8,128)(2,1)S(1)} %pad_maximum_fusion.1.refs_6_.refs_7_.refs_4_.refs_5_), channel_id=1, source_target_pairs={{0,2},{1,3},{2,4},{3,5},{4,6},{5,7},{6,8},{7,9},{8,10},{9,11},{10,... | collective-permute-start | bytes 1572872 | tf_op jit(solution)/shard_map/ppermute | solution.py:18
  21.1 1.0 copy.25
  22.1 1.9 %collective-permute-start.6 = (bf16[256,1024]{0,1:T(8,128)(2,1)}, bf16[256,1024]{0,1:T(8,128)(2,1)}, u32[]{:S(2)}, u32[]{:S(2)}) collective-permute-start(bf16[256,1024]{0,1:T(8,128)(2,1)} %bitcast.51), channel_id=1, source_target_pairs={{0,1},{1,0},{2,3},{3,2},{4,5},{5,4},{6,7},{7,6},{8,9},{9,8},{10,11... | collective-permute-start | bytes 1572872 | tf_op jit(solution)/shard_map/ppermute | solution.py:23
  24.9 0.6 copy-done.11
  25.5 0.6 select_reduce_fusion
  26.2 0.6 copy-done.10
  27.4 2.4 %collective-permute-start.1 = (bf16[256,1024]{1,0:T(8,128)(2,1)S(1)}, bf16[256,1024]{1,0:T(8,128)(2,1)S(1)}, u32[]{:S(2)}, u32[]{:S(2)}) collective-permute-start(bf16[256,1024]{1,0:T(8,128)(2,1)S(1)} %collective-permute-done.refs_2_.refs_3_), channel_id=1, source_target_pairs={{0,1},{1,0},{2,3},{3,2},{4,5},{5,4},{6,7},{7,6},{8,9},{9,8},{10,11... | collective-permute-start | bytes 1572872 | tf_op jit(solution)/shard_map/ppermute | solution.py:23
  29.8 3.3 %collective-permute-done.2.refs_8_.refs_9_ = bf16[256,1024]{1,0:T(8,128)(2,1)} collective-permute-done((bf16[256,1024]{1,0:T(8,128)(2,1)S(1)}, bf16[256,1024]{1,0:T(8,128)(2,1)}, u32[]{:S(2)}, u32[]{:S(2)}) %collective-permute-start.2) | collective-permute-done | bytes 524320 | tf_op jit(solution)/shard_map/ppermute | solution.py:18
  33.1 1.9 %collective-permute-start.3 = (bf16[256,1024]{1,0:T(8,128)(2,1)}, bf16[256,1024]{1,0:T(8,128)(2,1)}, u32[]{:S(2)}, u32[]{:S(2)}) collective-permute-start(bf16[256,1024]{1,0:T(8,128)(2,1)} %collective-permute-done.2.refs_8_.refs_9_), channel_id=1, source_target_pairs={{0,1},{1,0},{2,3},{3,2},{4,5},{5,4},{6,7},{7,6},{8,9},{9,8},{10,11... | collective-permute-start | bytes 1572872 | tf_op jit(solution)/shard_map/ppermute | solution.py:23
  35.2 0.8 copy.27.infoc
  35.9 1.9 %fusion = bf16[512,32,1,16]{0,3,2,1:T(8,128)(2,1)} fusion(s32[]{:T(128)S(6)} %select_n.294, bf16[256,32,2,16]{0,3,2,1:T(8,128)(2,1)} %bitcast.52, bf16[256,32,2,16]{0,3,2,1:T(8,128)(2,1)} %bitcast.24), kind=kLoop, calls=%fused_computation.4 | loop fusion | flops 1048576 | bytes 1572868 | tf_op jit(solution)/shard_map/concatenate | solution.py:169
  37.8 2.1 %copy.29.xsel_ref = bf16[512,512]{1,0:T(8,128)(2,1)} copy(bf16[512,512]{0,1:T(8,128)(2,1)} %bitcast.53) | data formatting | bytes 1048576 | tf_op jit(solution)/shard_map/reshape | solution.py:171
  39.9 1.2 %collective-permute-done.5.refs_10_.refs_11_ = bf16[256,1024]{1,0:T(8,128)(2,1)} collective-permute-done((bf16[256,1024]{1,0:T(8,128)(2,1)S(1)}, bf16[256,1024]{1,0:T(8,128)(2,1)}, u32[]{:S(2)}, u32[]{:S(2)}) %collective-permute-start.5) | collective-permute-done | bytes 524320 | tf_op jit(solution)/shard_map/ppermute | solution.py:34
  41.1 10.1 %shard_map.111 = (f32[256,512]{1,0:T(8,128)}, f32[256,512]{1,0:T(8,128)}, f32[256,512]{1,0:T(8,128)}, f32[256,512]{1,0:T(8,128)}) custom-call(s32[256,21]{1,0:T(8,128)} %copy.27.infoc, s32[21,256]{1,0:T(8,128)} %copy-done.7, bf16[256,1024]{1,0:T(8,128)(2,1)} %copy-done.1, bf16[256,1024]{1,0:T(8,128)(2,1)} %copy-done.1, bf16[256,1024]{1,0:T(8,128)(2,1)} %copy-done.4, ...), custom_call_target="tpu_custom_call" | custom-call | flops 1677721600 | bytes 7340032 | tf_op jit(solution)/shard_map/pallas_call | solution.py:250
  51.3 0.8 copy-done.5
  52.1 6.3 %shard_map.112 = (bf16[256,512]{1,0:T(8,128)(2,1)}, bf16[256,512]{1,0:T(8,128)(2,1)}, bf16[256,512]{1,0:T(8,128)(2,1)}, bf16[256,512]{1,0:T(8,128)(2,1)}) custom-call(s32[256,21]{1,0:T(8,128)} %copy.27.infoc, s32[21,256]{1,0:T(8,128)} %copy-done.7, bf16[256,1024]{1,0:T(8,128)(2,1)} %copy-done.1, bf16[256,1024]{1,0:T(8,128)(2,1)} %copy-done.1, ...), custom_call_target="tpu_custom_call" | custom-call | flops 671088640 | bytes 6291456 | tf_op jit(solution)/shard_map/pallas_call | solution.py:250
  58.4 1.9 %pad_maximum_fusion.2.joined_ref = bf16[256,1024]{1,0:T(8,128)(2,1)} fusion(bf16[256,512]{1,0:T(8,128)(2,1)} %get-tuple-element.19, bf16[256,512]{1,0:T(8,128)(2,1)} %get-tuple-element.18), kind=kLoop, calls=%fused_computation.7 | loop fusion | flops 1048576 | bytes 1048576 | tf_op jit(solution)/shard_map/concatenate | solution.py:352
  60.3 50.7 %shard_map.113 = f32[8,16,128]{2,1,0:T(8,128)} custom-call(bf16[512,512]{1,0:T(8,128)(2,1)} %copy.29.xsel_ref, bf16[256,1024]{1,0:T(8,128)(2,1)} %pad_maximum_fusion.2.joined_ref), custom_call_target="tpu_custom_call" | custom-call | tf_op jit(solution)/shard_map/pallas_call | solution.py:145
  110.9 0.8 copy_bitcast_fusion
  111.8 0.6 fusion.17
  (52 shorter events, 1.3 us)
Async XLA Ops:
  0.6 1.2 %copy-start = (bf16[1024,512]{1,0:T(8,128)(2,1)S(1)}, bf16[1024,512]{1,0:T(8,128)(2,1)}, u32[]{:S(2)}) copy-start(bf16[1024,512]{1,0:T(8,128)(2,1)} %param.9) | copy-start | bytes 3145732
  0.6 2.7 %copy-start.8 = (bf16[1,256,512]{2,1,0:T(8,128)(2,1)S(1)}, bf16[1,256,512]{2,1,0:T(8,128)(2,1)}, u32[]{:S(2)}) copy-start(bf16[1,256,512]{2,1,0:T(8,128)(2,1)} %param.12) | copy-start | bytes 786436
  0.7 14.9 %copy-start.6 = (bf16[1024,512]{1,0:T(8,128)(2,1)S(1)}, bf16[1024,512]{1,0:T(8,128)(2,1)}, u32[]{:S(2)}) copy-start(bf16[1024,512]{1,0:T(8,128)(2,1)} %param.10) | copy-start | bytes 3145732
  3.4 12.2 %copy-start.3 = (bf16[1,256,1024]{2,1,0:T(8,128)(2,1)S(1)}, bf16[1,256,1024]{2,1,0:T(8,128)(2,1)}, u32[]{:S(2)}) copy-start(bf16[1,256,1024]{2,1,0:T(8,128)(2,1)} %param.8) | copy-start | bytes 1572868
  3.4 12.6 %copy-start.1 = (bf16[256,1024]{1,0:T(8,128)(2,1)}, bf16[256,1024]{1,0:T(8,128)(2,1)S(1)}, u32[]{:S(2)}) copy-start(bf16[256,1024]{1,0:T(8,128)(2,1)S(1)} %pad_maximum_fusion.refs_0_.refs_1_) | copy-start | bytes 1572868
  3.4 12.6 %copy-start.9 = (bf16[1,256,512]{2,1,0:T(8,128)(2,1)S(1)}, bf16[1,256,512]{2,1,0:T(8,128)(2,1)}, u32[]{:S(2)}) copy-start(bf16[1,256,512]{2,1,0:T(8,128)(2,1)} %param.11) | copy-start | bytes 786436
  3.5 23.9 %collective-permute-start = (bf16[256,1024]{1,0:T(8,128)(2,1)S(1)}, bf16[256,1024]{1,0:T(8,128)(2,1)S(1)}, u32[]{:S(2)}, u32[]{:S(2)}) collective-permute-start(bf16[256,1024]{1,0:T(8,128)(2,1)S(1)} %pad_maximum_fusion.refs_0_.refs_1_), channel_id=1, source_target_pairs={{0,62},{1,63},{2,0},{3,1},{4,2},{5,3},{6,4},{7,5},{8,6},{9,7},{10,... | collective-permute-start | bytes 1572872 | tf_op jit(solution)/shard_map/ppermute | solution.py:18
  6.9 33.0 %collective-permute-start.4 = (bf16[256,1024]{1,0:T(8,128)(2,1)S(1)}, bf16[256,1024]{1,0:T(8,128)(2,1)}, u32[]{:S(2)}, u32[]{:S(2)}) collective-permute-start(bf16[256,1024]{1,0:T(8,128)(2,1)S(1)} %pad_maximum_fusion.refs_0_.refs_1_), channel_id=1, source_target_pairs={{0,61},{1,0},{2,63},{3,2},{4,1},{5,4},{6,3},{7,6},{8,5},{9,8},{10,... | collective-permute-start | bytes 1572872 | tf_op jit(solution)/shard_map/ppermute | solution.py:34
  16.1 6.0 %copy-start.2 = (bf16[256,1024]{1,0:T(8,128)(2,1)}, bf16[256,1024]{1,0:T(8,128)(2,1)S(1)}, u32[]{:S(2)}) copy-start(bf16[256,1024]{1,0:T(8,128)(2,1)S(1)} %pad_maximum_fusion.1.refs_6_.refs_7_.refs_4_.refs_5_) | copy-start | bytes 1572868
  16.1 17.0 %collective-permute-start.2 = (bf16[256,1024]{1,0:T(8,128)(2,1)S(1)}, bf16[256,1024]{1,0:T(8,128)(2,1)}, u32[]{:S(2)}, u32[]{:S(2)}) collective-permute-start(bf16[256,1024]{1,0:T(8,128)(2,1)S(1)} %pad_maximum_fusion.1.refs_6_.refs_7_.refs_4_.refs_5_), channel_id=1, source_target_pairs={{0,2},{1,3},{2,4},{3,5},{4,6},{5,7},{6,8},{7,9},{8,10},{9,11},{10,... | collective-permute-start | bytes 1572872 | tf_op jit(solution)/shard_map/ppermute | solution.py:18
  21.1 20.1 %collective-permute-start.5 = (bf16[256,1024]{1,0:T(8,128)(2,1)S(1)}, bf16[256,1024]{1,0:T(8,128)(2,1)}, u32[]{:S(2)}, u32[]{:S(2)}) collective-permute-start(bf16[256,1024]{1,0:T(8,128)(2,1)S(1)} %pad_maximum_fusion.1.refs_6_.refs_7_.refs_4_.refs_5_), channel_id=1, source_target_pairs={{0,1},{1,4},{2,3},{3,6},{4,5},{5,8},{6,7},{7,10},{8,9},{9,12},{10,... | collective-permute-start | bytes 1572872 | tf_op jit(solution)/shard_map/ppermute | solution.py:34
  22.1 13.8 %collective-permute-start.6 = (bf16[256,1024]{0,1:T(8,128)(2,1)}, bf16[256,1024]{0,1:T(8,128)(2,1)}, u32[]{:S(2)}, u32[]{:S(2)}) collective-permute-start(bf16[256,1024]{0,1:T(8,128)(2,1)} %bitcast.51), channel_id=1, source_target_pairs={{0,1},{1,0},{2,3},{3,2},{4,5},{5,4},{6,7},{7,6},{8,9},{9,8},{10,11... | collective-permute-start | bytes 1572872 | tf_op jit(solution)/shard_map/ppermute | solution.py:23
  24.9 0.7 copy-start.11
  26.2 0.7 copy-start.10
  27.4 10.5 %copy-start.4 = (bf16[256,1024]{1,0:T(8,128)(2,1)}, bf16[256,1024]{1,0:T(8,128)(2,1)S(1)}, u32[]{:S(2)}) copy-start(bf16[256,1024]{1,0:T(8,128)(2,1)S(1)} %collective-permute-done.refs_2_.refs_3_) | copy-start | bytes 1572868
  27.4 23.9 %collective-permute-start.1 = (bf16[256,1024]{1,0:T(8,128)(2,1)S(1)}, bf16[256,1024]{1,0:T(8,128)(2,1)S(1)}, u32[]{:S(2)}, u32[]{:S(2)}) collective-permute-start(bf16[256,1024]{1,0:T(8,128)(2,1)S(1)} %collective-permute-done.refs_2_.refs_3_), channel_id=1, source_target_pairs={{0,1},{1,0},{2,3},{3,2},{4,5},{5,4},{6,7},{7,6},{8,9},{9,8},{10,11... | collective-permute-start | bytes 1572872 | tf_op jit(solution)/shard_map/ppermute | solution.py:23
  33.1 18.1 %collective-permute-start.3 = (bf16[256,1024]{1,0:T(8,128)(2,1)}, bf16[256,1024]{1,0:T(8,128)(2,1)}, u32[]{:S(2)}, u32[]{:S(2)}) collective-permute-start(bf16[256,1024]{1,0:T(8,128)(2,1)} %collective-permute-done.2.refs_8_.refs_9_), channel_id=1, source_target_pairs={{0,1},{1,0},{2,3},{3,2},{4,5},{5,4},{6,7},{7,6},{8,9},{9,8},{10,11... | collective-permute-start | bytes 1572872 | tf_op jit(solution)/shard_map/ppermute | solution.py:23
  35.2 0.8 copy-start.7
  51.2 0.8 copy-start.5

commit v13 on v9

--- a/solution.py
+++ b/solution.py
@@ -46,7 +46,7 @@
     )
 
 
-def reduce_kernel(groups, spread, xsel_ref, joined_ref, out_ref, joined_land, part_ref, sent, landed, sums, mixed, finals, sems):
+def reduce_kernel(groups, spread, own_ref, other_ref, joined_ref, out_ref, joined_land, part_ref, sent, landed, sums, mixed, finals, sems):
     me = lax.axis_index("ctx")
     group = lax.axis_index("dp")
     core = me % 2
@@ -72,9 +72,9 @@
     pair.start()
     rows = joined_ref.shape[0]
     contract = (((0,), (0,)), ((), ()))
-    acc = lax.dot_general(xsel_ref[:rows], joined_ref[...], contract, preferred_element_type=jnp.float32)
+    acc = lax.dot_general(own_ref[...], joined_ref[...], contract, preferred_element_type=jnp.float32)
     pair.wait()
-    acc = acc + lax.dot_general(xsel_ref[rows:], joined_land[...], contract, preferred_element_type=jnp.float32)
+    acc = acc + lax.dot_general(other_ref[...], joined_land[...], contract, preferred_element_type=jnp.float32)
     _, _, share, lanes = part_ref.shape
     for index in range(spread):
         part_ref[index] = acc[:, index * lanes:(index + 1) * lanes].reshape(groups, share, lanes)
@@ -137,14 +137,14 @@
     out_ref[...] = finals[...]
 
 
-def reduce_blocks(xsel, joined, share, spread):
+def reduce_blocks(own, other, joined, share, spread):
     rows, width = joined.shape
-    groups = xsel.shape[1] // share
+    groups = own.shape[1] // share
     lanes = width // spread
     vmem = pl.BlockSpec(memory_space=pltpu.VMEM)
     finals = pl.pallas_call(
         functools.partial(reduce_kernel, groups, spread),
-        in_specs=[vmem, vmem],
+        in_specs=[vmem, vmem, vmem],
         out_specs=vmem,
         out_shape=jax.ShapeDtypeStruct((spread, share, lanes), jnp.float32),
         scratch_shapes=[
@@ -158,18 +158,18 @@
             pltpu.SemaphoreType.DMA((7, max(groups, spread))),
         ],
         compiler_params=pltpu.CompilerParams(collective_id=1, has_side_effects=True),
-    )(xsel, joined)
+    )(own, other, joined)
     return finals.transpose(1, 0, 2).reshape(share, width)
 
 
-def reduce_rows(local, partner_events, joined, myself, cycle_size):
-    width = local.shape[1]
-    share = width // cycle_size
-    core = myself % 2
-    both_events = jnp.concatenate([local, partner_events], axis=0)
-    halves = both_events.reshape(both_events.shape[0], width // (2 * share), 2, share)
-    kept = lax.dynamic_index_in_dim(halves, core, 2, keepdims=False).reshape(both_events.shape[0], width // 2)
-    acc = reduce_blocks(kept, joined, share, lax.axis_size("dp"))
+def select_features(events, share, bit):
+    width = events.shape[1]
+    halves = events.reshape(events.shape[0], width // (2 * share), 2, share)
+    return lax.dynamic_index_in_dim(halves, bit, 2, keepdims=False).reshape(events.shape[0], width // 2)
+
+
+def reduce_rows(own, other, joined, share):
+    acc = reduce_blocks(own, other, joined, share, lax.axis_size("dp"))
     return acc
 
 
@@ -319,7 +319,9 @@
             packed[:, features:].reshape(rows, nheads, HD),
         )
 
-    partner_events = exchange(local, "ctx", 1)
+    share = local.shape[1] // cycle_size
+    own_events = select_features(local, share, myself % 2)
+    other_events = exchange(select_features(local, share, 1 - myself % 2), "ctx", 1)
     kv = jnp.concatenate([keys, values[0]], axis=1)
     qg = jnp.concatenate([queries, grad_out[0]], axis=1)
     kv_from, kv_anchor = relayed(kv, myself, 1)
@@ -336,7 +338,7 @@
     attended = out_b.reshape(1, rows, features)
     grad_values = dv_b.reshape(1, rows, features)
     joined = jnp.concatenate([dq_b, dk_b], axis=1)
-    mine = reduce_rows(local, partner_events, joined, myself, cycle_size)
+    mine = reduce_rows(own_events, other_events, joined, share)
     grad_wq = mine[:, :features].astype(jnp.bfloat16)
     grad_wk = mine[:, features:].astype(jnp.bfloat16)
     return (attended, grad_values, grad_wq, grad_wk)

time: 108 us -> 107 us (level)
  Pallas kernels: 62.4 us -> 60.3 us
  waiting for transfers between devices: 6.57 us -> 8.29 us
    pallas_call x1, Pallas kernels: 49.6 us -> 47.5 us  [reduce_blocks(): pl.pallas_call(functools.partial(reduce_kernel, groups, spread), in_specs...]
    ppermute x2, waiting for transfers between devices: 2.42 us -> 4.35 us  [relayed(): mixed = lax.ppermute(value, 'ctx', pairs)]
    unnamed x23 -> x25, local copies, waits for them, and re-layouts: 3.53 us -> 4.25 us
  transfers between devices with their start and end apart: 7 -> 7, of which waited for: 2 -> 2; matrix products, arithmetic and copies ran while one was open for 4% -> 5% of each run, Pallas kernels for 0% -> 12%
where the time goes in v13:
time: 107 us; the launch traced here: 106 us
  Pallas kernels  60.3 us (56%)
  starting transfers between devices  23.3 us (22%)
  waiting for transfers between devices  8.29 us (8%)
  local copies, waits for them, and re-layouts  6.81 us (6%)
  other arithmetic  3.91 us (4%)
  matrix products  1.9 us (2%)
  between operations  1.77 us (2%)
    pallas_call x1, Pallas kernels, reduce_blocks(): pl.pallas_call(functools.partial(reduce_kernel, groups, spread), in_specs...  47.5 us
    pallas_call x1, Pallas kernels, attention_tiles(): pl.pallas_call(functools.partial(tiles_kernel, span, alpha, scale), grid=...  12.8 us
    ppermute x2, starting transfers between devices, relayed(): mixed = lax.ppermute(value, 'ctx', pairs)  8.69 us
    ppermute x2, starting transfers between devices, shifted(): return lax.ppermute(value, axis, pairs)  8.38 us
    ppermute x3, starting transfers between devices, exchange(): lax.ppermute(value, axis, [(source, source ^ mask) for source in range(co...  6.24 us
    ppermute x2, waiting for transfers between devices, relayed(): mixed = lax.ppermute(value, 'ctx', pairs)  4.35 us
    unnamed x25, local copies, waits for them, and re-layouts  4.25 us
    ppermute x2, waiting for transfers between devices, shifted(): return lax.ppermute(value, axis, pairs)  3.94 us
  transfers between devices with their start and end apart: 7, of which 2 were waited for; matrix products, arithmetic and copies ran while one was open for 5% of the time, Pallas kernels for 12%

profile of v13, /device:TPU:6, one launch (start us, length us, event | category | flops | bytes accessed | tf_op | source)
XLA Modules:
  0.0 106.3 jit_solution(14362923947482077690)
XLA Ops:
  0.7 1.2 %copy-done = bf16[1024,512]{1,0:T(8,128)(2,1)S(1)} copy-done((bf16[1024,512]{1,0:T(8,128)(2,1)S(1)}, bf16[1024,512]{1,0:T(8,128)(2,1)}, u32[]{:S(2)}) %copy-start) | copy-done | bytes 1048600
  1.9 1.5 %convolution_convert_fusion.1 = bf16[256,512]{1,0:T(8,128)(2,1)S(1)} fusion(bf16[1024,512]{1,0:T(8,128)(2,1)S(1)} %copy-done, bf16[1,256,1024]{2,1,0:T(8,128)(2,1)} %param.8), kind=kOutput, calls=%fused_computation.1 | convolution fusion | flops 268566528 | bytes 1835008 | tf_op jit(solution)/shard_map/dot_general | solution.py:288
  3.5 3.4 %collective-permute-start = (bf16[256,1024]{1,0:T(8,128)(2,1)S(1)}, bf16[256,1024]{1,0:T(8,128)(2,1)}, u32[]{:S(2)}, u32[]{:S(2)}) collective-permute-start(bf16[256,1024]{1,0:T(8,128)(2,1)S(1)} %pad_maximum_fusion.refs_0_.refs_1_), channel_id=1, source_target_pairs={{0,62},{1,63},{2,0},{3,1},{4,2},{5,3},{6,4},{7,5},{8,6},{9,7},{10,... | collective-permute-start | bytes 1572872 | tf_op jit(solution)/shard_map/ppermute | solution.py:18
  6.9 8.7 %collective-permute-start.1 = (bf16[256,1024]{1,0:T(8,128)(2,1)S(1)}, bf16[256,1024]{1,0:T(8,128)(2,1)}, u32[]{:S(2)}, u32[]{:S(2)}) collective-permute-start(bf16[256,1024]{1,0:T(8,128)(2,1)S(1)} %pad_maximum_fusion.refs_0_.refs_1_), channel_id=1, source_target_pairs={{0,61},{1,0},{2,63},{3,2},{4,1},{5,4},{6,3},{7,6},{8,5},{9,8},{10,... | collective-permute-start | bytes 1572872 | tf_op jit(solution)/shard_map/ppermute | solution.py:34
  15.6 0.4 convolution_convert_fusion
  16.1 4.9 %collective-permute-start.3 = (bf16[256,1024]{1,0:T(8,128)(2,1)S(1)}, bf16[256,1024]{1,0:T(8,128)(2,1)}, u32[]{:S(2)}, u32[]{:S(2)}) collective-permute-start(bf16[256,1024]{1,0:T(8,128)(2,1)S(1)} %pad_maximum_fusion.1.refs_8_.refs_9_), channel_id=1, source_target_pairs={{0,2},{1,3},{2,4},{3,5},{4,6},{5,7},{6,8},{7,9},{8,10},{9,11},{10,... | collective-permute-start | bytes 1572872 | tf_op jit(solution)/shard_map/ppermute | solution.py:18
  21.1 0.2 copy.24
  21.5 1.9 %collective-permute-start.6 = (bf16[256,512]{1,0:T(8,128)(2,1)S(1)}, bf16[256,512]{1,0:T(8,128)(2,1)S(1)}, u32[]{:S(2)}, u32[]{:S(2)}) collective-permute-start(bf16[256,512]{1,0:T(8,128)(2,1)S(1)} %copy.25), channel_id=1, source_target_pairs={{0,1},{1,0},{2,3},{3,2},{4,5},{5,4},{6,7},{7,6},{8,9},{9,8},{10,11... | collective-permute-start | bytes 786440 | tf_op jit(solution)/shard_map/ppermute | solution.py:23
  24.3 0.6 copy-done.10
  25.0 0.6 select_reduce_fusion
  25.7 0.6 copy-done.9
  26.8 2.4 %collective-permute-start.2 = (bf16[256,1024]{1,0:T(8,128)(2,1)}, bf16[256,1024]{1,0:T(8,128)(2,1)S(1)}, u32[]{:S(2)}, u32[]{:S(2)}) collective-permute-start(bf16[256,1024]{1,0:T(8,128)(2,1)} %collective-permute-done.refs_2_.refs_3_), channel_id=1, source_target_pairs={{0,1},{1,0},{2,3},{3,2},{4,5},{5,4},{6,7},{7,6},{8,9},{9,8},{10,11... | collective-permute-start | bytes 1572872 | tf_op jit(solution)/shard_map/ppermute | solution.py:23
  29.2 3.9 %collective-permute-done.3.refs_10_.refs_11_ = bf16[256,1024]{1,0:T(8,128)(2,1)} collective-permute-done((bf16[256,1024]{1,0:T(8,128)(2,1)S(1)}, bf16[256,1024]{1,0:T(8,128)(2,1)}, u32[]{:S(2)}, u32[]{:S(2)}) %collective-permute-start.3) | collective-permute-done | bytes 524320 | tf_op jit(solution)/shard_map/ppermute | solution.py:18
  33.1 1.9 %collective-permute-start.5 = (bf16[256,1024]{1,0:T(8,128)(2,1)}, bf16[256,1024]{1,0:T(8,128)(2,1)}, u32[]{:S(2)}, u32[]{:S(2)}) collective-permute-start(bf16[256,1024]{1,0:T(8,128)(2,1)} %collective-permute-done.3.refs_10_.refs_11_), channel_id=1, source_target_pairs={{0,1},{1,0},{2,3},{3,2},{4,5},{5,4},{6,7},{7,6},{8,9},{9,8},{10,11... | collective-permute-start | bytes 1572872 | tf_op jit(solution)/shard_map/ppermute | solution.py:23
  35.2 0.8 copy.23.infoc
  35.9 0.8 copy.26.own_ref
  36.8 4.3 %collective-permute-done.4.refs_12_.refs_13_ = bf16[256,1024]{1,0:T(8,128)(2,1)} collective-permute-done((bf16[256,1024]{1,0:T(8,128)(2,1)S(1)}, bf16[256,1024]{1,0:T(8,128)(2,1)}, u32[]{:S(2)}, u32[]{:S(2)}) %collective-permute-start.4) | collective-permute-done | bytes 524320 | tf_op jit(solution)/shard_map/ppermute | solution.py:34
  41.1 0.8 copy-done.11
  41.9 12.8 %shard_map.111 = (bf16[256,512]{1,0:T(8,128)(2,1)}, bf16[256,512]{1,0:T(8,128)(2,1)}, bf16[256,512]{1,0:T(8,128)(2,1)}, bf16[256,512]{1,0:T(8,128)(2,1)}) custom-call(s32[256,21]{1,0:T(8,128)} %copy.23.infoc, s32[21,256]{1,0:T(8,128)} %copy-done.8, bf16[256,1024]{1,0:T(8,128)(2,1)} %copy-done.3, bf16[256,1024]{1,0:T(8,128)(2,1)} %copy-done.3, ...), custom_call_target="tpu_custom_call" | custom-call | flops 2348810240 | bytes 9437184 | tf_op jit(solution)/shard_map/pallas_call | solution.py:240
  54.7 1.9 %pad_maximum_fusion.2.joined_ref = bf16[256,1024]{1,0:T(8,128)(2,1)} fusion(bf16[256,512]{1,0:T(8,128)(2,1)} %get-tuple-element.11, bf16[256,512]{1,0:T(8,128)(2,1)} %get-tuple-element.10), kind=kLoop, calls=%fused_computation.4 | loop fusion | flops 1048576 | bytes 1048576 | tf_op jit(solution)/shard_map/concatenate | solution.py:340
  56.6 0.7 copy-done.5
  57.3 47.5 %shard_map.112 = f32[8,16,128]{2,1,0:T(8,128)} custom-call(bf16[256,512]{1,0:T(8,128)(2,1)} %copy.26.own_ref, bf16[256,512]{1,0:T(8,128)(2,1)} %copy-done.5, bf16[256,1024]{1,0:T(8,128)(2,1)} %pad_maximum_fusion.2.joined_ref), custom_call_target="tpu_custom_call" | custom-call | tf_op jit(solution)/shard_map/pallas_call | solution.py:145
  104.8 0.8 copy_bitcast_fusion
  105.7 0.6 fusion.16
  (52 shorter events, 1.0 us)
Async XLA Ops:
  0.6 1.2 %copy-start = (bf16[1024,512]{1,0:T(8,128)(2,1)S(1)}, bf16[1024,512]{1,0:T(8,128)(2,1)}, u32[]{:S(2)}) copy-start(bf16[1024,512]{1,0:T(8,128)(2,1)} %param.9) | copy-start | bytes 3145732
  0.6 2.7 %copy-start.6 = (bf16[1,256,512]{2,1,0:T(8,128)(2,1)S(1)}, bf16[1,256,512]{2,1,0:T(8,128)(2,1)}, u32[]{:S(2)}) copy-start(bf16[1,256,512]{2,1,0:T(8,128)(2,1)} %param.12) | copy-start | bytes 786436
  0.7 14.9 %copy-start.2 = (bf16[1024,512]{1,0:T(8,128)(2,1)S(1)}, bf16[1024,512]{1,0:T(8,128)(2,1)}, u32[]{:S(2)}) copy-start(bf16[1024,512]{1,0:T(8,128)(2,1)} %param.10) | copy-start | bytes 3145732
  3.4 12.2 %copy-start.1 = (bf16[1,256,1024]{2,1,0:T(8,128)(2,1)S(1)}, bf16[1,256,1024]{2,1,0:T(8,128)(2,1)}, u32[]{:S(2)}) copy-start(bf16[1,256,1024]{2,1,0:T(8,128)(2,1)} %param.8) | copy-start | bytes 1572868
  3.4 12.6 %copy-start.3 = (bf16[256,1024]{1,0:T(8,128)(2,1)}, bf16[256,1024]{1,0:T(8,128)(2,1)S(1)}, u32[]{:S(2)}) copy-start(bf16[256,1024]{1,0:T(8,128)(2,1)S(1)} %pad_maximum_fusion.refs_0_.refs_1_) | copy-start | bytes 1572868
  3.4 12.6 %copy-start.7 = (bf16[1,256,512]{2,1,0:T(8,128)(2,1)S(1)}, bf16[1,256,512]{2,1,0:T(8,128)(2,1)}, u32[]{:S(2)}) copy-start(bf16[1,256,512]{2,1,0:T(8,128)(2,1)} %param.11) | copy-start | bytes 786436
  3.5 23.3 %collective-permute-start = (bf16[256,1024]{1,0:T(8,128)(2,1)S(1)}, bf16[256,1024]{1,0:T(8,128)(2,1)}, u32[]{:S(2)}, u32[]{:S(2)}) collective-permute-start(bf16[256,1024]{1,0:T(8,128)(2,1)S(1)} %pad_maximum_fusion.refs_0_.refs_1_), channel_id=1, source_target_pairs={{0,62},{1,63},{2,0},{3,1},{4,2},{5,3},{6,4},{7,5},{8,6},{9,7},{10,... | collective-permute-start | bytes 1572872 | tf_op jit(solution)/shard_map/ppermute | solution.py:18
  6.9 29.9 %collective-permute-start.1 = (bf16[256,1024]{1,0:T(8,128)(2,1)S(1)}, bf16[256,1024]{1,0:T(8,128)(2,1)}, u32[]{:S(2)}, u32[]{:S(2)}) collective-permute-start(bf16[256,1024]{1,0:T(8,128)(2,1)S(1)} %pad_maximum_fusion.refs_0_.refs_1_), channel_id=1, source_target_pairs={{0,61},{1,0},{2,63},{3,2},{4,1},{5,4},{6,3},{7,6},{8,5},{9,8},{10,... | collective-permute-start | bytes 1572872 | tf_op jit(solution)/shard_map/ppermute | solution.py:34
  16.1 5.2 %copy-start.4 = (bf16[256,1024]{1,0:T(8,128)(2,1)}, bf16[256,1024]{1,0:T(8,128)(2,1)S(1)}, u32[]{:S(2)}) copy-start(bf16[256,1024]{1,0:T(8,128)(2,1)S(1)} %pad_maximum_fusion.1.refs_8_.refs_9_) | copy-start | bytes 1572868
  16.1 17.0 %collective-permute-start.3 = (bf16[256,1024]{1,0:T(8,128)(2,1)S(1)}, bf16[256,1024]{1,0:T(8,128)(2,1)}, u32[]{:S(2)}, u32[]{:S(2)}) collective-permute-start(bf16[256,1024]{1,0:T(8,128)(2,1)S(1)} %pad_maximum_fusion.1.refs_8_.refs_9_), channel_id=1, source_target_pairs={{0,2},{1,3},{2,4},{3,5},{4,6},{5,7},{6,8},{7,9},{8,10},{9,11},{10,... | collective-permute-start | bytes 1572872 | tf_op jit(solution)/shard_map/ppermute | solution.py:18
  21.1 20.1 %collective-permute-start.4 = (bf16[256,1024]{1,0:T(8,128)(2,1)S(1)}, bf16[256,1024]{1,0:T(8,128)(2,1)}, u32[]{:S(2)}, u32[]{:S(2)}) collective-permute-start(bf16[256,1024]{1,0:T(8,128)(2,1)S(1)} %pad_maximum_fusion.1.refs_8_.refs_9_), channel_id=1, source_target_pairs={{0,1},{1,4},{2,3},{3,6},{4,5},{5,8},{6,7},{7,10},{8,9},{9,12},{10,... | collective-permute-start | bytes 1572872 | tf_op jit(solution)/shard_map/ppermute | solution.py:34
  21.5 35.1 %collective-permute-start.6 = (bf16[256,512]{1,0:T(8,128)(2,1)S(1)}, bf16[256,512]{1,0:T(8,128)(2,1)S(1)}, u32[]{:S(2)}, u32[]{:S(2)}) collective-permute-start(bf16[256,512]{1,0:T(8,128)(2,1)S(1)} %copy.25), channel_id=1, source_target_pairs={{0,1},{1,0},{2,3},{3,2},{4,5},{5,4},{6,7},{7,6},{8,9},{9,8},{10,11... | collective-permute-start | bytes 786440 | tf_op jit(solution)/shard_map/ppermute | solution.py:23
  24.3 0.7 copy-start.10
  25.6 0.7 copy-start.9
  26.8 14.3 %collective-permute-start.2 = (bf16[256,1024]{1,0:T(8,128)(2,1)}, bf16[256,1024]{1,0:T(8,128)(2,1)S(1)}, u32[]{:S(2)}, u32[]{:S(2)}) collective-permute-start(bf16[256,1024]{1,0:T(8,128)(2,1)} %collective-permute-done.refs_2_.refs_3_), channel_id=1, source_target_pairs={{0,1},{1,0},{2,3},{3,2},{4,5},{5,4},{6,7},{7,6},{8,9},{9,8},{10,11... | collective-permute-start | bytes 1572872 | tf_op jit(solution)/shard_map/ppermute | solution.py:23
  33.1 8.0 %collective-permute-start.5 = (bf16[256,1024]{1,0:T(8,128)(2,1)}, bf16[256,1024]{1,0:T(8,128)(2,1)}, u32[]{:S(2)}, u32[]{:S(2)}) collective-permute-start(bf16[256,1024]{1,0:T(8,128)(2,1)} %collective-permute-done.3.refs_10_.refs_11_), channel_id=1, source_target_pairs={{0,1},{1,0},{2,3},{3,2},{4,5},{5,4},{6,7},{7,6},{8,9},{9,8},{10,11... | collective-permute-start | bytes 1572872 | tf_op jit(solution)/shard_map/ppermute | solution.py:23
  35.2 0.8 copy-start.8
  41.1 0.8 copy-start.11
  56.6 0.7 copy-start.5

commit v14 on v13

--- a/solution.py
+++ b/solution.py
@@ -70,14 +70,21 @@
         device_id_type=mesh_id,
     )
     pair.start()
-    rows = joined_ref.shape[0]
     contract = (((0,), (0,)), ((), ()))
-    acc = lax.dot_general(own_ref[...], joined_ref[...], contract, preferred_element_type=jnp.float32)
+    accs = [
+        lax.dot_general(own_ref[...], joined_ref[half], contract, preferred_element_type=jnp.float32)
+        for half in range(2)
+    ]
     pair.wait()
-    acc = acc + lax.dot_general(other_ref[...], joined_land[...], contract, preferred_element_type=jnp.float32)
+    accs = [
+        accs[half] + lax.dot_general(other_ref[...], joined_land[half], contract, preferred_element_type=jnp.float32)
+        for half in range(2)
+    ]
     _, _, share, lanes = part_ref.shape
+    features = joined_ref.shape[2]
     for index in range(spread):
-        part_ref[index] = acc[:, index * lanes:(index + 1) * lanes].reshape(groups, share, lanes)
+        half, column = divmod(index * lanes, features)
+        part_ref[index] = accs[half][:, column:column + lanes].reshape(groups, share, lanes)
     sent[...] = part_ref[...].astype(sent.dtype)
     copies = []
     for step in range(1, spread):
@@ -138,7 +145,8 @@
 
 
 def reduce_blocks(own, other, joined, share, spread):
-    rows, width = joined.shape
+    _, rows, features = joined.shape
+    width = 2 * features
     groups = own.shape[1] // share
     lanes = width // spread
     vmem = pl.BlockSpec(memory_space=pltpu.VMEM)
@@ -148,7 +156,7 @@
         out_specs=vmem,
         out_shape=jax.ShapeDtypeStruct((spread, share, lanes), jnp.float32),
         scratch_shapes=[
-            pltpu.VMEM((rows, width), jnp.bfloat16),
+            pltpu.VMEM((2, rows, features), jnp.bfloat16),
             pltpu.VMEM((spread, groups, share, lanes), jnp.float32),
             pltpu.VMEM((spread, groups, share, lanes), jnp.bfloat16),
             pltpu.VMEM((spread, groups, share, lanes), jnp.bfloat16),
@@ -179,7 +187,7 @@
     gs = refs[1:count:2]
     ks = refs[count:2 * count:2]
     vs = refs[count + 1:2 * count:2]
-    out_ref, dq_ref, dk_ref, dv_ref = refs[2 * count:]
+    out_ref, dqk_ref, dv_ref = refs[2 * count:]
     lanes = 2 * span + 1
 
     def valid(qa, ka):
@@ -220,8 +228,8 @@
         dk = dk + b
         dv = dv + c
     out_ref[...] = out.astype(out_ref.dtype)
-    dq_ref[...] = dq.astype(dq_ref.dtype)
-    dk_ref[...] = dk.astype(dk_ref.dtype)
+    dqk_ref[0] = dq.astype(dqk_ref.dtype)
+    dqk_ref[1] = dk.astype(dqk_ref.dtype)
     dv_ref[...] = dv.astype(dv_ref.dtype)
 
 
@@ -241,8 +249,8 @@
         functools.partial(tiles_kernel, span, alpha, scale),
         grid=(nheads,),
         in_specs=specs,
-        out_specs=[blk(0)] * 4,
-        out_shape=[shape] * 4,
+        out_specs=[blk(0), pl.BlockSpec((2, rows, HD), lambda h: (0, 0, h)), blk(0)],
+        out_shape=[shape, jax.ShapeDtypeStruct((2, rows, nheads * HD), jnp.bfloat16), shape],
         cost_estimate=pl.CostEstimate(
             flops=nheads * (2 * span + 1) * 5 * tile,
             transcendentals=nheads * (2 * span + 1) * rows * rows,
@@ -332,12 +340,11 @@
         [d[0] for d in described] + [d[1] for d in described] + [d[2].astype(jnp.int32) for d in described]
     ).astype(jnp.int32)
     infoc = infor.T
-    out_b, dq_b, dk_b, dv_b = attention_tiles(
+    out_b, joined, dv_b = attention_tiles(
         [qg] + qg_from[1:], [kv] + kv_from[1:], infoc, infor, nheads, alpha, scale
     )
     attended = out_b.reshape(1, rows, features)
     grad_values = dv_b.reshape(1, rows, features)
-    joined = jnp.concatenate([dq_b, dk_b], axis=1)
     mine = reduce_rows(own_events, other_events, joined, share)
     grad_wq = mine[:, :features].astype(jnp.bfloat16)
     grad_wk = mine[:, features:].astype(jnp.bfloat16)

time: 107 us -> 106 us (level)
  other arithmetic: 3.91 us -> 2.04 us
    concatenate x1 -> x0, other arithmetic: 1.87 us -> none  [body(): joined = jnp.concatenate([dq_b, dk_b], axis=1)]
  transfers between devices with their start and end apart: 7 -> 7, of which waited for: 2 -> 2; matrix products, arithmetic and copies ran while one was open for 5% -> 4% of each run, Pallas kernels for 12% -> 12%
where the time goes in v14:
time: 106 us; the launch traced here: 105 us
  Pallas kernels  60.5 us (57%)
  starting transfers between devices  23.3 us (22%)
  waiting for transfers between devices  8.27 us (8%)
  local copies, waits for them, and re-layouts  6.81 us (6%)
  other arithmetic  2.04 us (2%)
  matrix products  1.9 us (2%)
  between operations  1.78 us (2%)
    pallas_call x1, Pallas kernels, reduce_blocks(): pl.pallas_call(functools.partial(reduce_kernel, groups, spread), in_specs...  47.7 us
    pallas_call x1, Pallas kernels, attention_tiles(): pl.pallas_call(functools.partial(tiles_kernel, span, alpha, scale), grid=...  12.8 us
    ppermute x2, starting transfers between devices, relayed(): mixed = lax.ppermute(value, 'ctx', pairs)  8.69 us
    ppermute x2, starting transfers between devices, shifted(): return lax.ppermute(value, axis, pairs)  8.38 us
    ppermute x3, starting transfers between devices, exchange(): lax.ppermute(value, axis, [(source, source ^ mask) for source in range(co...  6.24 us
    ppermute x2, waiting for transfers between devices, relayed(): mixed = lax.ppermute(value, 'ctx', pairs)  4.33 us
    unnamed x25, local copies, waits for them, and re-layouts  4.22 us
    ppermute x2, waiting for transfers between devices, shifted(): return lax.ppermute(value, axis, pairs)  3.94 us
  transfers between devices with their start and end apart: 7, of which 2 were waited for; matrix products, arithmetic and copies ran while one was open for 4% of the time, Pallas kernels for 12%

profile of v14, /device:TPU:6, one launch (start us, length us, event | category | flops | bytes accessed | tf_op | source)
XLA Modules:
  0.0 104.6 jit_solution(17289628133087934473)
XLA Ops:
  0.7 1.2 %copy-done = bf16[1024,512]{1,0:T(8,128)(2,1)S(1)} copy-done((bf16[1024,512]{1,0:T(8,128)(2,1)S(1)}, bf16[1024,512]{1,0:T(8,128)(2,1)}, u32[]{:S(2)}) %copy-start) | copy-done | bytes 1048600
  1.9 1.5 %convolution_convert_fusion.1 = bf16[256,512]{1,0:T(8,128)(2,1)S(1)} fusion(bf16[1024,512]{1,0:T(8,128)(2,1)S(1)} %copy-done, bf16[1,256,1024]{2,1,0:T(8,128)(2,1)} %param.8), kind=kOutput, calls=%fused_computation.1 | convolution fusion | flops 268566528 | bytes 1835008 | tf_op jit(solution)/shard_map/dot_general | solution.py:296
  3.5 3.4 %collective-permute-start = (bf16[256,1024]{1,0:T(8,128)(2,1)S(1)}, bf16[256,1024]{1,0:T(8,128)(2,1)}, u32[]{:S(2)}, u32[]{:S(2)}) collective-permute-start(bf16[256,1024]{1,0:T(8,128)(2,1)S(1)} %pad_maximum_fusion.refs_0_.refs_1_), channel_id=1, source_target_pairs={{0,62},{1,63},{2,0},{3,1},{4,2},{5,3},{6,4},{7,5},{8,6},{9,7},{10,... | collective-permute-start | bytes 1572872 | tf_op jit(solution)/shard_map/ppermute | solution.py:18
  6.9 8.7 %collective-permute-start.1 = (bf16[256,1024]{1,0:T(8,128)(2,1)S(1)}, bf16[256,1024]{1,0:T(8,128)(2,1)}, u32[]{:S(2)}, u32[]{:S(2)}) collective-permute-start(bf16[256,1024]{1,0:T(8,128)(2,1)S(1)} %pad_maximum_fusion.refs_0_.refs_1_), channel_id=1, source_target_pairs={{0,61},{1,0},{2,63},{3,2},{4,1},{5,4},{6,3},{7,6},{8,5},{9,8},{10,... | collective-permute-start | bytes 1572872 | tf_op jit(solution)/shard_map/ppermute | solution.py:34
  15.6 0.4 convolution_convert_fusion
  16.1 4.9 %collective-permute-start.3 = (bf16[256,1024]{1,0:T(8,128)(2,1)S(1)}, bf16[256,1024]{1,0:T(8,128)(2,1)}, u32[]{:S(2)}, u32[]{:S(2)}) collective-permute-start(bf16[256,1024]{1,0:T(8,128)(2,1)S(1)} %pad_maximum_fusion.1.refs_8_.refs_9_), channel_id=1, source_target_pairs={{0,2},{1,3},{2,4},{3,5},{4,6},{5,7},{6,8},{7,9},{8,10},{9,11},{10,... | collective-permute-start | bytes 1572872 | tf_op jit(solution)/shard_map/ppermute | solution.py:18
  21.1 0.2 copy.24
  21.4 0.1 copy.25
  21.5 1.9 %collective-permute-start.6 = (bf16[256,512]{1,0:T(8,128)(2,1)S(1)}, bf16[256,512]{1,0:T(8,128)(2,1)S(1)}, u32[]{:S(2)}, u32[]{:S(2)}) collective-permute-start(bf16[256,512]{1,0:T(8,128)(2,1)S(1)} %copy.25), channel_id=1, source_target_pairs={{0,1},{1,0},{2,3},{3,2},{4,5},{5,4},{6,7},{7,6},{8,9},{9,8},{10,11... | collective-permute-start | bytes 786440 | tf_op jit(solution)/shard_map/ppermute | solution.py:23
  24.3 0.6 copy-done.10
  25.0 0.6 select_reduce_fusion
  25.7 0.6 copy-done.9
  26.8 2.4 %collective-permute-start.2 = (bf16[256,1024]{1,0:T(8,128)(2,1)}, bf16[256,1024]{1,0:T(8,128)(2,1)S(1)}, u32[]{:S(2)}, u32[]{:S(2)}) collective-permute-start(bf16[256,1024]{1,0:T(8,128)(2,1)} %collective-permute-done.refs_2_.refs_3_), channel_id=1, source_target_pairs={{0,1},{1,0},{2,3},{3,2},{4,5},{5,4},{6,7},{7,6},{8,9},{9,8},{10,11... | collective-permute-start | bytes 1572872 | tf_op jit(solution)/shard_map/ppermute | solution.py:23
  29.2 3.9 %collective-permute-done.3.refs_10_.refs_11_ = bf16[256,1024]{1,0:T(8,128)(2,1)} collective-permute-done((bf16[256,1024]{1,0:T(8,128)(2,1)S(1)}, bf16[256,1024]{1,0:T(8,128)(2,1)}, u32[]{:S(2)}, u32[]{:S(2)}) %collective-permute-start.3) | collective-permute-done | bytes 524320 | tf_op jit(solution)/shard_map/ppermute | solution.py:18
  33.1 1.9 %collective-permute-start.5 = (bf16[256,1024]{1,0:T(8,128)(2,1)}, bf16[256,1024]{1,0:T(8,128)(2,1)}, u32[]{:S(2)}, u32[]{:S(2)}) collective-permute-start(bf16[256,1024]{1,0:T(8,128)(2,1)} %collective-permute-done.3.refs_10_.refs_11_), channel_id=1, source_target_pairs={{0,1},{1,0},{2,3},{3,2},{4,5},{5,4},{6,7},{7,6},{8,9},{9,8},{10,11... | collective-permute-start | bytes 1572872 | tf_op jit(solution)/shard_map/ppermute | solution.py:23
  35.2 0.8 copy.23.infoc
  35.9 0.8 copy.26.own_ref
  36.8 4.3 %collective-permute-done.4.refs_12_.refs_13_ = bf16[256,1024]{1,0:T(8,128)(2,1)} collective-permute-done((bf16[256,1024]{1,0:T(8,128)(2,1)S(1)}, bf16[256,1024]{1,0:T(8,128)(2,1)}, u32[]{:S(2)}, u32[]{:S(2)}) %collective-permute-start.4) | collective-permute-done | bytes 524320 | tf_op jit(solution)/shard_map/ppermute | solution.py:34
  41.1 0.8 copy-done.11
  41.9 12.8 %shard_map.111 = (bf16[256,512]{1,0:T(8,128)(2,1)}, bf16[2,256,512]{2,1,0:T(8,128)(2,1)}, bf16[256,512]{1,0:T(8,128)(2,1)}) custom-call(s32[256,21]{1,0:T(8,128)} %copy.23.infoc, s32[21,256]{1,0:T(8,128)} %copy-done.8, bf16[256,1024]{1,0:T(8,128)(2,1)} %copy-done.3, bf16[256,1024]{1,0:T(8,128)(2,1)} %copy-done.3, ...), custom_call_target="tpu_custom_call" | custom-call | flops 2348810240 | bytes 9437184 | tf_op jit(solution)/shard_map/pallas_call | solution.py:248
  54.7 0.7 copy-done.5
  55.4 47.7 %shard_map.112 = f32[8,16,128]{2,1,0:T(8,128)} custom-call(bf16[256,512]{1,0:T(8,128)(2,1)} %copy.26.own_ref, bf16[256,512]{1,0:T(8,128)(2,1)} %copy-done.5, bf16[2,256,512]{2,1,0:T(8,128)(2,1)} %get-tuple-element.9.joined_ref), custom_call_target="tpu_custom_call" | custom-call | tf_op jit(solution)/shard_map/pallas_call | solution.py:153
  103.1 0.8 copy_bitcast_fusion
  103.9 0.6 fusion.16
  (51 shorter events, 0.9 us)
Async XLA Ops:
  0.6 1.2 %copy-start = (bf16[1024,512]{1,0:T(8,128)(2,1)S(1)}, bf16[1024,512]{1,0:T(8,128)(2,1)}, u32[]{:S(2)}) copy-start(bf16[1024,512]{1,0:T(8,128)(2,1)} %param.9) | copy-start | bytes 3145732
  0.6 2.7 %copy-start.6 = (bf16[1,256,512]{2,1,0:T(8,128)(2,1)S(1)}, bf16[1,256,512]{2,1,0:T(8,128)(2,1)}, u32[]{:S(2)}) copy-start(bf16[1,256,512]{2,1,0:T(8,128)(2,1)} %param.12) | copy-start | bytes 786436
  0.7 14.9 %copy-start.2 = (bf16[1024,512]{1,0:T(8,128)(2,1)S(1)}, bf16[1024,512]{1,0:T(8,128)(2,1)}, u32[]{:S(2)}) copy-start(bf16[1024,512]{1,0:T(8,128)(2,1)} %param.10) | copy-start | bytes 3145732
  3.4 12.2 %copy-start.1 = (bf16[1,256,1024]{2,1,0:T(8,128)(2,1)S(1)}, bf16[1,256,1024]{2,1,0:T(8,128)(2,1)}, u32[]{:S(2)}) copy-start(bf16[1,256,1024]{2,1,0:T(8,128)(2,1)} %param.8) | copy-start | bytes 1572868
  3.4 12.6 %copy-start.3 = (bf16[256,1024]{1,0:T(8,128)(2,1)}, bf16[256,1024]{1,0:T(8,128)(2,1)S(1)}, u32[]{:S(2)}) copy-start(bf16[256,1024]{1,0:T(8,128)(2,1)S(1)} %pad_maximum_fusion.refs_0_.refs_1_) | copy-start | bytes 1572868
  3.4 12.6 %copy-start.7 = (bf16[1,256,512]{2,1,0:T(8,128)(2,1)S(1)}, bf16[1,256,512]{2,1,0:T(8,128)(2,1)}, u32[]{:S(2)}) copy-start(bf16[1,256,512]{2,1,0:T(8,128)(2,1)} %param.11) | copy-start | bytes 786436
  3.5 23.3 %collective-permute-start = (bf16[256,1024]{1,0:T(8,128)(2,1)S(1)}, bf16[256,1024]{1,0:T(8,128)(2,1)}, u32[]{:S(2)}, u32[]{:S(2)}) collective-permute-start(bf16[256,1024]{1,0:T(8,128)(2,1)S(1)} %pad_maximum_fusion.refs_0_.refs_1_), channel_id=1, source_target_pairs={{0,62},{1,63},{2,0},{3,1},{4,2},{5,3},{6,4},{7,5},{8,6},{9,7},{10,... | collective-permute-start | bytes 1572872 | tf_op jit(solution)/shard_map/ppermute | solution.py:18
  6.9 29.9 %collective-permute-start.1 = (bf16[256,1024]{1,0:T(8,128)(2,1)S(1)}, bf16[256,1024]{1,0:T(8,128)(2,1)}, u32[]{:S(2)}, u32[]{:S(2)}) collective-permute-start(bf16[256,1024]{1,0:T(8,128)(2,1)S(1)} %pad_maximum_fusion.refs_0_.refs_1_), channel_id=1, source_target_pairs={{0,61},{1,0},{2,63},{3,2},{4,1},{5,4},{6,3},{7,6},{8,5},{9,8},{10,... | collective-permute-start | bytes 1572872 | tf_op jit(solution)/shard_map/ppermute | solution.py:34
  16.1 5.2 %copy-start.4 = (bf16[256,1024]{1,0:T(8,128)(2,1)}, bf16[256,1024]{1,0:T(8,128)(2,1)S(1)}, u32[]{:S(2)}) copy-start(bf16[256,1024]{1,0:T(8,128)(2,1)S(1)} %pad_maximum_fusion.1.refs_8_.refs_9_) | copy-start | bytes 1572868
  16.1 17.0 %collective-permute-start.3 = (bf16[256,1024]{1,0:T(8,128)(2,1)S(1)}, bf16[256,1024]{1,0:T(8,128)(2,1)}, u32[]{:S(2)}, u32[]{:S(2)}) collective-permute-start(bf16[256,1024]{1,0:T(8,128)(2,1)S(1)} %pad_maximum_fusion.1.refs_8_.refs_9_), channel_id=1, source_target_pairs={{0,2},{1,3},{2,4},{3,5},{4,6},{5,7},{6,8},{7,9},{8,10},{9,11},{10,... | collective-permute-start | bytes 1572872 | tf_op jit(solution)/shard_map/ppermute | solution.py:18
  21.1 20.1 %collective-permute-start.4 = (bf16[256,1024]{1,0:T(8,128)(2,1)S(1)}, bf16[256,1024]{1,0:T(8,128)(2,1)}, u32[]{:S(2)}, u32[]{:S(2)}) collective-permute-start(bf16[256,1024]{1,0:T(8,128)(2,1)S(1)} %pad_maximum_fusion.1.refs_8_.refs_9_), channel_id=1, source_target_pairs={{0,1},{1,4},{2,3},{3,6},{4,5},{5,8},{6,7},{7,10},{8,9},{9,12},{10,... | collective-permute-start | bytes 1572872 | tf_op jit(solution)/shard_map/ppermute | solution.py:34
  21.5 33.2 %collective-permute-start.6 = (bf16[256,512]{1,0:T(8,128)(2,1)S(1)}, bf16[256,512]{1,0:T(8,128)(2,1)S(1)}, u32[]{:S(2)}, u32[]{:S(2)}) collective-permute-start(bf16[256,512]{1,0:T(8,128)(2,1)S(1)} %copy.25), channel_id=1, source_target_pairs={{0,1},{1,0},{2,3},{3,2},{4,5},{5,4},{6,7},{7,6},{8,9},{9,8},{10,11... | collective-permute-start | bytes 786440 | tf_op jit(solution)/shard_map/ppermute | solution.py:23
  24.3 0.7 copy-start.10
  25.6 0.7 copy-start.9
  26.8 14.3 %collective-permute-start.2 = (bf16[256,1024]{1,0:T(8,128)(2,1)}, bf16[256,1024]{1,0:T(8,128)(2,1)S(1)}, u32[]{:S(2)}, u32[]{:S(2)}) collective-permute-start(bf16[256,1024]{1,0:T(8,128)(2,1)} %collective-permute-done.refs_2_.refs_3_), channel_id=1, source_target_pairs={{0,1},{1,0},{2,3},{3,2},{4,5},{5,4},{6,7},{7,6},{8,9},{9,8},{10,11... | collective-permute-start | bytes 1572872 | tf_op jit(solution)/shard_map/ppermute | solution.py:23
  33.1 8.0 %collective-permute-start.5 = (bf16[256,1024]{1,0:T(8,128)(2,1)}, bf16[256,1024]{1,0:T(8,128)(2,1)}, u32[]{:S(2)}, u32[]{:S(2)}) collective-permute-start(bf16[256,1024]{1,0:T(8,128)(2,1)} %collective-permute-done.3.refs_10_.refs_11_), channel_id=1, source_target_pairs={{0,1},{1,0},{2,3},{3,2},{4,5},{5,4},{6,7},{7,6},{8,9},{9,8},{10,11... | collective-permute-start | bytes 1572872 | tf_op jit(solution)/shard_map/ppermute | solution.py:23
  35.2 0.8 copy-start.8
  41.1 0.8 copy-start.11
  54.7 0.7 copy-start.5

commit v15 on v14

--- a/solution.py
+++ b/solution.py
@@ -46,7 +46,7 @@
     )
 
 
-def reduce_kernel(groups, spread, own_ref, other_ref, joined_ref, out_ref, joined_land, part_ref, sent, landed, sums, mixed, finals, sems):
+def reduce_kernel(groups, spread, own_ref, other_ref, joined_ref, wq_ref, wk_ref, joined_land, part_ref, sent, landed, sums, mixed, finals, sems):
     me = lax.axis_index("ctx")
     group = lax.axis_index("dp")
     core = me % 2
@@ -141,7 +141,10 @@
         copies.append(copy)
     for copy in copies:
         copy.wait()
-    out_ref[...] = finals[...]
+    for index in range(spread):
+        half, column = divmod(index * lanes, features)
+        target = (wq_ref, wk_ref)[half]
+        target[:, column:column + lanes] = finals[index].astype(target.dtype)
 
 
 def reduce_blocks(own, other, joined, share, spread):
@@ -150,11 +153,11 @@
     groups = own.shape[1] // share
     lanes = width // spread
     vmem = pl.BlockSpec(memory_space=pltpu.VMEM)
-    finals = pl.pallas_call(
+    return pl.pallas_call(
         functools.partial(reduce_kernel, groups, spread),
         in_specs=[vmem, vmem, vmem],
-        out_specs=vmem,
-        out_shape=jax.ShapeDtypeStruct((spread, share, lanes), jnp.float32),
+        out_specs=[vmem, vmem],
+        out_shape=[jax.ShapeDtypeStruct((share, features), jnp.bfloat16)] * 2,
         scratch_shapes=[
             pltpu.VMEM((2, rows, features), jnp.bfloat16),
             pltpu.VMEM((spread, groups, share, lanes), jnp.float32),
@@ -167,7 +170,6 @@
         ],
         compiler_params=pltpu.CompilerParams(collective_id=1, has_side_effects=True),
     )(own, other, joined)
-    return finals.transpose(1, 0, 2).reshape(share, width)
 
 
 def select_features(events, share, bit):
@@ -345,9 +347,7 @@
     )
     attended = out_b.reshape(1, rows, features)
     grad_values = dv_b.reshape(1, rows, features)
-    mine = reduce_rows(own_events, other_events, joined, share)
-    grad_wq = mine[:, :features].astype(jnp.bfloat16)
-    grad_wk = mine[:, features:].astype(jnp.bfloat16)
+    grad_wq, grad_wk = reduce_rows(own_events, other_events, joined, share)
     return (attended, grad_values, grad_wq, grad_wk)
 
 

time: 106 us -> 106 us (level)
    unnamed x25 -> x27, local copies, waits for them, and re-layouts: 4.22 us -> 5.37 us
where the time goes in v15:
time: 106 us; the launch traced here: 105 us
  Pallas kernels  60.8 us (57%)
  starting transfers between devices  23.3 us (22%)
  waiting for transfers between devices  8.27 us (8%)
  local copies, waits for them, and re-layouts  7.34 us (7%)
  matrix products  1.9 us (2%)
  between operations  1.78 us (2%)
  other arithmetic  1.2 us (1%)
    pallas_call x1, Pallas kernels, reduce_blocks(): pl.pallas_call(functools.partial(reduce_kernel, groups, spread), in_specs...  48 us
    pallas_call x1, Pallas kernels, attention_tiles(): pl.pallas_call(functools.partial(tiles_kernel, span, alpha, scale), grid=...  12.8 us
    ppermute x2, starting transfers between devices, relayed(): mixed = lax.ppermute(value, 'ctx', pairs)  8.69 us
    ppermute x2, starting transfers between devices, shifted(): return lax.ppermute(value, axis, pairs)  8.38 us
    ppermute x3, starting transfers between devices, exchange(): lax.ppermute(value, axis, [(source, source ^ mask) for source in range(co...  6.24 us
    unnamed x27, local copies, waits for them, and re-layouts  5.37 us
    ppermute x2, waiting for transfers between devices, relayed(): mixed = lax.ppermute(value, 'ctx', pairs)  4.33 us
    ppermute x2, waiting for transfers between devices, shifted(): return lax.ppermute(value, axis, pairs)  3.93 us
  transfers between devices with their start and end apart: 7, of which 2 were waited for; matrix products, arithmetic and copies ran while one was open for 4% of the time, Pallas kernels for 12%

profile of v15, /device:TPU:6, one launch (start us, length us, event | category | flops | bytes accessed | tf_op | source)
XLA Modules:
  0.0 104.6 jit_solution(3934654663013987872)
XLA Ops:
  0.7 1.2 %copy-done = bf16[1024,512]{1,0:T(8,128)(2,1)S(1)} copy-done((bf16[1024,512]{1,0:T(8,128)(2,1)S(1)}, bf16[1024,512]{1,0:T(8,128)(2,1)}, u32[]{:S(2)}) %copy-start) | copy-done | bytes 1048600
  1.9 1.5 %convolution_convert_fusion.1 = bf16[256,512]{1,0:T(8,128)(2,1)S(1)} fusion(bf16[1024,512]{1,0:T(8,128)(2,1)S(1)} %copy-done, bf16[1,256,1024]{2,1,0:T(8,128)(2,1)} %param.8), kind=kOutput, calls=%fused_computation.1 | convolution fusion | flops 268566528 | bytes 1835008 | tf_op jit(solution)/shard_map/dot_general | solution.py:298
  3.5 3.4 %collective-permute-start = (bf16[256,1024]{1,0:T(8,128)(2,1)S(1)}, bf16[256,1024]{1,0:T(8,128)(2,1)}, u32[]{:S(2)}, u32[]{:S(2)}) collective-permute-start(bf16[256,1024]{1,0:T(8,128)(2,1)S(1)} %pad_maximum_fusion.refs_0_.refs_1_), channel_id=1, source_target_pairs={{0,62},{1,63},{2,0},{3,1},{4,2},{5,3},{6,4},{7,5},{8,6},{9,7},{10,... | collective-permute-start | bytes 1572872 | tf_op jit(solution)/shard_map/ppermute | solution.py:18
  6.9 8.7 %collective-permute-start.1 = (bf16[256,1024]{1,0:T(8,128)(2,1)S(1)}, bf16[256,1024]{1,0:T(8,128)(2,1)}, u32[]{:S(2)}, u32[]{:S(2)}) collective-permute-start(bf16[256,1024]{1,0:T(8,128)(2,1)S(1)} %pad_maximum_fusion.refs_0_.refs_1_), channel_id=1, source_target_pairs={{0,61},{1,0},{2,63},{3,2},{4,1},{5,4},{6,3},{7,6},{8,5},{9,8},{10,... | collective-permute-start | bytes 1572872 | tf_op jit(solution)/shard_map/ppermute | solution.py:34
  15.6 0.4 convolution_convert_fusion
  16.1 4.9 %collective-permute-start.3 = (bf16[256,1024]{1,0:T(8,128)(2,1)S(1)}, bf16[256,1024]{1,0:T(8,128)(2,1)}, u32[]{:S(2)}, u32[]{:S(2)}) collective-permute-start(bf16[256,1024]{1,0:T(8,128)(2,1)S(1)} %pad_maximum_fusion.1.refs_8_.refs_9_), channel_id=1, source_target_pairs={{0,2},{1,3},{2,4},{3,5},{4,6},{5,7},{6,8},{7,9},{8,10},{9,11},{10,... | collective-permute-start | bytes 1572872 | tf_op jit(solution)/shard_map/ppermute | solution.py:18
  21.1 0.2 copy.23
  21.4 0.1 copy.24
  21.5 1.9 %collective-permute-start.6 = (bf16[256,512]{1,0:T(8,128)(2,1)S(1)}, bf16[256,512]{1,0:T(8,128)(2,1)S(1)}, u32[]{:S(2)}, u32[]{:S(2)}) collective-permute-start(bf16[256,512]{1,0:T(8,128)(2,1)S(1)} %copy.24), channel_id=1, source_target_pairs={{0,1},{1,0},{2,3},{3,2},{4,5},{5,4},{6,7},{7,6},{8,9},{9,8},{10,11... | collective-permute-start | bytes 786440 | tf_op jit(solution)/shard_map/ppermute | solution.py:23
  24.3 0.6 copy-done.11
  25.0 0.6 select_reduce_fusion
  25.7 0.6 copy-done.10
  26.6 0.1 convert_reduce_fusion
  26.8 2.4 %collective-permute-start.2 = (bf16[256,1024]{1,0:T(8,128)(2,1)}, bf16[256,1024]{1,0:T(8,128)(2,1)}, u32[]{:S(2)}, u32[]{:S(2)}) collective-permute-start(bf16[256,1024]{1,0:T(8,128)(2,1)} %collective-permute-done.refs_2_.refs_3_), channel_id=1, source_target_pairs={{0,1},{1,0},{2,3},{3,2},{4,5},{5,4},{6,7},{7,6},{8,9},{9,8},{10,11... | collective-permute-start | bytes 1572872 | tf_op jit(solution)/shard_map/ppermute | solution.py:23
  29.2 3.9 %collective-permute-done.3.refs_10_.refs_11_ = bf16[256,1024]{1,0:T(8,128)(2,1)} collective-permute-done((bf16[256,1024]{1,0:T(8,128)(2,1)S(1)}, bf16[256,1024]{1,0:T(8,128)(2,1)}, u32[]{:S(2)}, u32[]{:S(2)}) %collective-permute-start.3) | collective-permute-done | bytes 524320 | tf_op jit(solution)/shard_map/ppermute | solution.py:18
  33.1 1.9 %collective-permute-start.5 = (bf16[256,1024]{1,0:T(8,128)(2,1)}, bf16[256,1024]{1,0:T(8,128)(2,1)}, u32[]{:S(2)}, u32[]{:S(2)}) collective-permute-start(bf16[256,1024]{1,0:T(8,128)(2,1)} %collective-permute-done.3.refs_10_.refs_11_), channel_id=1, source_target_pairs={{0,1},{1,0},{2,3},{3,2},{4,5},{5,4},{6,7},{7,6},{8,9},{9,8},{10,11... | collective-permute-start | bytes 1572872 | tf_op jit(solution)/shard_map/ppermute | solution.py:23
  35.2 0.8 copy.22.infoc
  35.9 0.8 copy.25.own_ref
  36.8 4.3 %collective-permute-done.4.refs_12_.refs_13_ = bf16[256,1024]{1,0:T(8,128)(2,1)} collective-permute-done((bf16[256,1024]{1,0:T(8,128)(2,1)S(1)}, bf16[256,1024]{1,0:T(8,128)(2,1)}, u32[]{:S(2)}, u32[]{:S(2)}) %collective-permute-start.4) | collective-permute-done | bytes 524320 | tf_op jit(solution)/shard_map/ppermute | solution.py:34
  41.1 12.8 %shard_map.111 = (bf16[256,512]{1,0:T(8,128)(2,1)}, bf16[2,256,512]{2,1,0:T(8,128)(2,1)}, bf16[256,512]{1,0:T(8,128)(2,1)}) custom-call(s32[256,21]{1,0:T(8,128)} %copy.22.infoc, s32[21,256]{1,0:T(8,128)} %copy-done.8, bf16[256,1024]{1,0:T(8,128)(2,1)} %copy-done.3, bf16[256,1024]{1,0:T(8,128)(2,1)} %copy-done.3, ...), custom_call_target="tpu_custom_call" | custom-call | flops 2348810240 | bytes 9437184 | tf_op jit(solution)/shard_map/pallas_call | solution.py:250
  53.9 0.7 copy-done.7
  54.6 48.0 %shard_map.112 = (bf16[16,512]{1,0:T(8,128)(2,1)}, bf16[16,512]{1,0:T(8,128)(2,1)}) custom-call(bf16[256,512]{1,0:T(8,128)(2,1)} %copy.25.own_ref, bf16[256,512]{1,0:T(8,128)(2,1)} %copy-done.7, bf16[2,256,512]{2,1,0:T(8,128)(2,1)} %get-tuple-element.11.joined_ref), custom_call_target="tpu_custom_call" | custom-call | tf_op jit(solution)/shard_map/pallas_call | solution.py:156
  102.6 1.3 %copy.29 = bf16[16,512]{1,0:T(8,128)(2,1)} copy(bf16[16,512]{1,0:T(8,128)(2,1)} %get-tuple-element.56) | data formatting | bytes 32768
  103.9 0.6 copy.30
  (51 shorter events, 0.8 us)
Async XLA Ops:
  0.6 1.2 %copy-start = (bf16[1024,512]{1,0:T(8,128)(2,1)S(1)}, bf16[1024,512]{1,0:T(8,128)(2,1)}, u32[]{:S(2)}) copy-start(bf16[1024,512]{1,0:T(8,128)(2,1)} %param.9) | copy-start | bytes 3145732
  0.6 2.7 %copy-start.5 = (bf16[1,256,512]{2,1,0:T(8,128)(2,1)S(1)}, bf16[1,256,512]{2,1,0:T(8,128)(2,1)}, u32[]{:S(2)}) copy-start(bf16[1,256,512]{2,1,0:T(8,128)(2,1)} %param.12) | copy-start | bytes 786436
  0.7 14.9 %copy-start.2 = (bf16[1024,512]{1,0:T(8,128)(2,1)S(1)}, bf16[1024,512]{1,0:T(8,128)(2,1)}, u32[]{:S(2)}) copy-start(bf16[1024,512]{1,0:T(8,128)(2,1)} %param.10) | copy-start | bytes 3145732
  3.4 12.2 %copy-start.1 = (bf16[1,256,1024]{2,1,0:T(8,128)(2,1)S(1)}, bf16[1,256,1024]{2,1,0:T(8,128)(2,1)}, u32[]{:S(2)}) copy-start(bf16[1,256,1024]{2,1,0:T(8,128)(2,1)} %param.8) | copy-start | bytes 1572868
  3.4 12.6 %copy-start.3 = (bf16[256,1024]{1,0:T(8,128)(2,1)}, bf16[256,1024]{1,0:T(8,128)(2,1)S(1)}, u32[]{:S(2)}) copy-start(bf16[256,1024]{1,0:T(8,128)(2,1)S(1)} %pad_maximum_fusion.refs_0_.refs_1_) | copy-start | bytes 1572868
  3.4 12.6 %copy-start.6 = (bf16[1,256,512]{2,1,0:T(8,128)(2,1)S(1)}, bf16[1,256,512]{2,1,0:T(8,128)(2,1)}, u32[]{:S(2)}) copy-start(bf16[1,256,512]{2,1,0:T(8,128)(2,1)} %param.11) | copy-start | bytes 786436
  3.5 23.3 %collective-permute-start = (bf16[256,1024]{1,0:T(8,128)(2,1)S(1)}, bf16[256,1024]{1,0:T(8,128)(2,1)}, u32[]{:S(2)}, u32[]{:S(2)}) collective-permute-start(bf16[256,1024]{1,0:T(8,128)(2,1)S(1)} %pad_maximum_fusion.refs_0_.refs_1_), channel_id=1, source_target_pairs={{0,62},{1,63},{2,0},{3,1},{4,2},{5,3},{6,4},{7,5},{8,6},{9,7},{10,... | collective-permute-start | bytes 1572872 | tf_op jit(solution)/shard_map/ppermute | solution.py:18
  6.9 29.9 %collective-permute-start.1 = (bf16[256,1024]{1,0:T(8,128)(2,1)S(1)}, bf16[256,1024]{1,0:T(8,128)(2,1)}, u32[]{:S(2)}, u32[]{:S(2)}) collective-permute-start(bf16[256,1024]{1,0:T(8,128)(2,1)S(1)} %pad_maximum_fusion.refs_0_.refs_1_), channel_id=1, source_target_pairs={{0,61},{1,0},{2,63},{3,2},{4,1},{5,4},{6,3},{7,6},{8,5},{9,8},{10,... | collective-permute-start | bytes 1572872 | tf_op jit(solution)/shard_map/ppermute | solution.py:34
  16.1 5.2 %copy-start.4 = (bf16[256,1024]{1,0:T(8,128)(2,1)}, bf16[256,1024]{1,0:T(8,128)(2,1)S(1)}, u32[]{:S(2)}) copy-start(bf16[256,1024]{1,0:T(8,128)(2,1)S(1)} %pad_maximum_fusion.1.refs_8_.refs_9_) | copy-start | bytes 1572868
  16.1 17.0 %collective-permute-start.3 = (bf16[256,1024]{1,0:T(8,128)(2,1)S(1)}, bf16[256,1024]{1,0:T(8,128)(2,1)}, u32[]{:S(2)}, u32[]{:S(2)}) collective-permute-start(bf16[256,1024]{1,0:T(8,128)(2,1)S(1)} %pad_maximum_fusion.1.refs_8_.refs_9_), channel_id=1, source_target_pairs={{0,2},{1,3},{2,4},{3,5},{4,6},{5,7},{6,8},{7,9},{8,10},{9,11},{10,... | collective-permute-start | bytes 1572872 | tf_op jit(solution)/shard_map/ppermute | solution.py:18
  21.1 20.1 %collective-permute-start.4 = (bf16[256,1024]{1,0:T(8,128)(2,1)S(1)}, bf16[256,1024]{1,0:T(8,128)(2,1)}, u32[]{:S(2)}, u32[]{:S(2)}) collective-permute-start(bf16[256,1024]{1,0:T(8,128)(2,1)S(1)} %pad_maximum_fusion.1.refs_8_.refs_9_), channel_id=1, source_target_pairs={{0,1},{1,4},{2,3},{3,6},{4,5},{5,8},{6,7},{7,10},{8,9},{9,12},{10,... | collective-permute-start | bytes 1572872 | tf_op jit(solution)/shard_map/ppermute | solution.py:34
  21.5 32.4 %collective-permute-start.6 = (bf16[256,512]{1,0:T(8,128)(2,1)S(1)}, bf16[256,512]{1,0:T(8,128)(2,1)S(1)}, u32[]{:S(2)}, u32[]{:S(2)}) collective-permute-start(bf16[256,512]{1,0:T(8,128)(2,1)S(1)} %copy.24), channel_id=1, source_target_pairs={{0,1},{1,0},{2,3},{3,2},{4,5},{5,4},{6,7},{7,6},{8,9},{9,8},{10,11... | collective-permute-start | bytes 786440 | tf_op jit(solution)/shard_map/ppermute | solution.py:23
  24.3 0.7 copy-start.11
  25.6 0.7 copy-start.10
  26.8 14.3 %collective-permute-start.2 = (bf16[256,1024]{1,0:T(8,128)(2,1)}, bf16[256,1024]{1,0:T(8,128)(2,1)}, u32[]{:S(2)}, u32[]{:S(2)}) collective-permute-start(bf16[256,1024]{1,0:T(8,128)(2,1)} %collective-permute-done.refs_2_.refs_3_), channel_id=1, source_target_pairs={{0,1},{1,0},{2,3},{3,2},{4,5},{5,4},{6,7},{7,6},{8,9},{9,8},{10,11... | collective-permute-start | bytes 1572872 | tf_op jit(solution)/shard_map/ppermute | solution.py:23
  33.1 8.0 %collective-permute-start.5 = (bf16[256,1024]{1,0:T(8,128)(2,1)}, bf16[256,1024]{1,0:T(8,128)(2,1)}, u32[]{:S(2)}, u32[]{:S(2)}) collective-permute-start(bf16[256,1024]{1,0:T(8,128)(2,1)} %collective-permute-done.3.refs_10_.refs_11_), channel_id=1, source_target_pairs={{0,1},{1,0},{2,3},{3,2},{4,5},{5,4},{6,7},{7,6},{8,9},{9,8},{10,11... | collective-permute-start | bytes 1572872 | tf_op jit(solution)/shard_map/ppermute | solution.py:23
  35.2 0.8 copy-start.8
  53.9 0.7 copy-start.7
  102.6 1.3 %copy-start.9 = (bf16[16,512]{1,0:T(8,128)(2,1)S(1)}, bf16[16,512]{1,0:T(8,128)(2,1)}, u32[]{:S(2)}) copy-start(bf16[16,512]{1,0:T(8,128)(2,1)} %get-tuple-element.57) | copy-start | bytes 49156

commit v16 on v15

--- a/solution.py
+++ b/solution.py
@@ -338,10 +338,9 @@
     qg_from, qg_anchor = relayed(qg, myself, -1)
 
     described = [describe(anchor) for anchor in [myself] + kv_anchor + qg_anchor]
-    infor = jnp.stack(
-        [d[0] for d in described] + [d[1] for d in described] + [d[2].astype(jnp.int32) for d in described]
-    ).astype(jnp.int32)
-    infoc = infor.T
+    columns = [d[0] for d in described] + [d[1] for d in described] + [d[2].astype(jnp.int32) for d in described]
+    infor = jnp.stack(columns).astype(jnp.int32)
+    infoc = jnp.stack(columns, axis=1).astype(jnp.int32)
     out_b, joined, dv_b = attention_tiles(
         [qg] + qg_from[1:], [kv] + kv_from[1:], infoc, infor, nheads, alpha, scale
     )

time: 106 us -> 107 us (level)
  waiting for transfers between devices: 8.27 us -> 6.36 us
  local copies, waits for them, and re-layouts: 7.34 us -> 9.18 us
  Pallas kernels: 60.8 us -> 62.2 us
    another operation x2 -> x4, local copies, waits for them, and re-layouts: 0.17 us -> 2.78 us  [the longest x1 1.84 us: body(): infor = jnp.stack(columns).astype(jnp.int32)]
    ppermute x2, waiting for transfers between devices: 4.33 us -> 2.5 us  [relayed(): mixed = lax.ppermute(value, 'ctx', pairs)]
    pallas_call x1, Pallas kernels: 48 us -> 49.4 us  [reduce_blocks(): pl.pallas_call(functools.partial(reduce_kernel, groups, spread), in_specs...]
    unnamed x27 -> x25, local copies, waits for them, and re-layouts: 5.37 us -> 5.37 us
  transfers between devices with their start and end apart: 7 -> 7, of which waited for: 2 -> 2; matrix products, arithmetic and copies ran while one was open for 4% -> 5% of each run, Pallas kernels for 12% -> 12%
where the time goes in v16:
time: 107 us; the launch traced here: 106 us
  Pallas kernels  62.2 us (58%)
  starting transfers between devices  23.3 us (22%)
  local copies, waits for them, and re-layouts  9.18 us (9%)
  waiting for transfers between devices  6.36 us (6%)
  matrix products  1.9 us (2%)
  between operations  1.8 us (2%)
  other arithmetic  1.26 us (1%)
    pallas_call x1, Pallas kernels, reduce_blocks(): pl.pallas_call(functools.partial(reduce_kernel, groups, spread), in_specs...  49.4 us
    pallas_call x1, Pallas kernels, attention_tiles(): pl.pallas_call(functools.partial(tiles_kernel, span, alpha, scale), grid=...  12.8 us
    ppermute x2, starting transfers between devices, relayed(): mixed = lax.ppermute(value, 'ctx', pairs)  8.69 us
    ppermute x2, starting transfers between devices, shifted(): return lax.ppermute(value, axis, pairs)  8.38 us
    ppermute x3, starting transfers between devices, exchange(): lax.ppermute(value, axis, [(source, source ^ mask) for source in range(co...  6.24 us
    unnamed x25, local copies, waits for them, and re-layouts  5.37 us
    ppermute x2, waiting for transfers between devices, shifted(): return lax.ppermute(value, axis, pairs)  3.85 us
    ppermute x2, waiting for transfers between devices, relayed(): mixed = lax.ppermute(value, 'ctx', pairs)  2.5 us
  transfers between devices with their start and end apart: 7, of which 2 were waited for; matrix products, arithmetic and copies ran while one was open for 5% of the time, Pallas kernels for 12%

profile of v16, /device:TPU:6, one launch (start us, length us, event | category | flops | bytes accessed | tf_op | source)
XLA Modules:
  0.0 106.0 jit_solution(8094846839418389066)
XLA Ops:
  0.7 1.2 %copy-done = bf16[1024,512]{1,0:T(8,128)(2,1)S(1)} copy-done((bf16[1024,512]{1,0:T(8,128)(2,1)S(1)}, bf16[1024,512]{1,0:T(8,128)(2,1)}, u32[]{:S(2)}) %copy-start) | copy-done | bytes 1048600
  1.9 1.5 %convolution_convert_fusion.1 = bf16[256,512]{1,0:T(8,128)(2,1)S(1)} fusion(bf16[1024,512]{1,0:T(8,128)(2,1)S(1)} %copy-done, bf16[1,256,1024]{2,1,0:T(8,128)(2,1)} %param.8), kind=kOutput, calls=%fused_computation.1 | convolution fusion | flops 268566528 | bytes 1835008 | tf_op jit(solution)/shard_map/dot_general | solution.py:298
  3.5 3.4 %collective-permute-start = (bf16[256,1024]{1,0:T(8,128)(2,1)S(1)}, bf16[256,1024]{1,0:T(8,128)(2,1)}, u32[]{:S(2)}, u32[]{:S(2)}) collective-permute-start(bf16[256,1024]{1,0:T(8,128)(2,1)S(1)} %pad_maximum_fusion.refs_0_.refs_1_), channel_id=1, source_target_pairs={{0,62},{1,63},{2,0},{3,1},{4,2},{5,3},{6,4},{7,5},{8,6},{9,7},{10,... | collective-permute-start | bytes 1572872 | tf_op jit(solution)/shard_map/ppermute | solution.py:18
  6.9 8.7 %collective-permute-start.1 = (bf16[256,1024]{1,0:T(8,128)(2,1)S(1)}, bf16[256,1024]{1,0:T(8,128)(2,1)}, u32[]{:S(2)}, u32[]{:S(2)}) collective-permute-start(bf16[256,1024]{1,0:T(8,128)(2,1)S(1)} %pad_maximum_fusion.refs_0_.refs_1_), channel_id=1, source_target_pairs={{0,61},{1,0},{2,63},{3,2},{4,1},{5,4},{6,3},{7,6},{8,5},{9,8},{10,... | collective-permute-start | bytes 1572872 | tf_op jit(solution)/shard_map/ppermute | solution.py:34
  15.6 0.4 convolution_convert_fusion
  16.1 4.9 %collective-permute-start.3 = (bf16[256,1024]{1,0:T(8,128)(2,1)S(1)}, bf16[256,1024]{1,0:T(8,128)(2,1)}, u32[]{:S(2)}, u32[]{:S(2)}) collective-permute-start(bf16[256,1024]{1,0:T(8,128)(2,1)S(1)} %pad_maximum_fusion.1.refs_8_.refs_9_), channel_id=1, source_target_pairs={{0,2},{1,3},{2,4},{3,5},{4,6},{5,7},{6,8},{7,9},{8,10},{9,11},{10,... | collective-permute-start | bytes 1572872 | tf_op jit(solution)/shard_map/ppermute | solution.py:18
  21.1 0.2 copy.40
  21.4 0.1 copy.41
  21.5 1.9 %collective-permute-start.6 = (bf16[256,512]{1,0:T(8,128)(2,1)S(1)}, bf16[256,512]{1,0:T(8,128)(2,1)S(1)}, u32[]{:S(2)}, u32[]{:S(2)}) collective-permute-start(bf16[256,512]{1,0:T(8,128)(2,1)S(1)} %copy.41), channel_id=1, source_target_pairs={{0,1},{1,0},{2,3},{3,2},{4,5},{5,4},{6,7},{7,6},{8,9},{9,8},{10,11... | collective-permute-start | bytes 786440 | tf_op jit(solution)/shard_map/ppermute | solution.py:23
  24.3 0.6 copy-done.10
  25.0 0.6 select_reduce_fusion
  25.7 0.6 copy-done.9
  26.9 2.4 %collective-permute-start.2 = (bf16[256,1024]{1,0:T(8,128)(2,1)}, bf16[256,1024]{1,0:T(8,128)(2,1)}, u32[]{:S(2)}, u32[]{:S(2)}) collective-permute-start(bf16[256,1024]{1,0:T(8,128)(2,1)} %collective-permute-done.refs_2_.refs_3_), channel_id=1, source_target_pairs={{0,1},{1,0},{2,3},{3,2},{4,5},{5,4},{6,7},{7,6},{8,9},{9,8},{10,11... | collective-permute-start | bytes 1572872 | tf_op jit(solution)/shard_map/ppermute | solution.py:23
  29.3 3.9 %collective-permute-done.3.refs_10_.refs_11_ = bf16[256,1024]{1,0:T(8,128)(2,1)} collective-permute-done((bf16[256,1024]{1,0:T(8,128)(2,1)S(1)}, bf16[256,1024]{1,0:T(8,128)(2,1)}, u32[]{:S(2)}, u32[]{:S(2)}) %collective-permute-start.3) | collective-permute-done | bytes 524320 | tf_op jit(solution)/shard_map/ppermute | solution.py:18
  33.1 1.9 %collective-permute-start.5 = (bf16[256,1024]{1,0:T(8,128)(2,1)}, bf16[256,1024]{1,0:T(8,128)(2,1)}, u32[]{:S(2)}, u32[]{:S(2)}) collective-permute-start(bf16[256,1024]{1,0:T(8,128)(2,1)} %collective-permute-done.3.refs_10_.refs_11_), channel_id=1, source_target_pairs={{0,1},{1,0},{2,3},{3,2},{4,5},{5,4},{6,7},{7,6},{8,9},{9,8},{10,11... | collective-permute-start | bytes 1572872 | tf_op jit(solution)/shard_map/ppermute | solution.py:23
  35.2 0.8 copy.39.infoc
  35.9 0.8 copy.42.own_ref
  36.8 1.8 %stack.91.infor = s32[21,256]{1,0:T(8,128)} concatenate(s32[1,256]{1,0:T(1,128)S(1)} %and_select_fusion.6, s32[1,256]{1,0:T(1,128)S(1)} %get-tuple-element.35, s32[1,256]{1,0:T(1,128)S(1)} %get-tuple-element.34, s32[1,256]{1,0:T(1,128)S(1)} %get-tuple-element.33, s32[1,256]{1,0:T(1,128)S(1)} %get-tuple-element.32, s32[1,256]{1,0:T(1,128)S(1)} %get-tuple-element.31, ...), dimensions={0} | concatenate | bytes 43008 | tf_op jit(solution)/shard_map/stack | solution.py:342
  38.6 2.5 %collective-permute-done.4.refs_12_.refs_13_ = bf16[256,1024]{1,0:T(8,128)(2,1)} collective-permute-done((bf16[256,1024]{1,0:T(8,128)(2,1)S(1)}, bf16[256,1024]{1,0:T(8,128)(2,1)}, u32[]{:S(2)}, u32[]{:S(2)}) %collective-permute-start.4) | collective-permute-done | bytes 524320 | tf_op jit(solution)/shard_map/ppermute | solution.py:34
  41.1 12.8 %shard_map.111 = (bf16[256,512]{1,0:T(8,128)(2,1)}, bf16[2,256,512]{2,1,0:T(8,128)(2,1)}, bf16[256,512]{1,0:T(8,128)(2,1)}) custom-call(s32[256,21]{1,0:T(8,128)} %copy.39.infoc, s32[21,256]{1,0:T(8,128)} %stack.91.infor, bf16[256,1024]{1,0:T(8,128)(2,1)} %copy-done.3, bf16[256,1024]{1,0:T(8,128)(2,1)} %copy-done.3, ...), custom_call_target="tpu_custom_call" | custom-call | flops 2348810240 | bytes 9437184 | tf_op jit(solution)/shard_map/pallas_call | solution.py:250
  53.9 0.7 copy-done.7
  54.6 49.4 %shard_map.112 = (bf16[16,512]{1,0:T(8,128)(2,1)}, bf16[16,512]{1,0:T(8,128)(2,1)}) custom-call(bf16[256,512]{1,0:T(8,128)(2,1)} %copy.42.own_ref, bf16[256,512]{1,0:T(8,128)(2,1)} %copy-done.7, bf16[2,256,512]{2,1,0:T(8,128)(2,1)} %get-tuple-element.11.joined_ref), custom_call_target="tpu_custom_call" | custom-call | tf_op jit(solution)/shard_map/pallas_call | solution.py:156
  104.1 1.3 %copy.46 = bf16[16,512]{1,0:T(8,128)(2,1)} copy(bf16[16,512]{1,0:T(8,128)(2,1)} %get-tuple-element.62) | data formatting | bytes 32768
  105.4 0.6 copy.47
  (54 shorter events, 1.0 us)
Async XLA Ops:
  0.6 1.2 %copy-start = (bf16[1024,512]{1,0:T(8,128)(2,1)S(1)}, bf16[1024,512]{1,0:T(8,128)(2,1)}, u32[]{:S(2)}) copy-start(bf16[1024,512]{1,0:T(8,128)(2,1)} %param.9) | copy-start | bytes 3145732
  0.6 2.7 %copy-start.5 = (bf16[1,256,512]{2,1,0:T(8,128)(2,1)S(1)}, bf16[1,256,512]{2,1,0:T(8,128)(2,1)}, u32[]{:S(2)}) copy-start(bf16[1,256,512]{2,1,0:T(8,128)(2,1)} %param.12) | copy-start | bytes 786436
  0.7 14.9 %copy-start.2 = (bf16[1024,512]{1,0:T(8,128)(2,1)S(1)}, bf16[1024,512]{1,0:T(8,128)(2,1)}, u32[]{:S(2)}) copy-start(bf16[1024,512]{1,0:T(8,128)(2,1)} %param.10) | copy-start | bytes 3145732
  3.4 12.2 %copy-start.1 = (bf16[1,256,1024]{2,1,0:T(8,128)(2,1)S(1)}, bf16[1,256,1024]{2,1,0:T(8,128)(2,1)}, u32[]{:S(2)}) copy-start(bf16[1,256,1024]{2,1,0:T(8,128)(2,1)} %param.8) | copy-start | bytes 1572868
  3.4 12.6 %copy-start.3 = (bf16[256,1024]{1,0:T(8,128)(2,1)}, bf16[256,1024]{1,0:T(8,128)(2,1)S(1)}, u32[]{:S(2)}) copy-start(bf16[256,1024]{1,0:T(8,128)(2,1)S(1)} %pad_maximum_fusion.refs_0_.refs_1_) | copy-start | bytes 1572868
  3.4 12.6 %copy-start.6 = (bf16[1,256,512]{2,1,0:T(8,128)(2,1)S(1)}, bf16[1,256,512]{2,1,0:T(8,128)(2,1)}, u32[]{:S(2)}) copy-start(bf16[1,256,512]{2,1,0:T(8,128)(2,1)} %param.11) | copy-start | bytes 786436
  3.5 23.4 %collective-permute-start = (bf16[256,1024]{1,0:T(8,128)(2,1)S(1)}, bf16[256,1024]{1,0:T(8,128)(2,1)}, u32[]{:S(2)}, u32[]{:S(2)}) collective-permute-start(bf16[256,1024]{1,0:T(8,128)(2,1)S(1)} %pad_maximum_fusion.refs_0_.refs_1_), channel_id=1, source_target_pairs={{0,62},{1,63},{2,0},{3,1},{4,2},{5,3},{6,4},{7,5},{8,6},{9,7},{10,... | collective-permute-start | bytes 1572872 | tf_op jit(solution)/shard_map/ppermute | solution.py:18
  6.9 31.7 %collective-permute-start.1 = (bf16[256,1024]{1,0:T(8,128)(2,1)S(1)}, bf16[256,1024]{1,0:T(8,128)(2,1)}, u32[]{:S(2)}, u32[]{:S(2)}) collective-permute-start(bf16[256,1024]{1,0:T(8,128)(2,1)S(1)} %pad_maximum_fusion.refs_0_.refs_1_), channel_id=1, source_target_pairs={{0,61},{1,0},{2,63},{3,2},{4,1},{5,4},{6,3},{7,6},{8,5},{9,8},{10,... | collective-permute-start | bytes 1572872 | tf_op jit(solution)/shard_map/ppermute | solution.py:34
  16.1 5.2 %copy-start.4 = (bf16[256,1024]{1,0:T(8,128)(2,1)}, bf16[256,1024]{1,0:T(8,128)(2,1)S(1)}, u32[]{:S(2)}) copy-start(bf16[256,1024]{1,0:T(8,128)(2,1)S(1)} %pad_maximum_fusion.1.refs_8_.refs_9_) | copy-start | bytes 1572868
  16.1 17.0 %collective-permute-start.3 = (bf16[256,1024]{1,0:T(8,128)(2,1)S(1)}, bf16[256,1024]{1,0:T(8,128)(2,1)}, u32[]{:S(2)}, u32[]{:S(2)}) collective-permute-start(bf16[256,1024]{1,0:T(8,128)(2,1)S(1)} %pad_maximum_fusion.1.refs_8_.refs_9_), channel_id=1, source_target_pairs={{0,2},{1,3},{2,4},{3,5},{4,6},{5,7},{6,8},{7,9},{8,10},{9,11},{10,... | collective-permute-start | bytes 1572872 | tf_op jit(solution)/shard_map/ppermute | solution.py:18
  21.1 20.1 %collective-permute-start.4 = (bf16[256,1024]{1,0:T(8,128)(2,1)S(1)}, bf16[256,1024]{1,0:T(8,128)(2,1)}, u32[]{:S(2)}, u32[]{:S(2)}) collective-permute-start(bf16[256,1024]{1,0:T(8,128)(2,1)S(1)} %pad_maximum_fusion.1.refs_8_.refs_9_), channel_id=1, source_target_pairs={{0,1},{1,4},{2,3},{3,6},{4,5},{5,8},{6,7},{7,10},{8,9},{9,12},{10,... | collective-permute-start | bytes 1572872 | tf_op jit(solution)/shard_map/ppermute | solution.py:34
  21.5 32.4 %collective-permute-start.6 = (bf16[256,512]{1,0:T(8,128)(2,1)S(1)}, bf16[256,512]{1,0:T(8,128)(2,1)S(1)}, u32[]{:S(2)}, u32[]{:S(2)}) collective-permute-start(bf16[256,512]{1,0:T(8,128)(2,1)S(1)} %copy.41), channel_id=1, source_target_pairs={{0,1},{1,0},{2,3},{3,2},{4,5},{5,4},{6,7},{7,6},{8,9},{9,8},{10,11... | collective-permute-start | bytes 786440 | tf_op jit(solution)/shard_map/ppermute | solution.py:23
  24.3 0.7 copy-start.10
  25.7 0.7 copy-start.9
  26.9 14.3 %collective-permute-start.2 = (bf16[256,1024]{1,0:T(8,128)(2,1)}, bf16[256,1024]{1,0:T(8,128)(2,1)}, u32[]{:S(2)}, u32[]{:S(2)}) collective-permute-start(bf16[256,1024]{1,0:T(8,128)(2,1)} %collective-permute-done.refs_2_.refs_3_), channel_id=1, source_target_pairs={{0,1},{1,0},{2,3},{3,2},{4,5},{5,4},{6,7},{7,6},{8,9},{9,8},{10,11... | collective-permute-start | bytes 1572872 | tf_op jit(solution)/shard_map/ppermute | solution.py:23
  33.1 8.0 %collective-permute-start.5 = (bf16[256,1024]{1,0:T(8,128)(2,1)}, bf16[256,1024]{1,0:T(8,128)(2,1)}, u32[]{:S(2)}, u32[]{:S(2)}) collective-permute-start(bf16[256,1024]{1,0:T(8,128)(2,1)} %collective-permute-done.3.refs_10_.refs_11_), channel_id=1, source_target_pairs={{0,1},{1,0},{2,3},{3,2},{4,5},{5,4},{6,7},{7,6},{8,9},{9,8},{10,11... | collective-permute-start | bytes 1572872 | tf_op jit(solution)/shard_map/ppermute | solution.py:23
  53.9 0.7 copy-start.7
  104.1 1.3 %copy-start.8 = (bf16[16,512]{1,0:T(8,128)(2,1)S(1)}, bf16[16,512]{1,0:T(8,128)(2,1)}, u32[]{:S(2)}) copy-start(bf16[16,512]{1,0:T(8,128)(2,1)} %get-tuple-element.63) | copy-start | bytes 49156
